TPU v7x, 32 devices: a whole 2x2x4 slice. The times are simulated.
32 devices in a mesh: section: 2 (over core), dp: 4 (over y, x), tensor: 4 (over z).
Axes of the slice: x: 2, y: 2, z: 4, core: 2. Of those that a mesh axis runs over, the one named last changes fastest.
Arguments:
- layer_input: bfloat16 [6, 16, 128, 768], P(None, ('dp', 'tensor')), may hold values from -6 to 6
- out_grad: bfloat16 [6, 16, 128, 768], P(None, ('dp', 'tensor')), may hold values from -6 to 6
- loss_mask: int32 [6, 16, 128], P(None, ('dp', 'tensor')), may hold values from 0 to 1, as said below
- query_key_value_weight: bfloat16 [2, 768, 3, 768], P('section', None, None, 'tensor'), may hold values from -0.21875 to 0.21875
- attention_output_weight: bfloat16 [2, 768, 768], P('section', 'tensor'), may hold values from -0.875 to 0.875
- gate_up_weight: bfloat16 [2, 768, 2, 3072], P('section', None, None, 'tensor'), may hold values from -0.21875 to 0.21875
- down_weight: bfloat16 [2, 3072, 768], P('section', 'tensor'), may hold values from -0.109375 to 0.109375
- norm1_gain: float32 [2, 768], P('section'), may hold values from 0.1 to 1.9
- norm1_bias: float32 [2, 768], P('section'), may hold values from -2.5 to 2.5
- norm2_gain: float32 [2, 768], P('section'), may hold values from 0.1 to 1.9
- norm2_bias: float32 [2, 768], P('section'), may hold values from -2.5 to 2.5
Outputs:
- layer_out: bfloat16 [2, 6, 16, 128, 768], P('section', None, ('dp', 'tensor'))
- input_grad: float32 [2, 6, 16, 128, 768], P('section', None, ('dp', 'tensor'))
- grad_qkv: float32 [2, 768, 3, 768], P('section', None, None, 'tensor')
- grad_out: float32 [2, 768, 768], P('section', 'tensor')
- grad_in: float32 [2, 768, 2, 3072], P('section', None, None, 'tensor')
- grad_down: float32 [2, 3072, 768], P('section', 'tensor')
- grad_norm1_gain: float32 [2, 768], P('section', 'tensor')
- grad_norm1_bias: float32 [2, 768], P('section', 'tensor')
- grad_norm2_gain: float32 [2, 768], P('section', 'tensor')
- grad_norm2_bias: float32 [2, 768], P('section', 'tensor')
Inputs may be any that keep to these rules, and one draw needn't show every extreme that they name: loss_mask holds 0 or 1; each sequence has 8 to 32 ones, and in every micro-batch some sequence has exactly 32.
All inputs are finite; a program needn't handle non-finite values.
Results may differ from a plain program's by a relative error of at most 0.034.
Values may be sent and summed in bfloat16 or wider, within the bound.
No kernel may reach another device: no remote copies, remote signals or barrier semaphores. Data moves between devices by JAX's collectives and lax.ppermute only.
A program may use at most 128 MiB of HBM per device.

v0:
```python
import math

import jax
import jax.numpy as jnp
import numpy as np
from jax import lax
from jax.sharding import PartitionSpec as P

HEADS = 12
HEAD_DIM = 64


NORM_EPSILON = 1e-05


def shifted(block, axis, distance):
    devices = range(lax.axis_size(axis))
    route = [(i - distance, i) for i in devices if i - distance in devices]
    return lax.ppermute(block, axis, route)


def power_slopes(total_heads):
    return [2.0 ** (-8.0 * (index + 1) / total_heads) for index in range(total_heads)]


def alibi_table(number_heads):
    closest = 2 ** int(math.floor(math.log2(number_heads)))
    slopes = power_slopes(closest)
    slopes = slopes + power_slopes(2 * closest)[0::2][: number_heads - closest]
    return np.array(slopes, dtype=np.float32)


def norm_rows(values, gain, offset):
    row_mean = jnp.mean(values, axis=-1, keepdims=True)
    centred = values - row_mean
    row_var = jnp.mean(centred * centred, axis=-1, keepdims=True)
    return centred * lax.rsqrt(row_var + NORM_EPSILON) * gain + offset


def gelu_product(gate_part, up_part):
    return jax.nn.gelu(gate_part, approximate=False) * up_part


def attention_weights(queries, key_heads, slopes):
    length = queries.shape[1]
    scores = jnp.einsum(
        "sqhe,skhe->shqk", queries, key_heads, preferred_element_type=jnp.float32
    ) * HEAD_DIM ** (-0.5)
    positions = jnp.arange(length)
    distance = jnp.abs(positions[:, None] - positions[None, :]).astype(jnp.float32)
    scores = scores - slopes[:, None, None] * distance[None, :, :]
    return jax.nn.softmax(scores, axis=-1)


def spread_rows(own_low, project):
    return project(lax.all_gather(own_low, "tensor", axis=0, tiled=True), jnp.int32(0))


def attention_total(term, row_count):
    return lax.psum_scatter(
        term(jnp.int32(0), row_count * lax.axis_size("tensor")),
        "tensor",
        scatter_dimension=0,
        tiled=True,
    )


def spread_middle(own_low, project):
    return project(lax.all_gather(own_low, "tensor", axis=0, tiled=True), jnp.int32(0))


def feed_total(term, row_count):
    return lax.psum_scatter(
        term(jnp.int32(0), row_count * lax.axis_size("tensor")),
        "tensor",
        scatter_dimension=0,
        tiled=True,
    )


def split_vectors(vectors):
    return lax.psum_scatter(vectors, "tensor", scatter_dimension=1, tiled=True)


def forward_core(own_in, weights, slopes, full):
    (
        query_key_value_weight,
        attention_output_weight,
        gate_up_weight,
        down_weight,
        gain_one,
        offset_one,
        gain_two,
        offset_two,
    ) = weights
    row_count = own_in.shape[0]
    length = own_in.shape[1]
    features = own_in.shape[2]
    local_heads = query_key_value_weight.shape[-1] // HEAD_DIM
    query_key_value_flat = query_key_value_weight.reshape(features, -1)
    input_weight_flat = gate_up_weight.reshape(features, -1)

    def project_qkv(block_row_set, first_row):
        projected_state = jnp.einsum(
            "rio,oa->ria", block_row_set, query_key_value_flat, preferred_element_type=jnp.float32
        )
        if full:
            return jnp.concatenate(
                [
                    block_row_set.astype(jnp.float32),
                    projected_state.astype(jnp.bfloat16).astype(jnp.float32),
                ],
                axis=-1,
            )
        return projected_state.astype(jnp.bfloat16)

    gathered = spread_rows(own_in.astype(jnp.bfloat16), project_qkv)
    if full:
        input_batch_every = gathered[..., :features].astype(jnp.bfloat16)
        projected_state = gathered[..., features:].astype(jnp.bfloat16)
    else:
        input_batch_every = None
        projected_state = gathered
    groups = projected_state.shape[0]
    split_heads = projected_state.reshape(groups, length, 3, local_heads, HEAD_DIM)
    queries = split_heads[:, :, 0]
    key_heads = split_heads[:, :, 1]
    value_heads = split_heads[:, :, 2]
    attention = attention_weights(queries, key_heads, slopes)
    attention_low = attention.astype(jnp.bfloat16)
    context_vectors = jnp.einsum(
        "shqk,skhe->sqhe", attention_low, value_heads, preferred_element_type=jnp.float32
    )
    context_vectors = context_vectors.astype(jnp.bfloat16).reshape(
        groups, length, local_heads * HEAD_DIM
    )

    def attention_term(first_row, row_total):
        return jnp.einsum(
            "jvp,pb->jvb",
            context_vectors,
            attention_output_weight,
            preferred_element_type=jnp.float32,
        )

    attention_output = attention_total(attention_term, row_count)
    first_sum = own_in + attention_output
    first_norm = norm_rows(first_sum, gain_one, offset_one)

    def project_feed(block_row_set, first_row):
        gated_rows = jnp.einsum(
            "rio,oa->ria", block_row_set, input_weight_flat, preferred_element_type=jnp.float32
        )
        if full:
            return jnp.concatenate([block_row_set.astype(jnp.float32), gated_rows], axis=-1)
        gate_part, up_part = jnp.split(gated_rows, 2, axis=-1)
        return gelu_product(gate_part, up_part).astype(jnp.bfloat16)

    spread = spread_middle(first_norm.astype(jnp.bfloat16), project_feed)
    if full:
        middle_every = spread[..., :features].astype(jnp.bfloat16)
        gated_product = spread[..., features:]
        gate_part, up_part = jnp.split(gated_product, 2, axis=-1)
        hidden_state = gelu_product(gate_part, up_part).astype(jnp.bfloat16)
    else:
        middle_every = None
        gated_product = None
        hidden_state = spread

    def feed_term(first_row, row_total):
        return jnp.einsum(
            "jvp,pb->jvb", hidden_state, down_weight, preferred_element_type=jnp.float32
        )

    mixed_rows = feed_total(feed_term, row_count)
    second_sum = first_norm + mixed_rows
    output = norm_rows(second_sum, gain_two, offset_two)
    if full:
        return (
            input_batch_every,
            queries,
            key_heads,
            value_heads,
            attention,
            attention_low,
            context_vectors,
            first_sum,
            middle_every,
            gated_product,
            hidden_state,
            second_sum,
        )
    return output


def backward_core(own_in, seed_grad, weights, slopes):
    (
        query_key_value_weight,
        attention_output_weight,
        gate_up_weight,
        down_weight,
        gain_one,
        offset_one,
        gain_two,
        offset_two,
    ) = weights
    features = own_in.shape[2]
    query_key_value_flat = query_key_value_weight.reshape(features, -1)
    input_weight_flat = gate_up_weight.reshape(features, -1)
    saved = forward_core(own_in, weights, slopes, True)
    (
        input_batch_every,
        queries,
        key_heads,
        value_heads,
        attention,
        attention_low,
        context_vectors,
        first_sum,
        middle_every,
        gated_product,
        hidden_state,
        second_sum,
    ) = saved
    groups = queries.shape[0]
    length = queries.shape[1]
    local_heads = queries.shape[2]
    first_norm, norm_one_back = jax.vjp(norm_rows, first_sum, gain_one, offset_one)
    _, norm_two_back = jax.vjp(norm_rows, second_sum, gain_two, offset_two)
    second_grad, gain_two_grad, offset_two_grad = norm_two_back(seed_grad)
    mixed_state_every = lax.all_gather(
        second_grad.astype(jnp.bfloat16), "tensor", axis=0, tiled=True
    )
    hidden_state_gradient = jnp.einsum(
        "tui,ai->tua", mixed_state_every, down_weight, preferred_element_type=jnp.float32
    )
    down_weight_gradient = jnp.einsum(
        "qce,qcn->en", hidden_state, mixed_state_every, preferred_element_type=jnp.float32
    )
    gate_part, up_part = jnp.split(gated_product, 2, axis=-1)
    _, gelu_back = jax.vjp(gelu_product, gate_part, up_part)
    gate_grad, up_grad = gelu_back(hidden_state_gradient)
    gated_product_gradient = jnp.concatenate([gate_grad, up_grad], axis=-1).astype(jnp.bfloat16)
    in_grad = jnp.einsum(
        "qvm,qvc->mc", middle_every, gated_product_gradient, preferred_element_type=jnp.float32
    ).reshape(gate_up_weight.shape)
    block_portion = gated_product_gradient
    first_grad = (
        lax.psum_scatter(
            jnp.einsum(
                "naz,iz->nai", block_portion, input_weight_flat, preferred_element_type=jnp.float32
            ),
            "tensor",
            scatter_dimension=0,
            tiled=True,
        )
        + second_grad
    )
    sum_grad, gain_one_grad, offset_one_grad = norm_one_back(first_grad)
    attention_output_every = lax.all_gather(
        sum_grad.astype(jnp.bfloat16), "tensor", axis=0, tiled=True
    )
    context_grad = jnp.einsum(
        "tui,ai->tua",
        attention_output_every,
        attention_output_weight,
        preferred_element_type=jnp.float32,
    ).astype(jnp.bfloat16)
    output_weight_grad = jnp.einsum(
        "qce,qcn->en", context_vectors, attention_output_every, preferred_element_type=jnp.float32
    )
    middle_results = (
        context_grad,
        output_weight_grad,
        down_weight_gradient,
        in_grad,
        sum_grad,
        gain_one_grad,
        offset_one_grad,
    )
    (
        context_grad,
        output_weight_grad,
        down_weight_gradient,
        in_grad,
        sum_grad,
        gain_one_grad,
        offset_one_grad,
    ) = middle_results
    context_heads = context_grad.reshape(groups, length, local_heads, HEAD_DIM)
    weights_grad = jnp.einsum(
        "sqhe,skhe->shqk", context_heads, value_heads, preferred_element_type=jnp.float32
    )
    value_grad = jnp.einsum(
        "shqk,sqhe->skhe", attention_low, context_heads, preferred_element_type=jnp.float32
    )
    score_grad = attention * (
        weights_grad - jnp.sum(attention * weights_grad, axis=-1, keepdims=True)
    )
    score_grad = score_grad.astype(jnp.bfloat16)
    query_grad = jnp.einsum(
        "shqk,skhe->sqhe", score_grad, key_heads, preferred_element_type=jnp.float32
    ) * HEAD_DIM ** (-0.5)
    key_grad = jnp.einsum(
        "shqk,sqhe->skhe", score_grad, queries, preferred_element_type=jnp.float32
    ) * HEAD_DIM ** (-0.5)
    projected_state_gradient = jnp.stack([query_grad, key_grad, value_grad], axis=2)
    projected_state_gradient = projected_state_gradient.reshape(groups, length, -1).astype(
        jnp.bfloat16
    )
    qkv_grad = jnp.einsum(
        "qvm,qvc->mc",
        input_batch_every,
        projected_state_gradient,
        preferred_element_type=jnp.float32,
    ).reshape(query_key_value_weight.shape)
    block_portion = projected_state_gradient
    input_rows = (
        lax.psum_scatter(
            jnp.einsum(
                "naz,iz->nai",
                block_portion,
                query_key_value_flat,
                preferred_element_type=jnp.float32,
            ),
            "tensor",
            scatter_dimension=0,
            tiled=True,
        )
        + sum_grad
    )
    vector_terms = jnp.stack([gain_one_grad, offset_one_grad, gain_two_grad, offset_two_grad])
    return (input_rows, (qkv_grad, output_weight_grad, in_grad, down_weight_gradient), vector_terms)


def body(
    layer_input,
    out_grad,
    loss_mask,
    query_key_value_weight,
    attention_output_weight,
    gate_up_weight,
    down_weight,
    norm1_gain,
    norm1_bias,
    norm2_gain,
    norm2_bias,
):
    section_rank = lax.axis_index("section")
    tensor_rank = lax.axis_index("tensor")
    micro_count = layer_input.shape[0]
    features = layer_input.shape[3]
    local_heads = query_key_value_weight.shape[-1] // HEAD_DIM
    slope_table = jnp.asarray(alibi_table(HEADS))
    slopes = lax.dynamic_slice_in_dim(slope_table, tensor_rank * local_heads, local_heads)
    weights = (
        query_key_value_weight[0],
        attention_output_weight[0],
        gate_up_weight[0],
        down_weight[0],
        norm1_gain[0],
        norm1_bias[0],
        norm2_gain[0],
        norm2_bias[0],
    )
    tick_count = micro_count + 1
    is_first = section_rank == 0
    row_shape = layer_input.shape[1:]

    def forward_tick(tick_index, loop_state):
        arrived, stored, outputs = loop_state
        slot_index = tick_index - section_rank
        in_range = (slot_index >= 0) & (slot_index < micro_count)
        safe_slot = jnp.clip(slot_index, 0, micro_count - 1)
        own_input = lax.dynamic_index_in_dim(
            layer_input, jnp.clip(tick_index, 0, micro_count - 1), 0, keepdims=False
        )
        current = jnp.where(is_first, own_input, arrived)
        result = forward_core(current.astype(jnp.float32), weights, slopes, False)
        result_low = result.astype(jnp.bfloat16)
        old_stored = lax.dynamic_index_in_dim(stored, safe_slot, 0, keepdims=False)
        stored = lax.dynamic_update_index_in_dim(
            stored, jnp.where(in_range, current, old_stored), safe_slot, 0
        )
        old_output = lax.dynamic_index_in_dim(outputs, safe_slot, 0, keepdims=False)
        outputs = lax.dynamic_update_index_in_dim(
            outputs, jnp.where(in_range, result_low, old_output), safe_slot, 0
        )
        arrived = shifted(result_low, "section", 1)
        return (arrived, stored, outputs)

    forward_start = (
        jnp.zeros(row_shape, jnp.bfloat16),
        jnp.zeros(layer_input.shape, jnp.bfloat16),
        jnp.zeros(layer_input.shape, jnp.bfloat16),
    )
    _, stored, layer_outs = lax.fori_loop(0, tick_count, forward_tick, forward_start)

    def backward_tick(tick_index, loop_state):
        arrived, totals, vectors, grads_out = loop_state
        slot_index = tick_index - (1 - section_rank)
        in_range = (slot_index >= 0) & (slot_index < micro_count)
        safe_slot = jnp.clip(slot_index, 0, micro_count - 1)
        own_in = lax.dynamic_index_in_dim(stored, safe_slot, 0, keepdims=False).astype(jnp.float32)
        top_grad = lax.dynamic_index_in_dim(out_grad, safe_slot, 0, keepdims=False).astype(
            jnp.float32
        )
        top_mask = lax.dynamic_index_in_dim(loss_mask, safe_slot, 0, keepdims=False).astype(
            jnp.float32
        )
        seed_grad = jnp.where(is_first, arrived, top_grad * top_mask[..., None])
        seed_grad = jnp.where(in_range, seed_grad, jnp.zeros_like(seed_grad))
        input_rows, matrices, vector_terms = backward_core(own_in, seed_grad, weights, slopes)
        totals = tuple((total + term for total, term in zip(totals, matrices)))
        vectors = vectors + vector_terms
        old_grad = lax.dynamic_index_in_dim(grads_out, safe_slot, 0, keepdims=False)
        grads_out = lax.dynamic_update_index_in_dim(
            grads_out, jnp.where(in_range, input_rows, old_grad), safe_slot, 0
        )
        arrived = shifted(input_rows, "section", -1)
        return (arrived, totals, vectors, grads_out)

    zero_totals = tuple((jnp.zeros(weight_item.shape, jnp.float32) for weight_item in weights[:4]))
    zero_vectors = jnp.zeros((4, features), jnp.float32)
    backward_start = (
        jnp.zeros(row_shape, jnp.float32),
        zero_totals,
        zero_vectors,
        jnp.zeros(layer_input.shape, jnp.float32),
    )
    _, totals, vectors, grads_out = lax.fori_loop(0, tick_count, backward_tick, backward_start)
    vector_slices = split_vectors(vectors)
    qkv_sum, out_sum, in_sum, down_sum, vector_slices = lax.psum(
        (totals[0], totals[1], totals[2], totals[3], vector_slices), "dp"
    )
    return (
        layer_outs[None],
        grads_out[None],
        qkv_sum[None],
        out_sum[None],
        in_sum[None],
        down_sum[None],
        vector_slices[0][None],
        vector_slices[1][None],
        vector_slices[2][None],
        vector_slices[3][None],
    )


def solution(mesh):
    placed = (
        P(None, ("dp", "tensor"), None, None),
        P(None, ("dp", "tensor"), None, None),
        P(None, ("dp", "tensor"), None),
        P("section", None, None, "tensor"),
        P("section", "tensor", None),
        P("section", None, None, "tensor"),
        P("section", "tensor", None),
        P("section", None),
        P("section", None),
        P("section", None),
        P("section", None),
    )
    return jax.shard_map(
        body,
        mesh=mesh,
        in_specs=placed,
        out_specs=(
            P("section", None, ("dp", "tensor"), None, None),
            P("section", None, ("dp", "tensor"), None, None),
            P("section", None, None, "tensor"),
            P("section", "tensor", None),
            P("section", None, None, "tensor"),
            P("section", "tensor", None),
            P("section", "tensor"),
            P("section", "tensor"),
            P("section", "tensor"),
            P("section", "tensor"),
        ),
        check_vma=False,
    )
```

profile of v0, /device:TPU:1, one launch (start us, length us, event | category | flops | bytes accessed | tf_op | source)
XLA Modules:
  0.0 2875.0 jit_solution(14754762932097729275)
XLA Ops:
  19.7 890.8 %while.47 = (s32[]{:T(128)}, bf16[1,128,768]{2,1,0:T(8,128)(2,1)S(1)}, bf16[6,1,128,768]{3,2,1,0:T(8,128)(2,1)}, bf16[6,1,128,768]{3,2,1,0:T(8,128)(2,1)}, pred[...) while((s32[]{:T(128)}, ...), condition=%wide.wide.region_9.10_spmd, body=%wide.wide.region_0.9_spmd.sunk | while | flops 2522974464 | bytes 57609232 | solution.py:397
  44.0 37.1 %reduce-scatter.12.cloned.1.call-done = f32[1,128,768]{2,1,0:T(8,128)} async-done(((f32[4,128,768]{2,1,0:T(8,128)}), f32[1,128,768]{2,1,0:T(8,128)}) %reduce-scatter.12.cloned.1.call-update) | async-done | bytes 393232 | tf_op jit(solution)/shard_map/while/body/eval_jaxpr/reduce_scatter | solution.py:60
  108.0 36.1 %reduce-scatter.14.cloned.1.call-done = f32[1,128,768]{2,1,0:T(8,128)} async-done(((f32[4,128,768]{2,1,0:T(8,128)}), f32[1,128,768]{2,1,0:T(8,128)}) %reduce-scatter.14.cloned.1.call-update) | async-done | bytes 393232 | tf_op jit(solution)/shard_map/while/body/eval_jaxpr/reduce_scatter | solution.py:73
  172.5 35.3 %reduce-scatter.12.cloned.1.call-done = f32[1,128,768]{2,1,0:T(8,128)} async-done(((f32[4,128,768]{2,1,0:T(8,128)}), f32[1,128,768]{2,1,0:T(8,128)}) %reduce-scatter.12.cloned.1.call-update) | async-done | bytes 393232 | tf_op jit(solution)/shard_map/while/body/eval_jaxpr/reduce_scatter | solution.py:60
  234.7 36.1 %reduce-scatter.14.cloned.1.call-done = f32[1,128,768]{2,1,0:T(8,128)} async-done(((f32[4,128,768]{2,1,0:T(8,128)}), f32[1,128,768]{2,1,0:T(8,128)}) %reduce-scatter.14.cloned.1.call-update) | async-done | bytes 393232 | tf_op jit(solution)/shard_map/while/body/eval_jaxpr/reduce_scatter | solution.py:73
  299.3 35.3 %reduce-scatter.12.cloned.1.call-done = f32[1,128,768]{2,1,0:T(8,128)} async-done(((f32[4,128,768]{2,1,0:T(8,128)}), f32[1,128,768]{2,1,0:T(8,128)}) %reduce-scatter.12.cloned.1.call-update) | async-done | bytes 393232 | tf_op jit(solution)/shard_map/while/body/eval_jaxpr/reduce_scatter | solution.py:60
  361.5 36.1 %reduce-scatter.14.cloned.1.call-done = f32[1,128,768]{2,1,0:T(8,128)} async-done(((f32[4,128,768]{2,1,0:T(8,128)}), f32[1,128,768]{2,1,0:T(8,128)}) %reduce-scatter.14.cloned.1.call-update) | async-done | bytes 393232 | tf_op jit(solution)/shard_map/while/body/eval_jaxpr/reduce_scatter | solution.py:73
  426.0 35.4 %reduce-scatter.12.cloned.1.call-done = f32[1,128,768]{2,1,0:T(8,128)} async-done(((f32[4,128,768]{2,1,0:T(8,128)}), f32[1,128,768]{2,1,0:T(8,128)}) %reduce-scatter.12.cloned.1.call-update) | async-done | bytes 393232 | tf_op jit(solution)/shard_map/while/body/eval_jaxpr/reduce_scatter | solution.py:60
  488.3 36.2 %reduce-scatter.14.cloned.1.call-done = f32[1,128,768]{2,1,0:T(8,128)} async-done(((f32[4,128,768]{2,1,0:T(8,128)}), f32[1,128,768]{2,1,0:T(8,128)}) %reduce-scatter.14.cloned.1.call-update) | async-done | bytes 393232 | tf_op jit(solution)/shard_map/while/body/eval_jaxpr/reduce_scatter | solution.py:73
  552.9 35.3 %reduce-scatter.12.cloned.1.call-done = f32[1,128,768]{2,1,0:T(8,128)} async-done(((f32[4,128,768]{2,1,0:T(8,128)}), f32[1,128,768]{2,1,0:T(8,128)}) %reduce-scatter.12.cloned.1.call-update) | async-done | bytes 393232 | tf_op jit(solution)/shard_map/while/body/eval_jaxpr/reduce_scatter | solution.py:60
  615.1 36.1 %reduce-scatter.14.cloned.1.call-done = f32[1,128,768]{2,1,0:T(8,128)} async-done(((f32[4,128,768]{2,1,0:T(8,128)}), f32[1,128,768]{2,1,0:T(8,128)}) %reduce-scatter.14.cloned.1.call-update) | async-done | bytes 393232 | tf_op jit(solution)/shard_map/while/body/eval_jaxpr/reduce_scatter | solution.py:73
  679.7 35.3 %reduce-scatter.12.cloned.1.call-done = f32[1,128,768]{2,1,0:T(8,128)} async-done(((f32[4,128,768]{2,1,0:T(8,128)}), f32[1,128,768]{2,1,0:T(8,128)}) %reduce-scatter.12.cloned.1.call-update) | async-done | bytes 393232 | tf_op jit(solution)/shard_map/while/body/eval_jaxpr/reduce_scatter | solution.py:60
  741.9 36.1 %reduce-scatter.14.cloned.1.call-done = f32[1,128,768]{2,1,0:T(8,128)} async-done(((f32[4,128,768]{2,1,0:T(8,128)}), f32[1,128,768]{2,1,0:T(8,128)}) %reduce-scatter.14.cloned.1.call-update) | async-done | bytes 393232 | tf_op jit(solution)/shard_map/while/body/eval_jaxpr/reduce_scatter | solution.py:73
  806.4 35.4 %reduce-scatter.12.cloned.1.call-done = f32[1,128,768]{2,1,0:T(8,128)} async-done(((f32[4,128,768]{2,1,0:T(8,128)}), f32[1,128,768]{2,1,0:T(8,128)}) %reduce-scatter.12.cloned.1.call-update) | async-done | bytes 393232 | tf_op jit(solution)/shard_map/while/body/eval_jaxpr/reduce_scatter | solution.py:60
  868.6 36.2 %reduce-scatter.14.cloned.1.call-done = f32[1,128,768]{2,1,0:T(8,128)} async-done(((f32[4,128,768]{2,1,0:T(8,128)}), f32[1,128,768]{2,1,0:T(8,128)}) %reduce-scatter.14.cloned.1.call-update) | async-done | bytes 393232 | tf_op jit(solution)/shard_map/while/body/eval_jaxpr/reduce_scatter | solution.py:73
  912.8 1752.2 %while.48 = (s32[]{:T(128)}, f32[1,128,768]{2,1,0:T(8,128)}, f32[768,3,192]{0,2,1:T(8,128)}, f32[192,768]{1,0:T(8,128)}, f32[768,2,768]{2,1,0:T(2,128)}, /*index...) while((s32[]{:T(128)}, f32[1,128,768]{2,1,0:T(8,128)}, ...), condition=%wide.wide.region_30.31_spmd.clone, body=%wide.wide.region_10.30_spmd.clone.sunk | while | flops 7453913600 | bytes 261023984 | solution.py:431
  933.9 35.3 %reduce-scatter.16.cloned.1.call-done = f32[1,128,768]{2,1,0:T(8,128)} async-done(((f32[4,128,768]{2,1,0:T(8,128)}), f32[1,128,768]{2,1,0:T(8,128)}) %reduce-scatter.16.cloned.1.call-update) | async-done | bytes 393232 | tf_op jit(solution)/shard_map/while/body/eval_jaxpr/reduce_scatter | solution.py:60
  995.0 36.4 %reduce-scatter.18.cloned.1.call-done = f32[1,128,768]{2,1,0:T(8,128)} async-done(((f32[4,128,768]{2,1,0:T(8,128)}), f32[1,128,768]{2,1,0:T(8,128)}) %reduce-scatter.18.cloned.1.call-update) | async-done | bytes 393232 | tf_op jit(solution)/shard_map/while/body/eval_jaxpr/reduce_scatter | solution.py:73
  1058.2 37.1 %reduce-scatter.20.cloned.1.call-done = f32[1,128,768]{2,1,0:T(8,128)} async-done(((f32[4,128,768]{2,1,0:T(8,128)}), f32[1,128,768]{2,1,0:T(8,128)}) %reduce-scatter.20.cloned.1.call-update) | async-done | bytes 393232 | tf_op jit(solution)/shard_map/while/body/eval_jaxpr/reduce_scatter | solution.py:249
  1245.4 36.4 %reduce-scatter.18.cloned.1.call-done = f32[1,128,768]{2,1,0:T(8,128)} async-done(((f32[4,128,768]{2,1,0:T(8,128)}), f32[1,128,768]{2,1,0:T(8,128)}) %reduce-scatter.18.cloned.1.call-update) | async-done | bytes 393232 | tf_op jit(solution)/shard_map/while/body/eval_jaxpr/reduce_scatter | solution.py:73
  1308.6 37.1 %reduce-scatter.20.cloned.1.call-done = f32[1,128,768]{2,1,0:T(8,128)} async-done(((f32[4,128,768]{2,1,0:T(8,128)}), f32[1,128,768]{2,1,0:T(8,128)}) %reduce-scatter.20.cloned.1.call-update) | async-done | bytes 393232 | tf_op jit(solution)/shard_map/while/body/eval_jaxpr/reduce_scatter | solution.py:249
  1495.7 36.4 %reduce-scatter.18.cloned.1.call-done = f32[1,128,768]{2,1,0:T(8,128)} async-done(((f32[4,128,768]{2,1,0:T(8,128)}), f32[1,128,768]{2,1,0:T(8,128)}) %reduce-scatter.18.cloned.1.call-update) | async-done | bytes 393232 | tf_op jit(solution)/shard_map/while/body/eval_jaxpr/reduce_scatter | solution.py:73
  1558.8 37.1 %reduce-scatter.20.cloned.1.call-done = f32[1,128,768]{2,1,0:T(8,128)} async-done(((f32[4,128,768]{2,1,0:T(8,128)}), f32[1,128,768]{2,1,0:T(8,128)}) %reduce-scatter.20.cloned.1.call-update) | async-done | bytes 393232 | tf_op jit(solution)/shard_map/while/body/eval_jaxpr/reduce_scatter | solution.py:249
  1745.9 36.5 %reduce-scatter.18.cloned.1.call-done = f32[1,128,768]{2,1,0:T(8,128)} async-done(((f32[4,128,768]{2,1,0:T(8,128)}), f32[1,128,768]{2,1,0:T(8,128)}) %reduce-scatter.18.cloned.1.call-update) | async-done | bytes 393232 | tf_op jit(solution)/shard_map/while/body/eval_jaxpr/reduce_scatter | solution.py:73
  1809.2 37.1 %reduce-scatter.20.cloned.1.call-done = f32[1,128,768]{2,1,0:T(8,128)} async-done(((f32[4,128,768]{2,1,0:T(8,128)}), f32[1,128,768]{2,1,0:T(8,128)}) %reduce-scatter.20.cloned.1.call-update) | async-done | bytes 393232 | tf_op jit(solution)/shard_map/while/body/eval_jaxpr/reduce_scatter | solution.py:249
  1996.3 36.4 %reduce-scatter.18.cloned.1.call-done = f32[1,128,768]{2,1,0:T(8,128)} async-done(((f32[4,128,768]{2,1,0:T(8,128)}), f32[1,128,768]{2,1,0:T(8,128)}) %reduce-scatter.18.cloned.1.call-update) | async-done | bytes 393232 | tf_op jit(solution)/shard_map/while/body/eval_jaxpr/reduce_scatter | solution.py:73
  2059.5 37.1 %reduce-scatter.20.cloned.1.call-done = f32[1,128,768]{2,1,0:T(8,128)} async-done(((f32[4,128,768]{2,1,0:T(8,128)}), f32[1,128,768]{2,1,0:T(8,128)}) %reduce-scatter.20.cloned.1.call-update) | async-done | bytes 393232 | tf_op jit(solution)/shard_map/while/body/eval_jaxpr/reduce_scatter | solution.py:249
  2246.6 36.4 %reduce-scatter.18.cloned.1.call-done = f32[1,128,768]{2,1,0:T(8,128)} async-done(((f32[4,128,768]{2,1,0:T(8,128)}), f32[1,128,768]{2,1,0:T(8,128)}) %reduce-scatter.18.cloned.1.call-update) | async-done | bytes 393232 | tf_op jit(solution)/shard_map/while/body/eval_jaxpr/reduce_scatter | solution.py:73
  2309.8 37.1 %reduce-scatter.20.cloned.1.call-done = f32[1,128,768]{2,1,0:T(8,128)} async-done(((f32[4,128,768]{2,1,0:T(8,128)}), f32[1,128,768]{2,1,0:T(8,128)}) %reduce-scatter.20.cloned.1.call-update) | async-done | bytes 393232 | tf_op jit(solution)/shard_map/while/body/eval_jaxpr/reduce_scatter | solution.py:249
  2497.0 36.4 %reduce-scatter.18.cloned.1.call-done = f32[1,128,768]{2,1,0:T(8,128)} async-done(((f32[4,128,768]{2,1,0:T(8,128)}), f32[1,128,768]{2,1,0:T(8,128)}) %reduce-scatter.18.cloned.1.call-update) | async-done | bytes 393232 | tf_op jit(solution)/shard_map/while/body/eval_jaxpr/reduce_scatter | solution.py:73
  2560.2 37.0 %reduce-scatter.20.cloned.1.call-done = f32[1,128,768]{2,1,0:T(8,128)} async-done(((f32[4,128,768]{2,1,0:T(8,128)}), f32[1,128,768]{2,1,0:T(8,128)}) %reduce-scatter.20.cloned.1.call-update) | async-done | bytes 393232 | tf_op jit(solution)/shard_map/while/body/eval_jaxpr/reduce_scatter | solution.py:249
  2695.4 162.4 %all-reduce.3.cloned.1.call-done = (f32[1,768,3,192]{1,3,2,0:T(8,128)}, f32[1,192,768]{2,1,0:T(8,128)}, f32[1,768,2,768]{3,2,1,0:T(2,128)}, f32[1,768,768]{2,1,0:T(8,128)}) async-done(((f32[1,768,3,192]{1,3,2,0:T(8,128)}, f32[1,192,768]{2,1,0:T(8,128)}, f32[1,768,2,768]{3,2,1,0:T(2,128)}, f32[1,768,768]{2,1,0:T(8,128)}), (f32[1,768,3,192]{1,3,2,0:T(8,128)}, f32[1,192,768]{2,1,0:T(8,128)}, ...) | async-done | bytes 9437200 | tf_op jit(solution)/shard_map/psum | solution.py:433
  (1144 shorter events, 1641.0 us)
Async XLA Ops:
  19.7 61.4 %reduce-scatter.12.cloned.1.call-start = ((), (), s32[]{:S(2)}) async-start(), calls=%async_computation.9 | async-start | bytes 1966080 | tf_op jit(solution)/shard_map/while/body/eval_jaxpr/reduce_scatter | solution.py:60
  43.9 100.2 %reduce-scatter.14.cloned.1.call-start = ((), (), s32[]{:S(2)}) async-start(), calls=%async_computation.10 | async-start | bytes 1966080 | tf_op jit(solution)/shard_map/while/body/eval_jaxpr/reduce_scatter | solution.py:73
  172.4 98.4 %reduce-scatter.14.cloned.1.call-start = ((), (), s32[]{:S(2)}) async-start(), calls=%async_computation.10 | async-start | bytes 1966080 | tf_op jit(solution)/shard_map/while/body/eval_jaxpr/reduce_scatter | solution.py:73
  299.2 98.4 %reduce-scatter.14.cloned.1.call-start = ((), (), s32[]{:S(2)}) async-start(), calls=%async_computation.10 | async-start | bytes 1966080 | tf_op jit(solution)/shard_map/while/body/eval_jaxpr/reduce_scatter | solution.py:73
  425.9 98.5 %reduce-scatter.14.cloned.1.call-start = ((), (), s32[]{:S(2)}) async-start(), calls=%async_computation.10 | async-start | bytes 1966080 | tf_op jit(solution)/shard_map/while/body/eval_jaxpr/reduce_scatter | solution.py:73
  530.0 58.2 %reduce-scatter.12.cloned.1.call-start = ((), (), s32[]{:S(2)}) async-start(), calls=%async_computation.9 | async-start | bytes 1966080 | tf_op jit(solution)/shard_map/while/body/eval_jaxpr/reduce_scatter | solution.py:60
  552.8 98.4 %reduce-scatter.14.cloned.1.call-start = ((), (), s32[]{:S(2)}) async-start(), calls=%async_computation.10 | async-start | bytes 1966080 | tf_op jit(solution)/shard_map/while/body/eval_jaxpr/reduce_scatter | solution.py:73
  679.6 98.4 %reduce-scatter.14.cloned.1.call-start = ((), (), s32[]{:S(2)}) async-start(), calls=%async_computation.10 | async-start | bytes 1966080 | tf_op jit(solution)/shard_map/while/body/eval_jaxpr/reduce_scatter | solution.py:73
  783.6 58.2 %reduce-scatter.12.cloned.1.call-start = ((), (), s32[]{:S(2)}) async-start(), calls=%async_computation.9 | async-start | bytes 1966080 | tf_op jit(solution)/shard_map/while/body/eval_jaxpr/reduce_scatter | solution.py:60
  806.3 98.5 %reduce-scatter.14.cloned.1.call-start = ((), (), s32[]{:S(2)}) async-start(), calls=%async_computation.10 | async-start | bytes 1966080 | tf_op jit(solution)/shard_map/while/body/eval_jaxpr/reduce_scatter | solution.py:73
  933.8 97.6 %reduce-scatter.18.cloned.1.call-start = ((), (), s32[]{:S(2)}) async-start(), calls=%async_computation.12 | async-start | bytes 1966080 | tf_op jit(solution)/shard_map/while/body/eval_jaxpr/reduce_scatter | solution.py:73
  994.3 101.1 %reduce-scatter.20.cloned.1.call-start = ((), (), s32[]{:S(2)}) async-start(), calls=%async_computation.13 | async-start | bytes 1966080 | tf_op jit(solution)/shard_map/while/body/eval_jaxpr/reduce_scatter | solution.py:249
  1058.2 97.6 %reduce-scatter.22.cloned.1.call-start = ((), (), s32[]{:S(2)}) async-start(), calls=%async_computation.14 | async-start | bytes 1966080 | tf_op jit(solution)/shard_map/while/body/eval_jaxpr/reduce_scatter | solution.py:319
  1184.2 97.5 %reduce-scatter.18.cloned.1.call-start = ((), (), s32[]{:S(2)}) async-start(), calls=%async_computation.12 | async-start | bytes 1966080 | tf_op jit(solution)/shard_map/while/body/eval_jaxpr/reduce_scatter | solution.py:73
  1244.6 101.1 %reduce-scatter.20.cloned.1.call-start = ((), (), s32[]{:S(2)}) async-start(), calls=%async_computation.13 | async-start | bytes 1966080 | tf_op jit(solution)/shard_map/while/body/eval_jaxpr/reduce_scatter | solution.py:249
  1308.5 97.6 %reduce-scatter.22.cloned.1.call-start = ((), (), s32[]{:S(2)}) async-start(), calls=%async_computation.14 | async-start | bytes 1966080 | tf_op jit(solution)/shard_map/while/body/eval_jaxpr/reduce_scatter | solution.py:319
  1434.6 97.5 %reduce-scatter.18.cloned.1.call-start = ((), (), s32[]{:S(2)}) async-start(), calls=%async_computation.12 | async-start | bytes 1966080 | tf_op jit(solution)/shard_map/while/body/eval_jaxpr/reduce_scatter | solution.py:73
  1494.9 101.0 %reduce-scatter.20.cloned.1.call-start = ((), (), s32[]{:S(2)}) async-start(), calls=%async_computation.13 | async-start | bytes 1966080 | tf_op jit(solution)/shard_map/while/body/eval_jaxpr/reduce_scatter | solution.py:249
  1558.8 97.6 %reduce-scatter.22.cloned.1.call-start = ((), (), s32[]{:S(2)}) async-start(), calls=%async_computation.14 | async-start | bytes 1966080 | tf_op jit(solution)/shard_map/while/body/eval_jaxpr/reduce_scatter | solution.py:319
  1684.8 97.6 %reduce-scatter.18.cloned.1.call-start = ((), (), s32[]{:S(2)}) async-start(), calls=%async_computation.12 | async-start | bytes 1966080 | tf_op jit(solution)/shard_map/while/body/eval_jaxpr/reduce_scatter | solution.py:73
  1745.2 101.1 %reduce-scatter.20.cloned.1.call-start = ((), (), s32[]{:S(2)}) async-start(), calls=%async_computation.13 | async-start | bytes 1966080 | tf_op jit(solution)/shard_map/while/body/eval_jaxpr/reduce_scatter | solution.py:249
  1809.1 97.6 %reduce-scatter.22.cloned.1.call-start = ((), (), s32[]{:S(2)}) async-start(), calls=%async_computation.14 | async-start | bytes 1966080 | tf_op jit(solution)/shard_map/while/body/eval_jaxpr/reduce_scatter | solution.py:319
  1935.2 97.5 %reduce-scatter.18.cloned.1.call-start = ((), (), s32[]{:S(2)}) async-start(), calls=%async_computation.12 | async-start | bytes 1966080 | tf_op jit(solution)/shard_map/while/body/eval_jaxpr/reduce_scatter | solution.py:73
  1995.5 101.1 %reduce-scatter.20.cloned.1.call-start = ((), (), s32[]{:S(2)}) async-start(), calls=%async_computation.13 | async-start | bytes 1966080 | tf_op jit(solution)/shard_map/while/body/eval_jaxpr/reduce_scatter | solution.py:249
  2059.4 97.6 %reduce-scatter.22.cloned.1.call-start = ((), (), s32[]{:S(2)}) async-start(), calls=%async_computation.14 | async-start | bytes 1966080 | tf_op jit(solution)/shard_map/while/body/eval_jaxpr/reduce_scatter | solution.py:319
  2185.5 97.5 %reduce-scatter.18.cloned.1.call-start = ((), (), s32[]{:S(2)}) async-start(), calls=%async_computation.12 | async-start | bytes 1966080 | tf_op jit(solution)/shard_map/while/body/eval_jaxpr/reduce_scatter | solution.py:73
  2245.9 101.0 %reduce-scatter.20.cloned.1.call-start = ((), (), s32[]{:S(2)}) async-start(), calls=%async_computation.13 | async-start | bytes 1966080 | tf_op jit(solution)/shard_map/while/body/eval_jaxpr/reduce_scatter | solution.py:249
  2309.8 97.6 %reduce-scatter.22.cloned.1.call-start = ((), (), s32[]{:S(2)}) async-start(), calls=%async_computation.14 | async-start | bytes 1966080 | tf_op jit(solution)/shard_map/while/body/eval_jaxpr/reduce_scatter | solution.py:319
  2435.8 97.6 %reduce-scatter.18.cloned.1.call-start = ((), (), s32[]{:S(2)}) async-start(), calls=%async_computation.12 | async-start | bytes 1966080 | tf_op jit(solution)/shard_map/while/body/eval_jaxpr/reduce_scatter | solution.py:73
  2496.2 101.0 %reduce-scatter.20.cloned.1.call-start = ((), (), s32[]{:S(2)}) async-start(), calls=%async_computation.13 | async-start | bytes 1966080 | tf_op jit(solution)/shard_map/while/body/eval_jaxpr/reduce_scatter | solution.py:249
  2560.1 97.6 %reduce-scatter.22.cloned.1.call-start = ((), (), s32[]{:S(2)}) async-start(), calls=%async_computation.14 | async-start | bytes 1966080 | tf_op jit(solution)/shard_map/while/body/eval_jaxpr/reduce_scatter | solution.py:319
  2666.0 191.9 %all-reduce.3.cloned.1.call-start = ((), (), s32[]{:S(2)}) async-start(), calls=%async_computation.8 | async-start | bytes 18874368 | tf_op jit(solution)/shard_map/psum | solution.py:433
  (211 other events, 2319.3 us)
Sparse Core Ops, SparseCore 0:
  44.0 37.0 reduce-scatter.11
  107.1 36.9 reduce-scatter.13
  233.8 36.9 reduce-scatter.13
  360.6 36.9 reduce-scatter.13
  426.0 35.2 reduce-scatter.11
  487.4 37.0 reduce-scatter.13
  614.2 36.9 reduce-scatter.13
  741.0 36.9 reduce-scatter.13
  806.4 35.2 reduce-scatter.11
  867.7 37.0 reduce-scatter.13
  994.4 37.0 reduce-scatter.17
  1058.3 36.9 reduce-scatter.19
  1118.7 36.9 reduce-scatter.21
  1244.7 36.9 reduce-scatter.17
  1308.6 36.9 reduce-scatter.19
  1369.1 36.9 reduce-scatter.21
  1495.0 36.9 reduce-scatter.17
  1558.9 36.9 reduce-scatter.19
  1619.3 36.9 reduce-scatter.21
  1745.3 37.0 reduce-scatter.17
  1809.3 36.9 reduce-scatter.19
  1869.7 36.9 reduce-scatter.21
  1995.7 36.9 reduce-scatter.17
  2059.6 37.0 reduce-scatter.19
  2120.0 36.9 reduce-scatter.21
  2246.0 36.9 reduce-scatter.17
  2309.9 36.9 reduce-scatter.19
  2370.3 36.9 reduce-scatter.21
  2496.3 37.0 reduce-scatter.17
  2560.2 36.9 reduce-scatter.19
  2620.6 37.0 reduce-scatter.21
  2671.0 186.8 all-reduce.2
  (11 shorter events, 386.6 us)
Sparse Core Ops, SparseCore 1:
  2668.3 16.9 reduce-scatter.9
where the time goes:
time: 2880 us; the launch traced here: 2870 us
  waiting for transfers between devices  1530 us (53%)
  blocking collectives  683 us (24%)
  matrix products  274 us (10%)
  other arithmetic  209 us (7%)
  local copies, waits for them, and re-layouts  123 us (4%)
  starting transfers between devices  31.1 us (1%)
    reduce_scatter x14, waiting for transfers between devices, feed_total(): lax.psum_scatter(term(jnp.int32(0), row_count * lax.axis_size('tensor')),...  508 us
    reduce_scatter x14, waiting for transfers between devices, attention_total(): lax.psum_scatter(term(jnp.int32(0), row_count * lax.axis_size('tensor')),...  496 us
    reduce_scatter x7, waiting for transfers between devices, backward_core(): lax.psum_scatter(jnp.einsum('naz,iz->nai', block_portion, input_weight_fl...  260 us
    all_gather x14, blocking collectives, spread_rows(): lax.all_gather(own_low, 'tensor', axis=0, tiled=True)  235 us
    all_gather x14, blocking collectives, spread_middle(): lax.all_gather(own_low, 'tensor', axis=0, tiled=True)  219 us
    psum x1, waiting for transfers between devices, body(): lax.psum((totals[0], totals[1], totals[2], totals[3], vector_slices), 'dp')  162 us
    all_gather x7, blocking collectives, backward_core(): lax.all_gather(sum_grad.astype(jnp.bfloat16), 'tensor', axis=0, tiled=True)  111 us
    all_gather x7, blocking collectives, backward_core(): lax.all_gather(second_grad.astype(jnp.bfloat16), 'tensor', axis=0, tiled=...  110 us
  transfers between devices with their start and end apart: 58, of which 58 were waited for; matrix products, arithmetic and copies ran while one was open for 7% of the time, Pallas kernels for 0%

commit v1 on v0

v1 whole, which is shorter than its diff:
```python
import math

import jax
import jax.numpy as jnp
import numpy as np
from jax import lax
from jax.sharding import PartitionSpec as P

HEADS = 12
HEAD_DIM = 64
NORM_EPSILON = 1e-05
AXES = ("section", "dp", "tensor")
FEED_CHUNKS = 2

F32 = jnp.float32
BF16 = jnp.bfloat16


def power_slopes(total_heads):
    return [2.0 ** (-8.0 * (index + 1) / total_heads) for index in range(total_heads)]


def alibi_table(number_heads):
    closest = 2 ** int(math.floor(math.log2(number_heads)))
    slopes = power_slopes(closest)
    slopes = slopes + power_slopes(2 * closest)[0::2][: number_heads - closest]
    return np.array(slopes, dtype=np.float32)


def norm_rows(values, gain, offset):
    row_mean = jnp.mean(values, axis=-1, keepdims=True)
    centred = values - row_mean
    row_var = jnp.mean(centred * centred, axis=-1, keepdims=True)
    return centred * lax.rsqrt(row_var + NORM_EPSILON) * gain + offset


def gelu_product(gate_part, up_part):
    return jax.nn.gelu(gate_part, approximate=False) * up_part


def dot(a, b, ca, cb):
    return lax.dot_general(a, b, (((ca,), (cb,)), ((), ())), preferred_element_type=F32)


def exchange(block, section_mask=0, dp_masks=(0, 0), tensor_mask=0):
    dp = lax.axis_size("dp")
    tensor = lax.axis_size("tensor")
    pairs = []
    for s in range(lax.axis_size("section")):
        for d in range(dp):
            for t in range(tensor):
                target = ((s ^ section_mask) * dp + (d ^ dp_masks[s])) * tensor + (t ^ tensor_mask)
                pairs.append(((s * dp + d) * tensor + t, target))
    return lax.ppermute(block, AXES, pairs)


def swap(block):
    return exchange(block, section_mask=1)


FIRST = (1, 2)
SECOND = (2, 1)
PLANE = 4
DEPTH = 4


def gather_pieces(own):
    mine = own[0]
    next_one = exchange(mine, tensor_mask=1)
    next_two = exchange(jnp.stack([mine, next_one]), tensor_mask=2)
    remote = jnp.concatenate([next_one[None], next_two])
    first = exchange(remote, dp_masks=FIRST)
    second = exchange(jnp.stack([remote, first]), dp_masks=SECOND)
    return [[own[0], remote], [own[1], first], [own[2], second[0]], [own[3], second[1]]]


def assemble(pieces):
    return jnp.stack([jnp.concatenate([own[None], rest]) for own, rest in pieces])


def add_low(a, b):
    return (a.astype(F32) + b.astype(F32)).astype(BF16)


def scatter_pieces(terms):
    half = add_low(terms[:2], exchange(terms[2:], dp_masks=SECOND))
    quarter = add_low(half[0], exchange(half[1], dp_masks=FIRST))
    pair = add_low(quarter[:2], exchange(quarter[2:], tensor_mask=2))
    one = add_low(pair[0], exchange(pair[1], tensor_mask=1))
    mask = PLANE
    while mask < lax.axis_size("dp"):
        one = add_low(one, exchange(one, dp_masks=(mask, mask)))
        mask *= 2
    return one


def attention_weights(queries, key_heads, slopes):
    length = queries.shape[1]
    scores = jnp.einsum(
        "sqhe,skhe->shqk", queries, key_heads, preferred_element_type=F32
    ) * HEAD_DIM ** (-0.5)
    positions = jnp.arange(length)
    distance = jnp.abs(positions[:, None] - positions[None, :]).astype(F32)
    scores = scores - slopes[:, None, None] * distance[None, :, :]
    return jax.nn.softmax(scores, axis=-1)


def layer_forward(own_low, attn, feed, norms, slopes, seqs):
    rows, features = own_low.shape
    length = rows // seqs
    gain_one, offset_one, gain_two, offset_two = norms
    own_in = own_low.astype(F32)
    wqkv, wo = attn
    projected = dot(own_low, wqkv, 1, 1).astype(BF16)
    split = projected.reshape(seqs, length, 3, -1, HEAD_DIM)
    queries, key_heads, value_heads = split[:, :, 0], split[:, :, 1], split[:, :, 2]
    attention = attention_weights(queries, key_heads, slopes)
    attention_low = attention.astype(BF16)
    context = jnp.einsum(
        "shqk,skhe->sqhe", attention_low, value_heads, preferred_element_type=F32
    ).astype(BF16).reshape(rows, -1)
    attended = dot(context, wo, 1, 0)
    first_sum = own_in + attended
    first_norm = norm_rows(first_sum, gain_one, offset_one)
    first_low = first_norm.astype(BF16)
    first_all = jnp.concatenate([first_low, swap(first_low)])
    gated, hidden, mixed_terms = [], [], 0.0
    for gate_up, down in feed:
        gated_rows = dot(first_all, gate_up, 1, 1)
        gate_part, up_part = jnp.split(gated_rows, 2, axis=-1)
        hidden_rows = gelu_product(gate_part, up_part).astype(BF16)
        gated.append(gated_rows)
        hidden.append(hidden_rows)
        mixed_terms = mixed_terms + dot(hidden_rows, down, 1, 0)
    mixed = mixed_terms[:rows] + swap(mixed_terms[rows:].astype(BF16)).astype(F32)
    second_sum = first_norm + mixed
    output = norm_rows(second_sum, gain_two, offset_two)
    saved = (queries, key_heads, value_heads, attention, attention_low, context, first_sum, first_all, gated, hidden, second_sum)
    return output, saved


def layer_backward(own_low, seed_grad, attn, feed, norms, saved, seqs):
    queries, key_heads, value_heads, attention, attention_low, context, first_sum, first_all, gated, hidden, second_sum = saved
    rows, features = own_low.shape
    length = rows // seqs
    gain_one, offset_one, gain_two, offset_two = norms
    wqkv, wo = attn
    _, norm_two_back = jax.vjp(norm_rows, second_sum, gain_two, offset_two)
    second_grad, gain_two_grad, offset_two_grad = norm_two_back(seed_grad)
    mixed_low = second_grad.astype(BF16)
    mixed_all = jnp.concatenate([mixed_low, swap(mixed_low)])
    feed_grads, first_terms = [], 0.0
    for (gate_up, down), gated_rows, hidden_rows in zip(feed, gated, hidden):
        hidden_grad = dot(mixed_all, down, 1, 1)
        down_grad = dot(hidden_rows, mixed_all, 0, 0).astype(BF16)
        gate_part, up_part = jnp.split(gated_rows, 2, axis=-1)
        _, gelu_back = jax.vjp(gelu_product, gate_part, up_part)
        gate_grad, up_grad = gelu_back(hidden_grad)
        gated_grad = jnp.concatenate([gate_grad, up_grad], axis=-1).astype(BF16)
        gate_up_grad = dot(gated_grad, first_all, 0, 0).astype(BF16)
        feed_grads.append((gate_up_grad, down_grad))
        first_terms = first_terms + dot(gated_grad, gate_up, 1, 0)
    first_grad = first_terms[:rows] + swap(first_terms[rows:].astype(BF16)).astype(F32) + second_grad
    _, norm_one_back = jax.vjp(norm_rows, first_sum, gain_one, offset_one)
    sum_grad, gain_one_grad, offset_one_grad = norm_one_back(first_grad)
    attended_low = sum_grad.astype(BF16)
    context_grad = dot(attended_low, wo, 1, 1).astype(BF16)
    out_grad = dot(context, attended_low, 0, 0).astype(BF16)
    context_heads = context_grad.reshape(seqs, length, -1, HEAD_DIM)
    weights_grad = jnp.einsum(
        "sqhe,skhe->shqk", context_heads, value_heads, preferred_element_type=F32
    )
    value_grad = jnp.einsum(
        "shqk,sqhe->skhe", attention_low, context_heads, preferred_element_type=F32
    )
    score_grad = attention * (
        weights_grad - jnp.sum(attention * weights_grad, axis=-1, keepdims=True)
    )
    score_grad = score_grad.astype(BF16)
    query_grad = jnp.einsum(
        "shqk,skhe->sqhe", score_grad, key_heads, preferred_element_type=F32
    ) * HEAD_DIM ** (-0.5)
    key_grad = jnp.einsum(
        "shqk,sqhe->skhe", score_grad, queries, preferred_element_type=F32
    ) * HEAD_DIM ** (-0.5)
    projected_grad = jnp.stack([query_grad, key_grad, value_grad], axis=2).reshape(rows, -1).astype(BF16)
    qkv_grad = dot(projected_grad, own_low, 0, 0).astype(BF16)
    input_grad = dot(projected_grad, wqkv, 1, 0) + sum_grad
    vectors = jnp.stack([gain_one_grad, offset_one_grad, gain_two_grad, offset_two_grad])
    return input_grad, feed_grads, (qkv_grad, out_grad), vectors


def body(
    layer_input,
    out_grad,
    loss_mask,
    query_key_value_weight,
    attention_output_weight,
    gate_up_weight,
    down_weight,
    norm1_gain,
    norm1_bias,
    norm2_gain,
    norm2_bias,
):
    core = lax.axis_index("section")
    plane = lax.axis_index("dp")
    depth = lax.axis_index("tensor")
    is_first = core == 0
    micro, own_seqs, length, features = layer_input.shape
    local = query_key_value_weight.shape[-1]
    local_heads = local // HEAD_DIM
    units = down_weight.shape[1]
    part = HEAD_DIM // PLANE
    unit_part = units // 2 // PLANE // FEED_CHUNKS
    seqs = micro * own_seqs // 2
    rows = seqs * length

    steps = jnp.where(is_first, jnp.array([0, 1, 2, 3]), jnp.array([0, 2, 1, 3]))
    in_plane = jnp.bitwise_and(plane, PLANE - 1)

    def relative(slab):
        return [
            lax.dynamic_index_in_dim(slab, jnp.bitwise_xor(in_plane, steps[e]), 0, keepdims=False)
            for e in range(PLANE)
        ]

    qkv_rows = jnp.transpose(query_key_value_weight[0], (1, 2, 0))
    attn_rows = jnp.concatenate([qkv_rows, attention_output_weight], axis=0)
    attn_slab = attn_rows.reshape(2, 2, local_heads, PLANE, part, features)
    attn_slab = jnp.transpose(attn_slab, (0, 3, 1, 2, 4, 5)).reshape(2, PLANE, -1, features)
    gate_up_rows = jnp.transpose(gate_up_weight[0], (1, 2, 0))
    feed_rows = jnp.concatenate([gate_up_rows, down_weight], axis=0)
    feed_slab = feed_rows.reshape(3, 2, FEED_CHUNKS, PLANE, unit_part, features)
    feed_slab = jnp.transpose(feed_slab, (2, 1, 3, 0, 4, 5)).reshape(FEED_CHUNKS, 2, PLANE, -1, features)

    def share(slab):
        keep = lax.dynamic_index_in_dim(slab, core, 0, keepdims=False)
        got = swap(lax.dynamic_index_in_dim(slab, 1 - core, 0, keepdims=False))
        return jnp.where(is_first, keep, got), jnp.where(is_first, got, keep)

    attn_own = share(attn_slab)
    feed_own = [share(feed_slab[k]) for k in range(FEED_CHUNKS)]

    def gather_attn(own):
        full = assemble(gather_pieces(relative(own)))
        full = full.reshape(PLANE, DEPTH, 2, local_heads, part, features)
        mine = jnp.transpose(full, (2, 1, 3, 0, 4, 5)).reshape(2, -1, features)
        other = swap(mine)
        qk = jnp.where(is_first, mine, other)
        vo = jnp.where(is_first, other, mine)
        wqkv = jnp.concatenate([qk.reshape(-1, features), vo[0]])
        return wqkv, vo[1]

    def gather_feed(own):
        full = assemble(gather_pieces(relative(own)))
        full = full.reshape(PLANE * DEPTH, 3, unit_part, features)
        full = jnp.transpose(full, (1, 0, 2, 3)).reshape(3, -1, features)
        return full[:2].reshape(-1, features), full[2]

    attns = []
    feeds = []
    for layer in range(2):
        attns.append(gather_attn(attn_own[layer]))
        feeds.append([gather_feed(feed_own[k][layer]) for k in range(FEED_CHUNKS)])

    norm_table = jnp.concatenate([norm1_gain, norm1_bias, norm2_gain, norm2_bias])
    norm_other = swap(norm_table)
    norm_first = jnp.where(is_first, norm_table, norm_other)
    norm_second = jnp.where(is_first, norm_other, norm_table)
    norms = [tuple(table[i] for i in range(4)) for table in (norm_first, norm_second)]

    slope_table = jnp.asarray(alibi_table(HEADS)).reshape(DEPTH, local_heads)
    slopes = jnp.concatenate(
        [lax.dynamic_index_in_dim(slope_table, jnp.bitwise_xor(depth, j), 0, keepdims=False) for j in range(DEPTH)]
    )

    def own_half(whole):
        flat = whole.reshape((2, rows) + whole.shape[3:])
        return lax.dynamic_index_in_dim(flat, core, 0, keepdims=False)

    start = own_half(layer_input)
    seed = own_half(out_grad).astype(F32) * own_half(loss_mask).astype(F32)[..., None]

    middle, saved_first = layer_forward(start, attns[0], feeds[0], norms[0], slopes, seqs)
    middle_low = middle.astype(BF16)
    final, saved_second = layer_forward(middle_low, attns[1], feeds[1], norms[1], slopes, seqs)
    final_low = final.astype(BF16)

    def reduce_feed(grads):
        gate_up, down = grads
        full = jnp.concatenate([gate_up, down]).reshape(3, PLANE, DEPTH, unit_part, features)
        full = jnp.transpose(full, (1, 2, 0, 3, 4)).reshape(PLANE, DEPTH, -1, features)
        return scatter_pieces(full)

    def reduce_attn(grads):
        qkv, out = grads
        full = jnp.concatenate([qkv, out]).reshape(2, -1, features)
        keep = lax.dynamic_index_in_dim(full, core, 0, keepdims=False)
        got = swap(lax.dynamic_index_in_dim(full, 1 - core, 0, keepdims=False))
        full = add_low(keep, got).reshape(2, DEPTH, local_heads, PLANE, part, features)
        full = jnp.transpose(full, (3, 1, 0, 2, 4, 5)).reshape(PLANE, DEPTH, -1, features)
        return scatter_pieces(full)

    middle_grad, feed_grads, attn_grads, vectors_second = layer_backward(
        middle_low, seed, attns[1], feeds[1], norms[1], saved_second, seqs
    )
    feed_second = [reduce_feed(g) for g in feed_grads]
    attn_second = reduce_attn(attn_grads)
    start_grad, feed_grads, attn_grads, vectors_first = layer_backward(
        start, middle_grad, attns[0], feeds[0], norms[0], saved_first, seqs
    )
    feed_first = [reduce_feed(g) for g in feed_grads]
    attn_first = reduce_attn(attn_grads)

    def finish(first, second):
        keep = jnp.where(is_first, first, second)
        got = swap(jnp.where(is_first, second, first))
        both = jnp.stack([jnp.where(is_first, keep, got), jnp.where(is_first, got, keep)])
        near = exchange(both, dp_masks=FIRST)
        pair = jnp.stack([both, near])
        far = exchange(pair, dp_masks=SECOND)
        every = jnp.concatenate([pair, far])
        return jnp.stack(
            [
                lax.dynamic_index_in_dim(
                    every, steps[jnp.bitwise_xor(in_plane, index)], 0, keepdims=False
                )
                for index in range(PLANE)
            ]
        )

    feed_total = jnp.stack([finish(a, b) for a, b in zip(feed_first, feed_second)])
    feed_total = feed_total.reshape(FEED_CHUNKS, PLANE, 2, 3, unit_part, features)
    feed_total = jnp.transpose(feed_total, (3, 2, 0, 1, 4, 5)).reshape(3, units, features).astype(F32)
    grad_in = jnp.transpose(feed_total[:2], (2, 0, 1))
    grad_down = feed_total[2]
    attn_total = finish(attn_first, attn_second)
    attn_total = attn_total.reshape(PLANE, 2, 2, local_heads, part, features)
    attn_total = jnp.transpose(attn_total, (1, 2, 3, 0, 4, 5)).reshape(4, local, features).astype(F32)
    grad_qkv = jnp.transpose(attn_total[:3], (2, 0, 1))
    grad_out = attn_total[3]

    vectors = lax.psum(jnp.stack([vectors_first, vectors_second]), AXES)
    vectors = lax.dynamic_index_in_dim(vectors, core, 0, keepdims=False)
    vectors = lax.dynamic_slice_in_dim(vectors, depth * local, local, 1)

    def give(first, second):
        mine = jnp.where(is_first, first, second)
        got = swap(jnp.where(is_first, second, first))
        both = jnp.concatenate([jnp.where(is_first, mine, got), jnp.where(is_first, got, mine)])
        return both.reshape((1, micro, own_seqs, length, features))

    return (
        give(middle_low, final_low),
        give(start_grad, middle_grad),
        grad_qkv[None],
        grad_out[None],
        grad_in[None],
        grad_down[None],
        vectors[0][None],
        vectors[1][None],
        vectors[2][None],
        vectors[3][None],
    )


def solution(mesh):
    placed = (
        P(None, ("dp", "tensor"), None, None),
        P(None, ("dp", "tensor"), None, None),
        P(None, ("dp", "tensor"), None),
        P("section", None, None, "tensor"),
        P("section", "tensor", None),
        P("section", None, None, "tensor"),
        P("section", "tensor", None),
        P("section", None),
        P("section", None),
        P("section", None),
        P("section", None),
    )
    return jax.shard_map(
        body,
        mesh=mesh,
        in_specs=placed,
        out_specs=(
            P("section", None, ("dp", "tensor"), None, None),
            P("section", None, ("dp", "tensor"), None, None),
            P("section", None, None, "tensor"),
            P("section", "tensor", None),
            P("section", None, None, "tensor"),
            P("section", "tensor", None),
            P("section", "tensor"),
            P("section", "tensor"),
            P("section", "tensor"),
            P("section", "tensor"),
        ),
        check_vma=False,
    )
```

time: 2880 us -> 728 us (0.25)
  waiting for transfers between devices: 1530 us -> 221 us
  blocking collectives: 683 us -> 56.8 us
  matrix products: 274 us -> 86.2 us
  other arithmetic: 209 us -> 112 us
  starting transfers between devices: 31.1 us -> 83.1 us
    reduce_scatter x42 -> x0, waiting for transfers between devices: 1340 us -> none  [the longest x14 508 us: feed_total(): lax.psum_scatter(term(jnp.int32(0), row_count * lax.axis_size('tensor')),...]
    all_gather x42 -> x0, blocking collectives: 674 us -> none  [the longest x14 235 us: spread_rows(): lax.all_gather(own_low, 'tensor', axis=0, tiled=True)]
    ppermute x14 -> x75, waiting for transfers between devices: 16 us -> 221 us  [exchange(): return lax.ppermute(block, AXES, pairs)]
    dot_general x161 -> x46, matrix products: 268 us -> 78.7 us  [the longest x36 66.1 us: dot(): lax.dot_general(a, b, (((ca,), (cb,)), ((), ())), preferred_element_type=...]
    psum x1 -> x0, waiting for transfers between devices: 162 us -> none  [body(): lax.psum((totals[0], totals[1], totals[2], totals[3], vector_slices), 'dp')]
    ppermute x14 -> x75, starting transfers between devices: 29.8 us -> 83.1 us  [exchange(): return lax.ppermute(block, AXES, pairs)]
    add x21 -> x0, other arithmetic: 51.1 us -> none  [the longest x7 50.8 us: backward_tick(): totals = tuple((total + term for total, term in zip(totals, matrices)))]
    unnamed x26 -> x336, local copies, waits for them, and re-layouts: 11.6 us -> 61.6 us
  transfers between devices with their start and end apart: 58 -> 75, of which waited for: 58 -> 24; matrix products, arithmetic and copies ran while one was open for 7% -> 39% of each run, Pallas kernels for 0% -> 0%
where the time goes in v1:
time: 728 us; the launch traced here: 715 us
  waiting for transfers between devices  221 us (30%)
  local copies, waits for them, and re-layouts  142 us (20%)
  other arithmetic  112 us (15%)
  matrix products  86.2 us (12%)
  starting transfers between devices  83.1 us (11%)
  blocking collectives  56.8 us (8%)
  between operations  14.7 us (2%)
    ppermute x75, waiting for transfers between devices, exchange(): return lax.ppermute(block, AXES, pairs)  221 us
    ppermute x75, starting transfers between devices, exchange(): return lax.ppermute(block, AXES, pairs)  83.1 us
    dot_general x36, matrix products, dot(): lax.dot_general(a, b, (((ca,), (cb,)), ((), ())), preferred_element_type=...  66.1 us
    unnamed x336, local copies, waits for them, and re-layouts  61.6 us
    psum x1, blocking collectives, body(): vectors = lax.psum(jnp.stack([vectors_first, vectors_second]), AXES)  56.8 us
    convert_element_type x4, other arithmetic, layer_forward(): hidden_rows = gelu_product(gate_part, up_part).astype(BF16)  35.3 us
    convert_element_type x20, other arithmetic, add_low(): return (a.astype(F32) + b.astype(F32)).astype(BF16)  15.7 us
  transfers between devices with their start and end apart: 75, of which 24 were waited for; matrix products, arithmetic and copies ran while one was open for 39% of the time, Pallas kernels for 0%

profile of v1, /device:TPU:1, one launch (start us, length us, event | category | flops | bytes accessed | tf_op | source)
XLA Modules:
  0.0 715.3 jit_solution(875580347461121239)
XLA Ops:
  5.2 5.6 copy.111
  43.6 15.5 %collective-permute-done.20 = bf16[2,96,768]{2,1,0:T(8,128)(2,1)S(1)} collective-permute-done((bf16[2,96,768]{2,1,0:T(8,128)(2,1)S(1)}, bf16[2,96,768]{2,1,0:T(8,128)(2,1)S(1)}, u32[]{:S(2)}, u32[]{:S(2)}) %collective-permute-start.20) | collective-permute-done | bytes 294944 | tf_op jit(solution)/shard_map/ppermute | solution.py:54
  66.0 6.3 collective-permute-done.25
  77.3 35.1 %collective-permute-done.15 = bf16[2,144,768]{2,1,0:T(8,128)(2,1)S(1)} collective-permute-done((bf16[2,144,768]{2,1,0:T(8,128)(2,1)S(1)}, bf16[2,144,768]{2,1,0:T(8,128)(2,1)S(1)}, u32[]{:S(2)}, u32[]{:S(2)}) %collective-permute-start.15) | collective-permute-done | bytes 442400 | tf_op jit(solution)/shard_map/ppermute | solution.py:54
  113.7 8.2 %collective-permute-done.30 = bf16[2,144,768]{2,1,0:T(8,128)(2,1)S(1)} collective-permute-done((bf16[2,144,768]{2,1,0:T(8,128)(2,1)S(1)}, bf16[2,144,768]{2,1,0:T(8,128)(2,1)S(1)}, u32[]{:S(2)}, u32[]{:S(2)}) %collective-permute-start.30) | collective-permute-done | bytes 442400 | tf_op jit(solution)/shard_map/ppermute | solution.py:54
  124.3 7.0 collective-permute-done.10
  132.8 8.1 %collective-permute-done.26 = bf16[2,144,768]{2,1,0:T(8,128)(2,1)S(1)} collective-permute-done((bf16[2,144,768]{2,1,0:T(8,128)(2,1)S(1)}, bf16[2,144,768]{2,1,0:T(8,128)(2,1)S(1)}, u32[]{:S(2)}, u32[]{:S(2)}) %collective-permute-start.26) | collective-permute-done | bytes 442400 | tf_op jit(solution)/shard_map/ppermute | solution.py:54
  147.1 4.7 collective-permute-done.11
  153.3 12.8 %collective-permute-done.27 = bf16[3,144,768]{2,1,0:T(8,128)(2,1)S(1)} collective-permute-done((bf16[3,144,768]{2,1,0:T(8,128)(2,1)S(1)}, bf16[3,144,768]{2,1,0:T(8,128)(2,1)S(1)}, u32[]{:S(2)}, u32[]{:S(2)}) %collective-permute-start.27) | collective-permute-done | bytes 663584 | tf_op jit(solution)/shard_map/ppermute | solution.py:54
  170.4 8.7 %collective-permute-start.5 = (bf16[2,768,768]{2,1,0:T(8,128)(2,1)S(1)}, bf16[2,768,768]{2,1,0:T(8,128)(2,1)S(1)}, u32[]{:S(2)}, u32[]{:S(2)}) collective-permute-start(bf16[2,768,768]{2,1,0:T(8,128)(2,1)S(1)} %bitcast.654), channel_id=1, source_target_pairs={{0,16},{1,17},{2,18},{3,19},{4,20},{5,21},{6,22},{7,23},{8,24},{9,... | collective-permute-start | bytes 7077896 | tf_op jit(solution)/shard_map/ppermute | solution.py:54
  181.5 21.4 %collective-permute-done.12 = bf16[2,3,144,768]{3,2,1,0:T(8,128)(2,1)S(1)} collective-permute-done((bf16[2,3,144,768]{3,2,1,0:T(8,128)(2,1)S(1)}, bf16[2,3,144,768]{3,2,1,0:T(8,128)(2,1)S(1)}, u32[]{:S(2)}, u32[]{:S(2)}) %collective-permute-start.12) | collective-permute-done | bytes 1327136 | tf_op jit(solution)/shard_map/ppermute | solution.py:54
  211.5 6.4 reshape.509
  217.9 4.9 fusion.211
  230.8 4.5 fusion.222
  252.2 5.9 multiply_convert_fusion.9
  262.3 17.0 %multiply_convert_fusion.8 = (bf16[768,768]{1,0:T(8,128)(2,1)S(1)}, f32[768,768]{1,0:T(8,128)}) fusion(f32[768,1536]{1,0:T(8,128)S(1)} %fusion.185), kind=kLoop, calls=%fused_computation.103 | loop fusion | flops 38928384 | bytes 8257536 | tf_op jit(solution)/shard_map/convert_element_type | solution.py:131
  288.0 4.6 reshape.510
  292.5 5.0 fusion.210
  320.6 6.0 multiply_convert_fusion.6
  328.6 6.3 multiply_convert_fusion.7
  483.6 56.8 %psum.7 = f32[2,4,768]{2,1,0:T(4,128)} all-reduce(f32[2,4,768]{2,1,0:T(4,128)} %pad_maximum_fusion.73), channel_id=1, replica_groups=mesh['section'=2,'dp'=4,'tensor'=4] {'section','dp','tensor'}, use_global_device_ids=true, to_apply=%region_30.31 | all-reduce | flops 6144 | bytes 49152 | tf_op jit(solution)/shard_map/psum | solution.py:344
  542.0 4.1 broadcast_select_fusion.6
  564.6 17.5 %collective-permute-done.59 = bf16[2,144,768]{2,1,0:T(8,128)(2,1)S(1)} collective-permute-done((bf16[2,144,768]{2,1,0:T(8,128)(2,1)S(1)}, bf16[2,144,768]{2,1,0:T(8,128)(2,1)S(1)}, u32[]{:S(2)}, u32[]{:S(2)}) %collective-permute-start.59) | collective-permute-done | bytes 442400 | tf_op jit(solution)/shard_map/ppermute | solution.py:54
  584.2 7.4 %collective-permute-done.70 = bf16[2,144,768]{2,1,0:T(8,128)(2,1)S(1)} collective-permute-done((bf16[2,144,768]{2,1,0:T(8,128)(2,1)S(1)}, bf16[2,144,768]{2,1,0:T(8,128)(2,1)S(1)}, u32[]{:S(2)}, u32[]{:S(2)}) %collective-permute-start.70) | collective-permute-done | bytes 442400 | tf_op jit(solution)/shard_map/ppermute | solution.py:54
  601.5 22.7 %collective-permute-done.55 = bf16[2,144,768]{2,1,0:T(8,128)(2,1)S(1)} collective-permute-done((bf16[2,144,768]{2,1,0:T(8,128)(2,1)S(1)}, bf16[2,144,768]{2,1,0:T(8,128)(2,1)S(1)}, u32[]{:S(2)}, u32[]{:S(2)}) %collective-permute-start.55) | collective-permute-done | bytes 442400 | tf_op jit(solution)/shard_map/ppermute | solution.py:54
  626.4 7.3 %collective-permute-done.66 = bf16[2,144,768]{2,1,0:T(8,128)(2,1)S(1)} collective-permute-done((bf16[2,144,768]{2,1,0:T(8,128)(2,1)S(1)}, bf16[2,144,768]{2,1,0:T(8,128)(2,1)S(1)}, u32[]{:S(2)}, u32[]{:S(2)}) %collective-permute-start.66) | collective-permute-done | bytes 442400 | tf_op jit(solution)/shard_map/ppermute | solution.py:54
  639.0 5.1 collective-permute-start.61
  651.8 10.8 %collective-permute-done.48 = bf16[2,96,768]{2,1,0:T(8,128)(2,1)S(1)} collective-permute-done((bf16[2,96,768]{2,1,0:T(8,128)(2,1)S(1)}, bf16[2,96,768]{2,1,0:T(8,128)(2,1)S(1)}, u32[]{:S(2)}, u32[]{:S(2)}) %collective-permute-start.48) | collective-permute-done | bytes 294944 | tf_op jit(solution)/shard_map/ppermute | solution.py:54
  668.0 12.4 %collective-permute-done.43 = bf16[2,96,768]{2,1,0:T(8,128)(2,1)S(1)} collective-permute-done((bf16[2,96,768]{2,1,0:T(8,128)(2,1)S(1)}, bf16[2,96,768]{2,1,0:T(8,128)(2,1)S(1)}, u32[]{:S(2)}, u32[]{:S(2)}) %collective-permute-start.43) | collective-permute-done | bytes 294944 | tf_op jit(solution)/shard_map/ppermute | solution.py:54
  680.8 4.7 collective-permute-done.44
  689.5 4.6 collective-permute-done.51
  700.8 8.3 %copy.162 = f32[1,768,2,768]{3,2,1,0:T(2,128)} copy(f32[1,768,2,768]{1,3,2,0:T(8,128)} %bitcast.625) | data formatting | bytes 9437184
  (771 shorter events, 345.0 us)
Async XLA Ops:
  13.7 26.5 %collective-permute-start.8 = (bf16[4,144,768]{2,1,0:T(8,128)(2,1)}, bf16[4,144,768]{2,1,0:T(8,128)(2,1)}, u32[]{:S(2)}, u32[]{:S(2)}) collective-permute-start(bf16[4,144,768]{2,1,0:T(8,128)(2,1)} %dynamic-slice_bitcast_fusion.3), channel_id=1, source_target_pairs={{0,16},{1,17},{2,18},{3,19},{4,20},{5,21},{6,22},{7,23},{8,24},{9,... | collective-permute-start | bytes 2654216 | tf_op jit(solution)/shard_map/ppermute | solution.py:54
  31.0 29.3 %collective-permute-start.2 = (bf16[2,96,768]{2,1,0:T(8,128)(2,1)S(1)}, bf16[2,96,768]{2,1,0:T(8,128)(2,1)S(1)}, u32[]{:S(2)}, u32[]{:S(2)}) collective-permute-start(bf16[2,96,768]{2,1,0:T(8,128)(2,1)S(1)} %pad_maximum_fusion.70), channel_id=1, source_target_pairs={{0,2},{1,3},{2,0},{3,1},{4,6},{5,7},{6,4},{7,5},{8,10},{9,11},{10,... | collective-permute-start | bytes 884744 | tf_op jit(solution)/shard_map/ppermute | solution.py:54
  62.0 50.3 %collective-permute-start.15 = (bf16[2,144,768]{2,1,0:T(8,128)(2,1)S(1)}, bf16[2,144,768]{2,1,0:T(8,128)(2,1)S(1)}, u32[]{:S(2)}, u32[]{:S(2)}) collective-permute-start(bf16[2,144,768]{2,1,0:T(8,128)(2,1)S(1)} %pad_maximum_fusion.64), channel_id=1, source_target_pairs={{0,2},{1,3},{2,0},{3,1},{4,6},{5,7},{6,4},{7,5},{8,10},{9,11},{10,... | collective-permute-start | bytes 1327112 | tf_op jit(solution)/shard_map/ppermute | solution.py:54
  65.3 56.6 %collective-permute-start.30 = (bf16[2,144,768]{2,1,0:T(8,128)(2,1)S(1)}, bf16[2,144,768]{2,1,0:T(8,128)(2,1)S(1)}, u32[]{:S(2)}, u32[]{:S(2)}) collective-permute-start(bf16[2,144,768]{2,1,0:T(8,128)(2,1)S(1)} %pad_maximum_fusion.67), channel_id=1, source_target_pairs={{0,2},{1,3},{2,0},{3,1},{4,6},{5,7},{6,4},{7,5},{8,10},{9,11},{10,... | collective-permute-start | bytes 1327112 | tf_op jit(solution)/shard_map/ppermute | solution.py:54
  72.3 59.0 %collective-permute-start.10 = (bf16[2,144,768]{2,1,0:T(8,128)(2,1)S(1)}, bf16[2,144,768]{2,1,0:T(8,128)(2,1)S(1)}, u32[]{:S(2)}, u32[]{:S(2)}) collective-permute-start(bf16[2,144,768]{2,1,0:T(8,128)(2,1)S(1)} %pad_maximum_fusion.63), channel_id=1, source_target_pairs={{0,2},{1,3},{2,0},{3,1},{4,6},{5,7},{6,4},{7,5},{8,10},{9,11},{10,... | collective-permute-start | bytes 1327112 | tf_op jit(solution)/shard_map/ppermute | solution.py:54
  72.6 68.2 %collective-permute-start.26 = (bf16[2,144,768]{2,1,0:T(8,128)(2,1)S(1)}, bf16[2,144,768]{2,1,0:T(8,128)(2,1)S(1)}, u32[]{:S(2)}, u32[]{:S(2)}) collective-permute-start(bf16[2,144,768]{2,1,0:T(8,128)(2,1)S(1)} %pad_maximum_fusion.66), channel_id=1, source_target_pairs={{0,2},{1,3},{2,0},{3,1},{4,6},{5,7},{6,4},{7,5},{8,10},{9,11},{10,... | collective-permute-start | bytes 1327112 | tf_op jit(solution)/shard_map/ppermute | solution.py:54
  75.8 93.7 %collective-permute-start.4 = (bf16[2,3,96,768]{3,2,1,0:T(8,128)(2,1)S(1)}, bf16[2,3,96,768]{3,2,1,0:T(8,128)(2,1)S(1)}, u32[]{:S(2)}, u32[]{:S(2)}) collective-permute-start(bf16[2,3,96,768]{3,2,1,0:T(8,128)(2,1)S(1)} %pad_maximum_fusion.51), channel_id=1, source_target_pairs={{0,8},{1,9},{2,10},{3,11},{4,12},{5,13},{6,14},{7,15},{8,0},{9,1},... | collective-permute-start | bytes 2654216 | tf_op jit(solution)/shard_map/ppermute | solution.py:54
  112.4 58.0 %collective-permute-start.22 = (bf16[2,3,96,768]{3,2,1,0:T(8,128)(2,1)S(1)}, bf16[2,3,96,768]{3,2,1,0:T(8,128)(2,1)S(1)}, u32[]{:S(2)}, u32[]{:S(2)}) collective-permute-start(bf16[2,3,96,768]{3,2,1,0:T(8,128)(2,1)S(1)} %pad_maximum_fusion.52), channel_id=1, source_target_pairs={{0,8},{1,9},{2,10},{3,11},{4,12},{5,13},{6,14},{7,15},{8,0},{9,1},... | collective-permute-start | bytes 2654216 | tf_op jit(solution)/shard_map/ppermute | solution.py:54
  143.7 37.5 %collective-permute-start.17 = (bf16[2,3,144,768]{3,2,1,0:T(8,128)(2,1)S(1)}, bf16[2,3,144,768]{3,2,1,0:T(8,128)(2,1)S(1)}, u32[]{:S(2)}, u32[]{:S(2)}) collective-permute-start(bf16[2,3,144,768]{3,2,1,0:T(8,128)(2,1)S(1)} %pad_maximum_fusion.40), channel_id=1, source_target_pairs={{0,8},{1,9},{2,10},{3,11},{4,12},{5,13},{6,14},{7,15},{8,0},{9,1},... | collective-permute-start | bytes 3981320 | tf_op jit(solution)/shard_map/ppermute | solution.py:54
  151.9 88.4 %collective-permute-start.32 = (bf16[2,3,144,768]{3,2,1,0:T(8,128)(2,1)}, bf16[2,3,144,768]{3,2,1,0:T(8,128)(2,1)}, u32[]{:S(2)}, u32[]{:S(2)}) collective-permute-start(bf16[2,3,144,768]{3,2,1,0:T(8,128)(2,1)} %pad_maximum_fusion.42), channel_id=1, source_target_pairs={{0,8},{1,9},{2,10},{3,11},{4,12},{5,13},{6,14},{7,15},{8,0},{9,1},... | collective-permute-start | bytes 3981320 | tf_op jit(solution)/shard_map/ppermute | solution.py:54
  166.1 36.8 %collective-permute-start.12 = (bf16[2,3,144,768]{3,2,1,0:T(8,128)(2,1)S(1)}, bf16[2,3,144,768]{3,2,1,0:T(8,128)(2,1)S(1)}, u32[]{:S(2)}, u32[]{:S(2)}) collective-permute-start(bf16[2,3,144,768]{3,2,1,0:T(8,128)(2,1)S(1)} %pad_maximum_fusion.39), channel_id=1, source_target_pairs={{0,8},{1,9},{2,10},{3,11},{4,12},{5,13},{6,14},{7,15},{8,0},{9,1},... | collective-permute-start | bytes 3981320 | tf_op jit(solution)/shard_map/ppermute | solution.py:54
  169.5 142.3 %collective-permute-start.28 = (bf16[2,3,144,768]{3,2,1,0:T(8,128)(2,1)}, bf16[2,3,144,768]{3,2,1,0:T(8,128)(2,1)}, u32[]{:S(2)}, u32[]{:S(2)}) collective-permute-start(bf16[2,3,144,768]{3,2,1,0:T(8,128)(2,1)} %pad_maximum_fusion.41), channel_id=1, source_target_pairs={{0,8},{1,9},{2,10},{3,11},{4,12},{5,13},{6,14},{7,15},{8,0},{9,1},... | collective-permute-start | bytes 3981320 | tf_op jit(solution)/shard_map/ppermute | solution.py:54
  170.4 35.3 %collective-permute-start.5 = (bf16[2,768,768]{2,1,0:T(8,128)(2,1)S(1)}, bf16[2,768,768]{2,1,0:T(8,128)(2,1)S(1)}, u32[]{:S(2)}, u32[]{:S(2)}) collective-permute-start(bf16[2,768,768]{2,1,0:T(8,128)(2,1)S(1)} %bitcast.654), channel_id=1, source_target_pairs={{0,16},{1,17},{2,18},{3,19},{4,20},{5,21},{6,22},{7,23},{8,24},{9,... | collective-permute-start | bytes 7077896 | tf_op jit(solution)/shard_map/ppermute | solution.py:54
  181.2 99.8 %collective-permute-start.23 = (bf16[2,768,768]{2,1,0:T(8,128)(2,1)}, bf16[2,768,768]{2,1,0:T(8,128)(2,1)}, u32[]{:S(2)}, u32[]{:S(2)}) collective-permute-start(bf16[2,768,768]{2,1,0:T(8,128)(2,1)} %bitcast.92), channel_id=1, source_target_pairs={{0,16},{1,17},{2,18},{3,19},{4,20},{5,21},{6,22},{7,23},{8,24},{9,... | collective-permute-start | bytes 7077896 | tf_op jit(solution)/shard_map/ppermute | solution.py:54
  358.6 32.5 %collective-permute-start.34 = (bf16[384,768]{1,0:T(8,128)(2,1)S(1)}, bf16[384,768]{1,0:T(8,128)(2,1)S(1)}, u32[]{:S(2)}, u32[]{:S(2)}) collective-permute-start(bf16[384,768]{1,0:T(8,128)(2,1)S(1)} %get-tuple-element.70), channel_id=1, source_target_pairs={{0,16},{1,17},{2,18},{3,19},{4,20},{5,21},{6,22},{7,23},{8,24},{9,... | collective-permute-start | bytes 1769480 | tf_op jit(solution)/shard_map/ppermute | solution.py:54
  389.6 61.0 %collective-permute-start.57 = (bf16[2,4,144,768]{3,2,1,0:T(8,128)(2,1)}, bf16[2,4,144,768]{3,2,1,0:T(8,128)(2,1)}, u32[]{:S(2)}, u32[]{:S(2)}) collective-permute-start(bf16[2,4,144,768]{3,2,1,0:T(8,128)(2,1)} %bitcast.196), channel_id=1, source_target_pairs={{0,8},{1,9},{2,10},{3,11},{4,12},{5,13},{6,14},{7,15},{8,0},{9,1},... | collective-permute-start | bytes 5308424 | tf_op jit(solution)/shard_map/ppermute | solution.py:54
  390.8 63.1 %collective-permute-start.68 = (bf16[2,4,144,768]{3,2,1,0:T(8,128)(2,1)}, bf16[2,4,144,768]{3,2,1,0:T(8,128)(2,1)}, u32[]{:S(2)}, u32[]{:S(2)}) collective-permute-start(bf16[2,4,144,768]{3,2,1,0:T(8,128)(2,1)} %bitcast.217), channel_id=1, source_target_pairs={{0,8},{1,9},{2,10},{3,11},{4,12},{5,13},{6,14},{7,15},{8,0},{9,1},... | collective-permute-start | bytes 5308424 | tf_op jit(solution)/shard_map/ppermute | solution.py:54
  422.7 134.7 %collective-permute-start.45 = (bf16[1536,768]{1,0:T(8,128)(2,1)}, bf16[1536,768]{1,0:T(8,128)(2,1)}, u32[]{:S(2)}, u32[]{:S(2)}) collective-permute-start(bf16[1536,768]{1,0:T(8,128)(2,1)} %dynamic-slice_bitcast_fusion), channel_id=1, source_target_pairs={{0,16},{1,17},{2,18},{3,19},{4,20},{5,21},{6,22},{7,23},{8,24},{9,... | collective-permute-start | bytes 7077896 | tf_op jit(solution)/shard_map/ppermute | solution.py:54
  447.3 103.3 %collective-permute-start.53 = (bf16[2,4,144,768]{3,2,1,0:T(8,128)(2,1)}, bf16[2,4,144,768]{3,2,1,0:T(8,128)(2,1)}, u32[]{:S(2)}, u32[]{:S(2)}) collective-permute-start(bf16[2,4,144,768]{3,2,1,0:T(8,128)(2,1)} %bitcast.188), channel_id=1, source_target_pairs={{0,8},{1,9},{2,10},{3,11},{4,12},{5,13},{6,14},{7,15},{8,0},{9,1},... | collective-permute-start | bytes 5308424 | tf_op jit(solution)/shard_map/ppermute | solution.py:54
  450.6 102.2 %collective-permute-start.64 = (bf16[2,4,144,768]{3,2,1,0:T(8,128)(2,1)}, bf16[2,4,144,768]{3,2,1,0:T(8,128)(2,1)}, u32[]{:S(2)}, u32[]{:S(2)}) collective-permute-start(bf16[2,4,144,768]{3,2,1,0:T(8,128)(2,1)} %bitcast.209), channel_id=1, source_target_pairs={{0,8},{1,9},{2,10},{3,11},{4,12},{5,13},{6,14},{7,15},{8,0},{9,1},... | collective-permute-start | bytes 5308424 | tf_op jit(solution)/shard_map/ppermute | solution.py:54
  454.0 92.2 %collective-permute-start.58 = (bf16[4,144,768]{2,1,0:T(8,128)(2,1)}, bf16[4,144,768]{2,1,0:T(8,128)(2,1)}, u32[]{:S(2)}, u32[]{:S(2)}) collective-permute-start(bf16[4,144,768]{2,1,0:T(8,128)(2,1)} %slice_bitcast_fusion.13), channel_id=1, source_target_pairs={{0,4},{1,5},{2,6},{3,7},{4,0},{5,1},{6,2},{7,3},{8,12},{9,13},{10,... | collective-permute-start | bytes 2654216 | tf_op jit(solution)/shard_map/ppermute | solution.py:54
  458.3 90.6 %collective-permute-start.69 = (bf16[4,144,768]{2,1,0:T(8,128)(2,1)}, bf16[4,144,768]{2,1,0:T(8,128)(2,1)}, u32[]{:S(2)}, u32[]{:S(2)}) collective-permute-start(bf16[4,144,768]{2,1,0:T(8,128)(2,1)} %slice_bitcast_fusion.9), channel_id=1, source_target_pairs={{0,4},{1,5},{2,6},{3,7},{4,0},{5,1},{6,2},{7,3},{8,12},{9,13},{10,... | collective-permute-start | bytes 2654216 | tf_op jit(solution)/shard_map/ppermute | solution.py:54
  548.9 49.5 %collective-permute-start.40 = (bf16[1536,768]{1,0:T(8,128)(2,1)S(1)}, bf16[1536,768]{1,0:T(8,128)(2,1)S(1)}, u32[]{:S(2)}, u32[]{:S(2)}) collective-permute-start(bf16[1536,768]{1,0:T(8,128)(2,1)S(1)} %copy-done.58), channel_id=1, source_target_pairs={{0,16},{1,17},{2,18},{3,19},{4,20},{5,21},{6,22},{7,23},{8,24},{9,... | collective-permute-start | bytes 7077896 | tf_op jit(solution)/shard_map/ppermute | solution.py:54
  550.7 31.4 %collective-permute-start.59 = (bf16[2,144,768]{2,1,0:T(8,128)(2,1)S(1)}, bf16[2,144,768]{2,1,0:T(8,128)(2,1)S(1)}, u32[]{:S(2)}, u32[]{:S(2)}) collective-permute-start(bf16[2,144,768]{2,1,0:T(8,128)(2,1)S(1)} %slice.599), channel_id=1, source_target_pairs={{0,2},{1,3},{2,0},{3,1},{4,6},{5,7},{6,4},{7,5},{8,10},{9,11},{10,... | collective-permute-start | bytes 1327112 | tf_op jit(solution)/shard_map/ppermute | solution.py:54
  552.8 38.7 %collective-permute-start.70 = (bf16[2,144,768]{2,1,0:T(8,128)(2,1)S(1)}, bf16[2,144,768]{2,1,0:T(8,128)(2,1)S(1)}, u32[]{:S(2)}, u32[]{:S(2)}) collective-permute-start(bf16[2,144,768]{2,1,0:T(8,128)(2,1)S(1)} %slice.615), channel_id=1, source_target_pairs={{0,2},{1,3},{2,0},{3,1},{4,6},{5,7},{6,4},{7,5},{8,10},{9,11},{10,... | collective-permute-start | bytes 1327112 | tf_op jit(solution)/shard_map/ppermute | solution.py:54
  557.3 34.4 %collective-permute-start.54 = (bf16[4,144,768]{2,1,0:T(8,128)(2,1)S(1)}, bf16[4,144,768]{2,1,0:T(8,128)(2,1)S(1)}, u32[]{:S(2)}, u32[]{:S(2)}) collective-permute-start(bf16[4,144,768]{2,1,0:T(8,128)(2,1)S(1)} %slice_bitcast_fusion.15), channel_id=1, source_target_pairs={{0,4},{1,5},{2,6},{3,7},{4,0},{5,1},{6,2},{7,3},{8,12},{9,13},{10,... | collective-permute-start | bytes 2654216 | tf_op jit(solution)/shard_map/ppermute | solution.py:54
  561.9 31.5 %collective-permute-start.65 = (bf16[4,144,768]{2,1,0:T(8,128)(2,1)S(1)}, bf16[4,144,768]{2,1,0:T(8,128)(2,1)S(1)}, u32[]{:S(2)}, u32[]{:S(2)}) collective-permute-start(bf16[4,144,768]{2,1,0:T(8,128)(2,1)S(1)} %slice_bitcast_fusion.11), channel_id=1, source_target_pairs={{0,4},{1,5},{2,6},{3,7},{4,0},{5,1},{6,2},{7,3},{8,12},{9,13},{10,... | collective-permute-start | bytes 2654216 | tf_op jit(solution)/shard_map/ppermute | solution.py:54
  591.6 42.3 %collective-permute-start.60 = (bf16[144,768]{1,0:T(8,128)(2,1)S(1)}, bf16[144,768]{1,0:T(8,128)(2,1)S(1)}, u32[]{:S(2)}, u32[]{:S(2)}) collective-permute-start(bf16[144,768]{1,0:T(8,128)(2,1)S(1)} %slice_bitcast_fusion.33), channel_id=1, source_target_pairs={{0,1},{1,0},{2,3},{3,2},{4,5},{5,4},{6,7},{7,6},{8,9},{9,8},{10,11... | collective-permute-start | bytes 663560 | tf_op jit(solution)/shard_map/ppermute | solution.py:54
  591.7 52.3 %collective-permute-start.71 = (bf16[144,768]{1,0:T(8,128)(2,1)S(1)}, bf16[144,768]{1,0:T(8,128)(2,1)S(1)}, u32[]{:S(2)}, u32[]{:S(2)}) collective-permute-start(bf16[144,768]{1,0:T(8,128)(2,1)S(1)} %slice_bitcast_fusion.29), channel_id=1, source_target_pairs={{0,1},{1,0},{2,3},{3,2},{4,5},{5,4},{6,7},{7,6},{8,9},{9,8},{10,11... | collective-permute-start | bytes 663560 | tf_op jit(solution)/shard_map/ppermute | solution.py:54
  593.5 30.7 %collective-permute-start.55 = (bf16[2,144,768]{2,1,0:T(8,128)(2,1)S(1)}, bf16[2,144,768]{2,1,0:T(8,128)(2,1)S(1)}, u32[]{:S(2)}, u32[]{:S(2)}) collective-permute-start(bf16[2,144,768]{2,1,0:T(8,128)(2,1)S(1)} %slice.591), channel_id=1, source_target_pairs={{0,2},{1,3},{2,0},{3,1},{4,6},{5,7},{6,4},{7,5},{8,10},{9,11},{10,... | collective-permute-start | bytes 1327112 | tf_op jit(solution)/shard_map/ppermute | solution.py:54
  598.0 35.7 %collective-permute-start.66 = (bf16[2,144,768]{2,1,0:T(8,128)(2,1)S(1)}, bf16[2,144,768]{2,1,0:T(8,128)(2,1)S(1)}, u32[]{:S(2)}, u32[]{:S(2)}) collective-permute-start(bf16[2,144,768]{2,1,0:T(8,128)(2,1)S(1)} %slice.607), channel_id=1, source_target_pairs={{0,2},{1,3},{2,0},{3,1},{4,6},{5,7},{6,4},{7,5},{8,10},{9,11},{10,... | collective-permute-start | bytes 1327112 | tf_op jit(solution)/shard_map/ppermute | solution.py:54
  598.4 48.1 %collective-permute-start.47 = (bf16[4,96,768]{2,1,0:T(8,128)(2,1)S(1)}, bf16[4,96,768]{2,1,0:T(8,128)(2,1)S(1)}, u32[]{:S(2)}, u32[]{:S(2)}) collective-permute-start(bf16[4,96,768]{2,1,0:T(8,128)(2,1)S(1)} %slice_bitcast_fusion.25), channel_id=1, source_target_pairs={{0,4},{1,5},{2,6},{3,7},{4,0},{5,1},{6,2},{7,3},{8,12},{9,13},{10,... | collective-permute-start | bytes 1769480 | tf_op jit(solution)/shard_map/ppermute | solution.py:54
  (208 other events, 1843.7 us)

commit v2 on v1

v2 whole, which is shorter than its diff:
```python
import functools
import math

import jax
import jax.numpy as jnp
import numpy as np
from jax import lax
from jax.experimental import pallas as pl
from jax.experimental.pallas import tpu as pltpu
from jax.sharding import PartitionSpec as P

HEADS = 12
HEAD_DIM = 64
NORM_EPSILON = 1e-05
AXES = ("section", "dp", "tensor")
FEED_CHUNKS = 2
LANES = 128
GROUP = 3
GROUP_BACK = 3

F32 = jnp.float32
BF16 = jnp.bfloat16


def power_slopes(total_heads):
    return [2.0 ** (-8.0 * (index + 1) / total_heads) for index in range(total_heads)]


def alibi_table(number_heads):
    closest = 2 ** int(math.floor(math.log2(number_heads)))
    slopes = power_slopes(closest)
    slopes = slopes + power_slopes(2 * closest)[0::2][: number_heads - closest]
    return np.array(slopes, dtype=np.float32)


def norm_rows(values, gain, offset):
    row_mean = jnp.mean(values, axis=-1, keepdims=True)
    centred = values - row_mean
    row_var = jnp.mean(centred * centred, axis=-1, keepdims=True)
    return centred * lax.rsqrt(row_var + NORM_EPSILON) * gain + offset


def gelu_product(gate_part, up_part):
    return jax.nn.gelu(gate_part, approximate=False) * up_part


def dot(a, b, ca, cb):
    return lax.dot_general(a, b, (((ca,), (cb,)), ((), ())), preferred_element_type=F32)


def exchange(block, section_mask=0, dp_masks=(0, 0), tensor_mask=0):
    dp = lax.axis_size("dp")
    tensor = lax.axis_size("tensor")
    pairs = []
    for s in range(lax.axis_size("section")):
        for d in range(dp):
            for t in range(tensor):
                target = ((s ^ section_mask) * dp + (d ^ dp_masks[s])) * tensor + (t ^ tensor_mask)
                pairs.append(((s * dp + d) * tensor + t, target))
    return lax.ppermute(block, AXES, pairs)


def swap(block):
    return exchange(block, section_mask=1)


FIRST = (1, 2)
SECOND = (2, 1)
PLANE = 4
DEPTH = 4


def contract(a, b, ca, cb):
    return lax.dot_general(a, b, (((ca,), (cb,)), ((), ())), preferred_element_type=F32)


def head_masks(length):
    lane = lax.broadcasted_iota(jnp.int32, (length, LANES), 1)
    return [lane // HEAD_DIM == index for index in range(LANES // HEAD_DIM)]


def distances(length):
    across = lax.broadcasted_iota(jnp.int32, (length, length), 0)
    along = lax.broadcasted_iota(jnp.int32, (length, length), 1)
    return jnp.abs(across - along).astype(F32)


def attend_kernel(group, slopes_ref, projected_ref, context_ref):
    length, features = context_ref.shape
    masks = head_masks(length)
    distance = distances(length)
    per = len(masks)
    pairs = features // LANES
    for first in range(0, pairs, group):
        heads = [(pair, index) for pair in range(first, first + group) for index in range(per)]
        parts = {p: [slice(i * features + p * LANES, i * features + (p + 1) * LANES) for i in range(3)] for p, _ in heads}
        scores = []
        for pair, index in heads:
            key = projected_ref[:, parts[pair][1]]
            own = jnp.where(masks[index], key, jnp.zeros_like(key))
            scores.append(contract(own, projected_ref[:, parts[pair][0]], 1, 1))
        weights = []
        for (pair, index), score in zip(heads, scores):
            score = score * HEAD_DIM ** (-0.5) - slopes_ref[pair * per + index] * distance
            weight = jnp.exp(score - jnp.max(score, axis=0, keepdims=True))
            weight = weight * (1.0 / jnp.sum(weight, axis=0, keepdims=True))
            weights.append(weight.astype(BF16))
        for pair in range(first, first + group):
            value = projected_ref[:, parts[pair][2]]
            context = jnp.zeros((length, LANES), F32)
            for (other, index), weight in zip(heads, weights):
                if other == pair:
                    context = jnp.where(masks[index], contract(weight, value, 0, 0), context)
            context_ref[:, parts[pair][0]] = context.astype(BF16)


def attend_back_kernel(group, slopes_ref, projected_ref, context_grad_ref, grad_ref):
    length, features = context_grad_ref.shape
    masks = head_masks(length)
    distance = distances(length)
    per = len(masks)
    pairs = features // LANES
    for first in range(0, pairs, group):
        heads = [(pair, index) for pair in range(first, first + group) for index in range(per)]
        parts = {p: [slice(i * features + p * LANES, i * features + (p + 1) * LANES) for i in range(3)] for p, _ in heads}
        scores, weights_grads = [], []
        for pair, index in heads:
            key, value = projected_ref[:, parts[pair][1]], projected_ref[:, parts[pair][2]]
            own = jnp.where(masks[index], key, jnp.zeros_like(key))
            scores.append(contract(own, projected_ref[:, parts[pair][0]], 1, 1))
            own = jnp.where(masks[index], value, jnp.zeros_like(value))
            weights_grads.append(contract(own, context_grad_ref[:, parts[pair][0]], 1, 1))
        weights, score_grads = [], []
        for (pair, index), score, weights_grad in zip(heads, scores, weights_grads):
            score = score * HEAD_DIM ** (-0.5) - slopes_ref[pair * per + index] * distance
            weight = jnp.exp(score - jnp.max(score, axis=0, keepdims=True))
            weight = weight * (1.0 / jnp.sum(weight, axis=0, keepdims=True))
            mean_grad = jnp.sum(weight * weights_grad, axis=0, keepdims=True)
            score_grads.append((weight * (weights_grad - mean_grad)).astype(BF16))
            weights.append(weight.astype(BF16))
        for pair in range(first, first + group):
            query, key = projected_ref[:, parts[pair][0]], projected_ref[:, parts[pair][1]]
            context_grad = context_grad_ref[:, parts[pair][0]]
            grads = [jnp.zeros((length, LANES), F32)] * 3
            for (other, index), weight, score_grad in zip(heads, weights, score_grads):
                if other == pair:
                    new = [
                        contract(score_grad, key, 0, 0) * HEAD_DIM ** (-0.5),
                        contract(score_grad, query, 1, 0) * HEAD_DIM ** (-0.5),
                        contract(weight, context_grad, 1, 0),
                    ]
                    grads = [jnp.where(masks[index], n, g) for n, g in zip(new, grads)]
            for part, grad in zip(parts[pair], grads):
                grad_ref[:, part] = grad.astype(BF16)


def row_block(length, width):
    return pl.BlockSpec((length, width), lambda index: (index, 0))


def attend(projected, slopes, seqs):
    rows, width = projected.shape
    length, features = rows // seqs, width // 3
    return pl.pallas_call(
        functools.partial(attend_kernel, GROUP),
        grid=(seqs,),
        in_specs=[pl.BlockSpec(memory_space=pltpu.SMEM), row_block(length, width)],
        out_specs=row_block(length, features),
        out_shape=jax.ShapeDtypeStruct((rows, features), BF16),
        cost_estimate=pl.CostEstimate(
            flops=4 * rows * length * features, bytes_accessed=2 * rows * (width + features), transcendentals=rows * length * features // HEAD_DIM
        ),
        name="attend",
    )(slopes, projected)


def attend_back(projected, context_grad, slopes, seqs):
    rows, width = projected.shape
    length, features = rows // seqs, width // 3
    return pl.pallas_call(
        functools.partial(attend_back_kernel, GROUP_BACK),
        grid=(seqs,),
        in_specs=[
            pl.BlockSpec(memory_space=pltpu.SMEM),
            row_block(length, width),
            row_block(length, features),
        ],
        out_specs=row_block(length, width),
        out_shape=jax.ShapeDtypeStruct((rows, width), BF16),
        cost_estimate=pl.CostEstimate(
            flops=10 * rows * length * features, bytes_accessed=2 * rows * (2 * width + features), transcendentals=rows * length * features // HEAD_DIM
        ),
        name="attend_back",
    )(slopes, projected, context_grad)


def together(*trees):
    return lax.optimization_barrier(trees)


def near(chunk):
    return dict(chunk, near=exchange(chunk["own"][0], tensor_mask=1))


def far(chunk):
    mine, next_one = chunk["own"][0], chunk["near"]
    next_two = exchange(jnp.stack([mine, next_one]), tensor_mask=2)
    return dict(chunk, remote=jnp.concatenate([next_one[None], next_two]))


def first(chunk):
    return dict(chunk, first=exchange(chunk["remote"], dp_masks=FIRST))


def second(chunk):
    return dict(chunk, second=exchange(jnp.stack([chunk["remote"], chunk["first"]]), dp_masks=SECOND))


def assemble(chunk):
    rest = [chunk["remote"], chunk["first"], chunk["second"][0], chunk["second"][1]]
    return jnp.stack([jnp.concatenate([own[None], r]) for own, r in zip(chunk["own"], rest)])


def add_low(a, b):
    return (a.astype(F32) + b.astype(F32)).astype(BF16)


def reduce_second(terms):
    return add_low(terms[:2], exchange(terms[2:], dp_masks=SECOND))


def reduce_first(terms):
    return add_low(terms[0], exchange(terms[1], dp_masks=FIRST))


def reduce_near(terms):
    pairs = terms.reshape((2, 2) + terms.shape[1:])
    return add_low(pairs[:, 0], exchange(pairs[:, 1], tensor_mask=1))


def reduce_far(terms):
    one = add_low(terms[0], exchange(terms[1], tensor_mask=2))
    mask = PLANE
    while mask < lax.axis_size("dp"):
        one = add_low(one, exchange(one, dp_masks=(mask, mask)))
        mask *= 2
    return one


def attn_forward(own_low, weights, norms, slopes, seqs):
    wqkv, wo = weights
    projected = dot(own_low, wqkv, 1, 1).astype(BF16)
    context = attend(projected, slopes, seqs)
    first_sum = own_low.astype(F32) + dot(context, wo, 1, 0)
    first_norm = norm_rows(first_sum, norms[0], norms[1])
    return projected, context, first_sum, first_norm


def both_rows(rows_low):
    return jnp.concatenate([rows_low, swap(rows_low)])


def join_rows(terms):
    rows = terms.shape[0] // 2
    return terms[:rows] + swap(terms[rows:].astype(BF16)).astype(F32)


def feed_forward(first_all, weights):
    gate_up, down = weights
    gated = dot(first_all, gate_up, 1, 1)
    gate_part, up_part = jnp.split(gated, 2, axis=-1)
    hidden = gelu_product(gate_part, up_part).astype(BF16)
    return gated, hidden, dot(hidden, down, 1, 0)


def feed_backward(mixed_all, first_all, weights, gated, hidden):
    gate_up, down = weights
    hidden_grad = dot(mixed_all, down, 1, 1)
    down_grad = dot(hidden, mixed_all, 0, 0).astype(BF16)
    gate_part, up_part = jnp.split(gated, 2, axis=-1)
    _, gelu_back = jax.vjp(gelu_product, gate_part, up_part)
    gate_grad, up_grad = gelu_back(hidden_grad)
    gated_grad = jnp.concatenate([gate_grad, up_grad], axis=-1).astype(BF16)
    gate_up_grad = dot(gated_grad, first_all, 0, 0).astype(BF16)
    return gate_up_grad, down_grad, dot(gated_grad, gate_up, 1, 0)


def norm_backward(total, gain, offset, grad):
    _, back = jax.vjp(norm_rows, total, gain, offset)
    return back(grad)


def attn_backward(own_low, sum_grad, weights, projected, context, slopes, seqs):
    wqkv, wo = weights
    attended_low = sum_grad.astype(BF16)
    context_grad = dot(attended_low, wo, 1, 1).astype(BF16)
    out_grad = dot(context, attended_low, 0, 0).astype(BF16)
    projected_grad = attend_back(projected, context_grad, slopes, seqs)
    qkv_grad = dot(projected_grad, own_low, 0, 0).astype(BF16)
    return projected_grad, qkv_grad, out_grad


def body(
    layer_input,
    out_grad,
    loss_mask,
    query_key_value_weight,
    attention_output_weight,
    gate_up_weight,
    down_weight,
    norm1_gain,
    norm1_bias,
    norm2_gain,
    norm2_bias,
):
    core = lax.axis_index("section")
    plane = lax.axis_index("dp")
    depth = lax.axis_index("tensor")
    is_first = core == 0
    micro, own_seqs, length, features = layer_input.shape
    local = query_key_value_weight.shape[-1]
    local_heads = local // HEAD_DIM
    units = down_weight.shape[1]
    part = HEAD_DIM // PLANE
    unit_part = units // 2 // PLANE // FEED_CHUNKS
    seqs = micro * own_seqs // 2
    rows = seqs * length

    orders = [jnp.array([0, 1, 2, 3]), jnp.array([0, 2, 1, 3])]
    steps = jnp.where(is_first, orders[0], orders[1])
    in_plane = jnp.bitwise_and(plane, PLANE - 1)

    def relative(slab):
        return [
            lax.dynamic_index_in_dim(slab, jnp.bitwise_xor(in_plane, steps[e]), 0, keepdims=False)
            for e in range(PLANE)
        ]

    qkv_rows = jnp.transpose(query_key_value_weight[0], (1, 2, 0))
    attn_rows = jnp.concatenate([qkv_rows, attention_output_weight], axis=0)
    attn_slab = attn_rows.reshape(2, 2, local_heads, PLANE, part, features)
    attn_slab = jnp.transpose(attn_slab, (0, 3, 1, 2, 4, 5)).reshape(2, PLANE, -1, features)
    gate_up_rows = jnp.transpose(gate_up_weight[0], (1, 2, 0))
    feed_rows = jnp.concatenate([gate_up_rows, down_weight], axis=0)
    feed_slab = feed_rows.reshape(3, 2, FEED_CHUNKS, PLANE, unit_part, features)
    feed_slab = jnp.transpose(feed_slab, (2, 1, 3, 0, 4, 5)).reshape(FEED_CHUNKS, 2, PLANE, -1, features)

    def share(slab):
        keep = lax.dynamic_index_in_dim(slab, core, 0, keepdims=False)
        got = swap(lax.dynamic_index_in_dim(slab, 1 - core, 0, keepdims=False))
        return jnp.where(is_first, keep, got), jnp.where(is_first, got, keep)

    attn_in = [{"own": relative(own)} for own in share(attn_slab)]
    feed_in = [[{"own": relative(own)} for own in share(feed_slab[k])] for k in range(FEED_CHUNKS)]
    a0, a1 = attn_in
    (p0, p1), (q0, q1) = feed_in


    norm_table = jnp.concatenate([norm1_gain, norm1_bias, norm2_gain, norm2_bias])
    norm_other = swap(norm_table)
    norm_first = jnp.where(is_first, norm_table, norm_other)
    norm_second = jnp.where(is_first, norm_other, norm_table)
    norms = [tuple(table[i] for i in range(4)) for table in (norm_first, norm_second)]

    slope_table = jnp.asarray(alibi_table(HEADS)).reshape(DEPTH, local_heads)
    slopes = jnp.concatenate(
        [lax.dynamic_index_in_dim(slope_table, jnp.bitwise_xor(depth, j), 0, keepdims=False) for j in range(DEPTH)]
    )

    def own_half(whole):
        flat = whole.reshape((2, rows) + whole.shape[3:])
        return lax.dynamic_index_in_dim(flat, core, 0, keepdims=False)

    start = own_half(layer_input)
    seed = own_half(out_grad).astype(F32) * own_half(loss_mask).astype(F32)[..., None]


    def attn_weights(chunk):
        full = assemble(chunk).reshape(PLANE, DEPTH, 2, local_heads, part, features)
        mine = jnp.transpose(full, (2, 1, 3, 0, 4, 5)).reshape(2, -1, features)
        other = swap(mine)
        qk = jnp.where(is_first, mine, other)
        vo = jnp.where(is_first, other, mine)
        wqkv = jnp.concatenate([qk.reshape(-1, features), vo[0]])
        return wqkv, vo[1]

    def feed_weights(chunk):
        full = assemble(chunk).reshape(PLANE * DEPTH, 3, unit_part, features)
        full = jnp.transpose(full, (1, 0, 2, 3)).reshape(3, -1, features)
        return full[:2].reshape(-1, features), full[2]

    a0 = near(a0)
    a0, p0 = together(a0, p0)
    a0, p0 = far(a0), near(p0)
    a0, p0, q0 = together(a0, p0, q0)
    a0, p0, q0 = first(a0), far(p0), near(q0)
    a0, p0, q0, a1 = together(a0, p0, q0, a1)
    a0, p0, q0, a1 = second(a0), first(p0), far(q0), near(a1)
    attn0 = attn_weights(a0)
    p0, q0, a1, p1 = together(p0, q0, a1, p1)
    p0, q0, a1, p1 = second(p0), first(q0), far(a1), near(p1)
    projected0, context0, sum0, norm0 = attn_forward(start, attn0, norms[0], slopes, seqs)
    all0 = both_rows(norm0.astype(BF16))
    all0, p0, q0, a1, p1, q1 = together(all0, p0, q0, a1, p1, q1)
    q0, a1, p1, q1 = second(q0), first(a1), far(p1), near(q1)
    feed_p0 = feed_weights(p0)
    gated_p0, hidden_p0, mixed = feed_forward(all0, feed_p0)
    mixed, q0, a1, p1, q1 = together(mixed, q0, a1, p1, q1)
    a1, p1, q1 = second(a1), first(p1), far(q1)
    feed_q0 = feed_weights(q0)
    gated_q0, hidden_q0, more = feed_forward(all0, feed_q0)
    mixed = mixed + more
    mixed, a1, p1, q1 = together(mixed, a1, p1, q1)
    p1, q1 = second(p1), first(q1)
    attn1 = attn_weights(a1)
    total0 = norm0 + join_rows(mixed)
    middle_low = norm_rows(total0, norms[0][2], norms[0][3]).astype(BF16)
    projected1, context1, sum1, norm1 = attn_forward(middle_low, attn1, norms[1], slopes, seqs)
    all1 = both_rows(norm1.astype(BF16))
    all1, p1, q1 = together(all1, p1, q1)
    q1 = second(q1)
    feed_p1 = feed_weights(p1)
    gated_p1, hidden_p1, mixed = feed_forward(all1, feed_p1)
    mixed, q1 = together(mixed, q1)
    feed_q1 = feed_weights(q1)
    gated_q1, hidden_q1, more = feed_forward(all1, feed_q1)
    total1 = norm1 + join_rows(mixed + more)
    final_low = norm_rows(total1, norms[1][2], norms[1][3]).astype(BF16)

    def give(early, late):
        mine = jnp.where(is_first, early, late)
        got = swap(jnp.where(is_first, late, early))
        both = jnp.concatenate([jnp.where(is_first, mine, got), jnp.where(is_first, got, mine)])
        return both.reshape((1, micro, own_seqs, length, features))

    def feed_terms(gate_up, down):
        full = jnp.concatenate([gate_up, down]).reshape(3, PLANE, DEPTH, unit_part, features)
        return jnp.transpose(full, (1, 2, 0, 3, 4)).reshape(PLANE, DEPTH, -1, features)

    def attn_terms(qkv, out):
        full = jnp.concatenate([qkv, out]).reshape(2, -1, features)
        keep = lax.dynamic_index_in_dim(full, core, 0, keepdims=False)
        got = swap(lax.dynamic_index_in_dim(full, 1 - core, 0, keepdims=False))
        full = add_low(keep, got).reshape(2, DEPTH, local_heads, PLANE, part, features)
        return jnp.transpose(full, (3, 1, 0, 2, 4, 5)).reshape(PLANE, DEPTH, -1, features)

    def spread_first(pieces):
        one = jnp.concatenate(pieces)
        return jnp.stack([one, exchange(one, dp_masks=FIRST)])

    def spread_second(pair):
        return jnp.concatenate([pair, exchange(pair, dp_masks=SECOND)])

    second_grad, gain_two1, offset_two1 = norm_backward(total1, norms[1][2], norms[1][3], seed)
    mixed_all = both_rows(second_grad.astype(BF16))
    gate_up, down, terms = feed_backward(mixed_all, all1, feed_p1, gated_p1, hidden_p1)
    p1 = feed_terms(gate_up, down)
    p1, terms = together(p1, terms)
    p1 = reduce_second(p1)
    gate_up, down, more = feed_backward(mixed_all, all1, feed_q1, gated_q1, hidden_q1)
    q1 = feed_terms(gate_up, down)
    terms = terms + more
    terms, p1, q1 = together(terms, p1, q1)
    p1, q1 = reduce_first(p1), reduce_second(q1)
    first_grad = join_rows(terms) + second_grad
    sum_grad, gain_one1, offset_one1 = norm_backward(sum1, norms[1][0], norms[1][1], first_grad)
    projected_grad, qkv, out = attn_backward(middle_low, sum_grad, attn1, projected1, context1, slopes, seqs)
    a1 = attn_terms(qkv, out)
    layer_out = give(middle_low, final_low)
    projected_grad, a1, p1, q1, layer_out = together(projected_grad, a1, p1, q1, layer_out)
    a1, p1, q1 = reduce_second(a1), reduce_near(p1), reduce_first(q1)
    middle_grad = dot(projected_grad, attn1[0], 1, 0) + sum_grad
    second_grad, gain_two0, offset_two0 = norm_backward(total0, norms[0][2], norms[0][3], middle_grad)
    mixed_all = both_rows(second_grad.astype(BF16))
    gate_up, down, terms = feed_backward(mixed_all, all0, feed_p0, gated_p0, hidden_p0)
    p0 = feed_terms(gate_up, down)
    terms, a1, p1, q1, p0 = together(terms, a1, p1, q1, p0)
    a1, p1, q1, p0 = reduce_first(a1), reduce_far(p1), reduce_near(q1), reduce_second(p0)
    gate_up, down, more = feed_backward(mixed_all, all0, feed_q0, gated_q0, hidden_q0)
    q0 = feed_terms(gate_up, down)
    terms = terms + more
    terms, a1, p1, q1, p0, q0 = together(terms, a1, p1, q1, p0, q0)
    a1, q1, p0, q0 = reduce_near(a1), reduce_far(q1), reduce_first(p0), reduce_second(q0)
    first_grad = join_rows(terms) + second_grad
    sum_grad, gain_one0, offset_one0 = norm_backward(sum0, norms[0][0], norms[0][1], first_grad)
    vectors = jnp.stack(
        [gain_one0, offset_one0, gain_two0, offset_two0, gain_one1, offset_one1, gain_two1, offset_two1]
    )
    projected_grad, qkv, out = attn_backward(start, sum_grad, attn0, projected0, context0, slopes, seqs)
    a0 = attn_terms(qkv, out)
    projected_grad, a0, a1, q1, p0, q0, vectors = together(projected_grad, a0, a1, q1, p0, q0, vectors)
    a0, a1, p0, q0 = reduce_second(a0), reduce_far(a1), reduce_near(p0), reduce_first(q0)
    vectors = vectors + swap(vectors)
    start_grad = dot(projected_grad, attn0[0], 1, 0) + sum_grad
    input_grad = give(start_grad, middle_grad)
    input_grad, a0, a1, p0, q0, vectors = together(input_grad, a0, a1, p0, q0, vectors)
    a0, p0, q0 = reduce_first(a0), reduce_far(p0), reduce_near(q0)
    late = spread_first([p1, q1, a1])
    mask = 1
    while mask < lax.axis_size("dp"):
        vectors = vectors + exchange(vectors, dp_masks=(mask, mask))
        mask *= 2
    a0, p0, q0, late, vectors = together(a0, p0, q0, late, vectors)
    a0, q0 = reduce_near(a0), reduce_far(q0)
    late = spread_second(late)
    mask = 1
    while mask < lax.axis_size("tensor"):
        vectors = vectors + exchange(vectors, tensor_mask=mask)
        mask *= 2
    a0, p0, q0, late, vectors = together(a0, p0, q0, late, vectors)
    a0 = reduce_far(a0)
    feed_early = spread_second(spread_first([p0, q0]))
    attn_early = spread_second(spread_first([a0]))
    early = jnp.concatenate([feed_early, attn_early], axis=1)

    mine = jnp.where(is_first, early, late)
    got = swap(jnp.where(is_first, late, early))
    halves = [jnp.where(is_first, mine, got), jnp.where(is_first, got, mine)]
    both = jnp.stack(
        [
            jnp.stack(
                [
                    lax.dynamic_index_in_dim(half, order[jnp.bitwise_xor(in_plane, index)], 0, keepdims=False)
                    for half, order in zip(halves, orders)
                ]
            )
            for index in range(PLANE)
        ]
    )
    feed_rows = FEED_CHUNKS * 3 * unit_part
    feed_total = both[:, :, :feed_rows].reshape(PLANE, 2, FEED_CHUNKS, 3, unit_part, features)
    feed_total = jnp.transpose(feed_total, (3, 1, 2, 0, 4, 5)).reshape(3, units, features).astype(F32)
    grad_in = jnp.transpose(feed_total[:2], (2, 0, 1))
    grad_down = feed_total[2]
    attn_total = both[:, :, feed_rows:].reshape(PLANE, 2, 2, local_heads, part, features)
    attn_total = jnp.transpose(attn_total, (1, 2, 3, 0, 4, 5)).reshape(4, local, features).astype(F32)
    grad_qkv = jnp.transpose(attn_total[:3], (2, 0, 1))
    grad_out = attn_total[3]

    vectors = lax.dynamic_index_in_dim(vectors.reshape(2, 4, features), core, 0, keepdims=False)
    vectors = lax.dynamic_slice_in_dim(vectors, depth * local, local, 1)

    return (
        layer_out,
        input_grad,
        grad_qkv[None],
        grad_out[None],
        grad_in[None],
        grad_down[None],
        vectors[0][None],
        vectors[1][None],
        vectors[2][None],
        vectors[3][None],
    )


def solution(mesh):
    placed = (
        P(None, ("dp", "tensor"), None, None),
        P(None, ("dp", "tensor"), None, None),
        P(None, ("dp", "tensor"), None),
        P("section", None, None, "tensor"),
        P("section", "tensor", None),
        P("section", None, None, "tensor"),
        P("section", "tensor", None),
        P("section", None),
        P("section", None),
        P("section", None),
        P("section", None),
    )
    return jax.shard_map(
        body,
        mesh=mesh,
        in_specs=placed,
        out_specs=(
            P("section", None, ("dp", "tensor"), None, None),
            P("section", None, ("dp", "tensor"), None, None),
            P("section", None, None, "tensor"),
            P("section", "tensor", None),
            P("section", None, None, "tensor"),
            P("section", "tensor", None),
            P("section", "tensor"),
            P("section", "tensor"),
            P("section", "tensor"),
            P("section", "tensor"),
        ),
        check_vma=False,
    )
```

time: 728 us -> 618 us (0.85)
  local copies, waits for them, and re-layouts: 142 us -> 81 us
  blocking collectives: 56.8 us -> 0 us
  waiting for transfers between devices: 221 us -> 263 us
  other arithmetic: 112 us -> 84.4 us
  Pallas kernels: 0 us -> 22 us
  matrix products: 86.2 us -> 72.6 us
  starting transfers between devices: 83.1 us -> 70.9 us
    psum x1 -> x0, blocking collectives: 56.8 us -> none  [body(): vectors = lax.psum(jnp.stack([vectors_first, vectors_second]), AXES)]
    ppermute x75 -> x78, waiting for transfers between devices: 221 us -> 263 us  [exchange(): return lax.ppermute(block, AXES, pairs)]
    pallas_call x0 -> x4, Pallas kernels: none -> 22 us  [the longest x2 12 us: attend_back(): pl.pallas_call(functools.partial(attend_back_kernel, GROUP_BACK), grid=(s...]
    reshape x10 -> x5, local copies, waits for them, and re-layouts: 23.4 us -> 4.28 us  [the longest x4 2.93 us: feed_terms(): jnp.concatenate([gate_up, down])]
    unnamed x336 -> x331, local copies, waits for them, and re-layouts: 61.6 us -> 45.4 us
    slice x35 -> x28, local copies, waits for them, and re-layouts: 21.2 us -> 5.15 us  [the longest x12 1.91 us: feed_weights(): return (full[:2].reshape(-1, features), full[2])]
    another operation x58 -> x38, other arithmetic: 23.4 us -> 8.21 us  [the longest x18 3.23 us: assemble(): jnp.stack([jnp.concatenate([own[None], r]) for own, r in zip(chunk['own']...]
    convert_element_type x13 -> x9, other arithmetic: 39.4 us -> 25.9 us  [the longest x4 24.2 us: feed_forward(): hidden = gelu_product(gate_part, up_part).astype(BF16)]
  transfers between devices with their start and end apart: 75 -> 78, of which waited for: 24 -> 42; matrix products, arithmetic and copies ran while one was open for 39% -> 20% of each run, Pallas kernels for 0% -> 2%
where the time goes in v2:
time: 618 us; the launch traced here: 608 us
  waiting for transfers between devices  263 us (43%)
  other arithmetic  84.4 us (14%)
  local copies, waits for them, and re-layouts  81 us (13%)
  matrix products  72.6 us (12%)
  starting transfers between devices  70.9 us (11%)
  Pallas kernels  22 us (4%)
  between operations  14.7 us (2%)
    ppermute x78, waiting for transfers between devices, exchange(): return lax.ppermute(block, AXES, pairs)  263 us
    dot_general x36, matrix products, dot(): lax.dot_general(a, b, (((ca,), (cb,)), ((), ())), preferred_element_type=...  72.6 us
    ppermute x78, starting transfers between devices, exchange(): return lax.ppermute(block, AXES, pairs)  70.9 us
    unnamed x331, local copies, waits for them, and re-layouts  45.4 us
    convert_element_type x4, other arithmetic, feed_forward(): hidden = gelu_product(gate_part, up_part).astype(BF16)  24.2 us
    convert_element_type x26, other arithmetic, add_low(): return (a.astype(F32) + b.astype(F32)).astype(BF16)  16.2 us
  transfers between devices with their start and end apart: 78, of which 42 were waited for; matrix products, arithmetic and copies ran while one was open for 20% of the time, Pallas kernels for 2%

profile of v2, /device:TPU:1, one launch (start us, length us, event | category | flops | bytes accessed | tf_op | source)
XLA Modules:
  0.0 608.0 jit_solution(14779339845776545298)
XLA Ops:
  3.4 5.7 copy.68
  30.5 8.7 %collective-permute-done.3 = bf16[2,96,768]{2,1,0:T(8,128)(2,1)S(1)} collective-permute-done((bf16[2,96,768]{2,1,0:T(8,128)(2,1)S(1)}, bf16[2,96,768]{2,1,0:T(8,128)(2,1)S(1)}, u32[]{:S(2)}, u32[]{:S(2)}) %collective-permute-start.3) | collective-permute-done | bytes 294944 | tf_op jit(solution)/shard_map/ppermute | solution.py:60
  45.7 14.5 %collective-permute-done.7 = bf16[2,144,768]{2,1,0:T(8,128)(2,1)S(1)} collective-permute-done((bf16[2,144,768]{2,1,0:T(8,128)(2,1)S(1)}, bf16[2,144,768]{2,1,0:T(8,128)(2,1)S(1)}, u32[]{:S(2)}, u32[]{:S(2)}) %collective-permute-start.7) | collective-permute-done | bytes 442400 | tf_op jit(solution)/shard_map/ppermute | solution.py:60
  61.8 11.4 %collective-permute-done.9 = bf16[2,3,96,768]{3,2,1,0:T(8,128)(2,1)S(1)} collective-permute-done((bf16[2,3,96,768]{3,2,1,0:T(8,128)(2,1)S(1)}, bf16[2,3,96,768]{3,2,1,0:T(8,128)(2,1)S(1)}, u32[]{:S(2)}, u32[]{:S(2)}) %collective-permute-start.9) | collective-permute-done | bytes 884768 | tf_op jit(solution)/shard_map/ppermute | solution.py:60
  83.7 17.4 %collective-permute-done.14 = bf16[2,144,768]{2,1,0:T(8,128)(2,1)S(1)} collective-permute-done((bf16[2,144,768]{2,1,0:T(8,128)(2,1)S(1)}, bf16[2,144,768]{2,1,0:T(8,128)(2,1)S(1)}, u32[]{:S(2)}, u32[]{:S(2)}) %collective-permute-start.14) | collective-permute-done | bytes 442400 | tf_op jit(solution)/shard_map/ppermute | solution.py:60
  124.8 12.6 %collective-permute-done.18 = bf16[2,96,768]{2,1,0:T(8,128)(2,1)S(1)} collective-permute-done((bf16[2,96,768]{2,1,0:T(8,128)(2,1)S(1)}, bf16[2,96,768]{2,1,0:T(8,128)(2,1)S(1)}, u32[]{:S(2)}, u32[]{:S(2)}) %collective-permute-start.18) | collective-permute-done | bytes 294944 | tf_op jit(solution)/shard_map/ppermute | solution.py:60
  144.6 6.2 %multiply_convert_fusion.7 = (bf16[768,768]{1,0:T(8,128)(2,1)S(1)}, f32[768,768]{1,0:T(8,128)}) fusion(f32[768,1536]{1,0:T(8,128)S(1)} %fusion.116), kind=kLoop, calls=%fused_computation.102 | loop fusion | flops 38928384 | bytes 8257536 | tf_op jit(solution)/shard_map/convert_element_type | solution.py:272
  153.6 5.2 collective-permute-done.22
  171.4 5.9 multiply_convert_fusion.6
  179.0 7.0 %collective-permute-done.26 = bf16[2,144,768]{2,1,0:T(8,128)(2,1)S(1)} collective-permute-done((bf16[2,144,768]{2,1,0:T(8,128)(2,1)S(1)}, bf16[2,144,768]{2,1,0:T(8,128)(2,1)S(1)}, u32[]{:S(2)}, u32[]{:S(2)}) %collective-permute-start.26) | collective-permute-done | bytes 442400 | tf_op jit(solution)/shard_map/ppermute | solution.py:60
  210.7 8.1 %collective-permute-done.31 = bf16[3,144,768]{2,1,0:T(8,128)(2,1)S(1)} collective-permute-done((bf16[3,144,768]{2,1,0:T(8,128)(2,1)S(1)}, bf16[3,144,768]{2,1,0:T(8,128)(2,1)S(1)}, u32[]{:S(2)}, u32[]{:S(2)}) %collective-permute-start.31) | collective-permute-done | bytes 663584 | tf_op jit(solution)/shard_map/ppermute | solution.py:60
  225.6 6.0 multiply_convert_fusion.5
  232.7 6.6 %collective-permute-done.32 = bf16[2,3,144,768]{3,2,1,0:T(8,128)(2,1)S(1)} collective-permute-done((bf16[2,3,144,768]{3,2,1,0:T(8,128)(2,1)S(1)}, bf16[2,3,144,768]{3,2,1,0:T(8,128)(2,1)S(1)}, u32[]{:S(2)}, u32[]{:S(2)}) %collective-permute-start.32) | collective-permute-done | bytes 1327136 | tf_op jit(solution)/shard_map/ppermute | solution.py:60
  243.6 6.1 %multiply_convert_fusion.4 = (bf16[768,768]{1,0:T(8,128)(2,1)S(1)}, f32[768,768]{1,0:T(8,128)}) fusion(f32[768,1536]{1,0:T(8,128)S(1)} %fusion.122), kind=kLoop, calls=%fused_computation.63 | loop fusion | flops 38928384 | bytes 8257536 | tf_op jit(solution)/shard_map/convert_element_type | solution.py:272
  286.3 8.0 %collective-permute-done.35 = bf16[2,4,144,768]{3,2,1,0:T(8,128)(2,1)S(1)} collective-permute-done((bf16[2,4,144,768]{3,2,1,0:T(8,128)(2,1)S(1)}, bf16[2,4,144,768]{3,2,1,0:T(8,128)(2,1)S(1)}, u32[]{:S(2)}, u32[]{:S(2)}) %collective-permute-start.35) | collective-permute-done | bytes 1769504 | tf_op jit(solution)/shard_map/ppermute | solution.py:60
  304.8 6.1 attend_back.2
  322.7 18.6 %collective-permute-done.38 = bf16[4,144,768]{2,1,0:T(8,128)(2,1)S(1)} collective-permute-done((bf16[4,144,768]{2,1,0:T(8,128)(2,1)S(1)}, bf16[4,144,768]{2,1,0:T(8,128)(2,1)S(1)}, u32[]{:S(2)}, u32[]{:S(2)}) %collective-permute-start.38) | collective-permute-done | bytes 884768 | tf_op jit(solution)/shard_map/ppermute | solution.py:60
  341.5 6.7 %collective-permute-done.39 = bf16[2,4,144,768]{3,2,1,0:T(8,128)(2,1)S(1)} collective-permute-done((bf16[2,4,144,768]{3,2,1,0:T(8,128)(2,1)S(1)}, bf16[2,4,144,768]{3,2,1,0:T(8,128)(2,1)S(1)}, u32[]{:S(2)}, u32[]{:S(2)}) %collective-permute-start.39) | collective-permute-done | bytes 1769504 | tf_op jit(solution)/shard_map/ppermute | solution.py:60
  358.2 7.1 %collective-permute-done.43 = bf16[2,144,768]{2,1,0:T(8,128)(2,1)S(1)} collective-permute-done((bf16[2,144,768]{2,1,0:T(8,128)(2,1)S(1)}, bf16[2,144,768]{2,1,0:T(8,128)(2,1)S(1)}, u32[]{:S(2)}, u32[]{:S(2)}) %collective-permute-start.43) | collective-permute-done | bytes 442400 | tf_op jit(solution)/shard_map/ppermute | solution.py:60
  389.5 9.3 %collective-permute-done.46 = bf16[144,768]{1,0:T(8,128)(2,1)S(1)} collective-permute-done((bf16[144,768]{1,0:T(8,128)(2,1)S(1)}, bf16[144,768]{1,0:T(8,128)(2,1)S(1)}, u32[]{:S(2)}, u32[]{:S(2)}) %collective-permute-start.46) | collective-permute-done | bytes 221216 | tf_op jit(solution)/shard_map/ppermute | solution.py:60
  404.6 8.7 %collective-permute-done.48 = bf16[2,4,144,768]{3,2,1,0:T(8,128)(2,1)S(1)} collective-permute-done((bf16[2,4,144,768]{3,2,1,0:T(8,128)(2,1)S(1)}, bf16[2,4,144,768]{3,2,1,0:T(8,128)(2,1)S(1)}, u32[]{:S(2)}, u32[]{:S(2)}) %collective-permute-start.48) | collective-permute-done | bytes 1769504 | tf_op jit(solution)/shard_map/ppermute | solution.py:60
  425.9 5.9 attend_back.3
  444.1 10.9 %collective-permute-done.52 = bf16[144,768]{1,0:T(8,128)(2,1)S(1)} collective-permute-done((bf16[144,768]{1,0:T(8,128)(2,1)S(1)}, bf16[144,768]{1,0:T(8,128)(2,1)S(1)}, u32[]{:S(2)}, u32[]{:S(2)}) %collective-permute-start.52) | collective-permute-done | bytes 221216 | tf_op jit(solution)/shard_map/ppermute | solution.py:60
  456.0 7.4 %collective-permute-done.53 = bf16[4,144,768]{2,1,0:T(8,128)(2,1)} collective-permute-done((bf16[4,144,768]{2,1,0:T(8,128)(2,1)S(1)}, bf16[4,144,768]{2,1,0:T(8,128)(2,1)}, u32[]{:S(2)}, u32[]{:S(2)}) %collective-permute-start.53) | collective-permute-done | bytes 884768 | tf_op jit(solution)/shard_map/ppermute | solution.py:60
  464.7 7.3 %collective-permute-done.54 = bf16[2,4,144,768]{3,2,1,0:T(8,128)(2,1)} collective-permute-done((bf16[2,4,144,768]{3,2,1,0:T(8,128)(2,1)}, bf16[2,4,144,768]{3,2,1,0:T(8,128)(2,1)}, u32[]{:S(2)}, u32[]{:S(2)}) %collective-permute-start.54) | collective-permute-done | bytes 1769504 | tf_op jit(solution)/shard_map/ppermute | solution.py:60
  494.2 9.1 %collective-permute-done.56 = bf16[2,4,96,768]{3,2,1,0:T(8,128)(2,1)S(1)} collective-permute-done((bf16[2,4,96,768]{3,2,1,0:T(8,128)(2,1)S(1)}, bf16[2,4,96,768]{3,2,1,0:T(8,128)(2,1)S(1)}, u32[]{:S(2)}, u32[]{:S(2)}) %collective-permute-start.56) | collective-permute-done | bytes 1179680 | tf_op jit(solution)/shard_map/ppermute | solution.py:60
  508.7 5.4 collective-permute-done.66
  514.1 5.8 collective-permute-done.62
  525.7 11.0 %collective-permute-done.70 = f32[8,768]{1,0:T(8,128)S(1)} collective-permute-done((f32[8,768]{1,0:T(8,128)S(1)}, f32[8,768]{1,0:T(8,128)S(1)}, u32[]{:S(2)}, u32[]{:S(2)}) %collective-permute-start.70) | collective-permute-done | bytes 24608 | tf_op jit(solution)/shard_map/ppermute | solution.py:60
  542.8 6.3 %collective-permute-done.72 = bf16[288,768]{1,0:T(8,128)(2,1)S(1)} collective-permute-done((bf16[288,768]{1,0:T(8,128)(2,1)S(1)}, bf16[288,768]{1,0:T(8,128)(2,1)S(1)}, u32[]{:S(2)}, u32[]{:S(2)}) %collective-permute-start.72) | collective-permute-done | bytes 442400 | tf_op jit(solution)/shard_map/ppermute | solution.py:60
  554.9 12.0 %collective-permute-done.76 = bf16[2,96,768]{2,1,0:T(8,128)(2,1)S(1)} collective-permute-done((bf16[2,96,768]{2,1,0:T(8,128)(2,1)S(1)}, bf16[2,96,768]{2,1,0:T(8,128)(2,1)S(1)}, u32[]{:S(2)}, u32[]{:S(2)}) %collective-permute-start.76) | collective-permute-done | bytes 294944 | tf_op jit(solution)/shard_map/ppermute | solution.py:60
  597.6 8.3 %copy.107 = f32[1,768,2,768]{3,2,1,0:T(2,128)} copy(f32[1,768,2,768]{1,3,2,0:T(8,128)} %bitcast.520) | data formatting | bytes 9437184
  (749 shorter events, 318.2 us)
Async XLA Ops:
  39.3 20.9 %collective-permute-start.7 = (bf16[2,144,768]{2,1,0:T(8,128)(2,1)S(1)}, bf16[2,144,768]{2,1,0:T(8,128)(2,1)S(1)}, u32[]{:S(2)}, u32[]{:S(2)}) collective-permute-start(bf16[2,144,768]{2,1,0:T(8,128)(2,1)S(1)} %pad_maximum_fusion.58), channel_id=1, source_target_pairs={{0,2},{1,3},{2,0},{3,1},{4,6},{5,7},{6,4},{7,5},{8,10},{9,11},{10,... | collective-permute-start | bytes 1327112 | tf_op jit(solution)/shard_map/ppermute | solution.py:60
  39.4 20.9 %collective-permute-start.6 = (bf16[3,96,768]{2,1,0:T(8,128)(2,1)S(1)}, bf16[3,96,768]{2,1,0:T(8,128)(2,1)S(1)}, u32[]{:S(2)}, u32[]{:S(2)}) collective-permute-start(bf16[3,96,768]{2,1,0:T(8,128)(2,1)S(1)} %pad_maximum_fusion.57), channel_id=1, source_target_pairs={{0,4},{1,5},{2,6},{3,7},{4,0},{5,1},{6,2},{7,3},{8,12},{9,13},{10,... | collective-permute-start | bytes 1327112 | tf_op jit(solution)/shard_map/ppermute | solution.py:60
  40.4 19.8 %collective-permute-start.8 = (bf16[144,768]{1,0:T(8,128)(2,1)S(1)}, bf16[144,768]{1,0:T(8,128)(2,1)S(1)}, u32[]{:S(2)}, u32[]{:S(2)}) collective-permute-start(bf16[144,768]{1,0:T(8,128)(2,1)S(1)} %get-tuple-element.302), channel_id=1, source_target_pairs={{0,1},{1,0},{2,3},{3,2},{4,5},{5,4},{6,7},{7,6},{8,9},{9,8},{10,11... | collective-permute-start | bytes 663560 | tf_op jit(solution)/shard_map/ppermute | solution.py:60
  74.0 31.2 %collective-permute-start.10 = (bf16[2,768,768]{2,1,0:T(8,128)(2,1)S(1)}, bf16[2,768,768]{2,1,0:T(8,128)(2,1)}, u32[]{:S(2)}, u32[]{:S(2)}) collective-permute-start(bf16[2,768,768]{2,1,0:T(8,128)(2,1)S(1)} %bitcast.552), channel_id=1, source_target_pairs={{0,16},{1,17},{2,18},{3,19},{4,20},{5,21},{6,22},{7,23},{8,24},{9,... | collective-permute-start | bytes 7077896 | tf_op jit(solution)/shard_map/ppermute | solution.py:60
  78.1 24.0 %collective-permute-start.13 = (bf16[3,144,768]{2,1,0:T(8,128)(2,1)S(1)}, bf16[3,144,768]{2,1,0:T(8,128)(2,1)S(1)}, u32[]{:S(2)}, u32[]{:S(2)}) collective-permute-start(bf16[3,144,768]{2,1,0:T(8,128)(2,1)S(1)} %pad_maximum_fusion.53), channel_id=1, source_target_pairs={{0,4},{1,5},{2,6},{3,7},{4,0},{5,1},{6,2},{7,3},{8,12},{9,13},{10,... | collective-permute-start | bytes 1990664 | tf_op jit(solution)/shard_map/ppermute | solution.py:60
  80.1 21.1 %collective-permute-start.14 = (bf16[2,144,768]{2,1,0:T(8,128)(2,1)S(1)}, bf16[2,144,768]{2,1,0:T(8,128)(2,1)S(1)}, u32[]{:S(2)}, u32[]{:S(2)}) collective-permute-start(bf16[2,144,768]{2,1,0:T(8,128)(2,1)S(1)} %pad_maximum_fusion.59), channel_id=1, source_target_pairs={{0,2},{1,3},{2,0},{3,1},{4,6},{5,7},{6,4},{7,5},{8,10},{9,11},{10,... | collective-permute-start | bytes 1327112 | tf_op jit(solution)/shard_map/ppermute | solution.py:60
  81.4 20.6 %collective-permute-start.15 = (bf16[96,768]{1,0:T(8,128)(2,1)}, bf16[96,768]{1,0:T(8,128)(2,1)S(1)}, u32[]{:S(2)}, u32[]{:S(2)}) collective-permute-start(bf16[96,768]{1,0:T(8,128)(2,1)} %get-tuple-element.326), channel_id=1, source_target_pairs={{0,1},{1,0},{2,3},{3,2},{4,5},{5,4},{6,7},{7,6},{8,9},{9,8},{10,11... | collective-permute-start | bytes 442376 | tf_op jit(solution)/shard_map/ppermute | solution.py:60
  104.0 33.6 %collective-permute-start.16 = (bf16[2,3,144,768]{3,2,1,0:T(8,128)(2,1)}, bf16[2,3,144,768]{3,2,1,0:T(8,128)(2,1)}, u32[]{:S(2)}, u32[]{:S(2)}) collective-permute-start(bf16[2,3,144,768]{3,2,1,0:T(8,128)(2,1)} %pad_maximum_fusion.38), channel_id=1, source_target_pairs={{0,8},{1,9},{2,10},{3,11},{4,12},{5,13},{6,14},{7,15},{8,0},{9,1},... | collective-permute-start | bytes 3981320 | tf_op jit(solution)/shard_map/ppermute | solution.py:60
  120.0 17.5 %collective-permute-start.12 = (bf16[384,768]{1,0:T(8,128)(2,1)S(1)}, bf16[384,768]{1,0:T(8,128)(2,1)S(1)}, u32[]{:S(2)}, u32[]{:S(2)}) collective-permute-start(bf16[384,768]{1,0:T(8,128)(2,1)S(1)} %fusion.51), channel_id=1, source_target_pairs={{0,16},{1,17},{2,18},{3,19},{4,20},{5,21},{6,22},{7,23},{8,24},{9,... | collective-permute-start | bytes 1769480 | tf_op jit(solution)/shard_map/ppermute | solution.py:60
  137.6 21.1 %collective-permute-start.22 = (bf16[2,144,768]{2,1,0:T(8,128)(2,1)S(1)}, bf16[2,144,768]{2,1,0:T(8,128)(2,1)S(1)}, u32[]{:S(2)}, u32[]{:S(2)}) collective-permute-start(bf16[2,144,768]{2,1,0:T(8,128)(2,1)S(1)} %pad_maximum_fusion.61), channel_id=1, source_target_pairs={{0,2},{1,3},{2,0},{3,1},{4,6},{5,7},{6,4},{7,5},{8,10},{9,11},{10,... | collective-permute-start | bytes 1327112 | tf_op jit(solution)/shard_map/ppermute | solution.py:60
  137.9 25.6 %collective-permute-start.20 = (bf16[2,3,144,768]{3,2,1,0:T(8,128)(2,1)S(1)}, bf16[2,3,144,768]{3,2,1,0:T(8,128)(2,1)S(1)}, u32[]{:S(2)}, u32[]{:S(2)}) collective-permute-start(bf16[2,3,144,768]{3,2,1,0:T(8,128)(2,1)S(1)} %pad_maximum_fusion.39), channel_id=1, source_target_pairs={{0,8},{1,9},{2,10},{3,11},{4,12},{5,13},{6,14},{7,15},{8,0},{9,1},... | collective-permute-start | bytes 3981320 | tf_op jit(solution)/shard_map/ppermute | solution.py:60
  163.5 22.5 %collective-permute-start.26 = (bf16[2,144,768]{2,1,0:T(8,128)(2,1)S(1)}, bf16[2,144,768]{2,1,0:T(8,128)(2,1)S(1)}, u32[]{:S(2)}, u32[]{:S(2)}) collective-permute-start(bf16[2,144,768]{2,1,0:T(8,128)(2,1)S(1)} %pad_maximum_fusion.62), channel_id=1, source_target_pairs={{0,2},{1,3},{2,0},{3,1},{4,6},{5,7},{6,4},{7,5},{8,10},{9,11},{10,... | collective-permute-start | bytes 1327112 | tf_op jit(solution)/shard_map/ppermute | solution.py:60
  164.1 22.8 %collective-permute-start.24 = (bf16[2,3,96,768]{3,2,1,0:T(8,128)(2,1)S(1)}, bf16[2,3,96,768]{3,2,1,0:T(8,128)(2,1)S(1)}, u32[]{:S(2)}, u32[]{:S(2)}) collective-permute-start(bf16[2,3,96,768]{3,2,1,0:T(8,128)(2,1)S(1)} %pad_maximum_fusion.51), channel_id=1, source_target_pairs={{0,8},{1,9},{2,10},{3,11},{4,12},{5,13},{6,14},{7,15},{8,0},{9,1},... | collective-permute-start | bytes 2654216 | tf_op jit(solution)/shard_map/ppermute | solution.py:60
  190.1 28.6 %collective-permute-start.30 = (bf16[2,3,144,768]{3,2,1,0:T(8,128)(2,1)}, bf16[2,3,144,768]{3,2,1,0:T(8,128)(2,1)}, u32[]{:S(2)}, u32[]{:S(2)}) collective-permute-start(bf16[2,3,144,768]{3,2,1,0:T(8,128)(2,1)} %pad_maximum_fusion.40), channel_id=1, source_target_pairs={{0,8},{1,9},{2,10},{3,11},{4,12},{5,13},{6,14},{7,15},{8,0},{9,1},... | collective-permute-start | bytes 3981320 | tf_op jit(solution)/shard_map/ppermute | solution.py:60
  222.3 17.0 %collective-permute-start.32 = (bf16[2,3,144,768]{3,2,1,0:T(8,128)(2,1)S(1)}, bf16[2,3,144,768]{3,2,1,0:T(8,128)(2,1)S(1)}, u32[]{:S(2)}, u32[]{:S(2)}) collective-permute-start(bf16[2,3,144,768]{3,2,1,0:T(8,128)(2,1)S(1)} %pad_maximum_fusion.41), channel_id=1, source_target_pairs={{0,8},{1,9},{2,10},{3,11},{4,12},{5,13},{6,14},{7,15},{8,0},{9,1},... | collective-permute-start | bytes 3981320 | tf_op jit(solution)/shard_map/ppermute | solution.py:60
  272.6 21.7 %collective-permute-start.35 = (bf16[2,4,144,768]{3,2,1,0:T(8,128)(2,1)S(1)}, bf16[2,4,144,768]{3,2,1,0:T(8,128)(2,1)S(1)}, u32[]{:S(2)}, u32[]{:S(2)}) collective-permute-start(bf16[2,4,144,768]{3,2,1,0:T(8,128)(2,1)S(1)} %slice.406), channel_id=1, source_target_pairs={{0,8},{1,9},{2,10},{3,11},{4,12},{5,13},{6,14},{7,15},{8,0},{9,1},... | collective-permute-start | bytes 5308424 | tf_op jit(solution)/shard_map/ppermute | solution.py:60
  315.1 33.6 %collective-permute-start.37 = (bf16[1536,768]{1,0:T(8,128)(2,1)S(1)}, bf16[1536,768]{1,0:T(8,128)(2,1)S(1)}, u32[]{:S(2)}, u32[]{:S(2)}) collective-permute-start(bf16[1536,768]{1,0:T(8,128)(2,1)S(1)} %dynamic-slice_bitcast_fusion.1), channel_id=1, source_target_pairs={{0,16},{1,17},{2,18},{3,19},{4,20},{5,21},{6,22},{7,23},{8,24},{9,... | collective-permute-start | bytes 7077896 | tf_op jit(solution)/shard_map/ppermute | solution.py:60
  317.0 31.2 %collective-permute-start.39 = (bf16[2,4,144,768]{3,2,1,0:T(8,128)(2,1)S(1)}, bf16[2,4,144,768]{3,2,1,0:T(8,128)(2,1)S(1)}, u32[]{:S(2)}, u32[]{:S(2)}) collective-permute-start(bf16[2,4,144,768]{3,2,1,0:T(8,128)(2,1)S(1)} %slice.412), channel_id=1, source_target_pairs={{0,8},{1,9},{2,10},{3,11},{4,12},{5,13},{6,14},{7,15},{8,0},{9,1},... | collective-permute-start | bytes 5308424 | tf_op jit(solution)/shard_map/ppermute | solution.py:60
  319.5 21.7 %collective-permute-start.38 = (bf16[4,144,768]{2,1,0:T(8,128)(2,1)S(1)}, bf16[4,144,768]{2,1,0:T(8,128)(2,1)S(1)}, u32[]{:S(2)}, u32[]{:S(2)}) collective-permute-start(bf16[4,144,768]{2,1,0:T(8,128)(2,1)S(1)} %slice_bitcast_fusion.12), channel_id=1, source_target_pairs={{0,4},{1,5},{2,6},{3,7},{4,0},{5,1},{6,2},{7,3},{8,12},{9,13},{10,... | collective-permute-start | bytes 2654216 | tf_op jit(solution)/shard_map/ppermute | solution.py:60
  356.5 28.0 %collective-permute-start.44 = (bf16[4,144,768]{2,1,0:T(8,128)(2,1)S(1)}, bf16[4,144,768]{2,1,0:T(8,128)(2,1)S(1)}, u32[]{:S(2)}, u32[]{:S(2)}) collective-permute-start(bf16[4,144,768]{2,1,0:T(8,128)(2,1)S(1)} %slice_bitcast_fusion.11), channel_id=1, source_target_pairs={{0,4},{1,5},{2,6},{3,7},{4,0},{5,1},{6,2},{7,3},{8,12},{9,13},{10,... | collective-permute-start | bytes 2654216 | tf_op jit(solution)/shard_map/ppermute | solution.py:60
  357.9 26.9 %collective-permute-start.42 = (bf16[2,4,96,768]{3,2,1,0:T(8,128)(2,1)S(1)}, bf16[2,4,96,768]{3,2,1,0:T(8,128)(2,1)S(1)}, u32[]{:S(2)}, u32[]{:S(2)}) collective-permute-start(bf16[2,4,96,768]{3,2,1,0:T(8,128)(2,1)S(1)} %slice.415), channel_id=1, source_target_pairs={{0,8},{1,9},{2,10},{3,11},{4,12},{5,13},{6,14},{7,15},{8,0},{9,1},... | collective-permute-start | bytes 3538952 | tf_op jit(solution)/shard_map/ppermute | solution.py:60
  385.2 28.1 %collective-permute-start.48 = (bf16[2,4,144,768]{3,2,1,0:T(8,128)(2,1)S(1)}, bf16[2,4,144,768]{3,2,1,0:T(8,128)(2,1)S(1)}, u32[]{:S(2)}, u32[]{:S(2)}) collective-permute-start(bf16[2,4,144,768]{3,2,1,0:T(8,128)(2,1)S(1)} %slice.427), channel_id=1, source_target_pairs={{0,8},{1,9},{2,10},{3,11},{4,12},{5,13},{6,14},{7,15},{8,0},{9,1},... | collective-permute-start | bytes 5308424 | tf_op jit(solution)/shard_map/ppermute | solution.py:60
  438.8 35.7 %collective-permute-start.50 = (bf16[1536,768]{1,0:T(8,128)(2,1)}, bf16[1536,768]{1,0:T(8,128)(2,1)}, u32[]{:S(2)}, u32[]{:S(2)}) collective-permute-start(bf16[1536,768]{1,0:T(8,128)(2,1)} %dynamic-slice_bitcast_fusion), channel_id=1, source_target_pairs={{0,16},{1,17},{2,18},{3,19},{4,20},{5,21},{6,22},{7,23},{8,24},{9,... | collective-permute-start | bytes 7077896 | tf_op jit(solution)/shard_map/ppermute | solution.py:60
  440.6 31.5 %collective-permute-start.54 = (bf16[2,4,144,768]{3,2,1,0:T(8,128)(2,1)}, bf16[2,4,144,768]{3,2,1,0:T(8,128)(2,1)}, u32[]{:S(2)}, u32[]{:S(2)}) collective-permute-start(bf16[2,4,144,768]{3,2,1,0:T(8,128)(2,1)} %slice.437), channel_id=1, source_target_pairs={{0,8},{1,9},{2,10},{3,11},{4,12},{5,13},{6,14},{7,15},{8,0},{9,1},... | collective-permute-start | bytes 5308424 | tf_op jit(solution)/shard_map/ppermute | solution.py:60
  441.5 21.8 %collective-permute-start.53 = (bf16[4,144,768]{2,1,0:T(8,128)(2,1)S(1)}, bf16[4,144,768]{2,1,0:T(8,128)(2,1)}, u32[]{:S(2)}, u32[]{:S(2)}) collective-permute-start(bf16[4,144,768]{2,1,0:T(8,128)(2,1)S(1)} %slice_bitcast_fusion.10), channel_id=1, source_target_pairs={{0,4},{1,5},{2,6},{3,7},{4,0},{5,1},{6,2},{7,3},{8,12},{9,13},{10,... | collective-permute-start | bytes 2654216 | tf_op jit(solution)/shard_map/ppermute | solution.py:60
  484.9 18.4 %collective-permute-start.56 = (bf16[2,4,96,768]{3,2,1,0:T(8,128)(2,1)S(1)}, bf16[2,4,96,768]{3,2,1,0:T(8,128)(2,1)S(1)}, u32[]{:S(2)}, u32[]{:S(2)}) collective-permute-start(bf16[2,4,96,768]{3,2,1,0:T(8,128)(2,1)S(1)} %slice.439), channel_id=1, source_target_pairs={{0,8},{1,9},{2,10},{3,11},{4,12},{5,13},{6,14},{7,15},{8,0},{9,1},... | collective-permute-start | bytes 3538952 | tf_op jit(solution)/shard_map/ppermute | solution.py:60
  504.5 17.7 %collective-permute-start.64 = (bf16[384,768]{1,0:T(8,128)(2,1)S(1)}, bf16[384,768]{1,0:T(8,128)(2,1)S(1)}, u32[]{:S(2)}, u32[]{:S(2)}) collective-permute-start(bf16[384,768]{1,0:T(8,128)(2,1)S(1)} %constant_dynamic-update-slice_fusion), channel_id=1, source_target_pairs={{0,4},{1,5},{2,6},{3,7},{4,0},{5,1},{6,2},{7,3},{8,12},{9,13},{10,... | collective-permute-start | bytes 1769480 | tf_op jit(solution)/shard_map/ppermute | solution.py:60
  505.3 16.8 %collective-permute-start.63 = (bf16[2,144,768]{2,1,0:T(8,128)(2,1)S(1)}, bf16[2,144,768]{2,1,0:T(8,128)(2,1)S(1)}, u32[]{:S(2)}, u32[]{:S(2)}) collective-permute-start(bf16[2,144,768]{2,1,0:T(8,128)(2,1)S(1)} %slice_bitcast_fusion.23), channel_id=1, source_target_pairs={{0,1},{1,0},{2,3},{3,2},{4,5},{5,4},{6,7},{7,6},{8,9},{9,8},{10,11... | collective-permute-start | bytes 1327112 | tf_op jit(solution)/shard_map/ppermute | solution.py:60
  522.5 18.8 %collective-permute-start.69 = (bf16[2,384,768]{2,1,0:T(8,128)(2,1)S(1)}, bf16[2,384,768]{2,1,0:T(8,128)(2,1)S(1)}, u32[]{:S(2)}, u32[]{:S(2)}) collective-permute-start(bf16[2,384,768]{2,1,0:T(8,128)(2,1)S(1)} %pad_maximum_fusion.49), channel_id=1, source_target_pairs={{0,8},{1,9},{2,10},{3,11},{4,12},{5,13},{6,14},{7,15},{8,0},{9,1},... | collective-permute-start | bytes 3538952 | tf_op jit(solution)/shard_map/ppermute | solution.py:60
  523.3 17.8 %collective-permute-start.68 = (bf16[144,768]{1,0:T(8,128)(2,1)S(1)}, bf16[144,768]{1,0:T(8,128)(2,1)S(1)}, u32[]{:S(2)}, u32[]{:S(2)}) collective-permute-start(bf16[144,768]{1,0:T(8,128)(2,1)S(1)} %slice_bitcast_fusion.35), channel_id=1, source_target_pairs={{0,2},{1,3},{2,0},{3,1},{4,6},{5,7},{6,4},{7,5},{8,10},{9,11},{10,... | collective-permute-start | bytes 663560 | tf_op jit(solution)/shard_map/ppermute | solution.py:60
  524.2 17.0 %collective-permute-start.67 = (bf16[2,96,768]{2,1,0:T(8,128)(2,1)S(1)}, bf16[2,96,768]{2,1,0:T(8,128)(2,1)S(1)}, u32[]{:S(2)}, u32[]{:S(2)}) collective-permute-start(bf16[2,96,768]{2,1,0:T(8,128)(2,1)S(1)} %slice_bitcast_fusion.31), channel_id=1, source_target_pairs={{0,1},{1,0},{2,3},{3,2},{4,5},{5,4},{6,7},{7,6},{8,9},{9,8},{10,11... | collective-permute-start | bytes 884744 | tf_op jit(solution)/shard_map/ppermute | solution.py:60
  549.1 17.8 %collective-permute-start.73 = (bf16[2,288,768]{2,1,0:T(8,128)(2,1)S(1)}, bf16[2,288,768]{2,1,0:T(8,128)(2,1)S(1)}, u32[]{:S(2)}, u32[]{:S(2)}) collective-permute-start(bf16[2,288,768]{2,1,0:T(8,128)(2,1)S(1)} %pad_maximum_fusion.52), channel_id=1, source_target_pairs={{0,8},{1,9},{2,10},{3,11},{4,12},{5,13},{6,14},{7,15},{8,0},{9,1},... | collective-permute-start | bytes 2654216 | tf_op jit(solution)/shard_map/ppermute | solution.py:60
  (211 other events, 1788.5 us)

commit v3 on v2

--- a/solution.py
+++ b/solution.py
@@ -396,13 +396,13 @@
     a0, p0, q0 = first(a0), far(p0), near(q0)
     a0, p0, q0, a1 = together(a0, p0, q0, a1)
     a0, p0, q0, a1 = second(a0), first(p0), far(q0), near(a1)
+    a0, p0, q0, a1, p1 = together(a0, p0, q0, a1, p1)
+    p0, q0, a1, p1 = second(p0), first(q0), far(a1), near(p1)
     attn0 = attn_weights(a0)
-    p0, q0, a1, p1 = together(p0, q0, a1, p1)
-    p0, q0, a1, p1 = second(p0), first(q0), far(a1), near(p1)
     projected0, context0, sum0, norm0 = attn_forward(start, attn0, norms[0], slopes, seqs)
-    all0 = both_rows(norm0.astype(BF16))
-    all0, p0, q0, a1, p1, q1 = together(all0, p0, q0, a1, p1, q1)
+    low0, p0, q0, a1, p1, q1 = together(norm0.astype(BF16), p0, q0, a1, p1, q1)
     q0, a1, p1, q1 = second(q0), first(a1), far(p1), near(q1)
+    all0 = both_rows(low0)
     feed_p0 = feed_weights(p0)
     gated_p0, hidden_p0, mixed = feed_forward(all0, feed_p0)
     mixed, q0, a1, p1, q1 = together(mixed, q0, a1, p1, q1)
@@ -416,9 +416,9 @@
     total0 = norm0 + join_rows(mixed)
     middle_low = norm_rows(total0, norms[0][2], norms[0][3]).astype(BF16)
     projected1, context1, sum1, norm1 = attn_forward(middle_low, attn1, norms[1], slopes, seqs)
-    all1 = both_rows(norm1.astype(BF16))
-    all1, p1, q1 = together(all1, p1, q1)
+    low1, p1, q1 = together(norm1.astype(BF16), p1, q1)
     q1 = second(q1)
+    all1 = both_rows(low1)
     feed_p1 = feed_weights(p1)
     gated_p1, hidden_p1, mixed = feed_forward(all1, feed_p1)
     mixed, q1 = together(mixed, q1)
@@ -444,6 +444,12 @@
         full = add_low(keep, got).reshape(2, DEPTH, local_heads, PLANE, part, features)
         return jnp.transpose(full, (3, 1, 0, 2, 4, 5)).reshape(PLANE, DEPTH, -1, features)
 
+    def hand_over(block, source):
+        planes, depths = lax.axis_size("dp"), lax.axis_size("tensor")
+        count = planes * depths
+        pairs = [(source * count + i, (1 - source) * count + i) for i in range(count)]
+        return lax.ppermute(block, AXES, pairs)
+
     def spread_first(pieces):
         one = jnp.concatenate(pieces)
         return jnp.stack([one, exchange(one, dp_masks=FIRST)])
@@ -455,7 +461,7 @@
     mixed_all = both_rows(second_grad.astype(BF16))
     gate_up, down, terms = feed_backward(mixed_all, all1, feed_p1, gated_p1, hidden_p1)
     p1 = feed_terms(gate_up, down)
-    p1, terms = together(p1, terms)
+    p1, terms, mixed_all = together(p1, terms, mixed_all)
     p1 = reduce_second(p1)
     gate_up, down, more = feed_backward(mixed_all, all1, feed_q1, gated_q1, hidden_q1)
     q1 = feed_terms(gate_up, down)
@@ -465,16 +471,16 @@
     first_grad = join_rows(terms) + second_grad
     sum_grad, gain_one1, offset_one1 = norm_backward(sum1, norms[1][0], norms[1][1], first_grad)
     projected_grad, qkv, out = attn_backward(middle_low, sum_grad, attn1, projected1, context1, slopes, seqs)
-    a1 = attn_terms(qkv, out)
     layer_out = give(middle_low, final_low)
-    projected_grad, a1, p1, q1, layer_out = together(projected_grad, a1, p1, q1, layer_out)
+    projected_grad, qkv, out, p1, q1, layer_out = together(projected_grad, qkv, out, p1, q1, layer_out)
+    projected_grad, a1 = together(projected_grad, attn_terms(qkv, out))
     a1, p1, q1 = reduce_second(a1), reduce_near(p1), reduce_first(q1)
     middle_grad = dot(projected_grad, attn1[0], 1, 0) + sum_grad
     second_grad, gain_two0, offset_two0 = norm_backward(total0, norms[0][2], norms[0][3], middle_grad)
     mixed_all = both_rows(second_grad.astype(BF16))
     gate_up, down, terms = feed_backward(mixed_all, all0, feed_p0, gated_p0, hidden_p0)
     p0 = feed_terms(gate_up, down)
-    terms, a1, p1, q1, p0 = together(terms, a1, p1, q1, p0)
+    terms, mixed_all, a1, p1, q1, p0 = together(terms, mixed_all, a1, p1, q1, p0)
     a1, p1, q1, p0 = reduce_first(a1), reduce_far(p1), reduce_near(q1), reduce_second(p0)
     gate_up, down, more = feed_backward(mixed_all, all0, feed_q0, gated_q0, hidden_q0)
     q0 = feed_terms(gate_up, down)
@@ -487,9 +493,8 @@
         [gain_one0, offset_one0, gain_two0, offset_two0, gain_one1, offset_one1, gain_two1, offset_two1]
     )
     projected_grad, qkv, out = attn_backward(start, sum_grad, attn0, projected0, context0, slopes, seqs)
-    a0 = attn_terms(qkv, out)
-    projected_grad, a0, a1, q1, p0, q0, vectors = together(projected_grad, a0, a1, q1, p0, q0, vectors)
-    a0, a1, p0, q0 = reduce_second(a0), reduce_far(a1), reduce_near(p0), reduce_first(q0)
+    projected_grad, qkv, out, a1, q1, p0, q0, vectors = together(projected_grad, qkv, out, a1, q1, p0, q0, vectors)
+    a0, a1, p0, q0 = reduce_second(attn_terms(qkv, out)), reduce_far(a1), reduce_near(p0), reduce_first(q0)
     vectors = vectors + swap(vectors)
     start_grad = dot(projected_grad, attn0[0], 1, 0) + sum_grad
     input_grad = give(start_grad, middle_grad)
@@ -508,31 +513,36 @@
         vectors = vectors + exchange(vectors, tensor_mask=mask)
         mask *= 2
     a0, p0, q0, late, vectors = together(a0, p0, q0, late, vectors)
-    a0 = reduce_far(a0)
-    feed_early = spread_second(spread_first([p0, q0]))
-    attn_early = spread_second(spread_first([a0]))
-    early = jnp.concatenate([feed_early, attn_early], axis=1)
-
-    mine = jnp.where(is_first, early, late)
-    got = swap(jnp.where(is_first, late, early))
-    halves = [jnp.where(is_first, mine, got), jnp.where(is_first, got, mine)]
-    both = jnp.stack(
-        [
-            jnp.stack(
-                [
-                    lax.dynamic_index_in_dim(half, order[jnp.bitwise_xor(in_plane, index)], 0, keepdims=False)
-                    for half, order in zip(halves, orders)
-                ]
-            )
-            for index in range(PLANE)
-        ]
-    )
+    a0, feed_early = reduce_far(a0), spread_first([p0, q0])
+    late_got = hand_over(late, 0)
+    a0, feed_early, late_got = together(a0, feed_early, late_got)
+    attn_early, feed_early = spread_first([a0]), spread_second(feed_early)
+    attn_early, feed_early = together(attn_early, feed_early)
+    attn_early, feed_got = spread_second(attn_early), hand_over(feed_early, 1)
+    attn_got = hand_over(attn_early, 1)
+
+    def settle(early, early_got, late, late_got):
+        halves = [jnp.where(is_first, early, late_got), jnp.where(is_first, early_got, late)]
+        return jnp.stack(
+            [
+                jnp.stack(
+                    [
+                        lax.dynamic_index_in_dim(half, order[jnp.bitwise_xor(in_plane, index)], 0, keepdims=False)
+                        for half, order in zip(halves, orders)
+                    ]
+                )
+                for index in range(PLANE)
+            ]
+        )
+
     feed_rows = FEED_CHUNKS * 3 * unit_part
-    feed_total = both[:, :, :feed_rows].reshape(PLANE, 2, FEED_CHUNKS, 3, unit_part, features)
+    feed_both = settle(feed_early, feed_got, late[:, :feed_rows], late_got[:, :feed_rows])
+    attn_both = settle(attn_early, attn_got, late[:, feed_rows:], late_got[:, feed_rows:])
+    feed_total = feed_both.reshape(PLANE, 2, FEED_CHUNKS, 3, unit_part, features)
     feed_total = jnp.transpose(feed_total, (3, 1, 2, 0, 4, 5)).reshape(3, units, features).astype(F32)
     grad_in = jnp.transpose(feed_total[:2], (2, 0, 1))
     grad_down = feed_total[2]
-    attn_total = both[:, :, feed_rows:].reshape(PLANE, 2, 2, local_heads, part, features)
+    attn_total = attn_both.reshape(PLANE, 2, 2, local_heads, part, features)
     attn_total = jnp.transpose(attn_total, (1, 2, 3, 0, 4, 5)).reshape(4, local, features).astype(F32)
     grad_qkv = jnp.transpose(attn_total[:3], (2, 0, 1))
     grad_out = attn_total[3]

time: 618 us -> 570 us (0.922)
  waiting for transfers between devices: 263 us -> 229 us
  other arithmetic: 84.4 us -> 98.1 us
  matrix products: 72.6 us -> 60.1 us
  starting transfers between devices: 70.9 us -> 59.2 us
    ppermute x78 -> x77, waiting for transfers between devices: 263 us -> 229 us  [exchange(): return lax.ppermute(block, AXES, pairs)]
    ppermute x78 -> x77, starting transfers between devices: 70.9 us -> 53.6 us  [exchange(): return lax.ppermute(block, AXES, pairs)]
    dot_general x36, matrix products: 72.6 us -> 60.1 us  [dot(): lax.dot_general(a, b, (((ca,), (cb,)), ((), ())), preferred_element_type=...]
    unnamed x331 -> x324, local copies, waits for them, and re-layouts: 45.4 us -> 41 us
  transfers between devices with their start and end apart: 78 -> 80, of which waited for: 42 -> 37; matrix products, arithmetic and copies ran while one was open for 20% -> 29% of each run, Pallas kernels for 2% -> 4%
where the time goes in v3:
time: 570 us; the launch traced here: 559 us
  waiting for transfers between devices  229 us (40%)
  other arithmetic  98.1 us (17%)
  local copies, waits for them, and re-layouts  76.4 us (13%)
  matrix products  60.1 us (11%)
  starting transfers between devices  59.2 us (10%)
  Pallas kernels  21.9 us (4%)
  between operations  14.9 us (3%)
    ppermute x77, waiting for transfers between devices, exchange(): return lax.ppermute(block, AXES, pairs)  229 us
    dot_general x36, matrix products, dot(): lax.dot_general(a, b, (((ca,), (cb,)), ((), ())), preferred_element_type=...  60.1 us
    ppermute x77, starting transfers between devices, exchange(): return lax.ppermute(block, AXES, pairs)  53.6 us
    unnamed x324, local copies, waits for them, and re-layouts  41 us
    convert_element_type x4, other arithmetic, feed_forward(): hidden = gelu_product(gate_part, up_part).astype(BF16)  24.2 us
    convert_element_type x26, other arithmetic, add_low(): return (a.astype(F32) + b.astype(F32)).astype(BF16)  13.9 us
    pallas_call x2, Pallas kernels, attend_back(): pl.pallas_call(functools.partial(attend_back_kernel, GROUP_BACK), grid=(s...  11.9 us
  transfers between devices with their start and end apart: 80, of which 37 were waited for; matrix products, arithmetic and copies ran while one was open for 29% of the time, Pallas kernels for 4%

profile of v3, /device:TPU:1, one launch (start us, length us, event | category | flops | bytes accessed | tf_op | source)
XLA Modules:
  0.0 559.1 jit_solution(10943778552891241435)
XLA Ops:
  3.4 5.7 %copy.68 = bf16[1,768,2,768]{1,3,2,0:T(8,128)(2,1)S(1)} copy(bf16[1,768,2,768]{3,2,1,0:T(2,128)(2,1)} %param.19) | data formatting | bytes 4718592 | tf_op args[5]
  30.5 9.2 %collective-permute-done.3 = bf16[2,96,768]{2,1,0:T(8,128)(2,1)S(1)} collective-permute-done((bf16[2,96,768]{2,1,0:T(8,128)(2,1)S(1)}, bf16[2,96,768]{2,1,0:T(8,128)(2,1)S(1)}, u32[]{:S(2)}, u32[]{:S(2)}) %collective-permute-start.3) | collective-permute-done | bytes 294944 | tf_op jit(solution)/shard_map/ppermute | solution.py:60
  44.4 17.8 %collective-permute-done.7 = bf16[2,144,768]{2,1,0:T(8,128)(2,1)S(1)} collective-permute-done((bf16[2,144,768]{2,1,0:T(8,128)(2,1)S(1)}, bf16[2,144,768]{2,1,0:T(8,128)(2,1)S(1)}, u32[]{:S(2)}, u32[]{:S(2)}) %collective-permute-start.7) | collective-permute-done | bytes 442400 | tf_op jit(solution)/shard_map/ppermute | solution.py:60
  67.4 18.9 %collective-permute-done.11 = bf16[2,144,768]{2,1,0:T(8,128)(2,1)S(1)} collective-permute-done((bf16[2,144,768]{2,1,0:T(8,128)(2,1)S(1)}, bf16[2,144,768]{2,1,0:T(8,128)(2,1)S(1)}, u32[]{:S(2)}, u32[]{:S(2)}) %collective-permute-start.11) | collective-permute-done | bytes 442400 | tf_op jit(solution)/shard_map/ppermute | solution.py:60
  99.3 9.6 %collective-permute-done.17 = bf16[2,96,768]{2,1,0:T(8,128)(2,1)S(1)} collective-permute-done((bf16[2,96,768]{2,1,0:T(8,128)(2,1)S(1)}, bf16[2,96,768]{2,1,0:T(8,128)(2,1)S(1)}, u32[]{:S(2)}, u32[]{:S(2)}) %collective-permute-start.17) | collective-permute-done | bytes 294944 | tf_op jit(solution)/shard_map/ppermute | solution.py:60
  116.3 4.9 attend.2
  134.2 12.2 %collective-permute-done.22 = bf16[2,144,768]{2,1,0:T(8,128)(2,1)S(1)} collective-permute-done((bf16[2,144,768]{2,1,0:T(8,128)(2,1)S(1)}, bf16[2,144,768]{2,1,0:T(8,128)(2,1)S(1)}, u32[]{:S(2)}, u32[]{:S(2)}) %collective-permute-start.22) | collective-permute-done | bytes 442400 | tf_op jit(solution)/shard_map/ppermute | solution.py:60
  149.5 6.2 %multiply_convert_fusion.7 = (bf16[768,768]{1,0:T(8,128)(2,1)S(1)}, f32[768,768]{1,0:T(8,128)}) fusion(f32[768,1536]{1,0:T(8,128)S(1)} %fusion.117), kind=kLoop, calls=%fused_computation.99 | loop fusion | flops 38928384 | bytes 8257536 | tf_op jit(solution)/shard_map/convert_element_type | solution.py:272
  162.7 6.0 %multiply_convert_fusion.6 = (bf16[768,768]{1,0:T(8,128)(2,1)S(1)}, f32[768,768]{1,0:T(8,128)}) fusion(f32[768,1536]{1,0:T(8,128)S(1)} %fusion.119), kind=kLoop, calls=%fused_computation.86 | loop fusion | flops 38928384 | bytes 8257536 | tf_op jit(solution)/shard_map/convert_element_type | solution.py:272
  171.1 8.1 %collective-permute-done.26 = bf16[2,144,768]{2,1,0:T(8,128)(2,1)S(1)} collective-permute-done((bf16[2,144,768]{2,1,0:T(8,128)(2,1)S(1)}, bf16[2,144,768]{2,1,0:T(8,128)(2,1)S(1)}, u32[]{:S(2)}, u32[]{:S(2)}) %collective-permute-start.26) | collective-permute-done | bytes 442400 | tf_op jit(solution)/shard_map/ppermute | solution.py:60
  192.1 5.1 attend.3
  200.0 6.2 %collective-permute-done.29 = bf16[2,3,144,768]{3,2,1,0:T(8,128)(2,1)} collective-permute-done((bf16[2,3,144,768]{3,2,1,0:T(8,128)(2,1)}, bf16[2,3,144,768]{3,2,1,0:T(8,128)(2,1)}, u32[]{:S(2)}, u32[]{:S(2)}) %collective-permute-start.29) | collective-permute-done | bytes 1327136 | tf_op jit(solution)/shard_map/ppermute | solution.py:60
  214.2 6.0 %multiply_convert_fusion.5 = (bf16[768,768]{1,0:T(8,128)(2,1)S(1)}, f32[768,768]{1,0:T(8,128)}) fusion(f32[768,1536]{1,0:T(8,128)S(1)} %fusion.121), kind=kLoop, calls=%fused_computation.73 | loop fusion | flops 38928384 | bytes 8257536 | tf_op jit(solution)/shard_map/convert_element_type | solution.py:272
  221.3 7.4 %collective-permute-done.32 = bf16[2,3,144,768]{3,2,1,0:T(8,128)(2,1)S(1)} collective-permute-done((bf16[2,3,144,768]{3,2,1,0:T(8,128)(2,1)S(1)}, bf16[2,3,144,768]{3,2,1,0:T(8,128)(2,1)S(1)}, u32[]{:S(2)}, u32[]{:S(2)}) %collective-permute-start.32) | collective-permute-done | bytes 1327136 | tf_op jit(solution)/shard_map/ppermute | solution.py:60
  233.4 6.1 %multiply_convert_fusion.4 = (bf16[768,768]{1,0:T(8,128)(2,1)S(1)}, f32[768,768]{1,0:T(8,128)}) fusion(f32[768,1536]{1,0:T(8,128)S(1)} %fusion.123), kind=kLoop, calls=%fused_computation.60 | loop fusion | flops 38928384 | bytes 8257536 | tf_op jit(solution)/shard_map/convert_element_type | solution.py:272
  274.0 12.0 %collective-permute-done.35 = bf16[2,4,144,768]{3,2,1,0:T(8,128)(2,1)S(1)} collective-permute-done((bf16[2,4,144,768]{3,2,1,0:T(8,128)(2,1)S(1)}, bf16[2,4,144,768]{3,2,1,0:T(8,128)(2,1)S(1)}, u32[]{:S(2)}, u32[]{:S(2)}) %collective-permute-start.35) | collective-permute-done | bytes 1769504 | tf_op jit(solution)/shard_map/ppermute | solution.py:60
  297.7 6.1 %attend_back.2 = bf16[384,2304]{1,0:T(8,128)(2,1)} custom-call(f32[12]{0:T(128)} %pad_maximum_fusion.70.slopes_ref, bf16[384,2304]{1,0:T(8,128)(2,1)} %convolution_convert_fusion.2.projected_ref, bf16[384,768]{1,0:T(8,128)(2,1)} %convolution_convert_fusion.15.context_grad_ref), custom_call_target="tpu_custom_call" | custom-call | flops 377487360 | bytes 4128768 | tf_op jit(solution)/shard_map/attend_back/pallas_call | solution.py:180
  312.0 11.5 %collective-permute-done.38 = bf16[2,4,144,768]{3,2,1,0:T(8,128)(2,1)} collective-permute-done((bf16[2,4,144,768]{3,2,1,0:T(8,128)(2,1)}, bf16[2,4,144,768]{3,2,1,0:T(8,128)(2,1)}, u32[]{:S(2)}, u32[]{:S(2)}) %collective-permute-start.38) | collective-permute-done | bytes 1769504 | tf_op jit(solution)/shard_map/ppermute | solution.py:60
  326.5 4.0 collective-permute-done.40
  349.2 5.0 collective-permute-done.42
  370.3 15.3 %collective-permute-done.48 = bf16[2,4,144,768]{3,2,1,0:T(8,128)(2,1)S(1)} collective-permute-done((bf16[2,4,144,768]{3,2,1,0:T(8,128)(2,1)S(1)}, bf16[2,4,144,768]{3,2,1,0:T(8,128)(2,1)S(1)}, u32[]{:S(2)}, u32[]{:S(2)}) %collective-permute-start.48) | collective-permute-done | bytes 1769504 | tf_op jit(solution)/shard_map/ppermute | solution.py:60
  392.8 6.0 %collective-permute-done.51 = bf16[144,768]{1,0:T(8,128)(2,1)S(1)} collective-permute-done((bf16[144,768]{1,0:T(8,128)(2,1)S(1)}, bf16[144,768]{1,0:T(8,128)(2,1)S(1)}, u32[]{:S(2)}, u32[]{:S(2)}) %collective-permute-start.51) | collective-permute-done | bytes 221216 | tf_op jit(solution)/shard_map/ppermute | solution.py:60
  409.0 5.8 %attend_back.3 = bf16[384,2304]{1,0:T(8,128)(2,1)} custom-call(f32[12]{0:T(128)} %pad_maximum_fusion.70.slopes_ref, bf16[384,2304]{1,0:T(8,128)(2,1)} %convolution_convert_fusion.3.projected_ref, bf16[384,768]{1,0:T(8,128)(2,1)} %convolution_convert_fusion.14.context_grad_ref), custom_call_target="tpu_custom_call" | custom-call | flops 377487360 | bytes 4128768 | tf_op jit(solution)/shard_map/attend_back/pallas_call | solution.py:180
  434.7 6.7 %collective-permute-done.58 = bf16[2,144,768]{2,1,0:T(8,128)(2,1)S(1)} collective-permute-done((bf16[2,144,768]{2,1,0:T(8,128)(2,1)S(1)}, bf16[2,144,768]{2,1,0:T(8,128)(2,1)S(1)}, u32[]{:S(2)}, u32[]{:S(2)}) %collective-permute-start.58) | collective-permute-done | bytes 442400 | tf_op jit(solution)/shard_map/ppermute | solution.py:60
  446.1 7.3 %collective-permute-done.56 = bf16[2,4,96,768]{3,2,1,0:T(8,128)(2,1)S(1)} collective-permute-done((bf16[2,4,96,768]{3,2,1,0:T(8,128)(2,1)S(1)}, bf16[2,4,96,768]{3,2,1,0:T(8,128)(2,1)S(1)}, u32[]{:S(2)}, u32[]{:S(2)}) %collective-permute-start.56) | collective-permute-done | bytes 1179680 | tf_op jit(solution)/shard_map/ppermute | solution.py:60
  459.4 6.7 %collective-permute-done.66 = f32[8,768]{1,0:T(8,128)S(1)} collective-permute-done((f32[8,768]{1,0:T(8,128)S(1)}, f32[8,768]{1,0:T(8,128)S(1)}, u32[]{:S(2)}, u32[]{:S(2)}) %collective-permute-start.66) | collective-permute-done | bytes 24608 | tf_op jit(solution)/shard_map/ppermute | solution.py:60
  467.1 4.9 collective-permute-done.63
  476.8 11.6 %collective-permute-done.70 = f32[8,768]{1,0:T(8,128)S(1)} collective-permute-done((f32[8,768]{1,0:T(8,128)S(1)}, f32[8,768]{1,0:T(8,128)S(1)}, u32[]{:S(2)}, u32[]{:S(2)}) %collective-permute-start.70) | collective-permute-done | bytes 24608 | tf_op jit(solution)/shard_map/ppermute | solution.py:60
  497.2 8.6 %collective-permute-done.72 = bf16[96,768]{1,0:T(8,128)(2,1)S(1)} collective-permute-done((bf16[96,768]{1,0:T(8,128)(2,1)S(1)}, bf16[96,768]{1,0:T(8,128)(2,1)S(1)}, u32[]{:S(2)}, u32[]{:S(2)}) %collective-permute-start.72) | collective-permute-done | bytes 147488 | tf_op jit(solution)/shard_map/ppermute | solution.py:60
  507.4 4.9 collective-permute-done.75
  512.3 8.8 %collective-permute-done.76 = bf16[2,288,768]{2,1,0:T(8,128)(2,1)S(1)} collective-permute-done((bf16[2,288,768]{2,1,0:T(8,128)(2,1)S(1)}, bf16[2,288,768]{2,1,0:T(8,128)(2,1)S(1)}, u32[]{:S(2)}, u32[]{:S(2)}) %collective-permute-start.76) | collective-permute-done | bytes 884768 | tf_op jit(solution)/shard_map/ppermute | solution.py:60
  548.8 8.3 %copy.108 = f32[1,768,2,768]{3,2,1,0:T(2,128)} copy(f32[1,768,2,768]{1,3,2,0:T(8,128)} %bitcast.522) | data formatting | bytes 9437184
  (761 shorter events, 281.3 us)
Async XLA Ops:
  39.9 22.4 %collective-permute-start.7 = (bf16[2,144,768]{2,1,0:T(8,128)(2,1)S(1)}, bf16[2,144,768]{2,1,0:T(8,128)(2,1)S(1)}, u32[]{:S(2)}, u32[]{:S(2)}) collective-permute-start(bf16[2,144,768]{2,1,0:T(8,128)(2,1)S(1)} %pad_maximum_fusion.57), channel_id=1, source_target_pairs={{0,2},{1,3},{2,0},{3,1},{4,6},{5,7},{6,4},{7,5},{8,10},{9,11},{10,... | collective-permute-start | bytes 1327112 | tf_op jit(solution)/shard_map/ppermute | solution.py:60
  39.9 22.4 %collective-permute-start.6 = (bf16[3,96,768]{2,1,0:T(8,128)(2,1)S(1)}, bf16[3,96,768]{2,1,0:T(8,128)(2,1)S(1)}, u32[]{:S(2)}, u32[]{:S(2)}) collective-permute-start(bf16[3,96,768]{2,1,0:T(8,128)(2,1)S(1)} %pad_maximum_fusion.56), channel_id=1, source_target_pairs={{0,4},{1,5},{2,6},{3,7},{4,0},{5,1},{6,2},{7,3},{8,12},{9,13},{10,... | collective-permute-start | bytes 1327112 | tf_op jit(solution)/shard_map/ppermute | solution.py:60
  41.2 21.1 %collective-permute-start.8 = (bf16[144,768]{1,0:T(8,128)(2,1)S(1)}, bf16[144,768]{1,0:T(8,128)(2,1)S(1)}, u32[]{:S(2)}, u32[]{:S(2)}) collective-permute-start(bf16[144,768]{1,0:T(8,128)(2,1)S(1)} %get-tuple-element.327), channel_id=1, source_target_pairs={{0,1},{1,0},{2,3},{3,2},{4,5},{5,4},{6,7},{7,6},{8,9},{9,8},{10,11... | collective-permute-start | bytes 663560 | tf_op jit(solution)/shard_map/ppermute | solution.py:60
  62.4 23.9 %collective-permute-start.9 = (bf16[2,3,96,768]{3,2,1,0:T(8,128)(2,1)S(1)}, bf16[2,3,96,768]{3,2,1,0:T(8,128)(2,1)S(1)}, u32[]{:S(2)}, u32[]{:S(2)}) collective-permute-start(bf16[2,3,96,768]{3,2,1,0:T(8,128)(2,1)S(1)} %pad_maximum_fusion.45), channel_id=1, source_target_pairs={{0,8},{1,9},{2,10},{3,11},{4,12},{5,13},{6,14},{7,15},{8,0},{9,1},... | collective-permute-start | bytes 2654216 | tf_op jit(solution)/shard_map/ppermute | solution.py:60
  63.7 22.6 %collective-permute-start.10 = (bf16[3,144,768]{2,1,0:T(8,128)(2,1)S(1)}, bf16[3,144,768]{2,1,0:T(8,128)(2,1)S(1)}, u32[]{:S(2)}, u32[]{:S(2)}) collective-permute-start(bf16[3,144,768]{2,1,0:T(8,128)(2,1)S(1)} %pad_maximum_fusion.52), channel_id=1, source_target_pairs={{0,4},{1,5},{2,6},{3,7},{4,0},{5,1},{6,2},{7,3},{8,12},{9,13},{10,... | collective-permute-start | bytes 1990664 | tf_op jit(solution)/shard_map/ppermute | solution.py:60
  65.0 21.2 %collective-permute-start.11 = (bf16[2,144,768]{2,1,0:T(8,128)(2,1)S(1)}, bf16[2,144,768]{2,1,0:T(8,128)(2,1)S(1)}, u32[]{:S(2)}, u32[]{:S(2)}) collective-permute-start(bf16[2,144,768]{2,1,0:T(8,128)(2,1)S(1)} %pad_maximum_fusion.58), channel_id=1, source_target_pairs={{0,2},{1,3},{2,0},{3,1},{4,6},{5,7},{6,4},{7,5},{8,10},{9,11},{10,... | collective-permute-start | bytes 1327112 | tf_op jit(solution)/shard_map/ppermute | solution.py:60
  65.1 21.2 %collective-permute-start.12 = (bf16[96,768]{1,0:T(8,128)(2,1)S(1)}, bf16[96,768]{1,0:T(8,128)(2,1)S(1)}, u32[]{:S(2)}, u32[]{:S(2)}) collective-permute-start(bf16[96,768]{1,0:T(8,128)(2,1)S(1)} %get-tuple-element.351), channel_id=1, source_target_pairs={{0,1},{1,0},{2,3},{3,2},{4,5},{5,4},{6,7},{7,6},{8,9},{9,8},{10,11... | collective-permute-start | bytes 442376 | tf_op jit(solution)/shard_map/ppermute | solution.py:60
  87.8 21.1 %collective-permute-start.13 = (bf16[2,768,768]{2,1,0:T(8,128)(2,1)S(1)}, bf16[2,768,768]{2,1,0:T(8,128)(2,1)}, u32[]{:S(2)}, u32[]{:S(2)}) collective-permute-start(bf16[2,768,768]{2,1,0:T(8,128)(2,1)S(1)} %bitcast.559), channel_id=1, source_target_pairs={{0,16},{1,17},{2,18},{3,19},{4,20},{5,21},{6,22},{7,23},{8,24},{9,... | collective-permute-start | bytes 7077896 | tf_op jit(solution)/shard_map/ppermute | solution.py:60
  95.1 28.6 %collective-permute-start.18 = (bf16[144,768]{1,0:T(8,128)(2,1)}, bf16[144,768]{1,0:T(8,128)(2,1)}, u32[]{:S(2)}, u32[]{:S(2)}) collective-permute-start(bf16[144,768]{1,0:T(8,128)(2,1)} %get-tuple-element.370), channel_id=1, source_target_pairs={{0,1},{1,0},{2,3},{3,2},{4,5},{5,4},{6,7},{7,6},{8,9},{9,8},{10,11... | collective-permute-start | bytes 663560 | tf_op jit(solution)/shard_map/ppermute | solution.py:60
  97.6 26.1 %collective-permute-start.16 = (bf16[3,144,768]{2,1,0:T(8,128)(2,1)S(1)}, bf16[3,144,768]{2,1,0:T(8,128)(2,1)}, u32[]{:S(2)}, u32[]{:S(2)}) collective-permute-start(bf16[3,144,768]{2,1,0:T(8,128)(2,1)S(1)} %pad_maximum_fusion.53), channel_id=1, source_target_pairs={{0,4},{1,5},{2,6},{3,7},{4,0},{5,1},{6,2},{7,3},{8,12},{9,13},{10,... | collective-permute-start | bytes 1990664 | tf_op jit(solution)/shard_map/ppermute | solution.py:60
  99.0 24.7 %collective-permute-start.15 = (bf16[2,3,144,768]{3,2,1,0:T(8,128)(2,1)}, bf16[2,3,144,768]{3,2,1,0:T(8,128)(2,1)}, u32[]{:S(2)}, u32[]{:S(2)}) collective-permute-start(bf16[2,3,144,768]{3,2,1,0:T(8,128)(2,1)} %pad_maximum_fusion.36), channel_id=1, source_target_pairs={{0,8},{1,9},{2,10},{3,11},{4,12},{5,13},{6,14},{7,15},{8,0},{9,1},... | collective-permute-start | bytes 3981320 | tf_op jit(solution)/shard_map/ppermute | solution.py:60
  125.1 21.3 %collective-permute-start.22 = (bf16[2,144,768]{2,1,0:T(8,128)(2,1)S(1)}, bf16[2,144,768]{2,1,0:T(8,128)(2,1)S(1)}, u32[]{:S(2)}, u32[]{:S(2)}) collective-permute-start(bf16[2,144,768]{2,1,0:T(8,128)(2,1)S(1)} %pad_maximum_fusion.60), channel_id=1, source_target_pairs={{0,2},{1,3},{2,0},{3,1},{4,6},{5,7},{6,4},{7,5},{8,10},{9,11},{10,... | collective-permute-start | bytes 1327112 | tf_op jit(solution)/shard_map/ppermute | solution.py:60
  125.2 22.2 %collective-permute-start.19 = (bf16[384,768]{1,0:T(8,128)(2,1)S(1)}, bf16[384,768]{1,0:T(8,128)(2,1)S(1)}, u32[]{:S(2)}, u32[]{:S(2)}) collective-permute-start(bf16[384,768]{1,0:T(8,128)(2,1)S(1)} %fusion.53), channel_id=1, source_target_pairs={{0,16},{1,17},{2,18},{3,19},{4,20},{5,21},{6,22},{7,23},{8,24},{9,... | collective-permute-start | bytes 1769480 | tf_op jit(solution)/shard_map/ppermute | solution.py:60
  130.1 26.7 %collective-permute-start.23 = (bf16[144,768]{1,0:T(8,128)(2,1)S(1)}, bf16[144,768]{1,0:T(8,128)(2,1)S(1)}, u32[]{:S(2)}, u32[]{:S(2)}) collective-permute-start(bf16[144,768]{1,0:T(8,128)(2,1)S(1)} %copy-done.55), channel_id=1, source_target_pairs={{0,1},{1,0},{2,3},{3,2},{4,5},{5,4},{6,7},{7,6},{8,9},{9,8},{10,11... | collective-permute-start | bytes 663560 | tf_op jit(solution)/shard_map/ppermute | solution.py:60
  131.7 25.1 %collective-permute-start.21 = (bf16[3,96,768]{2,1,0:T(8,128)(2,1)S(1)}, bf16[3,96,768]{2,1,0:T(8,128)(2,1)S(1)}, u32[]{:S(2)}, u32[]{:S(2)}) collective-permute-start(bf16[3,96,768]{2,1,0:T(8,128)(2,1)S(1)} %pad_maximum_fusion.59), channel_id=1, source_target_pairs={{0,4},{1,5},{2,6},{3,7},{4,0},{5,1},{6,2},{7,3},{8,12},{9,13},{10,... | collective-permute-start | bytes 1327112 | tf_op jit(solution)/shard_map/ppermute | solution.py:60
  133.8 23.0 %collective-permute-start.20 = (bf16[2,3,144,768]{3,2,1,0:T(8,128)(2,1)S(1)}, bf16[2,3,144,768]{3,2,1,0:T(8,128)(2,1)S(1)}, u32[]{:S(2)}, u32[]{:S(2)}) collective-permute-start(bf16[2,3,144,768]{3,2,1,0:T(8,128)(2,1)S(1)} %pad_maximum_fusion.37), channel_id=1, source_target_pairs={{0,8},{1,9},{2,10},{3,11},{4,12},{5,13},{6,14},{7,15},{8,0},{9,1},... | collective-permute-start | bytes 3981320 | tf_op jit(solution)/shard_map/ppermute | solution.py:60
  156.9 22.4 %collective-permute-start.26 = (bf16[2,144,768]{2,1,0:T(8,128)(2,1)S(1)}, bf16[2,144,768]{2,1,0:T(8,128)(2,1)S(1)}, u32[]{:S(2)}, u32[]{:S(2)}) collective-permute-start(bf16[2,144,768]{2,1,0:T(8,128)(2,1)S(1)} %pad_maximum_fusion.61), channel_id=1, source_target_pairs={{0,2},{1,3},{2,0},{3,1},{4,6},{5,7},{6,4},{7,5},{8,10},{9,11},{10,... | collective-permute-start | bytes 1327112 | tf_op jit(solution)/shard_map/ppermute | solution.py:60
  157.0 22.4 %collective-permute-start.25 = (bf16[3,144,768]{2,1,0:T(8,128)(2,1)S(1)}, bf16[3,144,768]{2,1,0:T(8,128)(2,1)S(1)}, u32[]{:S(2)}, u32[]{:S(2)}) collective-permute-start(bf16[3,144,768]{2,1,0:T(8,128)(2,1)S(1)} %pad_maximum_fusion.54), channel_id=1, source_target_pairs={{0,4},{1,5},{2,6},{3,7},{4,0},{5,1},{6,2},{7,3},{8,12},{9,13},{10,... | collective-permute-start | bytes 1990664 | tf_op jit(solution)/shard_map/ppermute | solution.py:60
  157.4 22.0 %collective-permute-start.24 = (bf16[2,3,96,768]{3,2,1,0:T(8,128)(2,1)S(1)}, bf16[2,3,96,768]{3,2,1,0:T(8,128)(2,1)S(1)}, u32[]{:S(2)}, u32[]{:S(2)}) collective-permute-start(bf16[2,3,96,768]{3,2,1,0:T(8,128)(2,1)S(1)} %pad_maximum_fusion.46), channel_id=1, source_target_pairs={{0,8},{1,9},{2,10},{3,11},{4,12},{5,13},{6,14},{7,15},{8,0},{9,1},... | collective-permute-start | bytes 2654216 | tf_op jit(solution)/shard_map/ppermute | solution.py:60
  181.4 18.6 %collective-permute-start.30 = (bf16[3,144,768]{2,1,0:T(8,128)(2,1)S(1)}, bf16[3,144,768]{2,1,0:T(8,128)(2,1)}, u32[]{:S(2)}, u32[]{:S(2)}) collective-permute-start(bf16[3,144,768]{2,1,0:T(8,128)(2,1)S(1)} %pad_maximum_fusion.55), channel_id=1, source_target_pairs={{0,4},{1,5},{2,6},{3,7},{4,0},{5,1},{6,2},{7,3},{8,12},{9,13},{10,... | collective-permute-start | bytes 1990664 | tf_op jit(solution)/shard_map/ppermute | solution.py:60
  182.8 23.4 %collective-permute-start.29 = (bf16[2,3,144,768]{3,2,1,0:T(8,128)(2,1)}, bf16[2,3,144,768]{3,2,1,0:T(8,128)(2,1)}, u32[]{:S(2)}, u32[]{:S(2)}) collective-permute-start(bf16[2,3,144,768]{3,2,1,0:T(8,128)(2,1)} %pad_maximum_fusion.38), channel_id=1, source_target_pairs={{0,8},{1,9},{2,10},{3,11},{4,12},{5,13},{6,14},{7,15},{8,0},{9,1},... | collective-permute-start | bytes 3981320 | tf_op jit(solution)/shard_map/ppermute | solution.py:60
  211.7 17.0 %collective-permute-start.32 = (bf16[2,3,144,768]{3,2,1,0:T(8,128)(2,1)S(1)}, bf16[2,3,144,768]{3,2,1,0:T(8,128)(2,1)S(1)}, u32[]{:S(2)}, u32[]{:S(2)}) collective-permute-start(bf16[2,3,144,768]{3,2,1,0:T(8,128)(2,1)S(1)} %pad_maximum_fusion.39), channel_id=1, source_target_pairs={{0,8},{1,9},{2,10},{3,11},{4,12},{5,13},{6,14},{7,15},{8,0},{9,1},... | collective-permute-start | bytes 3981320 | tf_op jit(solution)/shard_map/ppermute | solution.py:60
  253.6 34.2 %collective-permute-start.39 = (bf16[384,768]{1,0:T(8,128)(2,1)}, bf16[384,768]{1,0:T(8,128)(2,1)}, u32[]{:S(2)}, u32[]{:S(2)}) collective-permute-start(bf16[384,768]{1,0:T(8,128)(2,1)} %get-tuple-element.501), channel_id=1, source_target_pairs={{0,16},{1,17},{2,18},{3,19},{4,20},{5,21},{6,22},{7,23},{8,24},{9,... | collective-permute-start | bytes 1769480 | tf_op jit(solution)/shard_map/ppermute | solution.py:60
  264.2 21.7 %collective-permute-start.35 = (bf16[2,4,144,768]{3,2,1,0:T(8,128)(2,1)S(1)}, bf16[2,4,144,768]{3,2,1,0:T(8,128)(2,1)S(1)}, u32[]{:S(2)}, u32[]{:S(2)}) collective-permute-start(bf16[2,4,144,768]{3,2,1,0:T(8,128)(2,1)S(1)} %slice.416), channel_id=1, source_target_pairs={{0,8},{1,9},{2,10},{3,11},{4,12},{5,13},{6,14},{7,15},{8,0},{9,1},... | collective-permute-start | bytes 5308424 | tf_op jit(solution)/shard_map/ppermute | solution.py:60
  291.4 19.2 %collective-permute-start.37 = (bf16[4,144,768]{2,1,0:T(8,128)(2,1)}, bf16[4,144,768]{2,1,0:T(8,128)(2,1)}, u32[]{:S(2)}, u32[]{:S(2)}) collective-permute-start(bf16[4,144,768]{2,1,0:T(8,128)(2,1)} %slice_bitcast_fusion.12), channel_id=1, source_target_pairs={{0,4},{1,5},{2,6},{3,7},{4,0},{5,1},{6,2},{7,3},{8,12},{9,13},{10,... | collective-permute-start | bytes 2654216 | tf_op jit(solution)/shard_map/ppermute | solution.py:60
  293.0 30.5 %collective-permute-start.38 = (bf16[2,4,144,768]{3,2,1,0:T(8,128)(2,1)}, bf16[2,4,144,768]{3,2,1,0:T(8,128)(2,1)}, u32[]{:S(2)}, u32[]{:S(2)}) collective-permute-start(bf16[2,4,144,768]{3,2,1,0:T(8,128)(2,1)} %slice.422), channel_id=1, source_target_pairs={{0,8},{1,9},{2,10},{3,11},{4,12},{5,13},{6,14},{7,15},{8,0},{9,1},... | collective-permute-start | bytes 5308424 | tf_op jit(solution)/shard_map/ppermute | solution.py:60
  357.8 27.8 %collective-permute-start.48 = (bf16[2,4,144,768]{3,2,1,0:T(8,128)(2,1)S(1)}, bf16[2,4,144,768]{3,2,1,0:T(8,128)(2,1)S(1)}, u32[]{:S(2)}, u32[]{:S(2)}) collective-permute-start(bf16[2,4,144,768]{3,2,1,0:T(8,128)(2,1)S(1)} %slice.437), channel_id=1, source_target_pairs={{0,8},{1,9},{2,10},{3,11},{4,12},{5,13},{6,14},{7,15},{8,0},{9,1},... | collective-permute-start | bytes 5308424 | tf_op jit(solution)/shard_map/ppermute | solution.py:60
  390.0 28.7 %collective-permute-start.52 = (bf16[4,144,768]{2,1,0:T(8,128)(2,1)}, bf16[4,144,768]{2,1,0:T(8,128)(2,1)}, u32[]{:S(2)}, u32[]{:S(2)}) collective-permute-start(bf16[4,144,768]{2,1,0:T(8,128)(2,1)} %slice_bitcast_fusion.10), channel_id=1, source_target_pairs={{0,4},{1,5},{2,6},{3,7},{4,0},{5,1},{6,2},{7,3},{8,12},{9,13},{10,... | collective-permute-start | bytes 2654216 | tf_op jit(solution)/shard_map/ppermute | solution.py:60
  392.6 29.6 %collective-permute-start.53 = (bf16[2,4,144,768]{3,2,1,0:T(8,128)(2,1)}, bf16[2,4,144,768]{3,2,1,0:T(8,128)(2,1)}, u32[]{:S(2)}, u32[]{:S(2)}) collective-permute-start(bf16[2,4,144,768]{3,2,1,0:T(8,128)(2,1)} %slice.447), channel_id=1, source_target_pairs={{0,8},{1,9},{2,10},{3,11},{4,12},{5,13},{6,14},{7,15},{8,0},{9,1},... | collective-permute-start | bytes 5308424 | tf_op jit(solution)/shard_map/ppermute | solution.py:60
  431.8 21.5 %collective-permute-start.56 = (bf16[2,4,96,768]{3,2,1,0:T(8,128)(2,1)S(1)}, bf16[2,4,96,768]{3,2,1,0:T(8,128)(2,1)S(1)}, u32[]{:S(2)}, u32[]{:S(2)}) collective-permute-start(bf16[2,4,96,768]{3,2,1,0:T(8,128)(2,1)S(1)} %bitcast.639), channel_id=1, source_target_pairs={{0,8},{1,9},{2,10},{3,11},{4,12},{5,13},{6,14},{7,15},{8,0},{9,1},... | collective-permute-start | bytes 3538952 | tf_op jit(solution)/shard_map/ppermute | solution.py:60
  472.6 19.7 %collective-permute-start.69 = (bf16[2,384,768]{2,1,0:T(8,128)(2,1)S(1)}, bf16[2,384,768]{2,1,0:T(8,128)(2,1)S(1)}, u32[]{:S(2)}, u32[]{:S(2)}) collective-permute-start(bf16[2,384,768]{2,1,0:T(8,128)(2,1)S(1)} %pad_maximum_fusion.44), channel_id=1, source_target_pairs={{0,8},{1,9},{2,10},{3,11},{4,12},{5,13},{6,14},{7,15},{8,0},{9,1},... | collective-permute-start | bytes 3538952 | tf_op jit(solution)/shard_map/ppermute | solution.py:60
  473.9 18.2 %collective-permute-start.68 = (bf16[144,768]{1,0:T(8,128)(2,1)S(1)}, bf16[144,768]{1,0:T(8,128)(2,1)S(1)}, u32[]{:S(2)}, u32[]{:S(2)}) collective-permute-start(bf16[144,768]{1,0:T(8,128)(2,1)S(1)} %slice_bitcast_fusion.35), channel_id=1, source_target_pairs={{0,2},{1,3},{2,0},{3,1},{4,6},{5,7},{6,4},{7,5},{8,10},{9,11},{10,... | collective-permute-start | bytes 663560 | tf_op jit(solution)/shard_map/ppermute | solution.py:60
  (207 other events, 1709.8 us)

commit v4 on v3

--- a/solution.py
+++ b/solution.py
@@ -203,21 +203,25 @@
 
 
 def far(chunk):
-    mine, next_one = chunk["own"][0], chunk["near"]
-    next_two = exchange(jnp.stack([mine, next_one]), tensor_mask=2)
-    return dict(chunk, remote=jnp.concatenate([next_one[None], next_two]))
+    return dict(chunk, far=exchange(jnp.stack([chunk["own"][0], chunk["near"]]), tensor_mask=2))
 
 
 def first(chunk):
-    return dict(chunk, first=exchange(chunk["remote"], dp_masks=FIRST))
+    remote = jnp.concatenate([chunk["near"][None], chunk["far"]])
+    return dict(
+        chunk,
+        remote=remote,
+        first=exchange(remote, dp_masks=FIRST),
+        second=exchange(remote, dp_masks=SECOND),
+    )
 
 
 def second(chunk):
-    return dict(chunk, second=exchange(jnp.stack([chunk["remote"], chunk["first"]]), dp_masks=SECOND))
+    return dict(chunk, third=exchange(chunk["first"], dp_masks=SECOND))
 
 
 def assemble(chunk):
-    rest = [chunk["remote"], chunk["first"], chunk["second"][0], chunk["second"][1]]
+    rest = [chunk["remote"], chunk["first"], chunk["second"], chunk["third"]]
     return jnp.stack([jnp.concatenate([own[None], r]) for own, r in zip(chunk["own"], rest)])
 
 
@@ -225,21 +229,32 @@
     return (a.astype(F32) + b.astype(F32)).astype(BF16)
 
 
+def halves(terms):
+    return terms[: PLANE // 2], terms[PLANE // 2 :]
+
+
 def reduce_second(terms):
-    return add_low(terms[:2], exchange(terms[2:], dp_masks=SECOND))
-
-
-def reduce_first(terms):
-    return add_low(terms[0], exchange(terms[1], dp_masks=FIRST))
-
-
-def reduce_near(terms):
+    return terms[0], exchange(terms[1], dp_masks=SECOND)
+
+
+def reduce_first(pair):
+    terms = add_low(*pair)
+    return terms[0], exchange(terms[1], dp_masks=FIRST)
+
+
+def reduce_near(pair):
+    terms = add_low(*pair)
     pairs = terms.reshape((2, 2) + terms.shape[1:])
-    return add_low(pairs[:, 0], exchange(pairs[:, 1], tensor_mask=1))
-
-
-def reduce_far(terms):
-    one = add_low(terms[0], exchange(terms[1], tensor_mask=2))
+    return pairs[:, 0], exchange(pairs[:, 1], tensor_mask=1)
+
+
+def reduce_far(pair):
+    terms = add_low(*pair)
+    return terms[0], exchange(terms[1], tensor_mask=2)
+
+
+def reduce_last(pair):
+    one = add_low(*pair)
     mask = PLANE
     while mask < lax.axis_size("dp"):
         one = add_low(one, exchange(one, dp_masks=(mask, mask)))
@@ -435,27 +450,22 @@
 
     def feed_terms(gate_up, down):
         full = jnp.concatenate([gate_up, down]).reshape(3, PLANE, DEPTH, unit_part, features)
-        return jnp.transpose(full, (1, 2, 0, 3, 4)).reshape(PLANE, DEPTH, -1, features)
+        return halves(jnp.transpose(full, (1, 2, 0, 3, 4)).reshape(PLANE, DEPTH, -1, features))
 
     def attn_terms(qkv, out):
         full = jnp.concatenate([qkv, out]).reshape(2, -1, features)
         keep = lax.dynamic_index_in_dim(full, core, 0, keepdims=False)
-        got = swap(lax.dynamic_index_in_dim(full, 1 - core, 0, keepdims=False))
-        full = add_low(keep, got).reshape(2, DEPTH, local_heads, PLANE, part, features)
-        return jnp.transpose(full, (3, 1, 0, 2, 4, 5)).reshape(PLANE, DEPTH, -1, features)
+        return keep, swap(lax.dynamic_index_in_dim(full, 1 - core, 0, keepdims=False))
+
+    def attn_pieces(pair):
+        full = add_low(*pair).reshape(2, DEPTH, local_heads, PLANE, part, features)
+        return halves(jnp.transpose(full, (3, 1, 0, 2, 4, 5)).reshape(PLANE, DEPTH, -1, features))
 
     def hand_over(block, source):
         planes, depths = lax.axis_size("dp"), lax.axis_size("tensor")
         count = planes * depths
         pairs = [(source * count + i, (1 - source) * count + i) for i in range(count)]
         return lax.ppermute(block, AXES, pairs)
-
-    def spread_first(pieces):
-        one = jnp.concatenate(pieces)
-        return jnp.stack([one, exchange(one, dp_masks=FIRST)])
-
-    def spread_second(pair):
-        return jnp.concatenate([pair, exchange(pair, dp_masks=SECOND)])
 
     second_grad, gain_two1, offset_two1 = norm_backward(total1, norms[1][2], norms[1][3], seed)
     mixed_all = both_rows(second_grad.astype(BF16))
@@ -474,7 +484,7 @@
     layer_out = give(middle_low, final_low)
     projected_grad, qkv, out, p1, q1, layer_out = together(projected_grad, qkv, out, p1, q1, layer_out)
     projected_grad, a1 = together(projected_grad, attn_terms(qkv, out))
-    a1, p1, q1 = reduce_second(a1), reduce_near(p1), reduce_first(q1)
+    a1, p1, q1 = reduce_second(attn_pieces(a1)), reduce_near(p1), reduce_first(q1)
     middle_grad = dot(projected_grad, attn1[0], 1, 0) + sum_grad
     second_grad, gain_two0, offset_two0 = norm_backward(total0, norms[0][2], norms[0][3], middle_grad)
     mixed_all = both_rows(second_grad.astype(BF16))
@@ -494,41 +504,54 @@
     )
     projected_grad, qkv, out = attn_backward(start, sum_grad, attn0, projected0, context0, slopes, seqs)
     projected_grad, qkv, out, a1, q1, p0, q0, vectors = together(projected_grad, qkv, out, a1, q1, p0, q0, vectors)
-    a0, a1, p0, q0 = reduce_second(attn_terms(qkv, out)), reduce_far(a1), reduce_near(p0), reduce_first(q0)
-    vectors = vectors + swap(vectors)
+    a0, q0 = attn_terms(qkv, out), reduce_first(q0)
+    shared = swap(vectors)
     start_grad = dot(projected_grad, attn0[0], 1, 0) + sum_grad
-    input_grad = give(start_grad, middle_grad)
-    input_grad, a0, a1, p0, q0, vectors = together(input_grad, a0, a1, p0, q0, vectors)
-    a0, p0, q0 = reduce_first(a0), reduce_far(p0), reduce_near(q0)
-    late = spread_first([p1, q1, a1])
+    start_grad, a0, q0, shared, vectors = together(start_grad, a0, q0, shared, vectors)
+    a0, a1, p0, q0 = reduce_second(attn_pieces(a0)), reduce_far(a1), reduce_near(p0), reduce_near(q0)
+    vectors = vectors + shared
     mask = 1
     while mask < lax.axis_size("dp"):
         vectors = vectors + exchange(vectors, dp_masks=(mask, mask))
         mask *= 2
-    a0, p0, q0, late, vectors = together(a0, p0, q0, late, vectors)
-    a0, q0 = reduce_near(a0), reduce_far(q0)
-    late = spread_second(late)
-    mask = 1
-    while mask < lax.axis_size("tensor"):
-        vectors = vectors + exchange(vectors, tensor_mask=mask)
-        mask *= 2
-    a0, p0, q0, late, vectors = together(a0, p0, q0, late, vectors)
-    a0, feed_early = reduce_far(a0), spread_first([p0, q0])
+    input_grad = give(start_grad, middle_grad)
+    a0, a1, p0, q0, vectors, input_grad = together(a0, a1, p0, q0, vectors, input_grad)
+    late = jnp.concatenate([reduce_last(p1), reduce_last(q1), reduce_last(a1)])
+    a0, p0, q0, late_first = reduce_first(a0), reduce_far(p0), reduce_far(q0), exchange(late, dp_masks=FIRST)
+    shared = exchange(vectors, tensor_mask=1)
+    a0, p0, q0, late, late_first, vectors, shared = together(a0, p0, q0, late, late_first, vectors, shared)
+    a0, late_second = reduce_near(a0), exchange(late, dp_masks=SECOND)
+    vectors = vectors + shared
+    shared = exchange(vectors, tensor_mask=2)
+    a0, late_second, late_first, p0, q0, vectors, shared = together(
+        a0, late_second, late_first, p0, q0, vectors, shared
+    )
+    a0, late_third = reduce_far(a0), exchange(late_first, dp_masks=SECOND)
+    vectors = vectors + shared
+    feed = jnp.concatenate([reduce_last(p0), reduce_last(q0)])
+    feed_first = exchange(feed, dp_masks=FIRST)
+    a0, late_third, feed, feed_first = together(a0, late_third, feed, feed_first)
+    attn = reduce_last(a0)
+    attn_first, attn_second = exchange(attn, dp_masks=FIRST), exchange(attn, dp_masks=SECOND)
+    feed_second = exchange(feed, dp_masks=SECOND)
+    late = jnp.stack([late, late_first, late_second, late_third])
     late_got = hand_over(late, 0)
-    a0, feed_early, late_got = together(a0, feed_early, late_got)
-    attn_early, feed_early = spread_first([a0]), spread_second(feed_early)
-    attn_early, feed_early = together(attn_early, feed_early)
-    attn_early, feed_got = spread_second(attn_early), hand_over(feed_early, 1)
-    attn_got = hand_over(attn_early, 1)
+    attn_first, attn_second, feed_second, feed_first, late_got = together(
+        attn_first, attn_second, feed_second, feed_first, late_got
+    )
+    attn_third, feed_third = exchange(attn_first, dp_masks=SECOND), exchange(feed_first, dp_masks=SECOND)
+    attn_early = jnp.stack([attn, attn_first, attn_second, attn_third])
+    feed_early = jnp.stack([feed, feed_first, feed_second, feed_third])
+    feed_got, attn_got = hand_over(feed_early, 1), hand_over(attn_early, 1)
 
     def settle(early, early_got, late, late_got):
-        halves = [jnp.where(is_first, early, late_got), jnp.where(is_first, early_got, late)]
+        parts = [jnp.where(is_first, early, late_got), jnp.where(is_first, early_got, late)]
         return jnp.stack(
             [
                 jnp.stack(
                     [
                         lax.dynamic_index_in_dim(half, order[jnp.bitwise_xor(in_plane, index)], 0, keepdims=False)
-                        for half, order in zip(halves, orders)
+                        for half, order in zip(parts, orders)
                     ]
                 )
                 for index in range(PLANE)

time: 570 us -> 589 us (1.033)
  starting transfers between devices: 59.2 us -> 76.8 us
    ppermute x77 -> x86, starting transfers between devices: 53.6 us -> 67.2 us  [exchange(): return lax.ppermute(block, AXES, pairs)]
    another operation x18, other arithmetic: 6.48 us -> 13.2 us  [assemble(): jnp.stack([jnp.concatenate([own[None], r]) for own, r in zip(chunk['own']...]
    another operation x19 -> x11, other arithmetic: 13 us -> 7.42 us  [the longest x6 5.9 us: second(): jnp.stack([chunk['remote'], chunk['first']])]
    unnamed x324 -> x318, local copies, waits for them, and re-layouts: 41 us -> 35.9 us
    ppermute x77 -> x86, waiting for transfers between devices: 229 us -> 226 us  [exchange(): return lax.ppermute(block, AXES, pairs)]
  transfers between devices with their start and end apart: 80 -> 89, of which waited for: 37 -> 36; matrix products, arithmetic and copies ran while one was open for 29% -> 30% of each run, Pallas kernels for 4% -> 4%
where the time goes in v4:
time: 589 us; the launch traced here: 579 us
  waiting for transfers between devices  226 us (38%)
  other arithmetic  98.3 us (17%)
  local copies, waits for them, and re-layouts  79.8 us (14%)
  starting transfers between devices  76.8 us (13%)
  matrix products  61.7 us (10%)
  Pallas kernels  21.8 us (4%)
  between operations  14.7 us (2%)
    ppermute x86, waiting for transfers between devices, exchange(): return lax.ppermute(block, AXES, pairs)  226 us
    ppermute x86, starting transfers between devices, exchange(): return lax.ppermute(block, AXES, pairs)  67.2 us
    dot_general x36, matrix products, dot(): lax.dot_general(a, b, (((ca,), (cb,)), ((), ())), preferred_element_type=...  61.7 us
    unnamed x318, local copies, waits for them, and re-layouts  35.9 us
    convert_element_type x4, other arithmetic, feed_forward(): hidden = gelu_product(gate_part, up_part).astype(BF16)  24.2 us
    convert_element_type x26, other arithmetic, add_low(): return (a.astype(F32) + b.astype(F32)).astype(BF16)  14.9 us
    another operation x18, other arithmetic, assemble(): jnp.stack([jnp.concatenate([own[None], r]) for own, r in zip(chunk['own']...  13.2 us
    pallas_call x2, Pallas kernels, attend_back(): pl.pallas_call(functools.partial(attend_back_kernel, GROUP_BACK), grid=(s...  11.8 us
  transfers between devices with their start and end apart: 89, of which 36 were waited for; matrix products, arithmetic and copies ran while one was open for 30% of the time, Pallas kernels for 4%

profile of v4, /device:TPU:1, one launch (start us, length us, event | category | flops | bytes accessed | tf_op | source)
XLA Modules:
  0.0 578.8 jit_solution(12781611277680919562)
XLA Ops:
  3.4 5.7 copy.68
  34.5 5.2 collective-permute-done.3
  45.7 6.7 %collective-permute-done.9 = bf16[144,768]{1,0:T(8,128)(2,1)S(1)} collective-permute-done((bf16[144,768]{1,0:T(8,128)(2,1)S(1)}, bf16[144,768]{1,0:T(8,128)(2,1)S(1)}, u32[]{:S(2)}, u32[]{:S(2)}) %collective-permute-start.9) | collective-permute-done | bytes 221216 | tf_op jit(solution)/shard_map/ppermute | solution.py:60
  52.4 9.8 %collective-permute-done.8 = bf16[2,144,768]{2,1,0:T(8,128)(2,1)S(1)} collective-permute-done((bf16[2,144,768]{2,1,0:T(8,128)(2,1)S(1)}, bf16[2,144,768]{2,1,0:T(8,128)(2,1)S(1)}, u32[]{:S(2)}, u32[]{:S(2)}) %collective-permute-start.8) | collective-permute-done | bytes 442400 | tf_op jit(solution)/shard_map/ppermute | solution.py:60
  67.4 9.4 %collective-permute-done.14 = bf16[96,768]{1,0:T(8,128)(2,1)S(1)} collective-permute-done((bf16[96,768]{1,0:T(8,128)(2,1)S(1)}, bf16[96,768]{1,0:T(8,128)(2,1)S(1)}, u32[]{:S(2)}, u32[]{:S(2)}) %collective-permute-start.14) | collective-permute-done | bytes 147488 | tf_op jit(solution)/shard_map/ppermute | solution.py:60
  76.8 9.2 %collective-permute-done.13 = bf16[2,144,768]{2,1,0:T(8,128)(2,1)S(1)} collective-permute-done((bf16[2,144,768]{2,1,0:T(8,128)(2,1)S(1)}, bf16[2,144,768]{2,1,0:T(8,128)(2,1)S(1)}, u32[]{:S(2)}, u32[]{:S(2)}) %collective-permute-start.13) | collective-permute-done | bytes 442400 | tf_op jit(solution)/shard_map/ppermute | solution.py:60
  133.3 6.2 %multiply_convert_fusion.7 = (bf16[768,768]{1,0:T(8,128)(2,1)S(1)}, f32[768,768]{1,0:T(8,128)}) fusion(f32[768,1536]{1,0:T(8,128)S(1)} %fusion.99), kind=kLoop, calls=%fused_computation.102 | loop fusion | flops 38928384 | bytes 8257536 | tf_op jit(solution)/shard_map/convert_element_type | solution.py:287
  140.6 9.4 %collective-permute-done.26 = bf16[2,144,768]{2,1,0:T(8,128)(2,1)S(1)} collective-permute-done((bf16[2,144,768]{2,1,0:T(8,128)(2,1)S(1)}, bf16[2,144,768]{2,1,0:T(8,128)(2,1)S(1)}, u32[]{:S(2)}, u32[]{:S(2)}) %collective-permute-start.26) | collective-permute-done | bytes 442400 | tf_op jit(solution)/shard_map/ppermute | solution.py:60
  159.6 6.0 %multiply_convert_fusion.6 = (bf16[768,768]{1,0:T(8,128)(2,1)S(1)}, f32[768,768]{1,0:T(8,128)}) fusion(f32[768,1536]{1,0:T(8,128)S(1)} %fusion.101), kind=kLoop, calls=%fused_computation.89 | loop fusion | flops 38928384 | bytes 8257536 | tf_op jit(solution)/shard_map/convert_element_type | solution.py:287
  168.4 6.9 %collective-permute-done.31 = bf16[2,144,768]{2,1,0:T(8,128)(2,1)S(1)} collective-permute-done((bf16[2,144,768]{2,1,0:T(8,128)(2,1)S(1)}, bf16[2,144,768]{2,1,0:T(8,128)(2,1)S(1)}, u32[]{:S(2)}, u32[]{:S(2)}) %collective-permute-start.31) | collective-permute-done | bytes 442400 | tf_op jit(solution)/shard_map/ppermute | solution.py:60
  188.4 5.1 attend.3
  196.4 5.6 collective-permute-done.34
  210.7 6.0 %multiply_convert_fusion.5 = (bf16[768,768]{1,0:T(8,128)(2,1)S(1)}, f32[768,768]{1,0:T(8,128)}) fusion(f32[768,1536]{1,0:T(8,128)S(1)} %fusion.103), kind=kLoop, calls=%fused_computation.76 | loop fusion | flops 38928384 | bytes 8257536 | tf_op jit(solution)/shard_map/convert_element_type | solution.py:287
  223.5 6.1 %multiply_convert_fusion.4 = (bf16[768,768]{1,0:T(8,128)(2,1)S(1)}, f32[768,768]{1,0:T(8,128)}) fusion(f32[768,1536]{1,0:T(8,128)S(1)} %fusion.105), kind=kLoop, calls=%fused_computation.63 | loop fusion | flops 38928384 | bytes 8257536 | tf_op jit(solution)/shard_map/convert_element_type | solution.py:287
  268.1 7.7 %collective-permute-done.41 = bf16[2,4,144,768]{3,2,1,0:T(8,128)(2,1)S(1)} collective-permute-done((bf16[2,4,144,768]{3,2,1,0:T(8,128)(2,1)S(1)}, bf16[2,4,144,768]{3,2,1,0:T(8,128)(2,1)S(1)}, u32[]{:S(2)}, u32[]{:S(2)}) %collective-permute-start.41) | collective-permute-done | bytes 1769504 | tf_op jit(solution)/shard_map/ppermute | solution.py:60
  284.2 6.1 %attend_back.2 = bf16[384,2304]{1,0:T(8,128)(2,1)} custom-call(f32[12]{0:T(128)} %pad_maximum_fusion.64.slopes_ref, bf16[384,2304]{1,0:T(8,128)(2,1)} %convolution_convert_fusion.2.projected_ref, bf16[384,768]{1,0:T(8,128)(2,1)} %convolution_convert_fusion.15.context_grad_ref), custom_call_target="tpu_custom_call" | custom-call | flops 377487360 | bytes 4128768 | tf_op jit(solution)/shard_map/attend_back/pallas_call | solution.py:180
  294.0 5.3 collective-permute-done.43
  299.3 10.9 %collective-permute-done.44 = bf16[2,4,144,768]{3,2,1,0:T(8,128)(2,1)} collective-permute-done((bf16[2,4,144,768]{3,2,1,0:T(8,128)(2,1)}, bf16[2,4,144,768]{3,2,1,0:T(8,128)(2,1)}, u32[]{:S(2)}, u32[]{:S(2)}) %collective-permute-start.44) | collective-permute-done | bytes 1769504 | tf_op jit(solution)/shard_map/ppermute | solution.py:60
  335.6 7.1 %collective-permute-done.48 = bf16[2,4,96,768]{3,2,1,0:T(8,128)(2,1)S(1)} collective-permute-done((bf16[2,4,96,768]{3,2,1,0:T(8,128)(2,1)S(1)}, bf16[2,4,96,768]{3,2,1,0:T(8,128)(2,1)S(1)}, u32[]{:S(2)}, u32[]{:S(2)}) %collective-permute-start.48) | collective-permute-done | bytes 1179680 | tf_op jit(solution)/shard_map/ppermute | solution.py:60
  364.8 13.0 %collective-permute-done.54 = bf16[2,4,144,768]{3,2,1,0:T(8,128)(2,1)S(1)} collective-permute-done((bf16[2,4,144,768]{3,2,1,0:T(8,128)(2,1)S(1)}, bf16[2,4,144,768]{3,2,1,0:T(8,128)(2,1)S(1)}, u32[]{:S(2)}, u32[]{:S(2)}) %collective-permute-start.54) | collective-permute-done | bytes 1769504 | tf_op jit(solution)/shard_map/ppermute | solution.py:60
  392.1 5.7 attend_back.3
  405.6 11.0 %collective-permute-done.59 = bf16[2,4,144,768]{3,2,1,0:T(8,128)(2,1)} collective-permute-done((bf16[2,4,144,768]{3,2,1,0:T(8,128)(2,1)}, bf16[2,4,144,768]{3,2,1,0:T(8,128)(2,1)}, u32[]{:S(2)}, u32[]{:S(2)}) %collective-permute-start.59) | collective-permute-done | bytes 1769504 | tf_op jit(solution)/shard_map/ppermute | solution.py:60
  427.8 7.5 %collective-permute-done.61 = bf16[4,144,768]{2,1,0:T(8,128)(2,1)S(1)} collective-permute-done((bf16[4,144,768]{2,1,0:T(8,128)(2,1)S(1)}, bf16[4,144,768]{2,1,0:T(8,128)(2,1)S(1)}, u32[]{:S(2)}, u32[]{:S(2)}) %collective-permute-start.61) | collective-permute-done | bytes 884768 | tf_op jit(solution)/shard_map/ppermute | solution.py:60
  440.8 13.1 %collective-permute-done.67 = f32[8,768]{1,0:T(8,128)S(1)} collective-permute-done((f32[8,768]{1,0:T(8,128)S(1)}, f32[8,768]{1,0:T(8,128)S(1)}, u32[]{:S(2)}, u32[]{:S(2)}) %collective-permute-start.67) | collective-permute-done | bytes 24608 | tf_op jit(solution)/shard_map/ppermute | solution.py:60
  458.6 8.3 %collective-permute-done.66 = bf16[2,144,768]{2,1,0:T(8,128)(2,1)S(1)} collective-permute-done((bf16[2,144,768]{2,1,0:T(8,128)(2,1)S(1)}, bf16[2,144,768]{2,1,0:T(8,128)(2,1)S(1)}, u32[]{:S(2)}, u32[]{:S(2)}) %collective-permute-start.66) | collective-permute-done | bytes 442400 | tf_op jit(solution)/shard_map/ppermute | solution.py:60
  471.9 6.2 %collective-permute-done.74 = f32[8,768]{1,0:T(8,128)S(1)} collective-permute-done((f32[8,768]{1,0:T(8,128)S(1)}, f32[8,768]{1,0:T(8,128)S(1)}, u32[]{:S(2)}, u32[]{:S(2)}) %collective-permute-start.74) | collective-permute-done | bytes 24608 | tf_op jit(solution)/shard_map/ppermute | solution.py:60
  478.1 6.1 %collective-permute-done.71 = bf16[144,768]{1,0:T(8,128)(2,1)S(1)} collective-permute-done((bf16[144,768]{1,0:T(8,128)(2,1)S(1)}, bf16[144,768]{1,0:T(8,128)(2,1)S(1)}, u32[]{:S(2)}, u32[]{:S(2)}) %collective-permute-start.71) | collective-permute-done | bytes 221216 | tf_op jit(solution)/shard_map/ppermute | solution.py:60
  500.8 8.2 %collective-permute-done.78 = bf16[96,768]{1,0:T(8,128)(2,1)S(1)} collective-permute-done((bf16[96,768]{1,0:T(8,128)(2,1)S(1)}, bf16[96,768]{1,0:T(8,128)(2,1)S(1)}, u32[]{:S(2)}, u32[]{:S(2)}) %collective-permute-start.78) | collective-permute-done | bytes 147488 | tf_op jit(solution)/shard_map/ppermute | solution.py:60
  516.8 8.1 %collective-permute-done.82 = bf16[96,768]{1,0:T(8,128)(2,1)S(1)} collective-permute-done((bf16[96,768]{1,0:T(8,128)(2,1)S(1)}, bf16[96,768]{1,0:T(8,128)(2,1)S(1)}, u32[]{:S(2)}, u32[]{:S(2)}) %collective-permute-start.82) | collective-permute-done | bytes 147488 | tf_op jit(solution)/shard_map/ppermute | solution.py:60
  526.4 7.6 %collective-permute-done.85 = bf16[96,768]{1,0:T(8,128)(2,1)S(1)} collective-permute-done((bf16[96,768]{1,0:T(8,128)(2,1)S(1)}, bf16[96,768]{1,0:T(8,128)(2,1)S(1)}, u32[]{:S(2)}, u32[]{:S(2)}) %collective-permute-start.85) | collective-permute-done | bytes 147488 | tf_op jit(solution)/shard_map/ppermute | solution.py:60
  534.1 5.8 %collective-permute-start.86 = (bf16[4,96,768]{2,1,0:T(8,128)(2,1)S(1)}, bf16[4,96,768]{2,1,0:T(8,128)(2,1)}, u32[]{:S(2)}, u32[]{:S(2)}) collective-permute-start(bf16[4,96,768]{2,1,0:T(8,128)(2,1)S(1)} %get-tuple-element.741), channel_id=1, source_target_pairs={{16,0},{17,1},{18,2},{19,3},{20,4},{21,5},{22,6},{23,7},{24,8},{25... | collective-permute-start | bytes 1769480 | tf_op jit(solution)/shard_map/ppermute | solution.py:468
  568.5 8.3 %copy.109 = f32[1,768,2,768]{3,2,1,0:T(2,128)} copy(f32[1,768,2,768]{1,3,2,0:T(8,128)} %bitcast.478) | data formatting | bytes 9437184
  (758 shorter events, 320.9 us)
Async XLA Ops:
  39.8 22.4 %collective-permute-start.8 = (bf16[2,144,768]{2,1,0:T(8,128)(2,1)S(1)}, bf16[2,144,768]{2,1,0:T(8,128)(2,1)S(1)}, u32[]{:S(2)}, u32[]{:S(2)}) collective-permute-start(bf16[2,144,768]{2,1,0:T(8,128)(2,1)S(1)} %pad_maximum_fusion.51), channel_id=1, source_target_pairs={{0,2},{1,3},{2,0},{3,1},{4,6},{5,7},{6,4},{7,5},{8,10},{9,11},{10,... | collective-permute-start | bytes 1327112 | tf_op jit(solution)/shard_map/ppermute | solution.py:60
  39.9 22.2 %collective-permute-start.7 = (bf16[3,96,768]{2,1,0:T(8,128)(2,1)S(1)}, bf16[3,96,768]{2,1,0:T(8,128)(2,1)S(1)}, u32[]{:S(2)}, u32[]{:S(2)}) collective-permute-start(bf16[3,96,768]{2,1,0:T(8,128)(2,1)S(1)} %pad_maximum_fusion.50), channel_id=1, source_target_pairs={{0,8},{1,9},{2,10},{3,11},{4,12},{5,13},{6,14},{7,15},{8,0},{9,1},... | collective-permute-start | bytes 1327112 | tf_op jit(solution)/shard_map/ppermute | solution.py:60
  41.2 21.0 %collective-permute-start.6 = (bf16[3,96,768]{2,1,0:T(8,128)(2,1)S(1)}, bf16[3,96,768]{2,1,0:T(8,128)(2,1)S(1)}, u32[]{:S(2)}, u32[]{:S(2)}) collective-permute-start(bf16[3,96,768]{2,1,0:T(8,128)(2,1)S(1)} %pad_maximum_fusion.50), channel_id=1, source_target_pairs={{0,4},{1,5},{2,6},{3,7},{4,0},{5,1},{6,2},{7,3},{8,12},{9,13},{10,... | collective-permute-start | bytes 1327112 | tf_op jit(solution)/shard_map/ppermute | solution.py:60
  62.2 23.8 %collective-permute-start.12 = (bf16[3,144,768]{2,1,0:T(8,128)(2,1)S(1)}, bf16[3,144,768]{2,1,0:T(8,128)(2,1)S(1)}, u32[]{:S(2)}, u32[]{:S(2)}) collective-permute-start(bf16[3,144,768]{2,1,0:T(8,128)(2,1)S(1)} %pad_maximum_fusion.44), channel_id=1, source_target_pairs={{0,8},{1,9},{2,10},{3,11},{4,12},{5,13},{6,14},{7,15},{8,0},{9,1},... | collective-permute-start | bytes 1990664 | tf_op jit(solution)/shard_map/ppermute | solution.py:60
  63.5 22.6 %collective-permute-start.11 = (bf16[3,144,768]{2,1,0:T(8,128)(2,1)S(1)}, bf16[3,144,768]{2,1,0:T(8,128)(2,1)}, u32[]{:S(2)}, u32[]{:S(2)}) collective-permute-start(bf16[3,144,768]{2,1,0:T(8,128)(2,1)S(1)} %pad_maximum_fusion.44), channel_id=1, source_target_pairs={{0,4},{1,5},{2,6},{3,7},{4,0},{5,1},{6,2},{7,3},{8,12},{9,13},{10,... | collective-permute-start | bytes 1990664 | tf_op jit(solution)/shard_map/ppermute | solution.py:60
  64.8 21.2 %collective-permute-start.13 = (bf16[2,144,768]{2,1,0:T(8,128)(2,1)S(1)}, bf16[2,144,768]{2,1,0:T(8,128)(2,1)S(1)}, u32[]{:S(2)}, u32[]{:S(2)}) collective-permute-start(bf16[2,144,768]{2,1,0:T(8,128)(2,1)S(1)} %pad_maximum_fusion.52), channel_id=1, source_target_pairs={{0,2},{1,3},{2,0},{3,1},{4,6},{5,7},{6,4},{7,5},{8,10},{9,11},{10,... | collective-permute-start | bytes 1327112 | tf_op jit(solution)/shard_map/ppermute | solution.py:60
  64.9 21.2 %collective-permute-start.10 = (bf16[3,96,768]{2,1,0:T(8,128)(2,1)S(1)}, bf16[3,96,768]{2,1,0:T(8,128)(2,1)S(1)}, u32[]{:S(2)}, u32[]{:S(2)}) collective-permute-start(bf16[3,96,768]{2,1,0:T(8,128)(2,1)S(1)} %collective-permute-done.6), channel_id=1, source_target_pairs={{0,8},{1,9},{2,10},{3,11},{4,12},{5,13},{6,14},{7,15},{8,0},{9,1},... | collective-permute-start | bytes 1327112 | tf_op jit(solution)/shard_map/ppermute | solution.py:60
  98.5 20.4 %collective-permute-start.17 = (bf16[3,144,768]{2,1,0:T(8,128)(2,1)}, bf16[3,144,768]{2,1,0:T(8,128)(2,1)}, u32[]{:S(2)}, u32[]{:S(2)}) collective-permute-start(bf16[3,144,768]{2,1,0:T(8,128)(2,1)} %collective-permute-done.11), channel_id=1, source_target_pairs={{0,8},{1,9},{2,10},{3,11},{4,12},{5,13},{6,14},{7,15},{8,0},{9,1},... | collective-permute-start | bytes 1990664 | tf_op jit(solution)/shard_map/ppermute | solution.py:60
  119.9 30.2 %collective-permute-start.25 = (bf16[3,96,768]{2,1,0:T(8,128)(2,1)S(1)}, bf16[3,96,768]{2,1,0:T(8,128)(2,1)S(1)}, u32[]{:S(2)}, u32[]{:S(2)}) collective-permute-start(bf16[3,96,768]{2,1,0:T(8,128)(2,1)S(1)} %pad_maximum_fusion.53), channel_id=1, source_target_pairs={{0,8},{1,9},{2,10},{3,11},{4,12},{5,13},{6,14},{7,15},{8,0},{9,1},... | collective-permute-start | bytes 1327112 | tf_op jit(solution)/shard_map/ppermute | solution.py:60
  120.2 29.9 %collective-permute-start.24 = (bf16[3,96,768]{2,1,0:T(8,128)(2,1)S(1)}, bf16[3,96,768]{2,1,0:T(8,128)(2,1)S(1)}, u32[]{:S(2)}, u32[]{:S(2)}) collective-permute-start(bf16[3,96,768]{2,1,0:T(8,128)(2,1)S(1)} %pad_maximum_fusion.53), channel_id=1, source_target_pairs={{0,4},{1,5},{2,6},{3,7},{4,0},{5,1},{6,2},{7,3},{8,12},{9,13},{10,... | collective-permute-start | bytes 1327112 | tf_op jit(solution)/shard_map/ppermute | solution.py:60
  127.7 22.3 %collective-permute-start.26 = (bf16[2,144,768]{2,1,0:T(8,128)(2,1)S(1)}, bf16[2,144,768]{2,1,0:T(8,128)(2,1)S(1)}, u32[]{:S(2)}, u32[]{:S(2)}) collective-permute-start(bf16[2,144,768]{2,1,0:T(8,128)(2,1)S(1)} %pad_maximum_fusion.54), channel_id=1, source_target_pairs={{0,2},{1,3},{2,0},{3,1},{4,6},{5,7},{6,4},{7,5},{8,10},{9,11},{10,... | collective-permute-start | bytes 1327112 | tf_op jit(solution)/shard_map/ppermute | solution.py:60
  151.1 24.2 %collective-permute-start.30 = (bf16[3,144,768]{2,1,0:T(8,128)(2,1)S(1)}, bf16[3,144,768]{2,1,0:T(8,128)(2,1)S(1)}, u32[]{:S(2)}, u32[]{:S(2)}) collective-permute-start(bf16[3,144,768]{2,1,0:T(8,128)(2,1)S(1)} %pad_maximum_fusion.46), channel_id=1, source_target_pairs={{0,8},{1,9},{2,10},{3,11},{4,12},{5,13},{6,14},{7,15},{8,0},{9,1},... | collective-permute-start | bytes 1990664 | tf_op jit(solution)/shard_map/ppermute | solution.py:60
  151.8 23.6 %collective-permute-start.29 = (bf16[3,144,768]{2,1,0:T(8,128)(2,1)S(1)}, bf16[3,144,768]{2,1,0:T(8,128)(2,1)}, u32[]{:S(2)}, u32[]{:S(2)}) collective-permute-start(bf16[3,144,768]{2,1,0:T(8,128)(2,1)S(1)} %pad_maximum_fusion.46), channel_id=1, source_target_pairs={{0,4},{1,5},{2,6},{3,7},{4,0},{5,1},{6,2},{7,3},{8,12},{9,13},{10,... | collective-permute-start | bytes 1990664 | tf_op jit(solution)/shard_map/ppermute | solution.py:60
  153.1 22.3 %collective-permute-start.31 = (bf16[2,144,768]{2,1,0:T(8,128)(2,1)S(1)}, bf16[2,144,768]{2,1,0:T(8,128)(2,1)S(1)}, u32[]{:S(2)}, u32[]{:S(2)}) collective-permute-start(bf16[2,144,768]{2,1,0:T(8,128)(2,1)S(1)} %pad_maximum_fusion.55), channel_id=1, source_target_pairs={{0,2},{1,3},{2,0},{3,1},{4,6},{5,7},{6,4},{7,5},{8,10},{9,11},{10,... | collective-permute-start | bytes 1327112 | tf_op jit(solution)/shard_map/ppermute | solution.py:60
  153.2 22.2 %collective-permute-start.28 = (bf16[3,96,768]{2,1,0:T(8,128)(2,1)S(1)}, bf16[3,96,768]{2,1,0:T(8,128)(2,1)S(1)}, u32[]{:S(2)}, u32[]{:S(2)}) collective-permute-start(bf16[3,96,768]{2,1,0:T(8,128)(2,1)S(1)} %collective-permute-done.24), channel_id=1, source_target_pairs={{0,8},{1,9},{2,10},{3,11},{4,12},{5,13},{6,14},{7,15},{8,0},{9,1},... | collective-permute-start | bytes 1327112 | tf_op jit(solution)/shard_map/ppermute | solution.py:60
  178.9 23.1 %collective-permute-start.34 = (bf16[3,144,768]{2,1,0:T(8,128)(2,1)}, bf16[3,144,768]{2,1,0:T(8,128)(2,1)}, u32[]{:S(2)}, u32[]{:S(2)}) collective-permute-start(bf16[3,144,768]{2,1,0:T(8,128)(2,1)} %collective-permute-done.29), channel_id=1, source_target_pairs={{0,8},{1,9},{2,10},{3,11},{4,12},{5,13},{6,14},{7,15},{8,0},{9,1},... | collective-permute-start | bytes 1990664 | tf_op jit(solution)/shard_map/ppermute | solution.py:60
  242.2 22.2 %collective-permute-start.45 = (bf16[384,768]{1,0:T(8,128)(2,1)S(1)}, bf16[384,768]{1,0:T(8,128)(2,1)S(1)}, u32[]{:S(2)}, u32[]{:S(2)}) collective-permute-start(bf16[384,768]{1,0:T(8,128)(2,1)S(1)} %get-tuple-element.627), channel_id=1, source_target_pairs={{0,16},{1,17},{2,18},{3,19},{4,20},{5,21},{6,22},{7,23},{8,24},{9,... | collective-permute-start | bytes 1769480 | tf_op jit(solution)/shard_map/ppermute | solution.py:60
  253.8 21.9 %collective-permute-start.41 = (bf16[2,4,144,768]{3,2,1,0:T(8,128)(2,1)S(1)}, bf16[2,4,144,768]{3,2,1,0:T(8,128)(2,1)S(1)}, u32[]{:S(2)}, u32[]{:S(2)}) collective-permute-start(bf16[2,4,144,768]{3,2,1,0:T(8,128)(2,1)S(1)} %bitcast.557), channel_id=1, source_target_pairs={{0,8},{1,9},{2,10},{3,11},{4,12},{5,13},{6,14},{7,15},{8,0},{9,1},... | collective-permute-start | bytes 5308424 | tf_op jit(solution)/shard_map/ppermute | solution.py:60
  278.7 20.6 %collective-permute-start.43 = (bf16[4,144,768]{2,1,0:T(8,128)(2,1)}, bf16[4,144,768]{2,1,0:T(8,128)(2,1)}, u32[]{:S(2)}, u32[]{:S(2)}) collective-permute-start(bf16[4,144,768]{2,1,0:T(8,128)(2,1)} %get-tuple-element.700), channel_id=1, source_target_pairs={{0,4},{1,5},{2,6},{3,7},{4,0},{5,1},{6,2},{7,3},{8,12},{9,13},{10,... | collective-permute-start | bytes 2654216 | tf_op jit(solution)/shard_map/ppermute | solution.py:60
  279.1 31.2 %collective-permute-start.44 = (bf16[2,4,144,768]{3,2,1,0:T(8,128)(2,1)}, bf16[2,4,144,768]{3,2,1,0:T(8,128)(2,1)}, u32[]{:S(2)}, u32[]{:S(2)}) collective-permute-start(bf16[2,4,144,768]{3,2,1,0:T(8,128)(2,1)} %bitcast.157), channel_id=1, source_target_pairs={{0,8},{1,9},{2,10},{3,11},{4,12},{5,13},{6,14},{7,15},{8,0},{9,1},... | collective-permute-start | bytes 5308424 | tf_op jit(solution)/shard_map/ppermute | solution.py:60
  315.2 20.4 %collective-permute-start.49 = (bf16[2,144,768]{2,1,0:T(8,128)(2,1)S(1)}, bf16[2,144,768]{2,1,0:T(8,128)(2,1)}, u32[]{:S(2)}, u32[]{:S(2)}) collective-permute-start(bf16[2,144,768]{2,1,0:T(8,128)(2,1)S(1)} %get-tuple-element.714), channel_id=1, source_target_pairs={{0,1},{1,0},{2,3},{3,2},{4,5},{5,4},{6,7},{7,6},{8,9},{9,8},{10,11... | collective-permute-start | bytes 1327112 | tf_op jit(solution)/shard_map/ppermute | solution.py:60
  350.1 27.7 %collective-permute-start.54 = (bf16[2,4,144,768]{3,2,1,0:T(8,128)(2,1)S(1)}, bf16[2,4,144,768]{3,2,1,0:T(8,128)(2,1)S(1)}, u32[]{:S(2)}, u32[]{:S(2)}) collective-permute-start(bf16[2,4,144,768]{3,2,1,0:T(8,128)(2,1)S(1)} %bitcast.556), channel_id=1, source_target_pairs={{0,8},{1,9},{2,10},{3,11},{4,12},{5,13},{6,14},{7,15},{8,0},{9,1},... | collective-permute-start | bytes 5308424 | tf_op jit(solution)/shard_map/ppermute | solution.py:60
  378.8 23.6 %collective-permute-start.56 = (bf16[2,96,768]{2,1,0:T(8,128)(2,1)}, bf16[2,96,768]{2,1,0:T(8,128)(2,1)}, u32[]{:S(2)}, u32[]{:S(2)}) collective-permute-start(bf16[2,96,768]{2,1,0:T(8,128)(2,1)} %get-tuple-element.744), channel_id=1, source_target_pairs={{0,1},{1,0},{2,3},{3,2},{4,5},{5,4},{6,7},{7,6},{8,9},{9,8},{10,11... | collective-permute-start | bytes 884744 | tf_op jit(solution)/shard_map/ppermute | solution.py:60
  381.2 21.2 %collective-permute-start.57 = (bf16[144,768]{1,0:T(8,128)(2,1)}, bf16[144,768]{1,0:T(8,128)(2,1)}, u32[]{:S(2)}, u32[]{:S(2)}) collective-permute-start(bf16[144,768]{1,0:T(8,128)(2,1)} %get-tuple-element.758), channel_id=1, source_target_pairs={{0,2},{1,3},{2,0},{3,1},{4,6},{5,7},{6,4},{7,5},{8,10},{9,11},{10,... | collective-permute-start | bytes 663560 | tf_op jit(solution)/shard_map/ppermute | solution.py:60
  385.0 20.7 %collective-permute-start.58 = (bf16[4,144,768]{2,1,0:T(8,128)(2,1)}, bf16[4,144,768]{2,1,0:T(8,128)(2,1)}, u32[]{:S(2)}, u32[]{:S(2)}) collective-permute-start(bf16[4,144,768]{2,1,0:T(8,128)(2,1)} %get-tuple-element.694), channel_id=1, source_target_pairs={{0,4},{1,5},{2,6},{3,7},{4,0},{5,1},{6,2},{7,3},{8,12},{9,13},{10,... | collective-permute-start | bytes 2654216 | tf_op jit(solution)/shard_map/ppermute | solution.py:60
  385.5 31.2 %collective-permute-start.59 = (bf16[2,4,144,768]{3,2,1,0:T(8,128)(2,1)}, bf16[2,4,144,768]{3,2,1,0:T(8,128)(2,1)}, u32[]{:S(2)}, u32[]{:S(2)}) collective-permute-start(bf16[2,4,144,768]{3,2,1,0:T(8,128)(2,1)} %bitcast.189), channel_id=1, source_target_pairs={{0,8},{1,9},{2,10},{3,11},{4,12},{5,13},{6,14},{7,15},{8,0},{9,1},... | collective-permute-start | bytes 5308424 | tf_op jit(solution)/shard_map/ppermute | solution.py:60
  419.5 39.1 %collective-permute-start.64 = (bf16[96,768]{1,0:T(8,128)(2,1)S(1)}, bf16[96,768]{1,0:T(8,128)(2,1)S(1)}, u32[]{:S(2)}, u32[]{:S(2)}) collective-permute-start(bf16[96,768]{1,0:T(8,128)(2,1)S(1)} %get-tuple-element.764), channel_id=1, source_target_pairs={{0,2},{1,3},{2,0},{3,1},{4,6},{5,7},{6,4},{7,5},{8,10},{9,11},{10,... | collective-permute-start | bytes 442376 | tf_op jit(solution)/shard_map/ppermute | solution.py:60
  427.7 30.8 %collective-permute-start.65 = (bf16[2,144,768]{2,1,0:T(8,128)(2,1)S(1)}, bf16[2,144,768]{2,1,0:T(8,128)(2,1)S(1)}, u32[]{:S(2)}, u32[]{:S(2)}) collective-permute-start(bf16[2,144,768]{2,1,0:T(8,128)(2,1)S(1)} %get-tuple-element.710), channel_id=1, source_target_pairs={{0,1},{1,0},{2,3},{3,2},{4,5},{5,4},{6,7},{7,6},{8,9},{9,8},{10,11... | collective-permute-start | bytes 1327112 | tf_op jit(solution)/shard_map/ppermute | solution.py:60
  435.5 21.1 %collective-permute-start.69 = (f32[384,768]{1,0:T(8,128)S(1)}, f32[384,768]{1,0:T(8,128)S(1)}, u32[]{:S(2)}, u32[]{:S(2)}) collective-permute-start(f32[384,768]{1,0:T(8,128)S(1)} %broadcast_select_fusion.6), channel_id=1, source_target_pairs={{0,16},{1,17},{2,18},{3,19},{4,20},{5,21},{6,22},{7,23},{8,24},{9,... | collective-permute-start | bytes 3538952 | tf_op jit(solution)/shard_map/ppermute | solution.py:60
  438.0 28.9 %collective-permute-start.63 = (bf16[2,4,96,768]{3,2,1,0:T(8,128)(2,1)S(1)}, bf16[2,4,96,768]{3,2,1,0:T(8,128)(2,1)S(1)}, u32[]{:S(2)}, u32[]{:S(2)}) collective-permute-start(bf16[2,4,96,768]{3,2,1,0:T(8,128)(2,1)S(1)} %bitcast.577), channel_id=1, source_target_pairs={{0,8},{1,9},{2,10},{3,11},{4,12},{5,13},{6,14},{7,15},{8,0},{9,1},... | collective-permute-start | bytes 3538952 | tf_op jit(solution)/shard_map/ppermute | solution.py:60
  468.1 20.8 %collective-permute-start.73 = (bf16[384,768]{1,0:T(8,128)(2,1)S(1)}, bf16[384,768]{1,0:T(8,128)(2,1)S(1)}, u32[]{:S(2)}, u32[]{:S(2)}) collective-permute-start(bf16[384,768]{1,0:T(8,128)(2,1)S(1)} %pad_maximum_fusion.48), channel_id=1, source_target_pairs={{0,4},{1,5},{2,6},{3,7},{4,0},{5,1},{6,2},{7,3},{8,12},{9,13},{10,... | collective-permute-start | bytes 1769480 | tf_op jit(solution)/shard_map/ppermute | solution.py:60
  534.1 24.7 %collective-permute-start.86 = (bf16[4,96,768]{2,1,0:T(8,128)(2,1)S(1)}, bf16[4,96,768]{2,1,0:T(8,128)(2,1)}, u32[]{:S(2)}, u32[]{:S(2)}) collective-permute-start(bf16[4,96,768]{2,1,0:T(8,128)(2,1)S(1)} %get-tuple-element.741), channel_id=1, source_target_pairs={{16,0},{17,1},{18,2},{19,3},{20,4},{21,5},{22,6},{23,7},{24,8},{25... | collective-permute-start | bytes 1769480 | tf_op jit(solution)/shard_map/ppermute | solution.py:468
  (215 other events, 1828.7 us)

commit v5 on v4

--- a/solution.py
+++ b/solution.py
@@ -14,6 +14,7 @@
 NORM_EPSILON = 1e-05
 AXES = ("section", "dp", "tensor")
 FEED_CHUNKS = 2
+NORM_ROWS = 16
 LANES = 128
 GROUP = 3
 GROUP_BACK = 3
@@ -194,6 +195,51 @@
     )(slopes, projected, context_grad)
 
 
+def settle_kernel(chunks, kinds, part, flags_ref, *refs):
+    *pieces, gate_up_ref, down_ref, held = refs
+    first = flags_ref[0] == 1
+    count = len(pieces) // 4
+    half_rows = chunks * count * part
+    for half in range(2):
+        for index in range(count):
+            mine = pieces[half * count + index]
+            other = pieces[(2 + half) * count + index]
+            place = flags_ref[1 + half * count + index]
+            for chunk in range(chunks):
+                base = pl.multiple_of(half * half_rows + chunk * count * part + place * part, part)
+                for kind in range(kinds):
+                    start = (chunk * kinds + kind) * part
+                    rows = jnp.where(first, mine[start : start + part, :], other[start : start + part, :]).astype(F32)
+                    if kind < kinds - 1:
+                        held[kind, pl.ds(base, part), :] = rows
+                    else:
+                        down_ref[pl.ds(base, part), :] = rows
+    for kind in range(kinds - 1):
+        gate_up_ref[:, kind, :] = jnp.transpose(held[kind])
+
+
+def settle(pieces, flags, chunks, kinds, part):
+    rows, features = pieces[0].shape
+    units = 2 * (len(pieces) // 4) * chunks * part
+    width = 2 * LANES
+    return pl.pallas_call(
+        functools.partial(settle_kernel, chunks, kinds, part),
+        grid=(features // width,),
+        in_specs=[pl.BlockSpec(memory_space=pltpu.SMEM)]
+        + [pl.BlockSpec((rows, width), lambda index: (0, index))] * len(pieces),
+        out_specs=[
+            pl.BlockSpec((width, kinds - 1, units), lambda index: (index, 0, 0)),
+            pl.BlockSpec((units, width), lambda index: (0, index)),
+        ],
+        out_shape=[
+            jax.ShapeDtypeStruct((features, kinds - 1, units), F32),
+            jax.ShapeDtypeStruct((units, features), F32),
+        ],
+        scratch_shapes=[pltpu.VMEM((kinds - 1, units, width), F32)],
+        name="settle",
+    )(flags, *pieces)
+
+
 def together(*trees):
     return lax.optimization_barrier(trees)
 
@@ -351,21 +397,23 @@
             for e in range(PLANE)
         ]
 
+    def share(slab):
+        keep = lax.dynamic_index_in_dim(slab, core, 0, keepdims=False)
+        got = swap(lax.dynamic_index_in_dim(slab, 1 - core, 0, keepdims=False))
+        return jnp.where(is_first, keep, got), jnp.where(is_first, got, keep)
+
     qkv_rows = jnp.transpose(query_key_value_weight[0], (1, 2, 0))
     attn_rows = jnp.concatenate([qkv_rows, attention_output_weight], axis=0)
     attn_slab = attn_rows.reshape(2, 2, local_heads, PLANE, part, features)
     attn_slab = jnp.transpose(attn_slab, (0, 3, 1, 2, 4, 5)).reshape(2, PLANE, -1, features)
+    attn_in = [{"own": relative(own)} for own in share(attn_slab)]
+    attn_in[0] = near(attn_in[0])
+    attn_in, gate_up_weight, down_weight = together(attn_in, gate_up_weight, down_weight)
     gate_up_rows = jnp.transpose(gate_up_weight[0], (1, 2, 0))
     feed_rows = jnp.concatenate([gate_up_rows, down_weight], axis=0)
     feed_slab = feed_rows.reshape(3, 2, FEED_CHUNKS, PLANE, unit_part, features)
     feed_slab = jnp.transpose(feed_slab, (2, 1, 3, 0, 4, 5)).reshape(FEED_CHUNKS, 2, PLANE, -1, features)
 
-    def share(slab):
-        keep = lax.dynamic_index_in_dim(slab, core, 0, keepdims=False)
-        got = swap(lax.dynamic_index_in_dim(slab, 1 - core, 0, keepdims=False))
-        return jnp.where(is_first, keep, got), jnp.where(is_first, got, keep)
-
-    attn_in = [{"own": relative(own)} for own in share(attn_slab)]
     feed_in = [[{"own": relative(own)} for own in share(feed_slab[k])] for k in range(FEED_CHUNKS)]
     a0, a1 = attn_in
     (p0, p1), (q0, q1) = feed_in
@@ -404,8 +452,6 @@
         full = jnp.transpose(full, (1, 0, 2, 3)).reshape(3, -1, features)
         return full[:2].reshape(-1, features), full[2]
 
-    a0 = near(a0)
-    a0, p0 = together(a0, p0)
     a0, p0 = far(a0), near(p0)
     a0, p0, q0 = together(a0, p0, q0)
     a0, p0, q0 = first(a0), far(p0), near(q0)
@@ -452,14 +498,22 @@
         full = jnp.concatenate([gate_up, down]).reshape(3, PLANE, DEPTH, unit_part, features)
         return halves(jnp.transpose(full, (1, 2, 0, 3, 4)).reshape(PLANE, DEPTH, -1, features))
 
-    def attn_terms(qkv, out):
+    def attn_terms(qkv, out, vectors):
+        spread = jnp.transpose(jnp.stack(vectors).reshape(4, DEPTH, local), (1, 0, 2)).reshape(DEPTH, features)
+        spread = [lax.dynamic_index_in_dim(spread, jnp.bitwise_xor(depth, j), 0) for j in range(DEPTH)]
+        spread = jnp.pad(jnp.concatenate(spread).astype(BF16), ((0, NORM_ROWS - DEPTH), (0, 0)))
         full = jnp.concatenate([qkv, out]).reshape(2, -1, features)
+        full = jnp.concatenate([full, jnp.stack([spread, spread])], axis=1)
         keep = lax.dynamic_index_in_dim(full, core, 0, keepdims=False)
         return keep, swap(lax.dynamic_index_in_dim(full, 1 - core, 0, keepdims=False))
 
     def attn_pieces(pair):
-        full = add_low(*pair).reshape(2, DEPTH, local_heads, PLANE, part, features)
-        return halves(jnp.transpose(full, (3, 1, 0, 2, 4, 5)).reshape(PLANE, DEPTH, -1, features))
+        full = add_low(*pair)
+        spread = full[-NORM_ROWS : DEPTH - NORM_ROWS]
+        spread = jnp.broadcast_to(spread[None, :, None], (PLANE, DEPTH, NORM_ROWS, features))
+        full = full[:-NORM_ROWS].reshape(2, DEPTH, local_heads, PLANE, part, features)
+        full = jnp.transpose(full, (3, 1, 0, 2, 4, 5)).reshape(PLANE, DEPTH, -1, features)
+        return halves(jnp.concatenate([full, spread], axis=2))
 
     def hand_over(block, source):
         planes, depths = lax.axis_size("dp"), lax.axis_size("tensor")
@@ -483,7 +537,8 @@
     projected_grad, qkv, out = attn_backward(middle_low, sum_grad, attn1, projected1, context1, slopes, seqs)
     layer_out = give(middle_low, final_low)
     projected_grad, qkv, out, p1, q1, layer_out = together(projected_grad, qkv, out, p1, q1, layer_out)
-    projected_grad, a1 = together(projected_grad, attn_terms(qkv, out))
+    vectors = [gain_one1, offset_one1, gain_two1, offset_two1]
+    projected_grad, a1 = together(projected_grad, attn_terms(qkv, out, vectors))
     a1, p1, q1 = reduce_second(attn_pieces(a1)), reduce_near(p1), reduce_first(q1)
     middle_grad = dot(projected_grad, attn1[0], 1, 0) + sum_grad
     second_grad, gain_two0, offset_two0 = norm_backward(total0, norms[0][2], norms[0][3], middle_grad)
@@ -499,79 +554,72 @@
     a1, q1, p0, q0 = reduce_near(a1), reduce_far(q1), reduce_first(p0), reduce_second(q0)
     first_grad = join_rows(terms) + second_grad
     sum_grad, gain_one0, offset_one0 = norm_backward(sum0, norms[0][0], norms[0][1], first_grad)
-    vectors = jnp.stack(
-        [gain_one0, offset_one0, gain_two0, offset_two0, gain_one1, offset_one1, gain_two1, offset_two1]
-    )
     projected_grad, qkv, out = attn_backward(start, sum_grad, attn0, projected0, context0, slopes, seqs)
-    projected_grad, qkv, out, a1, q1, p0, q0, vectors = together(projected_grad, qkv, out, a1, q1, p0, q0, vectors)
-    a0, q0 = attn_terms(qkv, out), reduce_first(q0)
-    shared = swap(vectors)
+    projected_grad, qkv, out, a1, q1, p0, q0 = together(projected_grad, qkv, out, a1, q1, p0, q0)
+    a0 = attn_terms(qkv, out, [gain_one0, offset_one0, gain_two0, offset_two0])
     start_grad = dot(projected_grad, attn0[0], 1, 0) + sum_grad
-    start_grad, a0, q0, shared, vectors = together(start_grad, a0, q0, shared, vectors)
-    a0, a1, p0, q0 = reduce_second(attn_pieces(a0)), reduce_far(a1), reduce_near(p0), reduce_near(q0)
-    vectors = vectors + shared
-    mask = 1
-    while mask < lax.axis_size("dp"):
-        vectors = vectors + exchange(vectors, dp_masks=(mask, mask))
-        mask *= 2
+    q0 = reduce_first(q0)
+    start_grad, a0 = together(start_grad, a0)
+    a0, a1, p0 = reduce_second(attn_pieces(a0)), reduce_far(a1), reduce_near(p0)
     input_grad = give(start_grad, middle_grad)
-    a0, a1, p0, q0, vectors, input_grad = together(a0, a1, p0, q0, vectors, input_grad)
-    late = jnp.concatenate([reduce_last(p1), reduce_last(q1), reduce_last(a1)])
-    a0, p0, q0, late_first = reduce_first(a0), reduce_far(p0), reduce_far(q0), exchange(late, dp_masks=FIRST)
-    shared = exchange(vectors, tensor_mask=1)
-    a0, p0, q0, late, late_first, vectors, shared = together(a0, p0, q0, late, late_first, vectors, shared)
-    a0, late_second = reduce_near(a0), exchange(late, dp_masks=SECOND)
-    vectors = vectors + shared
-    shared = exchange(vectors, tensor_mask=2)
-    a0, late_second, late_first, p0, q0, vectors, shared = together(
-        a0, late_second, late_first, p0, q0, vectors, shared
-    )
+    a0, a1, p0, q0, input_grad = together(a0, a1, p0, q0, input_grad)
+    attn_late = reduce_last(a1)
+    late = jnp.concatenate([reduce_last(p1), reduce_last(q1), attn_late[:-NORM_ROWS]])
+    a0, p0, q0, late_first = reduce_first(a0), reduce_far(p0), reduce_near(q0), exchange(late, dp_masks=FIRST)
+    a0, p0, q0, late, late_first = together(a0, p0, q0, late, late_first)
+    a0, q0, late_second = reduce_near(a0), reduce_far(q0), exchange(late, dp_masks=SECOND)
+    late_got = [hand_over(late, 0), hand_over(late_first, 0)]
+    a0, late_second, late_first, p0, q0 = together(a0, late_second, late_first, p0, q0)
     a0, late_third = reduce_far(a0), exchange(late_first, dp_masks=SECOND)
-    vectors = vectors + shared
     feed = jnp.concatenate([reduce_last(p0), reduce_last(q0)])
     feed_first = exchange(feed, dp_masks=FIRST)
-    a0, late_third, feed, feed_first = together(a0, late_third, feed, feed_first)
-    attn = reduce_last(a0)
+    late_got.append(hand_over(late_second, 0))
+    a0, late_third, feed, feed_first, late_got = together(a0, late_third, feed, feed_first, late_got)
+    attn_early = reduce_last(a0)
+    attn = attn_early[:-NORM_ROWS]
     attn_first, attn_second = exchange(attn, dp_masks=FIRST), exchange(attn, dp_masks=SECOND)
     feed_second = exchange(feed, dp_masks=SECOND)
-    late = jnp.stack([late, late_first, late_second, late_third])
-    late_got = hand_over(late, 0)
-    attn_first, attn_second, feed_second, feed_first, late_got = together(
-        attn_first, attn_second, feed_second, feed_first, late_got
+    late_got.append(hand_over(late_third, 0))
+    feed_got = [hand_over(feed, 1), hand_over(feed_first, 1)]
+    attn_first, attn_second, feed_second, feed_first, late_got, feed_got = together(
+        attn_first, attn_second, feed_second, feed_first, late_got, feed_got
     )
     attn_third, feed_third = exchange(attn_first, dp_masks=SECOND), exchange(feed_first, dp_masks=SECOND)
-    attn_early = jnp.stack([attn, attn_first, attn_second, attn_third])
-    feed_early = jnp.stack([feed, feed_first, feed_second, feed_third])
-    feed_got, attn_got = hand_over(feed_early, 1), hand_over(attn_early, 1)
-
-    def settle(early, early_got, late, late_got):
-        parts = [jnp.where(is_first, early, late_got), jnp.where(is_first, early_got, late)]
-        return jnp.stack(
-            [
-                jnp.stack(
-                    [
-                        lax.dynamic_index_in_dim(half, order[jnp.bitwise_xor(in_plane, index)], 0, keepdims=False)
-                        for half, order in zip(parts, orders)
-                    ]
-                )
-                for index in range(PLANE)
-            ]
-        )
+    feed_early = [feed, feed_first, feed_second, feed_third]
+    feed_got = feed_got + [hand_over(feed_second, 1), hand_over(feed_third, 1)]
+    attn_early_all = jnp.stack([attn, attn_first, attn_second, attn_third])
+    attn_got = hand_over(attn_early_all, 1)
 
     feed_rows = FEED_CHUNKS * 3 * unit_part
-    feed_both = settle(feed_early, feed_got, late[:, :feed_rows], late_got[:, :feed_rows])
-    attn_both = settle(attn_early, attn_got, late[:, feed_rows:], late_got[:, feed_rows:])
-    feed_total = feed_both.reshape(PLANE, 2, FEED_CHUNKS, 3, unit_part, features)
-    feed_total = jnp.transpose(feed_total, (3, 1, 2, 0, 4, 5)).reshape(3, units, features).astype(F32)
-    grad_in = jnp.transpose(feed_total[:2], (2, 0, 1))
-    grad_down = feed_total[2]
-    attn_total = attn_both.reshape(PLANE, 2, 2, local_heads, part, features)
+    late = [late, late_first, late_second, late_third]
+    early_half = [feed_early, [piece[:feed_rows] for piece in late_got]]
+    late_half = [feed_got, [piece[:feed_rows] for piece in late]]
+    flags = jnp.concatenate(
+        [is_first.astype(jnp.int32)[None]] + [jnp.bitwise_xor(in_plane, order) for order in orders]
+    )
+    grad_in, grad_down = settle(
+        early_half[0] + late_half[0] + early_half[1] + late_half[1], flags, FEED_CHUNKS, 3, unit_part
+    )
+    attn_late_all = jnp.stack([piece[feed_rows:] for piece in late])
+    attn_late_got = jnp.stack([piece[feed_rows:] for piece in late_got])
+    parts = [jnp.where(is_first, attn_early_all, attn_late_got), jnp.where(is_first, attn_got, attn_late_all)]
+    attn_total = jnp.stack(
+        [
+            jnp.stack(
+                [
+                    lax.dynamic_index_in_dim(half, order[jnp.bitwise_xor(in_plane, index)], 0, keepdims=False)
+                    for half, order in zip(parts, orders)
+                ]
+            )
+            for index in range(PLANE)
+        ]
+    )
+    attn_total = attn_total.reshape(PLANE, 2, 2, local_heads, part, features)
     attn_total = jnp.transpose(attn_total, (1, 2, 3, 0, 4, 5)).reshape(4, local, features).astype(F32)
     grad_qkv = jnp.transpose(attn_total[:3], (2, 0, 1))
     grad_out = attn_total[3]
 
-    vectors = lax.dynamic_index_in_dim(vectors.reshape(2, 4, features), core, 0, keepdims=False)
-    vectors = lax.dynamic_slice_in_dim(vectors, depth * local, local, 1)
+    vectors = jnp.where(is_first, attn_early[-1], attn_late[-1]).astype(F32).reshape(4, local)
 
     return (
         layer_out,

time: 589 us -> 574 us (0.975)
  waiting for transfers between devices: 226 us -> 175 us
  starting transfers between devices: 76.8 us -> 92.3 us
  other arithmetic: 98.3 us -> 106 us
  Pallas kernels: 21.8 us -> 29.2 us
  matrix products: 61.7 us -> 68.6 us
    ppermute x86 -> x81, waiting for transfers between devices: 226 us -> 175 us  [exchange(): return lax.ppermute(block, AXES, pairs)]
    ppermute x3 -> x9, starting transfers between devices: 9.62 us -> 24.5 us  [hand_over(): return lax.ppermute(block, AXES, pairs)]
    unnamed x318 -> x354, local copies, waits for them, and re-layouts: 35.9 us -> 22.5 us
    pallas_call x0 -> x1, Pallas kernels: none -> 7.71 us  [settle(): pl.pallas_call(functools.partial(settle_kernel, chunks, kinds, part), gri...]
    dot_general x36, matrix products: 61.7 us -> 68.6 us  [dot(): lax.dot_general(a, b, (((ca,), (cb,)), ((), ())), preferred_element_type=...]
    another operation x1 -> x19, local copies, waits for them, and re-layouts: 0.65 us -> 6.8 us  [the longest x8 5.73 us: attn_terms(): jnp.stack(vectors).reshape(4, DEPTH, local)]
    ppermute x86 -> x81, starting transfers between devices: 67.2 us -> 67.9 us  [exchange(): return lax.ppermute(block, AXES, pairs)]
  transfers between devices with their start and end apart: 89 -> 90, of which waited for: 36 -> 34; matrix products, arithmetic and copies ran while one was open for 30% -> 34% of each run, Pallas kernels for 4% -> 4%
where the time goes in v5:
time: 574 us; the launch traced here: 563 us
  waiting for transfers between devices  175 us (30%)
  other arithmetic  106 us (18%)
  starting transfers between devices  92.3 us (16%)
  local copies, waits for them, and re-layouts  76.5 us (13%)
  matrix products  68.6 us (12%)
  Pallas kernels  29.2 us (5%)
  between operations  14.7 us (3%)
    ppermute x81, waiting for transfers between devices, exchange(): return lax.ppermute(block, AXES, pairs)  175 us
    dot_general x36, matrix products, dot(): lax.dot_general(a, b, (((ca,), (cb,)), ((), ())), preferred_element_type=...  68.6 us
    ppermute x81, starting transfers between devices, exchange(): return lax.ppermute(block, AXES, pairs)  67.9 us
    ppermute x9, starting transfers between devices, hand_over(): return lax.ppermute(block, AXES, pairs)  24.5 us
    convert_element_type x4, other arithmetic, feed_forward(): hidden = gelu_product(gate_part, up_part).astype(BF16)  24.3 us
    unnamed x354, local copies, waits for them, and re-layouts  22.5 us
    convert_element_type x26, other arithmetic, add_low(): return (a.astype(F32) + b.astype(F32)).astype(BF16)  18 us
    another operation x18, other arithmetic, assemble(): jnp.stack([jnp.concatenate([own[None], r]) for own, r in zip(chunk['own']...  13.2 us
  transfers between devices with their start and end apart: 90, of which 34 were waited for; matrix products, arithmetic and copies ran while one was open for 34% of the time, Pallas kernels for 4%

profile of v5, /device:TPU:1, one launch (start us, length us, event | category | flops | bytes accessed | tf_op | source)
XLA Modules:
  0.0 562.8 jit_solution(16843365096108881524)
XLA Ops:
  13.5 5.6 %copy.69 = bf16[1,768,2,768]{1,3,2,0:T(8,128)(2,1)S(1)} copy(bf16[1,768,2,768]{3,2,1,0:T(2,128)(2,1)} %param.19) | data formatting | bytes 4718592 | tf_op jit(solution)/shard_map/optimization_barrier | solution.py:244
  28.4 9.7 %collective-permute-done.2 = bf16[2,96,768]{2,1,0:T(8,128)(2,1)S(1)} collective-permute-done((bf16[2,96,768]{2,1,0:T(8,128)(2,1)S(1)}, bf16[2,96,768]{2,1,0:T(8,128)(2,1)S(1)}, u32[]{:S(2)}, u32[]{:S(2)}) %collective-permute-start.2) | collective-permute-done | bytes 294944 | tf_op jit(solution)/shard_map/ppermute | solution.py:61
  40.8 4.3 collective-permute-start.9
  45.2 6.4 %collective-permute-done.9 = bf16[144,768]{1,0:T(8,128)(2,1)S(1)} collective-permute-done((bf16[144,768]{1,0:T(8,128)(2,1)S(1)}, bf16[144,768]{1,0:T(8,128)(2,1)S(1)}, u32[]{:S(2)}, u32[]{:S(2)}) %collective-permute-start.9) | collective-permute-done | bytes 221216 | tf_op jit(solution)/shard_map/ppermute | solution.py:61
  51.6 7.6 %collective-permute-done.8 = bf16[2,144,768]{2,1,0:T(8,128)(2,1)S(1)} collective-permute-done((bf16[2,144,768]{2,1,0:T(8,128)(2,1)S(1)}, bf16[2,144,768]{2,1,0:T(8,128)(2,1)S(1)}, u32[]{:S(2)}, u32[]{:S(2)}) %collective-permute-start.8) | collective-permute-done | bytes 442400 | tf_op jit(solution)/shard_map/ppermute | solution.py:61
  65.8 6.2 %collective-permute-done.14 = bf16[96,768]{1,0:T(8,128)(2,1)S(1)} collective-permute-done((bf16[96,768]{1,0:T(8,128)(2,1)S(1)}, bf16[96,768]{1,0:T(8,128)(2,1)S(1)}, u32[]{:S(2)}, u32[]{:S(2)}) %collective-permute-start.14) | collective-permute-done | bytes 147488 | tf_op jit(solution)/shard_map/ppermute | solution.py:61
  72.0 12.0 %collective-permute-done.13 = bf16[2,144,768]{2,1,0:T(8,128)(2,1)S(1)} collective-permute-done((bf16[2,144,768]{2,1,0:T(8,128)(2,1)S(1)}, bf16[2,144,768]{2,1,0:T(8,128)(2,1)S(1)}, u32[]{:S(2)}, u32[]{:S(2)}) %collective-permute-start.13) | collective-permute-done | bytes 442400 | tf_op jit(solution)/shard_map/ppermute | solution.py:61
  104.0 4.9 attend.2
  111.5 5.6 collective-permute-done.17
  130.5 6.2 %multiply_convert_fusion.7 = (bf16[768,768]{1,0:T(8,128)(2,1)S(1)}, f32[768,768]{1,0:T(8,128)}) fusion(f32[768,1536]{1,0:T(8,128)S(1)} %fusion.124), kind=kLoop, calls=%fused_computation.106 | loop fusion | flops 38928384 | bytes 8257536 | tf_op jit(solution)/shard_map/convert_element_type | solution.py:333
  137.8 10.5 %collective-permute-done.26 = bf16[2,144,768]{2,1,0:T(8,128)(2,1)S(1)} collective-permute-done((bf16[2,144,768]{2,1,0:T(8,128)(2,1)S(1)}, bf16[2,144,768]{2,1,0:T(8,128)(2,1)S(1)}, u32[]{:S(2)}, u32[]{:S(2)}) %collective-permute-start.26) | collective-permute-done | bytes 442400 | tf_op jit(solution)/shard_map/ppermute | solution.py:61
  157.7 6.0 %multiply_convert_fusion.6 = (bf16[768,768]{1,0:T(8,128)(2,1)S(1)}, f32[768,768]{1,0:T(8,128)}) fusion(f32[768,1536]{1,0:T(8,128)S(1)} %fusion.126), kind=kLoop, calls=%fused_computation.93 | loop fusion | flops 38928384 | bytes 8257536 | tf_op jit(solution)/shard_map/convert_element_type | solution.py:333
  166.5 6.0 %collective-permute-done.31 = bf16[2,144,768]{2,1,0:T(8,128)(2,1)S(1)} collective-permute-done((bf16[2,144,768]{2,1,0:T(8,128)(2,1)S(1)}, bf16[2,144,768]{2,1,0:T(8,128)(2,1)S(1)}, u32[]{:S(2)}, u32[]{:S(2)}) %collective-permute-start.31) | collective-permute-done | bytes 442400 | tf_op jit(solution)/shard_map/ppermute | solution.py:61
  185.6 5.1 attend.3
  193.6 5.6 collective-permute-done.34
  207.9 6.0 %multiply_convert_fusion.5 = (bf16[768,768]{1,0:T(8,128)(2,1)S(1)}, f32[768,768]{1,0:T(8,128)}) fusion(f32[768,1536]{1,0:T(8,128)S(1)} %fusion.128), kind=kLoop, calls=%fused_computation.80 | loop fusion | flops 38928384 | bytes 8257536 | tf_op jit(solution)/shard_map/convert_element_type | solution.py:333
  220.7 6.1 %multiply_convert_fusion.4 = (bf16[768,768]{1,0:T(8,128)(2,1)S(1)}, f32[768,768]{1,0:T(8,128)}) fusion(f32[768,1536]{1,0:T(8,128)S(1)} %fusion.130), kind=kLoop, calls=%fused_computation.67 | loop fusion | flops 38928384 | bytes 8257536 | tf_op jit(solution)/shard_map/convert_element_type | solution.py:333
  273.8 7.6 %collective-permute-done.41 = bf16[2,4,144,768]{3,2,1,0:T(8,128)(2,1)S(1)} collective-permute-done((bf16[2,4,144,768]{3,2,1,0:T(8,128)(2,1)S(1)}, bf16[2,4,144,768]{3,2,1,0:T(8,128)(2,1)S(1)}, u32[]{:S(2)}, u32[]{:S(2)}) %collective-permute-start.41) | collective-permute-done | bytes 1769504 | tf_op jit(solution)/shard_map/ppermute | solution.py:61
  292.5 5.7 %attend_back.2 = bf16[384,2304]{1,0:T(8,128)(2,1)} custom-call(f32[12]{0:T(128)} %pad_maximum_fusion.60.slopes_ref, bf16[384,2304]{1,0:T(8,128)(2,1)} %convolution_convert_fusion.2.projected_ref, bf16[384,768]{1,0:T(8,128)(2,1)} %convolution_convert_fusion.15.context_grad_ref), custom_call_target="tpu_custom_call" | custom-call | flops 377487360 | bytes 4128768 | tf_op jit(solution)/shard_map/attend_back/pallas_call | solution.py:181
  305.3 11.0 %collective-permute-done.44 = bf16[2,4,144,768]{3,2,1,0:T(8,128)(2,1)} collective-permute-done((bf16[2,4,144,768]{3,2,1,0:T(8,128)(2,1)}, bf16[2,4,144,768]{3,2,1,0:T(8,128)(2,1)}, u32[]{:S(2)}, u32[]{:S(2)}) %collective-permute-start.44) | collective-permute-done | bytes 1769504 | tf_op jit(solution)/shard_map/ppermute | solution.py:61
  377.2 14.4 %collective-permute-done.54 = bf16[2,4,144,768]{3,2,1,0:T(8,128)(2,1)S(1)} collective-permute-done((bf16[2,4,144,768]{3,2,1,0:T(8,128)(2,1)S(1)}, bf16[2,4,144,768]{3,2,1,0:T(8,128)(2,1)S(1)}, u32[]{:S(2)}, u32[]{:S(2)}) %collective-permute-start.54) | collective-permute-done | bytes 1769504 | tf_op jit(solution)/shard_map/ppermute | solution.py:61
  407.8 5.7 %attend_back.3 = bf16[384,2304]{1,0:T(8,128)(2,1)} custom-call(f32[12]{0:T(128)} %pad_maximum_fusion.60.slopes_ref, bf16[384,2304]{1,0:T(8,128)(2,1)} %convolution_convert_fusion.3.projected_ref, bf16[384,768]{1,0:T(8,128)(2,1)} %convolution_convert_fusion.14.context_grad_ref), custom_call_target="tpu_custom_call" | custom-call | flops 377487360 | bytes 4128768 | tf_op jit(solution)/shard_map/attend_back/pallas_call | solution.py:181
  418.4 11.0 %collective-permute-done.59 = bf16[2,4,144,768]{3,2,1,0:T(8,128)(2,1)} collective-permute-done((bf16[2,4,144,768]{3,2,1,0:T(8,128)(2,1)}, bf16[2,4,144,768]{3,2,1,0:T(8,128)(2,1)}, u32[]{:S(2)}, u32[]{:S(2)}) %collective-permute-start.59) | collective-permute-done | bytes 1769504 | tf_op jit(solution)/shard_map/ppermute | solution.py:61
  448.5 7.7 %collective-permute-done.63 = bf16[2,144,768]{2,1,0:T(8,128)(2,1)S(1)} collective-permute-done((bf16[2,144,768]{2,1,0:T(8,128)(2,1)S(1)}, bf16[2,144,768]{2,1,0:T(8,128)(2,1)S(1)}, u32[]{:S(2)}, u32[]{:S(2)}) %collective-permute-start.63) | collective-permute-done | bytes 442400 | tf_op jit(solution)/shard_map/ppermute | solution.py:61
  456.2 8.4 %collective-permute-done.64 = bf16[4,144,768]{2,1,0:T(8,128)(2,1)S(1)} collective-permute-done((bf16[4,144,768]{2,1,0:T(8,128)(2,1)S(1)}, bf16[4,144,768]{2,1,0:T(8,128)(2,1)S(1)}, u32[]{:S(2)}, u32[]{:S(2)}) %collective-permute-start.64) | collective-permute-done | bytes 884768 | tf_op jit(solution)/shard_map/ppermute | solution.py:61
  464.6 4.6 collective-permute-done.61
  494.1 3.8 collective-permute-done.72
  510.7 7.3 %collective-permute-start.83 = (bf16[288,768]{1,0:T(8,128)(2,1)S(1)}, bf16[288,768]{1,0:T(8,128)(2,1)S(1)}, u32[]{:S(2)}, u32[]{:S(2)}) collective-permute-start(bf16[288,768]{1,0:T(8,128)(2,1)S(1)} %pad_maximum_fusion.52.refs_0_), channel_id=1, source_target_pairs={{16,0},{17,1},{18,2},{19,3},{20,4},{21,5},{22,6},{23,7},{24,8},{25... | collective-permute-start | bytes 1327112 | tf_op jit(solution)/shard_map/ppermute | solution.py:522
  526.8 3.8 collective-permute-done.80
  530.9 3.8 collective-permute-done.85
  534.9 5.1 collective-permute-start.86
  554.9 7.7 %settle.1 = (f32[768,2,768]{2,1,0:T(2,128)}, f32[768,768]{1,0:T(8,128)}) custom-call(s32[9]{0:T(128)} %pad_add_fusion.flags_ref, bf16[288,768]{1,0:T(8,128)(2,1)} %copy-done.48, bf16[288,768]{1,0:T(8,128)(2,1)} %copy-done.110, bf16[288,768]{1,0:T(8,128)(2,1)} %copy-done.112, bf16[288,768]{1,0:T(8,128)(2,1)} %copy-done.114, bf16[288,768]{1,0:T(8,128)(2,1)} %copy-done.111, ...), custom_call_target="tpu_custom_call" | custom-call | tf_op jit(solution)/shard_map/settle/pallas_call | solution.py:225
  (812 shorter events, 327.0 us)
Async XLA Ops:
  38.2 21.0 %collective-permute-start.8 = (bf16[2,144,768]{2,1,0:T(8,128)(2,1)S(1)}, bf16[2,144,768]{2,1,0:T(8,128)(2,1)S(1)}, u32[]{:S(2)}, u32[]{:S(2)}) collective-permute-start(bf16[2,144,768]{2,1,0:T(8,128)(2,1)S(1)} %pad_maximum_fusion.47), channel_id=1, source_target_pairs={{0,2},{1,3},{2,0},{3,1},{4,6},{5,7},{6,4},{7,5},{8,10},{9,11},{10,... | collective-permute-start | bytes 1327112 | tf_op jit(solution)/shard_map/ppermute | solution.py:61
  38.4 20.8 %collective-permute-start.7 = (bf16[3,96,768]{2,1,0:T(8,128)(2,1)S(1)}, bf16[3,96,768]{2,1,0:T(8,128)(2,1)S(1)}, u32[]{:S(2)}, u32[]{:S(2)}) collective-permute-start(bf16[3,96,768]{2,1,0:T(8,128)(2,1)S(1)} %pad_maximum_fusion.46), channel_id=1, source_target_pairs={{0,8},{1,9},{2,10},{3,11},{4,12},{5,13},{6,14},{7,15},{8,0},{9,1},... | collective-permute-start | bytes 1327112 | tf_op jit(solution)/shard_map/ppermute | solution.py:61
  39.6 19.6 %collective-permute-start.6 = (bf16[3,96,768]{2,1,0:T(8,128)(2,1)S(1)}, bf16[3,96,768]{2,1,0:T(8,128)(2,1)S(1)}, u32[]{:S(2)}, u32[]{:S(2)}) collective-permute-start(bf16[3,96,768]{2,1,0:T(8,128)(2,1)S(1)} %pad_maximum_fusion.46), channel_id=1, source_target_pairs={{0,4},{1,5},{2,6},{3,7},{4,0},{5,1},{6,2},{7,3},{8,12},{9,13},{10,... | collective-permute-start | bytes 1327112 | tf_op jit(solution)/shard_map/ppermute | solution.py:61
  59.2 24.7 %collective-permute-start.12 = (bf16[3,144,768]{2,1,0:T(8,128)(2,1)S(1)}, bf16[3,144,768]{2,1,0:T(8,128)(2,1)S(1)}, u32[]{:S(2)}, u32[]{:S(2)}) collective-permute-start(bf16[3,144,768]{2,1,0:T(8,128)(2,1)S(1)} %pad_maximum_fusion.40), channel_id=1, source_target_pairs={{0,8},{1,9},{2,10},{3,11},{4,12},{5,13},{6,14},{7,15},{8,0},{9,1},... | collective-permute-start | bytes 1990664 | tf_op jit(solution)/shard_map/ppermute | solution.py:61
  60.3 23.6 %collective-permute-start.11 = (bf16[3,144,768]{2,1,0:T(8,128)(2,1)S(1)}, bf16[3,144,768]{2,1,0:T(8,128)(2,1)}, u32[]{:S(2)}, u32[]{:S(2)}) collective-permute-start(bf16[3,144,768]{2,1,0:T(8,128)(2,1)S(1)} %pad_maximum_fusion.40), channel_id=1, source_target_pairs={{0,4},{1,5},{2,6},{3,7},{4,0},{5,1},{6,2},{7,3},{8,12},{9,13},{10,... | collective-permute-start | bytes 1990664 | tf_op jit(solution)/shard_map/ppermute | solution.py:61
  61.6 22.3 %collective-permute-start.13 = (bf16[2,144,768]{2,1,0:T(8,128)(2,1)S(1)}, bf16[2,144,768]{2,1,0:T(8,128)(2,1)S(1)}, u32[]{:S(2)}, u32[]{:S(2)}) collective-permute-start(bf16[2,144,768]{2,1,0:T(8,128)(2,1)S(1)} %pad_maximum_fusion.48), channel_id=1, source_target_pairs={{0,2},{1,3},{2,0},{3,1},{4,6},{5,7},{6,4},{7,5},{8,10},{9,11},{10,... | collective-permute-start | bytes 1327112 | tf_op jit(solution)/shard_map/ppermute | solution.py:61
  61.7 22.2 %collective-permute-start.10 = (bf16[3,96,768]{2,1,0:T(8,128)(2,1)S(1)}, bf16[3,96,768]{2,1,0:T(8,128)(2,1)S(1)}, u32[]{:S(2)}, u32[]{:S(2)}) collective-permute-start(bf16[3,96,768]{2,1,0:T(8,128)(2,1)S(1)} %collective-permute-done.6), channel_id=1, source_target_pairs={{0,8},{1,9},{2,10},{3,11},{4,12},{5,13},{6,14},{7,15},{8,0},{9,1},... | collective-permute-start | bytes 1327112 | tf_op jit(solution)/shard_map/ppermute | solution.py:61
  95.6 21.4 %collective-permute-start.17 = (bf16[3,144,768]{2,1,0:T(8,128)(2,1)}, bf16[3,144,768]{2,1,0:T(8,128)(2,1)}, u32[]{:S(2)}, u32[]{:S(2)}) collective-permute-start(bf16[3,144,768]{2,1,0:T(8,128)(2,1)} %collective-permute-done.11), channel_id=1, source_target_pairs={{0,8},{1,9},{2,10},{3,11},{4,12},{5,13},{6,14},{7,15},{8,0},{9,1},... | collective-permute-start | bytes 1990664 | tf_op jit(solution)/shard_map/ppermute | solution.py:61
  118.1 30.2 %collective-permute-start.25 = (bf16[3,96,768]{2,1,0:T(8,128)(2,1)S(1)}, bf16[3,96,768]{2,1,0:T(8,128)(2,1)S(1)}, u32[]{:S(2)}, u32[]{:S(2)}) collective-permute-start(bf16[3,96,768]{2,1,0:T(8,128)(2,1)S(1)} %pad_maximum_fusion.49), channel_id=1, source_target_pairs={{0,8},{1,9},{2,10},{3,11},{4,12},{5,13},{6,14},{7,15},{8,0},{9,1},... | collective-permute-start | bytes 1327112 | tf_op jit(solution)/shard_map/ppermute | solution.py:61
  118.4 29.9 %collective-permute-start.24 = (bf16[3,96,768]{2,1,0:T(8,128)(2,1)S(1)}, bf16[3,96,768]{2,1,0:T(8,128)(2,1)S(1)}, u32[]{:S(2)}, u32[]{:S(2)}) collective-permute-start(bf16[3,96,768]{2,1,0:T(8,128)(2,1)S(1)} %pad_maximum_fusion.49), channel_id=1, source_target_pairs={{0,4},{1,5},{2,6},{3,7},{4,0},{5,1},{6,2},{7,3},{8,12},{9,13},{10,... | collective-permute-start | bytes 1327112 | tf_op jit(solution)/shard_map/ppermute | solution.py:61
  126.1 22.2 %collective-permute-start.26 = (bf16[2,144,768]{2,1,0:T(8,128)(2,1)S(1)}, bf16[2,144,768]{2,1,0:T(8,128)(2,1)S(1)}, u32[]{:S(2)}, u32[]{:S(2)}) collective-permute-start(bf16[2,144,768]{2,1,0:T(8,128)(2,1)S(1)} %pad_maximum_fusion.50), channel_id=1, source_target_pairs={{0,2},{1,3},{2,0},{3,1},{4,6},{5,7},{6,4},{7,5},{8,10},{9,11},{10,... | collective-permute-start | bytes 1327112 | tf_op jit(solution)/shard_map/ppermute | solution.py:61
  127.7 20.6 %collective-permute-start.23 = (bf16[3,144,768]{2,1,0:T(8,128)(2,1)}, bf16[3,144,768]{2,1,0:T(8,128)(2,1)S(1)}, u32[]{:S(2)}, u32[]{:S(2)}) collective-permute-start(bf16[3,144,768]{2,1,0:T(8,128)(2,1)} %collective-permute-done.18), channel_id=1, source_target_pairs={{0,8},{1,9},{2,10},{3,11},{4,12},{5,13},{6,14},{7,15},{8,0},{9,1},... | collective-permute-start | bytes 1990664 | tf_op jit(solution)/shard_map/ppermute | solution.py:61
  149.3 23.2 %collective-permute-start.30 = (bf16[3,144,768]{2,1,0:T(8,128)(2,1)S(1)}, bf16[3,144,768]{2,1,0:T(8,128)(2,1)S(1)}, u32[]{:S(2)}, u32[]{:S(2)}) collective-permute-start(bf16[3,144,768]{2,1,0:T(8,128)(2,1)S(1)} %pad_maximum_fusion.42), channel_id=1, source_target_pairs={{0,8},{1,9},{2,10},{3,11},{4,12},{5,13},{6,14},{7,15},{8,0},{9,1},... | collective-permute-start | bytes 1990664 | tf_op jit(solution)/shard_map/ppermute | solution.py:61
  150.0 22.5 %collective-permute-start.29 = (bf16[3,144,768]{2,1,0:T(8,128)(2,1)S(1)}, bf16[3,144,768]{2,1,0:T(8,128)(2,1)}, u32[]{:S(2)}, u32[]{:S(2)}) collective-permute-start(bf16[3,144,768]{2,1,0:T(8,128)(2,1)S(1)} %pad_maximum_fusion.42), channel_id=1, source_target_pairs={{0,4},{1,5},{2,6},{3,7},{4,0},{5,1},{6,2},{7,3},{8,12},{9,13},{10,... | collective-permute-start | bytes 1990664 | tf_op jit(solution)/shard_map/ppermute | solution.py:61
  151.1 21.4 %collective-permute-start.31 = (bf16[2,144,768]{2,1,0:T(8,128)(2,1)S(1)}, bf16[2,144,768]{2,1,0:T(8,128)(2,1)S(1)}, u32[]{:S(2)}, u32[]{:S(2)}) collective-permute-start(bf16[2,144,768]{2,1,0:T(8,128)(2,1)S(1)} %pad_maximum_fusion.51), channel_id=1, source_target_pairs={{0,2},{1,3},{2,0},{3,1},{4,6},{5,7},{6,4},{7,5},{8,10},{9,11},{10,... | collective-permute-start | bytes 1327112 | tf_op jit(solution)/shard_map/ppermute | solution.py:61
  151.2 21.3 %collective-permute-start.28 = (bf16[3,96,768]{2,1,0:T(8,128)(2,1)S(1)}, bf16[3,96,768]{2,1,0:T(8,128)(2,1)S(1)}, u32[]{:S(2)}, u32[]{:S(2)}) collective-permute-start(bf16[3,96,768]{2,1,0:T(8,128)(2,1)S(1)} %collective-permute-done.24), channel_id=1, source_target_pairs={{0,8},{1,9},{2,10},{3,11},{4,12},{5,13},{6,14},{7,15},{8,0},{9,1},... | collective-permute-start | bytes 1327112 | tf_op jit(solution)/shard_map/ppermute | solution.py:61
  175.0 18.6 %collective-permute-start.36 = (bf16[3,144,768]{2,1,0:T(8,128)(2,1)S(1)}, bf16[3,144,768]{2,1,0:T(8,128)(2,1)}, u32[]{:S(2)}, u32[]{:S(2)}) collective-permute-start(bf16[3,144,768]{2,1,0:T(8,128)(2,1)S(1)} %pad_maximum_fusion.43), channel_id=1, source_target_pairs={{0,8},{1,9},{2,10},{3,11},{4,12},{5,13},{6,14},{7,15},{8,0},{9,1},... | collective-permute-start | bytes 1990664 | tf_op jit(solution)/shard_map/ppermute | solution.py:61
  176.3 22.9 %collective-permute-start.34 = (bf16[3,144,768]{2,1,0:T(8,128)(2,1)}, bf16[3,144,768]{2,1,0:T(8,128)(2,1)}, u32[]{:S(2)}, u32[]{:S(2)}) collective-permute-start(bf16[3,144,768]{2,1,0:T(8,128)(2,1)} %collective-permute-done.29), channel_id=1, source_target_pairs={{0,8},{1,9},{2,10},{3,11},{4,12},{5,13},{6,14},{7,15},{8,0},{9,1},... | collective-permute-start | bytes 1990664 | tf_op jit(solution)/shard_map/ppermute | solution.py:61
  242.7 27.1 %collective-permute-start.45 = (bf16[384,768]{1,0:T(8,128)(2,1)S(1)}, bf16[384,768]{1,0:T(8,128)(2,1)S(1)}, u32[]{:S(2)}, u32[]{:S(2)}) collective-permute-start(bf16[384,768]{1,0:T(8,128)(2,1)S(1)} %get-tuple-element.631), channel_id=1, source_target_pairs={{0,16},{1,17},{2,18},{3,19},{4,20},{5,21},{6,22},{7,23},{8,24},{9,... | collective-permute-start | bytes 1769480 | tf_op jit(solution)/shard_map/ppermute | solution.py:61
  259.7 21.7 %collective-permute-start.41 = (bf16[2,4,144,768]{3,2,1,0:T(8,128)(2,1)S(1)}, bf16[2,4,144,768]{3,2,1,0:T(8,128)(2,1)S(1)}, u32[]{:S(2)}, u32[]{:S(2)}) collective-permute-start(bf16[2,4,144,768]{3,2,1,0:T(8,128)(2,1)S(1)} %bitcast.547), channel_id=1, source_target_pairs={{0,8},{1,9},{2,10},{3,11},{4,12},{5,13},{6,14},{7,15},{8,0},{9,1},... | collective-permute-start | bytes 5308424 | tf_op jit(solution)/shard_map/ppermute | solution.py:61
  284.8 20.6 %collective-permute-start.43 = (bf16[4,144,768]{2,1,0:T(8,128)(2,1)}, bf16[4,144,768]{2,1,0:T(8,128)(2,1)}, u32[]{:S(2)}, u32[]{:S(2)}) collective-permute-start(bf16[4,144,768]{2,1,0:T(8,128)(2,1)} %get-tuple-element.694), channel_id=1, source_target_pairs={{0,4},{1,5},{2,6},{3,7},{4,0},{5,1},{6,2},{7,3},{8,12},{9,13},{10,... | collective-permute-start | bytes 2654216 | tf_op jit(solution)/shard_map/ppermute | solution.py:61
  285.2 31.2 %collective-permute-start.44 = (bf16[2,4,144,768]{3,2,1,0:T(8,128)(2,1)}, bf16[2,4,144,768]{3,2,1,0:T(8,128)(2,1)}, u32[]{:S(2)}, u32[]{:S(2)}) collective-permute-start(bf16[2,4,144,768]{3,2,1,0:T(8,128)(2,1)} %bitcast.157), channel_id=1, source_target_pairs={{0,8},{1,9},{2,10},{3,11},{4,12},{5,13},{6,14},{7,15},{8,0},{9,1},... | collective-permute-start | bytes 5308424 | tf_op jit(solution)/shard_map/ppermute | solution.py:61
  320.9 30.1 %collective-permute-start.49 = (bf16[2,144,768]{2,1,0:T(8,128)(2,1)}, bf16[2,144,768]{2,1,0:T(8,128)(2,1)}, u32[]{:S(2)}, u32[]{:S(2)}) collective-permute-start(bf16[2,144,768]{2,1,0:T(8,128)(2,1)} %get-tuple-element.708), channel_id=1, source_target_pairs={{0,1},{1,0},{2,3},{3,2},{4,5},{5,4},{6,7},{7,6},{8,9},{9,8},{10,11... | collective-permute-start | bytes 1327112 | tf_op jit(solution)/shard_map/ppermute | solution.py:61
  324.3 26.6 %collective-permute-start.50 = (bf16[4,144,768]{2,1,0:T(8,128)(2,1)}, bf16[4,144,768]{2,1,0:T(8,128)(2,1)}, u32[]{:S(2)}, u32[]{:S(2)}) collective-permute-start(bf16[4,144,768]{2,1,0:T(8,128)(2,1)} %get-tuple-element.690), channel_id=1, source_target_pairs={{0,4},{1,5},{2,6},{3,7},{4,0},{5,1},{6,2},{7,3},{8,12},{9,13},{10,... | collective-permute-start | bytes 2654216 | tf_op jit(solution)/shard_map/ppermute | solution.py:61
  362.8 28.7 %collective-permute-start.54 = (bf16[2,4,144,768]{3,2,1,0:T(8,128)(2,1)S(1)}, bf16[2,4,144,768]{3,2,1,0:T(8,128)(2,1)S(1)}, u32[]{:S(2)}, u32[]{:S(2)}) collective-permute-start(bf16[2,4,144,768]{3,2,1,0:T(8,128)(2,1)S(1)} %bitcast.546), channel_id=1, source_target_pairs={{0,8},{1,9},{2,10},{3,11},{4,12},{5,13},{6,14},{7,15},{8,0},{9,1},... | collective-permute-start | bytes 5308424 | tf_op jit(solution)/shard_map/ppermute | solution.py:61
  392.7 25.6 %collective-permute-start.56 = (bf16[2,112,768]{2,1,0:T(8,128)(2,1)}, bf16[2,112,768]{2,1,0:T(8,128)(2,1)}, u32[]{:S(2)}, u32[]{:S(2)}) collective-permute-start(bf16[2,112,768]{2,1,0:T(8,128)(2,1)} %get-tuple-element.728), channel_id=1, source_target_pairs={{0,1},{1,0},{2,3},{3,2},{4,5},{5,4},{6,7},{7,6},{8,9},{9,8},{10,11... | collective-permute-start | bytes 1032200 | tf_op jit(solution)/shard_map/ppermute | solution.py:61
  395.0 23.2 %collective-permute-start.57 = (bf16[144,768]{1,0:T(8,128)(2,1)}, bf16[144,768]{1,0:T(8,128)(2,1)}, u32[]{:S(2)}, u32[]{:S(2)}) collective-permute-start(bf16[144,768]{1,0:T(8,128)(2,1)} %get-tuple-element.752), channel_id=1, source_target_pairs={{0,2},{1,3},{2,0},{3,1},{4,6},{5,7},{6,4},{7,5},{8,10},{9,11},{10,... | collective-permute-start | bytes 663560 | tf_op jit(solution)/shard_map/ppermute | solution.py:61
  397.9 20.6 %collective-permute-start.58 = (bf16[4,144,768]{2,1,0:T(8,128)(2,1)}, bf16[4,144,768]{2,1,0:T(8,128)(2,1)}, u32[]{:S(2)}, u32[]{:S(2)}) collective-permute-start(bf16[4,144,768]{2,1,0:T(8,128)(2,1)} %get-tuple-element.688), channel_id=1, source_target_pairs={{0,4},{1,5},{2,6},{3,7},{4,0},{5,1},{6,2},{7,3},{8,12},{9,13},{10,... | collective-permute-start | bytes 2654216 | tf_op jit(solution)/shard_map/ppermute | solution.py:61
  398.3 31.2 %collective-permute-start.59 = (bf16[2,4,144,768]{3,2,1,0:T(8,128)(2,1)}, bf16[2,4,144,768]{3,2,1,0:T(8,128)(2,1)}, u32[]{:S(2)}, u32[]{:S(2)}) collective-permute-start(bf16[2,4,144,768]{3,2,1,0:T(8,128)(2,1)} %bitcast.189), channel_id=1, source_target_pairs={{0,8},{1,9},{2,10},{3,11},{4,12},{5,13},{6,14},{7,15},{8,0},{9,1},... | collective-permute-start | bytes 5308424 | tf_op jit(solution)/shard_map/ppermute | solution.py:61
  442.1 27.0 %collective-permute-start.61 = (bf16[2,4,112,768]{3,2,1,0:T(8,128)(2,1)S(1)}, bf16[2,4,112,768]{3,2,1,0:T(8,128)(2,1)S(1)}, u32[]{:S(2)}, u32[]{:S(2)}) collective-permute-start(bf16[2,4,112,768]{3,2,1,0:T(8,128)(2,1)S(1)} %get-tuple-element.678), channel_id=1, source_target_pairs={{0,8},{1,9},{2,10},{3,11},{4,12},{5,13},{6,14},{7,15},{8,0},{9,1},... | collective-permute-start | bytes 4128776 | tf_op jit(solution)/shard_map/ppermute | solution.py:61
  442.9 21.6 %collective-permute-start.64 = (bf16[4,144,768]{2,1,0:T(8,128)(2,1)S(1)}, bf16[4,144,768]{2,1,0:T(8,128)(2,1)S(1)}, u32[]{:S(2)}, u32[]{:S(2)}) collective-permute-start(bf16[4,144,768]{2,1,0:T(8,128)(2,1)S(1)} %get-tuple-element.686), channel_id=1, source_target_pairs={{0,4},{1,5},{2,6},{3,7},{4,0},{5,1},{6,2},{7,3},{8,12},{9,13},{10,... | collective-permute-start | bytes 2654216 | tf_op jit(solution)/shard_map/ppermute | solution.py:61
  510.7 19.9 %collective-permute-start.83 = (bf16[288,768]{1,0:T(8,128)(2,1)S(1)}, bf16[288,768]{1,0:T(8,128)(2,1)S(1)}, u32[]{:S(2)}, u32[]{:S(2)}) collective-permute-start(bf16[288,768]{1,0:T(8,128)(2,1)S(1)} %pad_maximum_fusion.52.refs_0_), channel_id=1, source_target_pairs={{16,0},{17,1},{18,2},{19,3},{20,4},{21,5},{22,6},{23,7},{24,8},{25... | collective-permute-start | bytes 1327112 | tf_op jit(solution)/shard_map/ppermute | solution.py:522
  (236 other events, 2085.1 us)

commit v6 on v5

--- a/solution.py
+++ b/solution.py
@@ -275,35 +275,39 @@
     return (a.astype(F32) + b.astype(F32)).astype(BF16)
 
 
-def halves(terms):
-    return terms[: PLANE // 2], terms[PLANE // 2 :]
-
-
-def reduce_second(terms):
-    return terms[0], exchange(terms[1], dp_masks=SECOND)
-
-
-def reduce_first(pair):
-    terms = add_low(*pair)
-    return terms[0], exchange(terms[1], dp_masks=FIRST)
-
-
-def reduce_near(pair):
-    terms = add_low(*pair)
-    pairs = terms.reshape((2, 2) + terms.shape[1:])
+def total_low(*parts):
+    return sum(part.astype(F32) for part in parts).astype(BF16)
+
+
+def reduce_open(terms):
+    return (
+        terms[0],
+        terms[1],
+        exchange(terms[3], dp_masks=SECOND),
+        exchange(terms[2], dp_masks=SECOND),
+    )
+
+
+def reduce_turn(parts):
+    return parts[0], exchange(total_low(parts[1], parts[2]), dp_masks=FIRST)
+
+
+def reduce_near(own, turned, opened):
+    pairs = total_low(own, turned, opened)
+    pairs = pairs.reshape((2, 2) + pairs.shape[1:])
     return pairs[:, 0], exchange(pairs[:, 1], tensor_mask=1)
 
 
 def reduce_far(pair):
-    terms = add_low(*pair)
+    terms = total_low(*pair)
     return terms[0], exchange(terms[1], tensor_mask=2)
 
 
 def reduce_last(pair):
-    one = add_low(*pair)
+    one = total_low(*pair)
     mask = PLANE
     while mask < lax.axis_size("dp"):
-        one = add_low(one, exchange(one, dp_masks=(mask, mask)))
+        one = total_low(one, exchange(one, dp_masks=(mask, mask)))
         mask *= 2
     return one
 
@@ -334,16 +338,16 @@
     return gated, hidden, dot(hidden, down, 1, 0)
 
 
-def feed_backward(mixed_all, first_all, weights, gated, hidden):
-    gate_up, down = weights
-    hidden_grad = dot(mixed_all, down, 1, 1)
-    down_grad = dot(hidden, mixed_all, 0, 0).astype(BF16)
+def feed_backward(mixed_all, weights, gated):
+    hidden_grad = dot(mixed_all, weights[1], 1, 1)
     gate_part, up_part = jnp.split(gated, 2, axis=-1)
     _, gelu_back = jax.vjp(gelu_product, gate_part, up_part)
     gate_grad, up_grad = gelu_back(hidden_grad)
-    gated_grad = jnp.concatenate([gate_grad, up_grad], axis=-1).astype(BF16)
-    gate_up_grad = dot(gated_grad, first_all, 0, 0).astype(BF16)
-    return gate_up_grad, down_grad, dot(gated_grad, gate_up, 1, 0)
+    return jnp.concatenate([gate_grad, up_grad], axis=-1).astype(BF16)
+
+
+def feed_weight_grads(mixed_all, first_all, gated_grad, hidden):
+    return dot(gated_grad, first_all, 0, 0).astype(BF16), dot(hidden, mixed_all, 0, 0).astype(BF16)
 
 
 def norm_backward(total, gain, offset, grad):
@@ -351,14 +355,10 @@
     return back(grad)
 
 
-def attn_backward(own_low, sum_grad, weights, projected, context, slopes, seqs):
-    wqkv, wo = weights
+def context_backward(sum_grad, weights, context):
     attended_low = sum_grad.astype(BF16)
-    context_grad = dot(attended_low, wo, 1, 1).astype(BF16)
-    out_grad = dot(context, attended_low, 0, 0).astype(BF16)
-    projected_grad = attend_back(projected, context_grad, slopes, seqs)
-    qkv_grad = dot(projected_grad, own_low, 0, 0).astype(BF16)
-    return projected_grad, qkv_grad, out_grad
+    context_grad = dot(attended_low, weights[1], 1, 1).astype(BF16)
+    return context_grad, dot(context, attended_low, 0, 0).astype(BF16)
 
 
 def body(
@@ -496,7 +496,8 @@
 
     def feed_terms(gate_up, down):
         full = jnp.concatenate([gate_up, down]).reshape(3, PLANE, DEPTH, unit_part, features)
-        return halves(jnp.transpose(full, (1, 2, 0, 3, 4)).reshape(PLANE, DEPTH, -1, features))
+        full = jnp.transpose(full, (1, 2, 0, 3, 4)).reshape(PLANE, DEPTH, -1, features)
+        return [full[e] for e in range(PLANE)]
 
     def attn_terms(qkv, out, vectors):
         spread = jnp.transpose(jnp.stack(vectors).reshape(4, DEPTH, local), (1, 0, 2)).reshape(DEPTH, features)
@@ -513,7 +514,8 @@
         spread = jnp.broadcast_to(spread[None, :, None], (PLANE, DEPTH, NORM_ROWS, features))
         full = full[:-NORM_ROWS].reshape(2, DEPTH, local_heads, PLANE, part, features)
         full = jnp.transpose(full, (3, 1, 0, 2, 4, 5)).reshape(PLANE, DEPTH, -1, features)
-        return halves(jnp.concatenate([full, spread], axis=2))
+        full = jnp.concatenate([full, spread], axis=2)
+        return [full[e] for e in range(PLANE)]
 
     def hand_over(block, source):
         planes, depths = lax.axis_size("dp"), lax.axis_size("tensor")
@@ -523,68 +525,114 @@
 
     second_grad, gain_two1, offset_two1 = norm_backward(total1, norms[1][2], norms[1][3], seed)
     mixed_all = both_rows(second_grad.astype(BF16))
-    gate_up, down, terms = feed_backward(mixed_all, all1, feed_p1, gated_p1, hidden_p1)
-    p1 = feed_terms(gate_up, down)
-    p1, terms, mixed_all = together(p1, terms, mixed_all)
-    p1 = reduce_second(p1)
-    gate_up, down, more = feed_backward(mixed_all, all1, feed_q1, gated_q1, hidden_q1)
-    q1 = feed_terms(gate_up, down)
-    terms = terms + more
-    terms, p1, q1 = together(terms, p1, q1)
-    p1, q1 = reduce_first(p1), reduce_second(q1)
+    grad_p = feed_backward(mixed_all, feed_p1, gated_p1)
+    p1 = feed_terms(*feed_weight_grads(mixed_all, all1, grad_p, hidden_p1))
+    mixed_all, grad_p, p1 = together(mixed_all, grad_p, p1)
+
+    p1_own, p1_half, p1_a, p1_b = reduce_open(p1)
+    terms = dot(grad_p, feed_p1[0], 1, 0)
+    grad_q = feed_backward(mixed_all, feed_q1, gated_q1)
+    terms = terms + dot(grad_q, feed_q1[0], 1, 0)
+    q1 = feed_terms(*feed_weight_grads(mixed_all, all1, grad_q, hidden_q1))
+    layer_out = give(middle_low, final_low)
+    terms, q1, p1_a, layer_out = together(terms, q1, p1_a, layer_out)
+
+    p1_own, p1_c = reduce_turn((p1_own, p1_half, p1_a))
     first_grad = join_rows(terms) + second_grad
     sum_grad, gain_one1, offset_one1 = norm_backward(sum1, norms[1][0], norms[1][1], first_grad)
-    projected_grad, qkv, out = attn_backward(middle_low, sum_grad, attn1, projected1, context1, slopes, seqs)
-    layer_out = give(middle_low, final_low)
-    projected_grad, qkv, out, p1, q1, layer_out = together(projected_grad, qkv, out, p1, q1, layer_out)
-    vectors = [gain_one1, offset_one1, gain_two1, offset_two1]
-    projected_grad, a1 = together(projected_grad, attn_terms(qkv, out, vectors))
-    a1, p1, q1 = reduce_second(attn_pieces(a1)), reduce_near(p1), reduce_first(q1)
+    context_grad, out = context_backward(sum_grad, attn1, context1)
+    context_grad, out, q1, p1_b = together(context_grad, out, q1, p1_b)
+
+    q1_own, q1_half, q1_a, q1_b = reduce_open(q1)
+    projected_grad = attend_back(projected1, context_grad, slopes, seqs)
+    qkv = dot(projected_grad, middle_low, 0, 0).astype(BF16)
+    projected_grad, qkv, q1_a, p1_c = together(projected_grad, qkv, q1_a, p1_c)
+
+    a1 = attn_terms(qkv, out, [gain_one1, offset_one1, gain_two1, offset_two1])
+    q1_own, q1_c = reduce_turn((q1_own, q1_half, q1_a))
+    p1 = reduce_near(p1_own, p1_c, p1_b)
     middle_grad = dot(projected_grad, attn1[0], 1, 0) + sum_grad
     second_grad, gain_two0, offset_two0 = norm_backward(total0, norms[0][2], norms[0][3], middle_grad)
-    mixed_all = both_rows(second_grad.astype(BF16))
-    gate_up, down, terms = feed_backward(mixed_all, all0, feed_p0, gated_p0, hidden_p0)
-    p0 = feed_terms(gate_up, down)
-    terms, mixed_all, a1, p1, q1, p0 = together(terms, mixed_all, a1, p1, q1, p0)
-    a1, p1, q1, p0 = reduce_first(a1), reduce_far(p1), reduce_near(q1), reduce_second(p0)
-    gate_up, down, more = feed_backward(mixed_all, all0, feed_q0, gated_q0, hidden_q0)
-    q0 = feed_terms(gate_up, down)
-    terms = terms + more
-    terms, a1, p1, q1, p0, q0 = together(terms, a1, p1, q1, p0, q0)
-    a1, q1, p0, q0 = reduce_near(a1), reduce_far(q1), reduce_first(p0), reduce_second(q0)
+    mixed_low = second_grad.astype(BF16)
+    mixed_low, a1, q1_b, p1 = together(mixed_low, a1, q1_b, p1)
+
+    mixed_all = both_rows(mixed_low)
+    a1_own, a1_half, a1_a, a1_b = reduce_open(attn_pieces(a1))
+    p1 = reduce_far(p1)
+    grad_p = feed_backward(mixed_all, feed_p0, gated_p0)
+    mixed_all, grad_p, a1_a, q1_c, p1 = together(mixed_all, grad_p, a1_a, q1_c, p1)
+
+    a1_own, a1_c = reduce_turn((a1_own, a1_half, a1_a))
+    q1 = reduce_near(q1_own, q1_c, q1_b)
+    p0 = feed_terms(*feed_weight_grads(mixed_all, all0, grad_p, hidden_p0))
+    terms = dot(grad_p, feed_p0[0], 1, 0)
+    mixed_all, terms, p0, a1_b, q1 = together(mixed_all, terms, p0, a1_b, q1)
+
+    p0_own, p0_half, p0_a, p0_b = reduce_open(p0)
+    q1 = reduce_far(q1)
+    grad_q = feed_backward(mixed_all, feed_q0, gated_q0)
+    terms = terms + dot(grad_q, feed_q0[0], 1, 0)
+    terms, grad_q, p0_a, a1_c, q1 = together(terms, grad_q, p0_a, a1_c, q1)
+
+    p0_own, p0_c = reduce_turn((p0_own, p0_half, p0_a))
+    a1 = reduce_near(a1_own, a1_c, a1_b)
+    q0 = feed_terms(*feed_weight_grads(mixed_all, all0, grad_q, hidden_q0))
     first_grad = join_rows(terms) + second_grad
     sum_grad, gain_one0, offset_one0 = norm_backward(sum0, norms[0][0], norms[0][1], first_grad)
-    projected_grad, qkv, out = attn_backward(start, sum_grad, attn0, projected0, context0, slopes, seqs)
-    projected_grad, qkv, out, a1, q1, p0, q0 = together(projected_grad, qkv, out, a1, q1, p0, q0)
+    sum_grad, q0, p0_b, a1 = together(sum_grad, q0, p0_b, a1)
+
+    q0_own, q0_half, q0_a, q0_b = reduce_open(q0)
+    a1 = reduce_far(a1)
+    context_grad, out = context_backward(sum_grad, attn0, context0)
+    projected_grad = attend_back(projected0, context_grad, slopes, seqs)
+    qkv = dot(projected_grad, start, 0, 0).astype(BF16)
+    projected_grad, qkv, out, q0_a, p0_c, a1 = together(projected_grad, qkv, out, q0_a, p0_c, a1)
+
     a0 = attn_terms(qkv, out, [gain_one0, offset_one0, gain_two0, offset_two0])
-    start_grad = dot(projected_grad, attn0[0], 1, 0) + sum_grad
-    q0 = reduce_first(q0)
-    start_grad, a0 = together(start_grad, a0)
-    a0, a1, p0 = reduce_second(attn_pieces(a0)), reduce_far(a1), reduce_near(p0)
-    input_grad = give(start_grad, middle_grad)
-    a0, a1, p0, q0, input_grad = together(a0, a1, p0, q0, input_grad)
+    q0_own, q0_c = reduce_turn((q0_own, q0_half, q0_a))
+    p0 = reduce_near(p0_own, p0_c, p0_b)
     attn_late = reduce_last(a1)
     late = jnp.concatenate([reduce_last(p1), reduce_last(q1), attn_late[:-NORM_ROWS]])
-    a0, p0, q0, late_first = reduce_first(a0), reduce_far(p0), reduce_near(q0), exchange(late, dp_masks=FIRST)
-    a0, p0, q0, late, late_first = together(a0, p0, q0, late, late_first)
-    a0, q0, late_second = reduce_near(a0), reduce_far(q0), exchange(late, dp_masks=SECOND)
-    late_got = [hand_over(late, 0), hand_over(late_first, 0)]
-    a0, late_second, late_first, p0, q0 = together(a0, late_second, late_first, p0, q0)
-    a0, late_third = reduce_far(a0), exchange(late_first, dp_masks=SECOND)
+    start_grad = dot(projected_grad, attn0[0], 1, 0) + sum_grad
+    start_grad, late, a0, q0_b, p0 = together(start_grad, late, a0, q0_b, p0)
+
+    a0_own, a0_half, a0_a, a0_b = reduce_open(attn_pieces(a0))
+    p0 = reduce_far(p0)
+    late_first = exchange(late, dp_masks=FIRST)
+    late_got = [hand_over(late, 0)]
+    a0_a, q0_c, p0, late_got = together(a0_a, q0_c, p0, late_got)
+
+    a0_own, a0_c = reduce_turn((a0_own, a0_half, a0_a))
+    q0 = reduce_near(q0_own, q0_c, q0_b)
+    late_second = exchange(late, dp_masks=SECOND)
+    input_grad = give(start_grad, middle_grad)
+    a0_b, q0, late_first, input_grad = together(a0_b, q0, late_first, input_grad)
+
+    q0 = reduce_far(q0)
+    late_got.append(hand_over(late_first, 0))
+    a0_c, q0, late_got = together(a0_c, q0, late_got)
+
+    a0 = reduce_near(a0_own, a0_c, a0_b)
+    late_third = exchange(late_first, dp_masks=SECOND)
     feed = jnp.concatenate([reduce_last(p0), reduce_last(q0)])
     feed_first = exchange(feed, dp_masks=FIRST)
+    a0, late_second, feed = together(a0, late_second, feed)
+
+    a0 = reduce_far(a0)
+    feed_second = exchange(feed, dp_masks=SECOND)
     late_got.append(hand_over(late_second, 0))
-    a0, late_third, feed, feed_first, late_got = together(a0, late_third, feed, feed_first, late_got)
+    feed_got = [hand_over(feed, 1)]
+    a0, feed_first, late_third, late_got, feed_got = together(a0, feed_first, late_third, late_got, feed_got)
+
     attn_early = reduce_last(a0)
     attn = attn_early[:-NORM_ROWS]
     attn_first, attn_second = exchange(attn, dp_masks=FIRST), exchange(attn, dp_masks=SECOND)
-    feed_second = exchange(feed, dp_masks=SECOND)
+    feed_third = exchange(feed_first, dp_masks=SECOND)
     late_got.append(hand_over(late_third, 0))
-    feed_got = [hand_over(feed, 1), hand_over(feed_first, 1)]
-    attn_first, attn_second, feed_second, feed_first, late_got, feed_got = together(
-        attn_first, attn_second, feed_second, feed_first, late_got, feed_got
-    )
-    attn_third, feed_third = exchange(attn_first, dp_masks=SECOND), exchange(feed_first, dp_masks=SECOND)
+    feed_got.append(hand_over(feed_first, 1))
+    attn_first, feed_second, late_got, feed_got = together(attn_first, feed_second, late_got, feed_got)
+
+    attn_third = exchange(attn_first, dp_masks=SECOND)
     feed_early = [feed, feed_first, feed_second, feed_third]
     feed_got = feed_got + [hand_over(feed_second, 1), hand_over(feed_third, 1)]
     attn_early_all = jnp.stack([attn, attn_first, attn_second, attn_third])

time: 574 us -> 565 us (0.984)
  waiting for transfers between devices: 175 us -> 190 us
  other arithmetic: 106 us -> 98.1 us
  starting transfers between devices: 92.3 us -> 84.6 us
    convert_element_type x0 -> x25, other arithmetic: none -> 16.2 us  [the longest x24 16.1 us: total_low(): return sum((part.astype(F32) for part in parts)).astype(BF16)]
    ppermute x81 -> x87, waiting for transfers between devices: 175 us -> 190 us  [exchange(): return lax.ppermute(block, AXES, pairs)]
    convert_element_type x26 -> x2, other arithmetic: 18 us -> 3.22 us  [add_low(): return (a.astype(F32) + b.astype(F32)).astype(BF16)]
    ppermute x9, starting transfers between devices: 24.5 us -> 16.8 us  [hand_over(): return lax.ppermute(block, AXES, pairs)]
    unnamed x354 -> x339, local copies, waits for them, and re-layouts: 22.5 us -> 25.1 us
    ppermute x81 -> x87, starting transfers between devices: 67.9 us -> 67.9 us  [exchange(): return lax.ppermute(block, AXES, pairs)]
  transfers between devices with their start and end apart: 90 -> 96, of which waited for: 34 -> 32; matrix products, arithmetic and copies ran while one was open for 34% -> 32% of each run, Pallas kernels for 4% -> 5%
where the time goes in v6:
time: 565 us; the launch traced here: 554 us
  waiting for transfers between devices  190 us (34%)
  other arithmetic  98.1 us (17%)
  starting transfers between devices  84.6 us (15%)
  local copies, waits for them, and re-layouts  74.5 us (13%)
  matrix products  63.6 us (11%)
  Pallas kernels  29.1 us (5%)
  between operations  14.4 us (3%)
    ppermute x87, waiting for transfers between devices, exchange(): return lax.ppermute(block, AXES, pairs)  190 us
    ppermute x87, starting transfers between devices, exchange(): return lax.ppermute(block, AXES, pairs)  67.9 us
    dot_general x36, matrix products, dot(): lax.dot_general(a, b, (((ca,), (cb,)), ((), ())), preferred_element_type=...  63.6 us
    unnamed x339, local copies, waits for them, and re-layouts  25.1 us
    convert_element_type x4, other arithmetic, feed_forward(): hidden = gelu_product(gate_part, up_part).astype(BF16)  24.3 us
    ppermute x9, starting transfers between devices, hand_over(): return lax.ppermute(block, AXES, pairs)  16.8 us
    convert_element_type x24, other arithmetic, total_low(): return sum((part.astype(F32) for part in parts)).astype(BF16)  16.1 us
    another operation x18, other arithmetic, assemble(): jnp.stack([jnp.concatenate([own[None], r]) for own, r in zip(chunk['own']...  13.1 us
  transfers between devices with their start and end apart: 96, of which 32 were waited for; matrix products, arithmetic and copies ran while one was open for 32% of the time, Pallas kernels for 5%

profile of v6, /device:TPU:1, one launch (start us, length us, event | category | flops | bytes accessed | tf_op | source)
XLA Modules:
  0.0 554.5 jit_solution(15733098796465656431)
XLA Ops:
  13.5 5.6 %copy.69 = bf16[1,768,2,768]{1,3,2,0:T(8,128)(2,1)S(1)} copy(bf16[1,768,2,768]{3,2,1,0:T(2,128)(2,1)} %param.19) | data formatting | bytes 4718592 | tf_op jit(solution)/shard_map/optimization_barrier | solution.py:244
  28.4 9.8 %collective-permute-done.3 = bf16[2,96,768]{2,1,0:T(8,128)(2,1)S(1)} collective-permute-done((bf16[2,96,768]{2,1,0:T(8,128)(2,1)S(1)}, bf16[2,96,768]{2,1,0:T(8,128)(2,1)S(1)}, u32[]{:S(2)}, u32[]{:S(2)}) %collective-permute-start.3) | collective-permute-done | bytes 294944 | tf_op jit(solution)/shard_map/ppermute | solution.py:61
  40.8 4.3 collective-permute-start.10
  45.2 6.4 %collective-permute-done.10 = bf16[144,768]{1,0:T(8,128)(2,1)S(1)} collective-permute-done((bf16[144,768]{1,0:T(8,128)(2,1)S(1)}, bf16[144,768]{1,0:T(8,128)(2,1)S(1)}, u32[]{:S(2)}, u32[]{:S(2)}) %collective-permute-start.10) | collective-permute-done | bytes 221216 | tf_op jit(solution)/shard_map/ppermute | solution.py:61
  51.6 7.6 %collective-permute-done.9 = bf16[2,144,768]{2,1,0:T(8,128)(2,1)S(1)} collective-permute-done((bf16[2,144,768]{2,1,0:T(8,128)(2,1)S(1)}, bf16[2,144,768]{2,1,0:T(8,128)(2,1)S(1)}, u32[]{:S(2)}, u32[]{:S(2)}) %collective-permute-start.9) | collective-permute-done | bytes 442400 | tf_op jit(solution)/shard_map/ppermute | solution.py:61
  65.8 6.2 %collective-permute-done.15 = bf16[96,768]{1,0:T(8,128)(2,1)S(1)} collective-permute-done((bf16[96,768]{1,0:T(8,128)(2,1)S(1)}, bf16[96,768]{1,0:T(8,128)(2,1)S(1)}, u32[]{:S(2)}, u32[]{:S(2)}) %collective-permute-start.15) | collective-permute-done | bytes 147488 | tf_op jit(solution)/shard_map/ppermute | solution.py:61
  72.0 12.0 %collective-permute-done.14 = bf16[2,144,768]{2,1,0:T(8,128)(2,1)S(1)} collective-permute-done((bf16[2,144,768]{2,1,0:T(8,128)(2,1)S(1)}, bf16[2,144,768]{2,1,0:T(8,128)(2,1)S(1)}, u32[]{:S(2)}, u32[]{:S(2)}) %collective-permute-start.14) | collective-permute-done | bytes 442400 | tf_op jit(solution)/shard_map/ppermute | solution.py:61
  103.9 4.9 attend.2
  111.4 5.6 %collective-permute-done.17 = bf16[3,144,768]{2,1,0:T(8,128)(2,1)} collective-permute-done((bf16[3,144,768]{2,1,0:T(8,128)(2,1)}, bf16[3,144,768]{2,1,0:T(8,128)(2,1)}, u32[]{:S(2)}, u32[]{:S(2)}) %collective-permute-start.17) | collective-permute-done | bytes 663584 | tf_op jit(solution)/shard_map/ppermute | solution.py:61
  129.5 6.2 %multiply_convert_fusion.7 = (bf16[768,768]{1,0:T(8,128)(2,1)S(1)}, f32[768,768]{1,0:T(8,128)}) fusion(f32[768,1536]{1,0:T(8,128)S(1)} %fusion.134), kind=kLoop, calls=%fused_computation.108 | loop fusion | flops 38928384 | bytes 8257536 | tf_op jit(solution)/shard_map/convert_element_type | solution.py:337
  139.3 6.6 %collective-permute-done.26 = bf16[2,144,768]{2,1,0:T(8,128)(2,1)S(1)} collective-permute-done((bf16[2,144,768]{2,1,0:T(8,128)(2,1)S(1)}, bf16[2,144,768]{2,1,0:T(8,128)(2,1)S(1)}, u32[]{:S(2)}, u32[]{:S(2)}) %collective-permute-start.26) | collective-permute-done | bytes 442400 | tf_op jit(solution)/shard_map/ppermute | solution.py:61
  155.3 6.0 %multiply_convert_fusion.6 = (bf16[768,768]{1,0:T(8,128)(2,1)S(1)}, f32[768,768]{1,0:T(8,128)}) fusion(f32[768,1536]{1,0:T(8,128)S(1)} %fusion.136), kind=kLoop, calls=%fused_computation.95 | loop fusion | flops 38928384 | bytes 8257536 | tf_op jit(solution)/shard_map/convert_element_type | solution.py:337
  164.1 7.7 %collective-permute-done.31 = bf16[2,144,768]{2,1,0:T(8,128)(2,1)S(1)} collective-permute-done((bf16[2,144,768]{2,1,0:T(8,128)(2,1)S(1)}, bf16[2,144,768]{2,1,0:T(8,128)(2,1)S(1)}, u32[]{:S(2)}, u32[]{:S(2)}) %collective-permute-start.31) | collective-permute-done | bytes 442400 | tf_op jit(solution)/shard_map/ppermute | solution.py:61
  185.0 5.1 attend.3
  193.0 5.6 %collective-permute-done.34 = bf16[3,144,768]{2,1,0:T(8,128)(2,1)} collective-permute-done((bf16[3,144,768]{2,1,0:T(8,128)(2,1)}, bf16[3,144,768]{2,1,0:T(8,128)(2,1)}, u32[]{:S(2)}, u32[]{:S(2)}) %collective-permute-start.34) | collective-permute-done | bytes 663584 | tf_op jit(solution)/shard_map/ppermute | solution.py:61
  206.0 6.0 %multiply_convert_fusion.5 = (bf16[768,768]{1,0:T(8,128)(2,1)S(1)}, f32[768,768]{1,0:T(8,128)}) fusion(f32[768,1536]{1,0:T(8,128)S(1)} %fusion.138), kind=kLoop, calls=%fused_computation.82 | loop fusion | flops 38928384 | bytes 8257536 | tf_op jit(solution)/shard_map/convert_element_type | solution.py:337
  219.3 6.1 %multiply_convert_fusion.4 = (bf16[768,768]{1,0:T(8,128)(2,1)S(1)}, f32[768,768]{1,0:T(8,128)}) fusion(f32[768,1536]{1,0:T(8,128)S(1)} %fusion.140), kind=kLoop, calls=%fused_computation.69 | loop fusion | flops 38928384 | bytes 8257536 | tf_op jit(solution)/shard_map/convert_element_type | solution.py:337
  277.2 11.3 %collective-permute-done.44 = bf16[4,144,768]{2,1,0:T(8,128)(2,1)} collective-permute-done((bf16[4,144,768]{2,1,0:T(8,128)(2,1)S(1)}, bf16[4,144,768]{2,1,0:T(8,128)(2,1)}, u32[]{:S(2)}, u32[]{:S(2)}) %collective-permute-start.44) | collective-permute-done | bytes 884768 | tf_op jit(solution)/shard_map/ppermute | solution.py:61
  304.2 5.7 %attend_back.2 = bf16[384,2304]{1,0:T(8,128)(2,1)} custom-call(f32[12]{0:T(128)} %pad_maximum_fusion.53.slopes_ref, bf16[384,2304]{1,0:T(8,128)(2,1)} %convolution_convert_fusion.2.projected_ref, bf16[384,768]{1,0:T(8,128)(2,1)} %convolution_convert_fusion.15.context_grad_ref), custom_call_target="tpu_custom_call" | custom-call | flops 377487360 | bytes 4128768 | tf_op jit(solution)/shard_map/attend_back/pallas_call | solution.py:181
  331.7 3.7 collective-permute-done.49
  347.9 5.3 collective-permute-done.53
  397.8 5.7 %attend_back.3 = bf16[384,2304]{1,0:T(8,128)(2,1)} custom-call(f32[12]{0:T(128)} %pad_maximum_fusion.53.slopes_ref, bf16[384,2304]{1,0:T(8,128)(2,1)} %convolution_convert_fusion.3.projected_ref, bf16[384,768]{1,0:T(8,128)(2,1)} %convolution_convert_fusion.14.context_grad_ref), custom_call_target="tpu_custom_call" | custom-call | flops 377487360 | bytes 4128768 | tf_op jit(solution)/shard_map/attend_back/pallas_call | solution.py:181
  407.8 4.1 collective-permute-done.62
  422.6 8.7 %collective-permute-done.66 = bf16[4,144,768]{2,1,0:T(8,128)(2,1)S(1)} collective-permute-done((bf16[4,144,768]{2,1,0:T(8,128)(2,1)S(1)}, bf16[4,144,768]{2,1,0:T(8,128)(2,1)S(1)}, u32[]{:S(2)}, u32[]{:S(2)}) %collective-permute-start.66) | collective-permute-done | bytes 884768 | tf_op jit(solution)/shard_map/ppermute | solution.py:61
  435.9 4.6 collective-permute-start.75
  442.9 10.1 %collective-permute-done.71 = bf16[144,768]{1,0:T(8,128)(2,1)S(1)} collective-permute-done((bf16[144,768]{1,0:T(8,128)(2,1)S(1)}, bf16[144,768]{1,0:T(8,128)(2,1)S(1)}, u32[]{:S(2)}, u32[]{:S(2)}) %collective-permute-start.71) | collective-permute-done | bytes 221216 | tf_op jit(solution)/shard_map/ppermute | solution.py:61
  457.2 19.6 %collective-permute-done.68 = bf16[4,112,768]{2,1,0:T(8,128)(2,1)S(1)} collective-permute-done((bf16[4,112,768]{2,1,0:T(8,128)(2,1)S(1)}, bf16[4,112,768]{2,1,0:T(8,128)(2,1)S(1)}, u32[]{:S(2)}, u32[]{:S(2)}) %collective-permute-start.68) | collective-permute-done | bytes 688160 | tf_op jit(solution)/shard_map/ppermute | solution.py:61
  479.3 11.1 %collective-permute-done.77 = bf16[144,768]{1,0:T(8,128)(2,1)S(1)} collective-permute-done((bf16[144,768]{1,0:T(8,128)(2,1)S(1)}, bf16[144,768]{1,0:T(8,128)(2,1)S(1)}, u32[]{:S(2)}, u32[]{:S(2)}) %collective-permute-start.77) | collective-permute-done | bytes 221216 | tf_op jit(solution)/shard_map/ppermute | solution.py:61
  491.0 8.9 %collective-permute-done.79 = bf16[2,112,768]{2,1,0:T(8,128)(2,1)S(1)} collective-permute-done((bf16[2,112,768]{2,1,0:T(8,128)(2,1)S(1)}, bf16[2,112,768]{2,1,0:T(8,128)(2,1)S(1)}, u32[]{:S(2)}, u32[]{:S(2)}) %collective-permute-start.79) | collective-permute-done | bytes 344096 | tf_op jit(solution)/shard_map/ppermute | solution.py:61
  506.4 9.1 %collective-permute-done.81 = bf16[112,768]{1,0:T(8,128)(2,1)S(1)} collective-permute-done((bf16[112,768]{1,0:T(8,128)(2,1)S(1)}, bf16[112,768]{1,0:T(8,128)(2,1)S(1)}, u32[]{:S(2)}, u32[]{:S(2)}) %collective-permute-start.81) | collective-permute-done | bytes 172064 | tf_op jit(solution)/shard_map/ppermute | solution.py:61
  521.6 4.3 collective-permute-done.86
  543.7 7.7 %settle.1 = (f32[768,2,768]{2,1,0:T(2,128)}, f32[768,768]{1,0:T(8,128)}) custom-call(s32[9]{0:T(128)} %pad_add_fusion.flags_ref, bf16[288,768]{1,0:T(8,128)(2,1)} %copy-done.44, bf16[288,768]{1,0:T(8,128)(2,1)} %copy-done.105, bf16[288,768]{1,0:T(8,128)(2,1)} %copy-done.107, bf16[288,768]{1,0:T(8,128)(2,1)} %copy-done.109, bf16[288,768]{1,0:T(8,128)(2,1)} %copy-done.106, ...), custom_call_target="tpu_custom_call" | custom-call | tf_op jit(solution)/shard_map/settle/pallas_call | solution.py:225
  (807 shorter events, 308.7 us)
Async XLA Ops:
  38.2 21.0 %collective-permute-start.9 = (bf16[2,144,768]{2,1,0:T(8,128)(2,1)S(1)}, bf16[2,144,768]{2,1,0:T(8,128)(2,1)S(1)}, u32[]{:S(2)}, u32[]{:S(2)}) collective-permute-start(bf16[2,144,768]{2,1,0:T(8,128)(2,1)S(1)} %pad_maximum_fusion.40), channel_id=1, source_target_pairs={{0,2},{1,3},{2,0},{3,1},{4,6},{5,7},{6,4},{7,5},{8,10},{9,11},{10,... | collective-permute-start | bytes 1327112 | tf_op jit(solution)/shard_map/ppermute | solution.py:61
  38.4 20.8 %collective-permute-start.7 = (bf16[3,96,768]{2,1,0:T(8,128)(2,1)S(1)}, bf16[3,96,768]{2,1,0:T(8,128)(2,1)S(1)}, u32[]{:S(2)}, u32[]{:S(2)}) collective-permute-start(bf16[3,96,768]{2,1,0:T(8,128)(2,1)S(1)} %pad_maximum_fusion.39), channel_id=1, source_target_pairs={{0,4},{1,5},{2,6},{3,7},{4,0},{5,1},{6,2},{7,3},{8,12},{9,13},{10,... | collective-permute-start | bytes 1327112 | tf_op jit(solution)/shard_map/ppermute | solution.py:61
  39.6 19.5 %collective-permute-start.8 = (bf16[3,96,768]{2,1,0:T(8,128)(2,1)S(1)}, bf16[3,96,768]{2,1,0:T(8,128)(2,1)S(1)}, u32[]{:S(2)}, u32[]{:S(2)}) collective-permute-start(bf16[3,96,768]{2,1,0:T(8,128)(2,1)S(1)} %pad_maximum_fusion.39), channel_id=1, source_target_pairs={{0,8},{1,9},{2,10},{3,11},{4,12},{5,13},{6,14},{7,15},{8,0},{9,1},... | collective-permute-start | bytes 1327112 | tf_op jit(solution)/shard_map/ppermute | solution.py:61
  59.2 24.7 %collective-permute-start.12 = (bf16[3,144,768]{2,1,0:T(8,128)(2,1)S(1)}, bf16[3,144,768]{2,1,0:T(8,128)(2,1)}, u32[]{:S(2)}, u32[]{:S(2)}) collective-permute-start(bf16[3,144,768]{2,1,0:T(8,128)(2,1)S(1)} %pad_maximum_fusion.33), channel_id=1, source_target_pairs={{0,4},{1,5},{2,6},{3,7},{4,0},{5,1},{6,2},{7,3},{8,12},{9,13},{10,... | collective-permute-start | bytes 1990664 | tf_op jit(solution)/shard_map/ppermute | solution.py:61
  60.4 23.6 %collective-permute-start.13 = (bf16[3,144,768]{2,1,0:T(8,128)(2,1)S(1)}, bf16[3,144,768]{2,1,0:T(8,128)(2,1)S(1)}, u32[]{:S(2)}, u32[]{:S(2)}) collective-permute-start(bf16[3,144,768]{2,1,0:T(8,128)(2,1)S(1)} %pad_maximum_fusion.33), channel_id=1, source_target_pairs={{0,8},{1,9},{2,10},{3,11},{4,12},{5,13},{6,14},{7,15},{8,0},{9,1},... | collective-permute-start | bytes 1990664 | tf_op jit(solution)/shard_map/ppermute | solution.py:61
  61.6 22.3 %collective-permute-start.14 = (bf16[2,144,768]{2,1,0:T(8,128)(2,1)S(1)}, bf16[2,144,768]{2,1,0:T(8,128)(2,1)S(1)}, u32[]{:S(2)}, u32[]{:S(2)}) collective-permute-start(bf16[2,144,768]{2,1,0:T(8,128)(2,1)S(1)} %pad_maximum_fusion.41), channel_id=1, source_target_pairs={{0,2},{1,3},{2,0},{3,1},{4,6},{5,7},{6,4},{7,5},{8,10},{9,11},{10,... | collective-permute-start | bytes 1327112 | tf_op jit(solution)/shard_map/ppermute | solution.py:61
  61.7 22.2 %collective-permute-start.11 = (bf16[3,96,768]{2,1,0:T(8,128)(2,1)S(1)}, bf16[3,96,768]{2,1,0:T(8,128)(2,1)S(1)}, u32[]{:S(2)}, u32[]{:S(2)}) collective-permute-start(bf16[3,96,768]{2,1,0:T(8,128)(2,1)S(1)} %collective-permute-done.7), channel_id=1, source_target_pairs={{0,8},{1,9},{2,10},{3,11},{4,12},{5,13},{6,14},{7,15},{8,0},{9,1},... | collective-permute-start | bytes 1327112 | tf_op jit(solution)/shard_map/ppermute | solution.py:61
  94.3 22.7 %collective-permute-start.17 = (bf16[3,144,768]{2,1,0:T(8,128)(2,1)}, bf16[3,144,768]{2,1,0:T(8,128)(2,1)}, u32[]{:S(2)}, u32[]{:S(2)}) collective-permute-start(bf16[3,144,768]{2,1,0:T(8,128)(2,1)} %collective-permute-done.12), channel_id=1, source_target_pairs={{0,8},{1,9},{2,10},{3,11},{4,12},{5,13},{6,14},{7,15},{8,0},{9,1},... | collective-permute-start | bytes 1990664 | tf_op jit(solution)/shard_map/ppermute | solution.py:61
  118.1 27.8 %collective-permute-start.24 = (bf16[3,96,768]{2,1,0:T(8,128)(2,1)S(1)}, bf16[3,96,768]{2,1,0:T(8,128)(2,1)S(1)}, u32[]{:S(2)}, u32[]{:S(2)}) collective-permute-start(bf16[3,96,768]{2,1,0:T(8,128)(2,1)S(1)} %pad_maximum_fusion.42), channel_id=1, source_target_pairs={{0,4},{1,5},{2,6},{3,7},{4,0},{5,1},{6,2},{7,3},{8,12},{9,13},{10,... | collective-permute-start | bytes 1327112 | tf_op jit(solution)/shard_map/ppermute | solution.py:61
  118.9 27.0 %collective-permute-start.25 = (bf16[3,96,768]{2,1,0:T(8,128)(2,1)S(1)}, bf16[3,96,768]{2,1,0:T(8,128)(2,1)S(1)}, u32[]{:S(2)}, u32[]{:S(2)}) collective-permute-start(bf16[3,96,768]{2,1,0:T(8,128)(2,1)S(1)} %pad_maximum_fusion.42), channel_id=1, source_target_pairs={{0,8},{1,9},{2,10},{3,11},{4,12},{5,13},{6,14},{7,15},{8,0},{9,1},... | collective-permute-start | bytes 1327112 | tf_op jit(solution)/shard_map/ppermute | solution.py:61
  124.8 21.1 %collective-permute-start.26 = (bf16[2,144,768]{2,1,0:T(8,128)(2,1)S(1)}, bf16[2,144,768]{2,1,0:T(8,128)(2,1)S(1)}, u32[]{:S(2)}, u32[]{:S(2)}) collective-permute-start(bf16[2,144,768]{2,1,0:T(8,128)(2,1)S(1)} %pad_maximum_fusion.43), channel_id=1, source_target_pairs={{0,2},{1,3},{2,0},{3,1},{4,6},{5,7},{6,4},{7,5},{8,10},{9,11},{10,... | collective-permute-start | bytes 1327112 | tf_op jit(solution)/shard_map/ppermute | solution.py:61
  125.0 20.9 %collective-permute-start.23 = (bf16[3,144,768]{2,1,0:T(8,128)(2,1)}, bf16[3,144,768]{2,1,0:T(8,128)(2,1)S(1)}, u32[]{:S(2)}, u32[]{:S(2)}) collective-permute-start(bf16[3,144,768]{2,1,0:T(8,128)(2,1)} %collective-permute-done.18), channel_id=1, source_target_pairs={{0,8},{1,9},{2,10},{3,11},{4,12},{5,13},{6,14},{7,15},{8,0},{9,1},... | collective-permute-start | bytes 1990664 | tf_op jit(solution)/shard_map/ppermute | solution.py:61
  146.9 24.9 %collective-permute-start.29 = (bf16[3,144,768]{2,1,0:T(8,128)(2,1)S(1)}, bf16[3,144,768]{2,1,0:T(8,128)(2,1)}, u32[]{:S(2)}, u32[]{:S(2)}) collective-permute-start(bf16[3,144,768]{2,1,0:T(8,128)(2,1)S(1)} %pad_maximum_fusion.35), channel_id=1, source_target_pairs={{0,4},{1,5},{2,6},{3,7},{4,0},{5,1},{6,2},{7,3},{8,12},{9,13},{10,... | collective-permute-start | bytes 1990664 | tf_op jit(solution)/shard_map/ppermute | solution.py:61
  148.1 23.8 %collective-permute-start.30 = (bf16[3,144,768]{2,1,0:T(8,128)(2,1)S(1)}, bf16[3,144,768]{2,1,0:T(8,128)(2,1)S(1)}, u32[]{:S(2)}, u32[]{:S(2)}) collective-permute-start(bf16[3,144,768]{2,1,0:T(8,128)(2,1)S(1)} %pad_maximum_fusion.35), channel_id=1, source_target_pairs={{0,8},{1,9},{2,10},{3,11},{4,12},{5,13},{6,14},{7,15},{8,0},{9,1},... | collective-permute-start | bytes 1990664 | tf_op jit(solution)/shard_map/ppermute | solution.py:61
  149.3 22.5 %collective-permute-start.31 = (bf16[2,144,768]{2,1,0:T(8,128)(2,1)S(1)}, bf16[2,144,768]{2,1,0:T(8,128)(2,1)S(1)}, u32[]{:S(2)}, u32[]{:S(2)}) collective-permute-start(bf16[2,144,768]{2,1,0:T(8,128)(2,1)S(1)} %pad_maximum_fusion.44), channel_id=1, source_target_pairs={{0,2},{1,3},{2,0},{3,1},{4,6},{5,7},{6,4},{7,5},{8,10},{9,11},{10,... | collective-permute-start | bytes 1327112 | tf_op jit(solution)/shard_map/ppermute | solution.py:61
  175.1 23.5 %collective-permute-start.34 = (bf16[3,144,768]{2,1,0:T(8,128)(2,1)}, bf16[3,144,768]{2,1,0:T(8,128)(2,1)}, u32[]{:S(2)}, u32[]{:S(2)}) collective-permute-start(bf16[3,144,768]{2,1,0:T(8,128)(2,1)} %collective-permute-done.29), channel_id=1, source_target_pairs={{0,8},{1,9},{2,10},{3,11},{4,12},{5,13},{6,14},{7,15},{8,0},{9,1},... | collective-permute-start | bytes 1990664 | tf_op jit(solution)/shard_map/ppermute | solution.py:61
  238.3 21.5 %collective-permute-start.42 = (bf16[384,768]{1,0:T(8,128)(2,1)S(1)}, bf16[384,768]{1,0:T(8,128)(2,1)S(1)}, u32[]{:S(2)}, u32[]{:S(2)}) collective-permute-start(bf16[384,768]{1,0:T(8,128)(2,1)S(1)} %get-tuple-element.654), channel_id=1, source_target_pairs={{0,16},{1,17},{2,18},{3,19},{4,20},{5,21},{6,22},{7,23},{8,24},{9,... | collective-permute-start | bytes 1769480 | tf_op jit(solution)/shard_map/ppermute | solution.py:61
  271.3 42.3 %collective-permute-start.46 = (bf16[4,144,768]{2,1,0:T(8,128)(2,1)}, bf16[4,144,768]{2,1,0:T(8,128)(2,1)}, u32[]{:S(2)}, u32[]{:S(2)}) collective-permute-start(bf16[4,144,768]{2,1,0:T(8,128)(2,1)} %add_convert_fusion.13), channel_id=1, source_target_pairs={{0,4},{1,5},{2,6},{3,7},{4,0},{5,1},{6,2},{7,3},{8,12},{9,13},{10,... | collective-permute-start | bytes 2654216 | tf_op jit(solution)/shard_map/ppermute | solution.py:61
  288.5 25.1 %collective-permute-start.45 = (bf16[4,144,768]{2,1,0:T(8,128)(2,1)}, bf16[4,144,768]{2,1,0:T(8,128)(2,1)}, u32[]{:S(2)}, u32[]{:S(2)}) collective-permute-start(bf16[4,144,768]{2,1,0:T(8,128)(2,1)} %bitcast.161), channel_id=1, source_target_pairs={{0,8},{1,9},{2,10},{3,11},{4,12},{5,13},{6,14},{7,15},{8,0},{9,1},... | collective-permute-start | bytes 2654216 | tf_op jit(solution)/shard_map/ppermute | solution.py:61
  303.0 28.7 %collective-permute-start.48 = (bf16[4,144,768]{2,1,0:T(8,128)(2,1)}, bf16[4,144,768]{2,1,0:T(8,128)(2,1)}, u32[]{:S(2)}, u32[]{:S(2)}) collective-permute-start(bf16[4,144,768]{2,1,0:T(8,128)(2,1)} %bitcast.596), channel_id=1, source_target_pairs={{0,8},{1,9},{2,10},{3,11},{4,12},{5,13},{6,14},{7,15},{8,0},{9,1},... | collective-permute-start | bytes 2654216 | tf_op jit(solution)/shard_map/ppermute | solution.py:61
  328.7 19.2 %collective-permute-start.52 = (bf16[4,144,768]{2,1,0:T(8,128)(2,1)}, bf16[4,144,768]{2,1,0:T(8,128)(2,1)S(1)}, u32[]{:S(2)}, u32[]{:S(2)}) collective-permute-start(bf16[4,144,768]{2,1,0:T(8,128)(2,1)} %add_convert_fusion.11), channel_id=1, source_target_pairs={{0,4},{1,5},{2,6},{3,7},{4,0},{5,1},{6,2},{7,3},{8,12},{9,13},{10,... | collective-permute-start | bytes 2654216 | tf_op jit(solution)/shard_map/ppermute | solution.py:61
  341.4 23.2 %collective-permute-start.54 = (bf16[4,112,768]{2,1,0:T(8,128)(2,1)S(1)}, bf16[4,112,768]{2,1,0:T(8,128)(2,1)S(1)}, u32[]{:S(2)}, u32[]{:S(2)}) collective-permute-start(bf16[4,112,768]{2,1,0:T(8,128)(2,1)S(1)} %get-tuple-element.708), channel_id=1, source_target_pairs={{0,8},{1,9},{2,10},{3,11},{4,12},{5,13},{6,14},{7,15},{8,0},{9,1},... | collective-permute-start | bytes 2064392 | tf_op jit(solution)/shard_map/ppermute | solution.py:61
  360.9 19.9 %collective-permute-start.57 = (bf16[4,112,768]{2,1,0:T(8,128)(2,1)S(1)}, bf16[4,112,768]{2,1,0:T(8,128)(2,1)S(1)}, u32[]{:S(2)}, u32[]{:S(2)}) collective-permute-start(bf16[4,112,768]{2,1,0:T(8,128)(2,1)S(1)} %fusion.35), channel_id=1, source_target_pairs={{0,4},{1,5},{2,6},{3,7},{4,0},{5,1},{6,2},{7,3},{8,12},{9,13},{10,... | collective-permute-start | bytes 2064392 | tf_op jit(solution)/shard_map/ppermute | solution.py:61
  369.1 24.7 %collective-permute-start.60 = (bf16[4,144,768]{2,1,0:T(8,128)(2,1)S(1)}, bf16[4,144,768]{2,1,0:T(8,128)(2,1)S(1)}, u32[]{:S(2)}, u32[]{:S(2)}) collective-permute-start(bf16[4,144,768]{2,1,0:T(8,128)(2,1)S(1)} %bitcast.598), channel_id=1, source_target_pairs={{0,8},{1,9},{2,10},{3,11},{4,12},{5,13},{6,14},{7,15},{8,0},{9,1},... | collective-permute-start | bytes 2654216 | tf_op jit(solution)/shard_map/ppermute | solution.py:61
  420.2 21.6 %collective-permute-start.70 = (bf16[4,144,768]{2,1,0:T(8,128)(2,1)S(1)}, bf16[4,144,768]{2,1,0:T(8,128)(2,1)S(1)}, u32[]{:S(2)}, u32[]{:S(2)}) collective-permute-start(bf16[4,144,768]{2,1,0:T(8,128)(2,1)S(1)} %add_convert_fusion.7), channel_id=1, source_target_pairs={{0,4},{1,5},{2,6},{3,7},{4,0},{5,1},{6,2},{7,3},{8,12},{9,13},{10,... | collective-permute-start | bytes 2654216 | tf_op jit(solution)/shard_map/ppermute | solution.py:61
  434.3 20.2 %collective-permute-start.69 = (bf16[4,112,768]{2,1,0:T(8,128)(2,1)S(1)}, bf16[4,112,768]{2,1,0:T(8,128)(2,1)S(1)}, u32[]{:S(2)}, u32[]{:S(2)}) collective-permute-start(bf16[4,112,768]{2,1,0:T(8,128)(2,1)S(1)} %get-tuple-element.706), channel_id=1, source_target_pairs={{0,8},{1,9},{2,10},{3,11},{4,12},{5,13},{6,14},{7,15},{8,0},{9,1},... | collective-permute-start | bytes 2064392 | tf_op jit(solution)/shard_map/ppermute | solution.py:61
  453.0 38.0 %collective-permute-start.80 = (bf16[384,768]{1,0:T(8,128)(2,1)S(1)}, bf16[384,768]{1,0:T(8,128)(2,1)S(1)}, u32[]{:S(2)}, u32[]{:S(2)}) collective-permute-start(bf16[384,768]{1,0:T(8,128)(2,1)S(1)} %pad_maximum_fusion.37), channel_id=1, source_target_pairs={{0,8},{1,9},{2,10},{3,11},{4,12},{5,13},{6,14},{7,15},{8,0},{9,1},... | collective-permute-start | bytes 1769480 | tf_op jit(solution)/shard_map/ppermute | solution.py:61
  453.0 23.8 %collective-permute-start.68 = (bf16[4,112,768]{2,1,0:T(8,128)(2,1)S(1)}, bf16[4,112,768]{2,1,0:T(8,128)(2,1)S(1)}, u32[]{:S(2)}, u32[]{:S(2)}) collective-permute-start(bf16[4,112,768]{2,1,0:T(8,128)(2,1)S(1)} %get-tuple-element.707), channel_id=1, source_target_pairs={{0,8},{1,9},{2,10},{3,11},{4,12},{5,13},{6,14},{7,15},{8,0},{9,1},... | collective-permute-start | bytes 2064392 | tf_op jit(solution)/shard_map/ppermute | solution.py:61
  454.9 21.9 %collective-permute-start.73 = (bf16[2,144,768]{2,1,0:T(8,128)(2,1)S(1)}, bf16[2,144,768]{2,1,0:T(8,128)(2,1)S(1)}, u32[]{:S(2)}, u32[]{:S(2)}) collective-permute-start(bf16[2,144,768]{2,1,0:T(8,128)(2,1)S(1)} %get-tuple-element.718), channel_id=1, source_target_pairs={{0,1},{1,0},{2,3},{3,2},{4,5},{5,4},{6,7},{7,6},{8,9},{9,8},{10,11... | collective-permute-start | bytes 1327112 | tf_op jit(solution)/shard_map/ppermute | solution.py:61
  455.1 24.2 %collective-permute-start.76 = (bf16[4,112,768]{2,1,0:T(8,128)(2,1)S(1)}, bf16[4,112,768]{2,1,0:T(8,128)(2,1)S(1)}, u32[]{:S(2)}, u32[]{:S(2)}) collective-permute-start(bf16[4,112,768]{2,1,0:T(8,128)(2,1)S(1)} %fusion.30), channel_id=1, source_target_pairs={{0,4},{1,5},{2,6},{3,7},{4,0},{5,1},{6,2},{7,3},{8,12},{9,13},{10,... | collective-permute-start | bytes 2064392 | tf_op jit(solution)/shard_map/ppermute | solution.py:61
  478.4 28.0 %collective-permute-start.83 = (bf16[384,768]{1,0:T(8,128)(2,1)S(1)}, bf16[384,768]{1,0:T(8,128)(2,1)S(1)}, u32[]{:S(2)}, u32[]{:S(2)}) collective-permute-start(bf16[384,768]{1,0:T(8,128)(2,1)S(1)} %collective-permute-done.74), channel_id=1, source_target_pairs={{0,8},{1,9},{2,10},{3,11},{4,12},{5,13},{6,14},{7,15},{8,0},{9,1},... | collective-permute-start | bytes 1769480 | tf_op jit(solution)/shard_map/ppermute | solution.py:61
  532.2 19.2 %collective-permute-start.92 = (bf16[4,96,768]{2,1,0:T(8,128)(2,1)S(1)}, bf16[4,96,768]{2,1,0:T(8,128)(2,1)S(1)}, u32[]{:S(2)}, u32[]{:S(2)}) collective-permute-start(bf16[4,96,768]{2,1,0:T(8,128)(2,1)S(1)} %get-tuple-element.755), channel_id=1, source_target_pairs={{16,0},{17,1},{18,2},{19,3},{20,4},{21,5},{22,6},{23,7},{24,8},{25... | collective-permute-start | bytes 1769480 | tf_op jit(solution)/shard_map/ppermute | solution.py:524
  (234 other events, 2239.5 us)

commit v7 on v6

--- a/solution.py
+++ b/solution.py
@@ -244,31 +244,40 @@
     return lax.optimization_barrier(trees)
 
 
-def near(chunk):
-    return dict(chunk, near=exchange(chunk["own"][0], tensor_mask=1))
-
-
-def far(chunk):
-    return dict(chunk, far=exchange(jnp.stack([chunk["own"][0], chunk["near"]]), tensor_mask=2))
-
-
 def first(chunk):
-    remote = jnp.concatenate([chunk["near"][None], chunk["far"]])
+    depth, every = lax.axis_index("tensor"), chunk["every"]
+    remote = jnp.stack([jnp.where(j < depth, every[j], every[j + 1]) for j in range(DEPTH - 1)])
     return dict(
         chunk,
-        remote=remote,
         first=exchange(remote, dp_masks=FIRST),
         second=exchange(remote, dp_masks=SECOND),
     )
 
 
+def by_depth(rest):
+    depth = lax.axis_index("tensor")
+    for mask in (1, 2):
+        crossed = jnp.bitwise_and(depth, mask) != 0
+        rest = [jnp.where(crossed, rest[j ^ mask], rest[j]) for j in range(DEPTH)]
+    return jnp.stack(rest)
+
+
 def second(chunk):
     return dict(chunk, third=exchange(chunk["first"], dp_masks=SECOND))
 
 
+def with_own(own, rest):
+    depth = lax.axis_index("tensor")
+    before = [rest[min(j, DEPTH - 2)] for j in range(DEPTH)]
+    after = [rest[max(j - 1, 0)] for j in range(DEPTH)]
+    return jnp.stack(
+        [jnp.where(j == depth, own, jnp.where(j < depth, b, a)) for j, b, a in zip(range(DEPTH), before, after)]
+    )
+
+
 def assemble(chunk):
-    rest = [chunk["remote"], chunk["first"], chunk["second"], chunk["third"]]
-    return jnp.stack([jnp.concatenate([own[None], r]) for own, r in zip(chunk["own"], rest)])
+    rest = [chunk["first"], chunk["second"], chunk["third"]]
+    return jnp.stack([chunk["every"]] + [with_own(own, r) for own, r in zip(chunk["own"][1:], rest)])
 
 
 def add_low(a, b):
@@ -292,19 +301,27 @@
     return parts[0], exchange(total_low(parts[1], parts[2]), dp_masks=FIRST)
 
 
+def reduce_along(own, turned, opened):
+    return lax.psum_scatter(total_low(own, turned, opened), "tensor", scatter_dimension=0)
+
+
 def reduce_near(own, turned, opened):
     pairs = total_low(own, turned, opened)
     pairs = pairs.reshape((2, 2) + pairs.shape[1:])
-    return pairs[:, 0], exchange(pairs[:, 1], tensor_mask=1)
+    odd = lax.axis_index("tensor") % 2 == 1
+    keep = jnp.where(odd, pairs[:, 1], pairs[:, 0])
+    return keep, exchange(jnp.where(odd, pairs[:, 0], pairs[:, 1]), tensor_mask=1)
 
 
 def reduce_far(pair):
     terms = total_low(*pair)
-    return terms[0], exchange(terms[1], tensor_mask=2)
-
-
-def reduce_last(pair):
-    one = total_low(*pair)
+    upper = lax.axis_index("tensor") // 2 == 1
+    keep = jnp.where(upper, terms[1], terms[0])
+    return keep, exchange(jnp.where(upper, terms[0], terms[1]), tensor_mask=2)
+
+
+def reduce_last(*parts):
+    one = total_low(*parts)
     mask = PLANE
     while mask < lax.axis_size("dp"):
         one = total_low(one, exchange(one, dp_masks=(mask, mask)))
@@ -402,22 +419,25 @@
         got = swap(lax.dynamic_index_in_dim(slab, 1 - core, 0, keepdims=False))
         return jnp.where(is_first, keep, got), jnp.where(is_first, got, keep)
 
+    def along(slab):
+        return lax.all_gather(slab, "tensor")
+
     qkv_rows = jnp.transpose(query_key_value_weight[0], (1, 2, 0))
     attn_rows = jnp.concatenate([qkv_rows, attention_output_weight], axis=0)
     attn_slab = attn_rows.reshape(2, 2, local_heads, PLANE, part, features)
     attn_slab = jnp.transpose(attn_slab, (0, 3, 1, 2, 4, 5)).reshape(2, PLANE, -1, features)
     attn_in = [{"own": relative(own)} for own in share(attn_slab)]
-    attn_in[0] = near(attn_in[0])
-    attn_in, gate_up_weight, down_weight = together(attn_in, gate_up_weight, down_weight)
+    a0, a1 = attn_in
+    mine = a0["own"][0]
+    beside = exchange(mine, tensor_mask=1)
+    mine, beside, gate_up_weight, down_weight = together(mine, beside, gate_up_weight, down_weight)
     gate_up_rows = jnp.transpose(gate_up_weight[0], (1, 2, 0))
     feed_rows = jnp.concatenate([gate_up_rows, down_weight], axis=0)
     feed_slab = feed_rows.reshape(3, 2, FEED_CHUNKS, PLANE, unit_part, features)
     feed_slab = jnp.transpose(feed_slab, (2, 1, 3, 0, 4, 5)).reshape(FEED_CHUNKS, 2, PLANE, -1, features)
 
     feed_in = [[{"own": relative(own)} for own in share(feed_slab[k])] for k in range(FEED_CHUNKS)]
-    a0, a1 = attn_in
     (p0, p1), (q0, q1) = feed_in
-
 
     norm_table = jnp.concatenate([norm1_gain, norm1_bias, norm2_gain, norm2_bias])
     norm_other = swap(norm_table)
@@ -425,10 +445,7 @@
     norm_second = jnp.where(is_first, norm_other, norm_table)
     norms = [tuple(table[i] for i in range(4)) for table in (norm_first, norm_second)]
 
-    slope_table = jnp.asarray(alibi_table(HEADS)).reshape(DEPTH, local_heads)
-    slopes = jnp.concatenate(
-        [lax.dynamic_index_in_dim(slope_table, jnp.bitwise_xor(depth, j), 0, keepdims=False) for j in range(DEPTH)]
-    )
+    slopes = jnp.asarray(alibi_table(HEADS))
 
     def own_half(whole):
         flat = whole.reshape((2, rows) + whole.shape[3:])
@@ -452,34 +469,52 @@
         full = jnp.transpose(full, (1, 0, 2, 3)).reshape(3, -1, features)
         return full[:2].reshape(-1, features), full[2]
 
-    a0, p0 = far(a0), near(p0)
-    a0, p0, q0 = together(a0, p0, q0)
-    a0, p0, q0 = first(a0), far(p0), near(q0)
-    a0, p0, q0, a1 = together(a0, p0, q0, a1)
-    a0, p0, q0, a1 = second(a0), first(p0), far(q0), near(a1)
-    a0, p0, q0, a1, p1 = together(a0, p0, q0, a1, p1)
-    p0, q0, a1, p1 = second(p0), first(q0), far(a1), near(p1)
+    def along_all(*chunks):
+        return along(jnp.concatenate([chunk["own"][0] for chunk in chunks]))
+
+    def cut(every, *chunks):
+        done = []
+        for chunk in chunks:
+            rows_here = chunk["own"][0].shape[0]
+            done.append(dict(chunk, every=every[:, :rows_here]))
+            every = every[:, rows_here:]
+        return done
+
+    beyond = exchange(jnp.stack([mine, beside]), tensor_mask=2)
+    p0, q0, a1, beyond, mine, beside = together(p0, q0, a1, beyond, mine, beside)
+    every0 = along_all(p0, q0, a1)
+    a0["every"] = by_depth([mine, beside, beyond[0], beyond[1]])
+    a0 = first(a0)
+    (a0,) = together(a0)
+    a0 = second(a0)
+    a0, every0, p1, q1 = together(a0, every0, p1, q1)
+    p0, q0, a1 = cut(every0, p0, q0, a1)
+    p0 = first(p0)
+    every1 = along_all(p1, q1)
     attn0 = attn_weights(a0)
     projected0, context0, sum0, norm0 = attn_forward(start, attn0, norms[0], slopes, seqs)
-    low0, p0, q0, a1, p1, q1 = together(norm0.astype(BF16), p0, q0, a1, p1, q1)
-    q0, a1, p1, q1 = second(q0), first(a1), far(p1), near(q1)
+    low0, p0 = together(norm0.astype(BF16), p0)
+    p0, q0 = second(p0), first(q0)
     all0 = both_rows(low0)
+    all0, p0 = together(all0, p0)
     feed_p0 = feed_weights(p0)
     gated_p0, hidden_p0, mixed = feed_forward(all0, feed_p0)
-    mixed, q0, a1, p1, q1 = together(mixed, q0, a1, p1, q1)
-    a1, p1, q1 = second(a1), first(p1), far(q1)
+    mixed, q0 = together(mixed, q0)
+    q0, a1 = second(q0), first(a1)
     feed_q0 = feed_weights(q0)
     gated_q0, hidden_q0, more = feed_forward(all0, feed_q0)
     mixed = mixed + more
-    mixed, a1, p1, q1 = together(mixed, a1, p1, q1)
-    p1, q1 = second(p1), first(q1)
+    mixed, a1, every1 = together(mixed, a1, every1)
+    p1, q1 = cut(every1, p1, q1)
+    a1, p1, q1 = second(a1), first(p1), first(q1)
     attn1 = attn_weights(a1)
     total0 = norm0 + join_rows(mixed)
     middle_low = norm_rows(total0, norms[0][2], norms[0][3]).astype(BF16)
     projected1, context1, sum1, norm1 = attn_forward(middle_low, attn1, norms[1], slopes, seqs)
     low1, p1, q1 = together(norm1.astype(BF16), p1, q1)
-    q1 = second(q1)
+    p1, q1 = second(p1), second(q1)
     all1 = both_rows(low1)
+    all1, p1 = together(all1, p1)
     feed_p1 = feed_weights(p1)
     gated_p1, hidden_p1, mixed = feed_forward(all1, feed_p1)
     mixed, q1 = together(mixed, q1)
@@ -500,9 +535,7 @@
         return [full[e] for e in range(PLANE)]
 
     def attn_terms(qkv, out, vectors):
-        spread = jnp.transpose(jnp.stack(vectors).reshape(4, DEPTH, local), (1, 0, 2)).reshape(DEPTH, features)
-        spread = [lax.dynamic_index_in_dim(spread, jnp.bitwise_xor(depth, j), 0) for j in range(DEPTH)]
-        spread = jnp.pad(jnp.concatenate(spread).astype(BF16), ((0, NORM_ROWS - DEPTH), (0, 0)))
+        spread = jnp.pad(jnp.stack(vectors).astype(BF16), ((0, NORM_ROWS - len(vectors)), (0, 0)))
         full = jnp.concatenate([qkv, out]).reshape(2, -1, features)
         full = jnp.concatenate([full, jnp.stack([spread, spread])], axis=1)
         keep = lax.dynamic_index_in_dim(full, core, 0, keepdims=False)
@@ -510,8 +543,7 @@
 
     def attn_pieces(pair):
         full = add_low(*pair)
-        spread = full[-NORM_ROWS : DEPTH - NORM_ROWS]
-        spread = jnp.broadcast_to(spread[None, :, None], (PLANE, DEPTH, NORM_ROWS, features))
+        spread = jnp.broadcast_to(full[-NORM_ROWS:], (PLANE, DEPTH, NORM_ROWS, features))
         full = full[:-NORM_ROWS].reshape(2, DEPTH, local_heads, PLANE, part, features)
         full = jnp.transpose(full, (3, 1, 0, 2, 4, 5)).reshape(PLANE, DEPTH, -1, features)
         full = jnp.concatenate([full, spread], axis=2)
@@ -550,87 +582,84 @@
 
     a1 = attn_terms(qkv, out, [gain_one1, offset_one1, gain_two1, offset_two1])
     q1_own, q1_c = reduce_turn((q1_own, q1_half, q1_a))
-    p1 = reduce_near(p1_own, p1_c, p1_b)
+    p1 = reduce_along(p1_own, p1_c, p1_b)
     middle_grad = dot(projected_grad, attn1[0], 1, 0) + sum_grad
     second_grad, gain_two0, offset_two0 = norm_backward(total0, norms[0][2], norms[0][3], middle_grad)
     mixed_low = second_grad.astype(BF16)
-    mixed_low, a1, q1_b, p1 = together(mixed_low, a1, q1_b, p1)
+    mixed_low, a1, q1_b = together(mixed_low, a1, q1_b)
 
     mixed_all = both_rows(mixed_low)
     a1_own, a1_half, a1_a, a1_b = reduce_open(attn_pieces(a1))
-    p1 = reduce_far(p1)
     grad_p = feed_backward(mixed_all, feed_p0, gated_p0)
-    mixed_all, grad_p, a1_a, q1_c, p1 = together(mixed_all, grad_p, a1_a, q1_c, p1)
+    mixed_all, grad_p, a1_a, q1_c = together(mixed_all, grad_p, a1_a, q1_c)
 
     a1_own, a1_c = reduce_turn((a1_own, a1_half, a1_a))
-    q1 = reduce_near(q1_own, q1_c, q1_b)
+    q1 = reduce_along(q1_own, q1_c, q1_b)
     p0 = feed_terms(*feed_weight_grads(mixed_all, all0, grad_p, hidden_p0))
     terms = dot(grad_p, feed_p0[0], 1, 0)
-    mixed_all, terms, p0, a1_b, q1 = together(mixed_all, terms, p0, a1_b, q1)
+    mixed_all, terms, p0, a1_b = together(mixed_all, terms, p0, a1_b)
 
     p0_own, p0_half, p0_a, p0_b = reduce_open(p0)
-    q1 = reduce_far(q1)
     grad_q = feed_backward(mixed_all, feed_q0, gated_q0)
     terms = terms + dot(grad_q, feed_q0[0], 1, 0)
-    terms, grad_q, p0_a, a1_c, q1 = together(terms, grad_q, p0_a, a1_c, q1)
+    terms, grad_q, p0_a, a1_c, p1 = together(terms, grad_q, p0_a, a1_c, p1)
 
     p0_own, p0_c = reduce_turn((p0_own, p0_half, p0_a))
-    a1 = reduce_near(a1_own, a1_c, a1_b)
+    a1 = reduce_along(a1_own, a1_c, a1_b)
     q0 = feed_terms(*feed_weight_grads(mixed_all, all0, grad_q, hidden_q0))
     first_grad = join_rows(terms) + second_grad
     sum_grad, gain_one0, offset_one0 = norm_backward(sum0, norms[0][0], norms[0][1], first_grad)
-    sum_grad, q0, p0_b, a1 = together(sum_grad, q0, p0_b, a1)
+    sum_grad, q0, p0_b = together(sum_grad, q0, p0_b)
 
     q0_own, q0_half, q0_a, q0_b = reduce_open(q0)
-    a1 = reduce_far(a1)
     context_grad, out = context_backward(sum_grad, attn0, context0)
     projected_grad = attend_back(projected0, context_grad, slopes, seqs)
     qkv = dot(projected_grad, start, 0, 0).astype(BF16)
-    projected_grad, qkv, out, q0_a, p0_c, a1 = together(projected_grad, qkv, out, q0_a, p0_c, a1)
+    projected_grad, qkv, out, q0_a, p0_c, q1 = together(projected_grad, qkv, out, q0_a, p0_c, q1)
 
     a0 = attn_terms(qkv, out, [gain_one0, offset_one0, gain_two0, offset_two0])
     q0_own, q0_c = reduce_turn((q0_own, q0_half, q0_a))
-    p0 = reduce_near(p0_own, p0_c, p0_b)
+    p0 = reduce_along(p0_own, p0_c, p0_b)
+    start_grad = dot(projected_grad, attn0[0], 1, 0) + sum_grad
+    start_grad, a1, a0, q0_b = together(start_grad, a1, a0, q0_b)
+
+    a0_own, a0_half, a0_a, a0_b = reduce_open(attn_pieces(a0))
     attn_late = reduce_last(a1)
     late = jnp.concatenate([reduce_last(p1), reduce_last(q1), attn_late[:-NORM_ROWS]])
-    start_grad = dot(projected_grad, attn0[0], 1, 0) + sum_grad
-    start_grad, late, a0, q0_b, p0 = together(start_grad, late, a0, q0_b, p0)
-
-    a0_own, a0_half, a0_a, a0_b = reduce_open(attn_pieces(a0))
-    p0 = reduce_far(p0)
     late_first = exchange(late, dp_masks=FIRST)
     late_got = [hand_over(late, 0)]
-    a0_a, q0_c, p0, late_got = together(a0_a, q0_c, p0, late_got)
+    a0_a, q0_c, late_got = together(a0_a, q0_c, late_got)
 
     a0_own, a0_c = reduce_turn((a0_own, a0_half, a0_a))
-    q0 = reduce_near(q0_own, q0_c, q0_b)
+    q0 = reduce_along(q0_own, q0_c, q0_b)
     late_second = exchange(late, dp_masks=SECOND)
     input_grad = give(start_grad, middle_grad)
-    a0_b, q0, late_first, input_grad = together(a0_b, q0, late_first, input_grad)
-
-    q0 = reduce_far(q0)
+    a0_b, late_first, input_grad = together(a0_b, late_first, input_grad)
+
     late_got.append(hand_over(late_first, 0))
-    a0_c, q0, late_got = together(a0_c, q0, late_got)
+    a0_c, late_got, p0 = together(a0_c, late_got, p0)
 
     a0 = reduce_near(a0_own, a0_c, a0_b)
     late_third = exchange(late_first, dp_masks=SECOND)
+    a0, late_second, q0 = together(a0, late_second, q0)
+
+    a0 = reduce_far(a0)
     feed = jnp.concatenate([reduce_last(p0), reduce_last(q0)])
     feed_first = exchange(feed, dp_masks=FIRST)
-    a0, late_second, feed = together(a0, late_second, feed)
-
-    a0 = reduce_far(a0)
     feed_second = exchange(feed, dp_masks=SECOND)
     late_got.append(hand_over(late_second, 0))
     feed_got = [hand_over(feed, 1)]
     a0, feed_first, late_third, late_got, feed_got = together(a0, feed_first, late_third, late_got, feed_got)
 
-    attn_early = reduce_last(a0)
+    attn_early = reduce_last(*a0)
     attn = attn_early[:-NORM_ROWS]
     attn_first, attn_second = exchange(attn, dp_masks=FIRST), exchange(attn, dp_masks=SECOND)
     feed_third = exchange(feed_first, dp_masks=SECOND)
     late_got.append(hand_over(late_third, 0))
     feed_got.append(hand_over(feed_first, 1))
-    attn_first, feed_second, late_got, feed_got = together(attn_first, feed_second, late_got, feed_got)
+    attn_first, attn_second, feed_second, late_got, feed_got = together(
+        attn_first, attn_second, feed_second, late_got, feed_got
+    )
 
     attn_third = exchange(attn_first, dp_masks=SECOND)
     feed_early = [feed, feed_first, feed_second, feed_third]
@@ -667,7 +696,8 @@
     grad_qkv = jnp.transpose(attn_total[:3], (2, 0, 1))
     grad_out = attn_total[3]
 
-    vectors = jnp.where(is_first, attn_early[-1], attn_late[-1]).astype(F32).reshape(4, local)
+    vectors = jnp.where(is_first, attn_early[-NORM_ROWS:], attn_late[-NORM_ROWS:]).astype(F32)
+    vectors = lax.dynamic_slice_in_dim(vectors, depth * local, local, 1)
 
     return (
         layer_out,

time: 565 us -> 606 us (1.073)
  other arithmetic: 98.1 us -> 126 us
  waiting for transfers between devices: 190 us -> 163 us
  matrix products: 63.6 us -> 84.3 us
  between operations: 14.4 us -> 28 us
    ppermute x87 -> x67, waiting for transfers between devices: 190 us -> 124 us  [exchange(): return lax.ppermute(block, AXES, pairs)]
    all_gather x0 -> x2, waiting for transfers between devices: none -> 29.9 us  [along(): return lax.all_gather(slab, 'tensor')]
    dot_general x36, matrix products: 63.6 us -> 84.3 us  [dot(): lax.dot_general(a, b, (((ca,), (cb,)), ((), ())), preferred_element_type=...]
    convert_element_type x24 -> x14, other arithmetic: 16.1 us -> 25.8 us  [total_low(): return sum((part.astype(F32) for part in parts)).astype(BF16)]
    reduce_scatter x0 -> x5, waiting for transfers between devices: none -> 7.35 us  [reduce_along(): lax.psum_scatter(total_low(own, turned, opened), 'tensor', scatter_dimens...]
    select_n x0 -> x11, other arithmetic: none -> 6.66 us  [the longest x6 5.55 us: with_own(): jnp.where(j == depth, own, jnp.where(j < depth, b, a))]
    unnamed x339 -> x310, local copies, waits for them, and re-layouts: 25.1 us -> 22.1 us
    another operation x28 -> x39, other arithmetic: 21 us -> 19.6 us  [the longest x12 11.3 us: with_own(): jnp.stack([jnp.where(j == depth, own, jnp.where(j < depth, b, a)) for j,...]
  transfers between devices with their start and end apart: 96 -> 83, of which waited for: 32 -> 30; matrix products, arithmetic and copies ran while one was open for 32% -> 37% of each run, Pallas kernels for 5% -> 5%
where the time goes in v7:
time: 606 us; the launch traced here: 597 us
  waiting for transfers between devices  163 us (27%)
  other arithmetic  126 us (21%)
  starting transfers between devices  89.1 us (15%)
  matrix products  84.3 us (14%)
  local copies, waits for them, and re-layouts  78 us (13%)
  Pallas kernels  28.8 us (5%)
  between operations  28 us (5%)
    ppermute x67, waiting for transfers between devices, exchange(): return lax.ppermute(block, AXES, pairs)  124 us
    dot_general x36, matrix products, dot(): lax.dot_general(a, b, (((ca,), (cb,)), ((), ())), preferred_element_type=...  84.3 us
    ppermute x67, starting transfers between devices, exchange(): return lax.ppermute(block, AXES, pairs)  68.5 us
    all_gather x2, waiting for transfers between devices, along(): return lax.all_gather(slab, 'tensor')  29.9 us
    convert_element_type x14, other arithmetic, total_low(): return sum((part.astype(F32) for part in parts)).astype(BF16)  25.8 us
    convert_element_type x4, other arithmetic, feed_forward(): hidden = gelu_product(gate_part, up_part).astype(BF16)  23.9 us
    unnamed x310, local copies, waits for them, and re-layouts  22.1 us
    ppermute x9, starting transfers between devices, hand_over(): return lax.ppermute(block, AXES, pairs)  19.7 us
  transfers between devices with their start and end apart: 83, of which 30 were waited for; matrix products, arithmetic and copies ran while one was open for 37% of the time, Pallas kernels for 5%

profile of v7, /device:TPU:1, one launch (start us, length us, event | category | flops | bytes accessed | tf_op | source)
XLA Modules:
  0.0 596.9 jit_solution(6236211483432178035)
XLA Ops:
  20.0 5.6 copy.65
  33.7 11.7 %collective-permute-done.5 = bf16[2,96,768]{2,1,0:T(8,128)(2,1)S(1)} collective-permute-done((bf16[2,96,768]{2,1,0:T(8,128)(2,1)S(1)}, bf16[2,96,768]{2,1,0:T(8,128)(2,1)S(1)}, u32[]{:S(2)}, u32[]{:S(2)}) %collective-permute-start.5) | collective-permute-done | bytes 294944 | tf_op jit(solution)/shard_map/ppermute | solution.py:61
  49.1 6.6 %collective-permute-done.6 = bf16[3,96,768]{2,1,0:T(8,128)(2,1)} collective-permute-done((bf16[3,96,768]{2,1,0:T(8,128)(2,1)S(1)}, bf16[3,96,768]{2,1,0:T(8,128)(2,1)}, u32[]{:S(2)}, u32[]{:S(2)}) %collective-permute-start.6) | collective-permute-done | bytes 442400 | tf_op jit(solution)/shard_map/ppermute | solution.py:61
  62.7 5.4 collective-permute-done.8
  68.1 29.9 %all-gather.5.cloned.1.call-done = bf16[1536,768]{1,0:T(8,128)(2,1)} async-done(((bf16[384,768]{1,0:T(8,128)(2,1)}), bf16[1536,768]{1,0:T(8,128)(2,1)}) %all-gather.5.cloned.1.call-update) | async-done | bytes 2359312 | tf_op jit(solution)/shard_map/all_gather | solution.py:423
  117.1 4.7 attend.2
  136.5 5.2 collective-permute-done.13
  148.9 6.0 multiply_convert_fusion.7
  160.3 7.9 %collective-permute-done.16 = bf16[3,144,768]{2,1,0:T(8,128)(2,1)S(1)} collective-permute-done((bf16[3,144,768]{2,1,0:T(8,128)(2,1)}, bf16[3,144,768]{2,1,0:T(8,128)(2,1)S(1)}, u32[]{:S(2)}, u32[]{:S(2)}) %collective-permute-start.16) | collective-permute-done | bytes 663584 | tf_op jit(solution)/shard_map/ppermute | solution.py:61
  171.3 6.0 multiply_convert_fusion.6
  185.0 4.3 collective-permute-done.20
  207.1 4.7 attend.3
  215.2 8.2 %collective-permute-done.22 = bf16[3,144,768]{2,1,0:T(8,128)(2,1)} collective-permute-done((bf16[3,144,768]{2,1,0:T(8,128)(2,1)}, bf16[3,144,768]{2,1,0:T(8,128)(2,1)}, u32[]{:S(2)}, u32[]{:S(2)}) %collective-permute-start.22) | collective-permute-done | bytes 663584 | tf_op jit(solution)/shard_map/ppermute | solution.py:61
  223.5 4.3 collective-permute-done.23
  230.0 8.4 %collective-permute-done.27 = bf16[3,144,768]{2,1,0:T(8,128)(2,1)S(1)} collective-permute-done((bf16[3,144,768]{2,1,0:T(8,128)(2,1)}, bf16[3,144,768]{2,1,0:T(8,128)(2,1)S(1)}, u32[]{:S(2)}, u32[]{:S(2)}) %collective-permute-start.27) | collective-permute-done | bytes 663584 | tf_op jit(solution)/shard_map/ppermute | solution.py:61
  245.1 6.0 %multiply_convert_fusion.5 = (bf16[768,768]{1,0:T(8,128)(2,1)S(1)}, f32[768,768]{1,0:T(8,128)}) fusion(f32[768,1536]{1,0:T(8,128)S(1)} %fusion.205), kind=kLoop, calls=%fused_computation.82 | loop fusion | flops 38928384 | bytes 8257536 | tf_op jit(solution)/shard_map/convert_element_type | solution.py:354
  258.7 6.0 %multiply_convert_fusion.4 = (bf16[768,768]{1,0:T(8,128)(2,1)S(1)}, f32[768,768]{1,0:T(8,128)}) fusion(f32[768,1536]{1,0:T(8,128)S(1)} %fusion.207), kind=kLoop, calls=%fused_computation.69 | loop fusion | flops 38928384 | bytes 8257536 | tf_op jit(solution)/shard_map/convert_element_type | solution.py:354
  316.3 11.0 %collective-permute-done.34 = bf16[4,144,768]{2,1,0:T(8,128)(2,1)} collective-permute-done((bf16[4,144,768]{2,1,0:T(8,128)(2,1)S(1)}, bf16[4,144,768]{2,1,0:T(8,128)(2,1)}, u32[]{:S(2)}, u32[]{:S(2)}) %collective-permute-start.34) | collective-permute-done | bytes 884768 | tf_op jit(solution)/shard_map/ppermute | solution.py:61
  330.9 5.7 attend_back.2
  354.3 5.0 multiply_reduce_fusion
  370.7 4.0 collective-permute-start.40
  377.0 6.4 %collective-permute-done.40 = bf16[4,112,768]{2,1,0:T(8,128)(2,1)S(1)} collective-permute-done((bf16[4,112,768]{2,1,0:T(8,128)(2,1)S(1)}, bf16[4,112,768]{2,1,0:T(8,128)(2,1)S(1)}, u32[]{:S(2)}, u32[]{:S(2)}) %collective-permute-start.40) | collective-permute-done | bytes 688160 | tf_op jit(solution)/shard_map/ppermute | solution.py:61
  399.6 5.7 add_convert_fusion.2
  429.8 5.9 attend_back.3
  458.8 4.8 fusion.36
  463.6 6.2 %reduce-scatter.10.cloned.1.call-done = bf16[1,112,768]{2,1,0:T(8,128)(2,1)} async-done(((bf16[4,112,768]{2,1,0:T(8,128)(2,1)}), bf16[1,112,768]{2,1,0:T(8,128)(2,1)}) %reduce-scatter.10.cloned.1.call-update) | async-done | bytes 172048 | tf_op jit(solution)/shard_map/reduce_scatter | solution.py:305
  494.7 5.7 collective-permute-done.52
  519.9 6.9 %collective-permute-done.59 = bf16[2,112,768]{2,1,0:T(8,128)(2,1)S(1)} collective-permute-done((bf16[2,112,768]{2,1,0:T(8,128)(2,1)S(1)}, bf16[2,112,768]{2,1,0:T(8,128)(2,1)S(1)}, u32[]{:S(2)}, u32[]{:S(2)}) %collective-permute-start.59) | collective-permute-done | bytes 344096 | tf_op jit(solution)/shard_map/ppermute | solution.py:61
  530.4 4.4 collective-permute-start.65
  541.2 5.8 collective-permute-done.61
  560.2 4.5 collective-permute-done.71
  578.9 7.7 %settle.1 = (f32[768,2,768]{2,1,0:T(2,128)}, f32[768,768]{1,0:T(8,128)}) custom-call(s32[9]{0:T(128)} %pad_add_fusion.flags_ref, bf16[288,768]{1,0:T(8,128)(2,1)} %copy-done.72, bf16[288,768]{1,0:T(8,128)(2,1)} %copy-done.100, bf16[288,768]{1,0:T(8,128)(2,1)} %copy-done.102, bf16[288,768]{1,0:T(8,128)(2,1)} %copy-done.104, bf16[288,768]{1,0:T(8,128)(2,1)} %copy-done.101, ...), custom_call_target="tpu_custom_call" | custom-call | tf_op jit(solution)/shard_map/settle/pallas_call | solution.py:225
  (748 shorter events, 348.3 us)
Async XLA Ops:
  7.2 90.8 %all-gather.5.cloned.1.call-start = ((), (), s32[]{:S(2)}) async-start(), calls=%async_computation.10 | async-start | bytes 2949120 | tf_op jit(solution)/shard_map/all_gather | solution.py:423
  46.3 135.2 %all-gather.7.cloned.1.call-start = ((), (), s32[]{:S(2)}) async-start(), calls=%async_computation.11 | async-start | bytes 2211840 | tf_op jit(solution)/shard_map/all_gather | solution.py:423
  129.3 27.0 %collective-permute-start.14 = (bf16[3,144,768]{2,1,0:T(8,128)(2,1)}, bf16[3,144,768]{2,1,0:T(8,128)(2,1)}, u32[]{:S(2)}, u32[]{:S(2)}) collective-permute-start(bf16[3,144,768]{2,1,0:T(8,128)(2,1)} %pad_maximum_fusion.36), channel_id=1, source_target_pairs={{0,4},{1,5},{2,6},{3,7},{4,0},{5,1},{6,2},{7,3},{8,12},{9,13},{10,... | collective-permute-start | bytes 1990664 | tf_op jit(solution)/shard_map/ppermute | solution.py:61
  130.3 26.0 %collective-permute-start.15 = (bf16[3,144,768]{2,1,0:T(8,128)(2,1)}, bf16[3,144,768]{2,1,0:T(8,128)(2,1)}, u32[]{:S(2)}, u32[]{:S(2)}) collective-permute-start(bf16[3,144,768]{2,1,0:T(8,128)(2,1)} %pad_maximum_fusion.36), channel_id=1, source_target_pairs={{0,8},{1,9},{2,10},{3,11},{4,12},{5,13},{6,14},{7,15},{8,0},{9,1},... | collective-permute-start | bytes 1990664 | tf_op jit(solution)/shard_map/ppermute | solution.py:61
  132.3 49.2 %collective-permute-start.17 = (bf16[3,96,768]{2,1,0:T(8,128)(2,1)}, bf16[3,96,768]{2,1,0:T(8,128)(2,1)}, u32[]{:S(2)}, u32[]{:S(2)}) collective-permute-start(bf16[3,96,768]{2,1,0:T(8,128)(2,1)} %pad_maximum_fusion.44), channel_id=1, source_target_pairs={{0,4},{1,5},{2,6},{3,7},{4,0},{5,1},{6,2},{7,3},{8,12},{9,13},{10,... | collective-permute-start | bytes 1327112 | tf_op jit(solution)/shard_map/ppermute | solution.py:61
  133.7 280.1 %reduce-scatter.6.cloned.1.call-start = ((), (), s32[]{:S(2)}) async-start(), calls=%async_computation.5 | async-start | bytes 1105920 | tf_op jit(solution)/shard_map/reduce_scatter | solution.py:305
  134.0 47.5 %collective-permute-start.18 = (bf16[3,96,768]{2,1,0:T(8,128)(2,1)}, bf16[3,96,768]{2,1,0:T(8,128)(2,1)}, u32[]{:S(2)}, u32[]{:S(2)}) collective-permute-start(bf16[3,96,768]{2,1,0:T(8,128)(2,1)} %pad_maximum_fusion.44), channel_id=1, source_target_pairs={{0,8},{1,9},{2,10},{3,11},{4,12},{5,13},{6,14},{7,15},{8,0},{9,1},... | collective-permute-start | bytes 1327112 | tf_op jit(solution)/shard_map/ppermute | solution.py:61
  195.2 20.0 %collective-permute-start.24 = (bf16[3,144,768]{2,1,0:T(8,128)(2,1)}, bf16[3,144,768]{2,1,0:T(8,128)(2,1)}, u32[]{:S(2)}, u32[]{:S(2)}) collective-permute-start(bf16[3,144,768]{2,1,0:T(8,128)(2,1)} %pad_maximum_fusion.38), channel_id=1, source_target_pairs={{0,4},{1,5},{2,6},{3,7},{4,0},{5,1},{6,2},{7,3},{8,12},{9,13},{10,... | collective-permute-start | bytes 1990664 | tf_op jit(solution)/shard_map/ppermute | solution.py:61
  195.8 19.4 %collective-permute-start.25 = (bf16[3,144,768]{2,1,0:T(8,128)(2,1)}, bf16[3,144,768]{2,1,0:T(8,128)(2,1)}, u32[]{:S(2)}, u32[]{:S(2)}) collective-permute-start(bf16[3,144,768]{2,1,0:T(8,128)(2,1)} %pad_maximum_fusion.38), channel_id=1, source_target_pairs={{0,8},{1,9},{2,10},{3,11},{4,12},{5,13},{6,14},{7,15},{8,0},{9,1},... | collective-permute-start | bytes 1990664 | tf_op jit(solution)/shard_map/ppermute | solution.py:61
  198.9 24.6 %collective-permute-start.22 = (bf16[3,144,768]{2,1,0:T(8,128)(2,1)}, bf16[3,144,768]{2,1,0:T(8,128)(2,1)}, u32[]{:S(2)}, u32[]{:S(2)}) collective-permute-start(bf16[3,144,768]{2,1,0:T(8,128)(2,1)} %pad_maximum_fusion.37), channel_id=1, source_target_pairs={{0,4},{1,5},{2,6},{3,7},{4,0},{5,1},{6,2},{7,3},{8,12},{9,13},{10,... | collective-permute-start | bytes 1990664 | tf_op jit(solution)/shard_map/ppermute | solution.py:61
  200.7 27.0 %collective-permute-start.23 = (bf16[3,144,768]{2,1,0:T(8,128)(2,1)}, bf16[3,144,768]{2,1,0:T(8,128)(2,1)}, u32[]{:S(2)}, u32[]{:S(2)}) collective-permute-start(bf16[3,144,768]{2,1,0:T(8,128)(2,1)} %pad_maximum_fusion.37), channel_id=1, source_target_pairs={{0,8},{1,9},{2,10},{3,11},{4,12},{5,13},{6,14},{7,15},{8,0},{9,1},... | collective-permute-start | bytes 1990664 | tf_op jit(solution)/shard_map/ppermute | solution.py:61
  229.8 22.7 %collective-permute-start.28 = (bf16[3,144,768]{2,1,0:T(8,128)(2,1)}, bf16[3,144,768]{2,1,0:T(8,128)(2,1)S(1)}, u32[]{:S(2)}, u32[]{:S(2)}) collective-permute-start(bf16[3,144,768]{2,1,0:T(8,128)(2,1)} %collective-permute-done.24), channel_id=1, source_target_pairs={{0,8},{1,9},{2,10},{3,11},{4,12},{5,13},{6,14},{7,15},{8,0},{9,1},... | collective-permute-start | bytes 1990664 | tf_op jit(solution)/shard_map/ppermute | solution.py:61
  276.8 21.7 %collective-permute-start.32 = (bf16[384,768]{1,0:T(8,128)(2,1)S(1)}, bf16[384,768]{1,0:T(8,128)(2,1)S(1)}, u32[]{:S(2)}, u32[]{:S(2)}) collective-permute-start(bf16[384,768]{1,0:T(8,128)(2,1)S(1)} %get-tuple-element.456), channel_id=1, source_target_pairs={{0,16},{1,17},{2,18},{3,19},{4,20},{5,21},{6,22},{7,23},{8,24},{9,... | collective-permute-start | bytes 1769480 | tf_op jit(solution)/shard_map/ppermute | solution.py:61
  308.2 19.1 %collective-permute-start.34 = (bf16[4,144,768]{2,1,0:T(8,128)(2,1)S(1)}, bf16[4,144,768]{2,1,0:T(8,128)(2,1)}, u32[]{:S(2)}, u32[]{:S(2)}) collective-permute-start(bf16[4,144,768]{2,1,0:T(8,128)(2,1)S(1)} %bitcast.958), channel_id=1, source_target_pairs={{0,8},{1,9},{2,10},{3,11},{4,12},{5,13},{6,14},{7,15},{8,0},{9,1},... | collective-permute-start | bytes 2654216 | tf_op jit(solution)/shard_map/ppermute | solution.py:61
  311.0 30.0 %collective-permute-start.36 = (bf16[4,144,768]{2,1,0:T(8,128)(2,1)}, bf16[4,144,768]{2,1,0:T(8,128)(2,1)}, u32[]{:S(2)}, u32[]{:S(2)}) collective-permute-start(bf16[4,144,768]{2,1,0:T(8,128)(2,1)} %add_convert_fusion.13), channel_id=1, source_target_pairs={{0,4},{1,5},{2,6},{3,7},{4,0},{5,1},{6,2},{7,3},{8,12},{9,13},{10,... | collective-permute-start | bytes 2654216 | tf_op jit(solution)/shard_map/ppermute | solution.py:61
  344.3 21.4 %collective-permute-start.37 = (bf16[1552,768]{1,0:T(8,128)(2,1)}, bf16[1552,768]{1,0:T(8,128)(2,1)}, u32[]{:S(2)}, u32[]{:S(2)}) collective-permute-start(bf16[1552,768]{1,0:T(8,128)(2,1)} %get-tuple-element.489), channel_id=1, source_target_pairs={{0,16},{1,17},{2,18},{3,19},{4,20},{5,21},{6,22},{7,23},{8,24},{9,... | collective-permute-start | bytes 7151624 | tf_op jit(solution)/shard_map/ppermute | solution.py:61
  345.2 20.5 %collective-permute-start.38 = (bf16[4,144,768]{2,1,0:T(8,128)(2,1)}, bf16[4,144,768]{2,1,0:T(8,128)(2,1)}, u32[]{:S(2)}, u32[]{:S(2)}) collective-permute-start(bf16[4,144,768]{2,1,0:T(8,128)(2,1)} %bitcast.247), channel_id=1, source_target_pairs={{0,8},{1,9},{2,10},{3,11},{4,12},{5,13},{6,14},{7,15},{8,0},{9,1},... | collective-permute-start | bytes 2654216 | tf_op jit(solution)/shard_map/ppermute | solution.py:61
  350.9 26.0 %collective-permute-start.41 = (bf16[4,144,768]{2,1,0:T(8,128)(2,1)}, bf16[4,144,768]{2,1,0:T(8,128)(2,1)}, u32[]{:S(2)}, u32[]{:S(2)}) collective-permute-start(bf16[4,144,768]{2,1,0:T(8,128)(2,1)} %add_convert_fusion.12), channel_id=1, source_target_pairs={{0,4},{1,5},{2,6},{3,7},{4,0},{5,1},{6,2},{7,3},{8,12},{9,13},{10,... | collective-permute-start | bytes 2654216 | tf_op jit(solution)/shard_map/ppermute | solution.py:61
  359.9 83.5 %reduce-scatter.8.cloned.1.call-start = ((), (), s32[]{:S(2)}) async-start(), calls=%async_computation.6 | async-start | bytes 1105920 | tf_op jit(solution)/shard_map/reduce_scatter | solution.py:305
  374.6 20.6 %collective-permute-start.42 = (bf16[4,112,768]{2,1,0:T(8,128)(2,1)S(1)}, bf16[4,112,768]{2,1,0:T(8,128)(2,1)}, u32[]{:S(2)}, u32[]{:S(2)}) collective-permute-start(bf16[4,112,768]{2,1,0:T(8,128)(2,1)S(1)} %get-tuple-element.517), channel_id=1, source_target_pairs={{0,8},{1,9},{2,10},{3,11},{4,12},{5,13},{6,14},{7,15},{8,0},{9,1},... | collective-permute-start | bytes 2064392 | tf_op jit(solution)/shard_map/ppermute | solution.py:61
  384.4 29.4 %collective-permute-start.44 = (bf16[4,112,768]{2,1,0:T(8,128)(2,1)}, bf16[4,112,768]{2,1,0:T(8,128)(2,1)}, u32[]{:S(2)}, u32[]{:S(2)}) collective-permute-start(bf16[4,112,768]{2,1,0:T(8,128)(2,1)} %fusion.35), channel_id=1, source_target_pairs={{0,4},{1,5},{2,6},{3,7},{4,0},{5,1},{6,2},{7,3},{8,12},{9,13},{10,... | collective-permute-start | bytes 2064392 | tf_op jit(solution)/shard_map/ppermute | solution.py:61
  395.2 18.6 %collective-permute-start.43 = (bf16[4,144,768]{2,1,0:T(8,128)(2,1)}, bf16[4,144,768]{2,1,0:T(8,128)(2,1)}, u32[]{:S(2)}, u32[]{:S(2)}) collective-permute-start(bf16[4,144,768]{2,1,0:T(8,128)(2,1)} %bitcast.264), channel_id=1, source_target_pairs={{0,8},{1,9},{2,10},{3,11},{4,12},{5,13},{6,14},{7,15},{8,0},{9,1},... | collective-permute-start | bytes 2654216 | tf_op jit(solution)/shard_map/ppermute | solution.py:61
  396.5 30.1 %collective-permute-start.46 = (bf16[4,144,768]{2,1,0:T(8,128)(2,1)}, bf16[4,144,768]{2,1,0:T(8,128)(2,1)}, u32[]{:S(2)}, u32[]{:S(2)}) collective-permute-start(bf16[4,144,768]{2,1,0:T(8,128)(2,1)} %bitcast.263), channel_id=1, source_target_pairs={{0,8},{1,9},{2,10},{3,11},{4,12},{5,13},{6,14},{7,15},{8,0},{9,1},... | collective-permute-start | bytes 2654216 | tf_op jit(solution)/shard_map/ppermute | solution.py:61
  399.4 70.5 %reduce-scatter.10.cloned.1.call-start = ((), (), s32[]{:S(2)}) async-start(), calls=%async_computation.7 | async-start | bytes 860160 | tf_op jit(solution)/shard_map/reduce_scatter | solution.py:305
  416.6 26.8 %collective-permute-start.48 = (bf16[4,144,768]{2,1,0:T(8,128)(2,1)}, bf16[4,144,768]{2,1,0:T(8,128)(2,1)}, u32[]{:S(2)}, u32[]{:S(2)}) collective-permute-start(bf16[4,144,768]{2,1,0:T(8,128)(2,1)} %add_convert_fusion.10), channel_id=1, source_target_pairs={{0,4},{1,5},{2,6},{3,7},{4,0},{5,1},{6,2},{7,3},{8,12},{9,13},{10,... | collective-permute-start | bytes 2654216 | tf_op jit(solution)/shard_map/ppermute | solution.py:61
  449.2 20.7 %collective-permute-start.49 = (bf16[1552,768]{1,0:T(8,128)(2,1)}, bf16[1552,768]{1,0:T(8,128)(2,1)}, u32[]{:S(2)}, u32[]{:S(2)}) collective-permute-start(bf16[1552,768]{1,0:T(8,128)(2,1)} %get-tuple-element.487), channel_id=1, source_target_pairs={{0,16},{1,17},{2,18},{3,19},{4,20},{5,21},{6,22},{7,23},{8,24},{9,... | collective-permute-start | bytes 7151624 | tf_op jit(solution)/shard_map/ppermute | solution.py:61
  451.7 60.1 %reduce-scatter.12.cloned.1.call-start = ((), (), s32[]{:S(2)}) async-start(), calls=%async_computation.8 | async-start | bytes 1105920 | tf_op jit(solution)/shard_map/reduce_scatter | solution.py:305
  455.3 29.7 %collective-permute-start.55 = (bf16[4,144,768]{2,1,0:T(8,128)(2,1)}, bf16[4,144,768]{2,1,0:T(8,128)(2,1)}, u32[]{:S(2)}, u32[]{:S(2)}) collective-permute-start(bf16[4,144,768]{2,1,0:T(8,128)(2,1)} %add_convert_fusion.8), channel_id=1, source_target_pairs={{0,4},{1,5},{2,6},{3,7},{4,0},{5,1},{6,2},{7,3},{8,12},{9,13},{10,... | collective-permute-start | bytes 2654216 | tf_op jit(solution)/shard_map/ppermute | solution.py:61
  458.8 69.2 %reduce-scatter.14.cloned.1.call-start = ((), (), s32[]{:S(2)}) async-start(), calls=%async_computation.9 | async-start | bytes 1105920 | tf_op jit(solution)/shard_map/reduce_scatter | solution.py:305
  488.6 23.1 %collective-permute-start.57 = (bf16[4,112,768]{2,1,0:T(8,128)(2,1)}, bf16[4,112,768]{2,1,0:T(8,128)(2,1)}, u32[]{:S(2)}, u32[]{:S(2)}) collective-permute-start(bf16[4,112,768]{2,1,0:T(8,128)(2,1)} %fusion.30), channel_id=1, source_target_pairs={{0,4},{1,5},{2,6},{3,7},{4,0},{5,1},{6,2},{7,3},{8,12},{9,13},{10,... | collective-permute-start | bytes 2064392 | tf_op jit(solution)/shard_map/ppermute | solution.py:61
  515.8 25.2 %collective-permute-start.63 = (bf16[384,768]{1,0:T(8,128)(2,1)}, bf16[384,768]{1,0:T(8,128)(2,1)S(1)}, u32[]{:S(2)}, u32[]{:S(2)}) collective-permute-start(bf16[384,768]{1,0:T(8,128)(2,1)} %collective-permute-done.52), channel_id=1, source_target_pairs={{0,8},{1,9},{2,10},{3,11},{4,12},{5,13},{6,14},{7,15},{8,0},{9,1},... | collective-permute-start | bytes 1769480 | tf_op jit(solution)/shard_map/ppermute | solution.py:61
  564.9 21.7 %collective-permute-start.72 = (bf16[4,96,768]{2,1,0:T(8,128)(2,1)S(1)}, bf16[4,96,768]{2,1,0:T(8,128)(2,1)}, u32[]{:S(2)}, u32[]{:S(2)}) collective-permute-start(bf16[4,96,768]{2,1,0:T(8,128)(2,1)S(1)} %get-tuple-element.621), channel_id=1, source_target_pairs={{16,0},{17,1},{18,2},{19,3},{20,4},{21,5},{22,6},{23,7},{24,8},{25... | collective-permute-start | bytes 1769480 | tf_op jit(solution)/shard_map/ppermute | solution.py:556
  (207 other events, 1878.2 us)
Sparse Core Ops, SparseCore 0:
  46.4 51.5 all-gather.4
  133.8 38.9 all-gather.6
  360.0 21.4 reduce-scatter.5
  399.5 23.0 reduce-scatter.7
  451.8 18.0 reduce-scatter.9
  472.0 25.2 reduce-scatter.11
  500.2 27.7 reduce-scatter.13

commit v8 on v6

--- a/solution.py
+++ b/solution.py
@@ -500,21 +500,18 @@
         return [full[e] for e in range(PLANE)]
 
     def attn_terms(qkv, out, vectors):
-        spread = jnp.transpose(jnp.stack(vectors).reshape(4, DEPTH, local), (1, 0, 2)).reshape(DEPTH, features)
-        spread = [lax.dynamic_index_in_dim(spread, jnp.bitwise_xor(depth, j), 0) for j in range(DEPTH)]
-        spread = jnp.pad(jnp.concatenate(spread).astype(BF16), ((0, NORM_ROWS - DEPTH), (0, 0)))
-        full = jnp.concatenate([qkv, out]).reshape(2, -1, features)
-        full = jnp.concatenate([full, jnp.stack([spread, spread])], axis=1)
+        spread = jnp.pad(jnp.stack(vectors).astype(BF16), ((0, NORM_ROWS - len(vectors)), (0, 0)))
+        spread = jnp.broadcast_to(spread, (2, PLANE, DEPTH, NORM_ROWS, features))
+        full = jnp.concatenate([qkv, out]).reshape(2, 2, DEPTH, local_heads, PLANE, part, features)
+        full = jnp.transpose(full, (0, 4, 2, 1, 3, 5, 6)).reshape(2, PLANE, DEPTH, -1, features)
+        return jnp.concatenate([full, spread], axis=3)
+
+    def attn_swap(full):
         keep = lax.dynamic_index_in_dim(full, core, 0, keepdims=False)
         return keep, swap(lax.dynamic_index_in_dim(full, 1 - core, 0, keepdims=False))
 
     def attn_pieces(pair):
-        full = add_low(*pair)
-        spread = full[-NORM_ROWS : DEPTH - NORM_ROWS]
-        spread = jnp.broadcast_to(spread[None, :, None], (PLANE, DEPTH, NORM_ROWS, features))
-        full = full[:-NORM_ROWS].reshape(2, DEPTH, local_heads, PLANE, part, features)
-        full = jnp.transpose(full, (3, 1, 0, 2, 4, 5)).reshape(PLANE, DEPTH, -1, features)
-        full = jnp.concatenate([full, spread], axis=2)
+        full = total_low(*pair)
         return [full[e] for e in range(PLANE)]
 
     def hand_over(block, source):
@@ -546,9 +543,10 @@
     q1_own, q1_half, q1_a, q1_b = reduce_open(q1)
     projected_grad = attend_back(projected1, context_grad, slopes, seqs)
     qkv = dot(projected_grad, middle_low, 0, 0).astype(BF16)
-    projected_grad, qkv, q1_a, p1_c = together(projected_grad, qkv, q1_a, p1_c)
-
     a1 = attn_terms(qkv, out, [gain_one1, offset_one1, gain_two1, offset_two1])
+    projected_grad, a1, q1_a, p1_c = together(projected_grad, a1, q1_a, p1_c)
+
+    a1 = attn_swap(a1)
     q1_own, q1_c = reduce_turn((q1_own, q1_half, q1_a))
     p1 = reduce_near(p1_own, p1_c, p1_b)
     middle_grad = dot(projected_grad, attn1[0], 1, 0) + sum_grad
@@ -576,80 +574,80 @@
 
     p0_own, p0_c = reduce_turn((p0_own, p0_half, p0_a))
     a1 = reduce_near(a1_own, a1_c, a1_b)
+    late = jnp.concatenate([reduce_last(p1), reduce_last(q1)])
+    late_first = exchange(late, dp_masks=FIRST)
     q0 = feed_terms(*feed_weight_grads(mixed_all, all0, grad_q, hidden_q0))
     first_grad = join_rows(terms) + second_grad
     sum_grad, gain_one0, offset_one0 = norm_backward(sum0, norms[0][0], norms[0][1], first_grad)
-    sum_grad, q0, p0_b, a1 = together(sum_grad, q0, p0_b, a1)
+    sum_grad, q0, p0_b, a1, late, late_first = together(sum_grad, q0, p0_b, a1, late, late_first)
 
     q0_own, q0_half, q0_a, q0_b = reduce_open(q0)
     a1 = reduce_far(a1)
     context_grad, out = context_backward(sum_grad, attn0, context0)
     projected_grad = attend_back(projected0, context_grad, slopes, seqs)
     qkv = dot(projected_grad, start, 0, 0).astype(BF16)
-    projected_grad, qkv, out, q0_a, p0_c, a1 = together(projected_grad, qkv, out, q0_a, p0_c, a1)
-
     a0 = attn_terms(qkv, out, [gain_one0, offset_one0, gain_two0, offset_two0])
+    late_second = exchange(late, dp_masks=SECOND)
+    projected_grad, a0, q0_a, p0_c, a1, late_second = together(projected_grad, a0, q0_a, p0_c, a1, late_second)
+
+    a0 = attn_swap(a0)
     q0_own, q0_c = reduce_turn((q0_own, q0_half, q0_a))
+    start_grad = dot(projected_grad, attn0[0], 1, 0) + sum_grad
+    start_grad, a0, q0_b = together(start_grad, a0, q0_b)
+
+    a0 = attn_pieces(a0)
+    a0_got = exchange(jnp.stack(a0[2:]), dp_masks=SECOND)
     p0 = reduce_near(p0_own, p0_c, p0_b)
+    input_grad = give(start_grad, middle_grad)
+    a0_got, q0_c, p0, input_grad = together(a0_got, q0_c, p0, input_grad)
+
+    a0_c = exchange(total_low(a0[1], a0_got[1]), dp_masks=FIRST)
+    q0 = reduce_near(q0_own, q0_c, q0_b)
+    p0 = reduce_far(p0)
+    late_third = exchange(late_first, dp_masks=SECOND)
+    late_got = [hand_over(late, 0), hand_over(late_first, 0)]
+    a0_c, q0, p0, late_third, late_got = together(a0_c, q0, p0, late_third, late_got)
+
+    a0 = reduce_near(a0[0], a0_got[0], a0_c)
+    q0 = reduce_far(q0)
     attn_late = reduce_last(a1)
-    late = jnp.concatenate([reduce_last(p1), reduce_last(q1), attn_late[:-NORM_ROWS]])
-    start_grad = dot(projected_grad, attn0[0], 1, 0) + sum_grad
-    start_grad, late, a0, q0_b, p0 = together(start_grad, late, a0, q0_b, p0)
-
-    a0_own, a0_half, a0_a, a0_b = reduce_open(attn_pieces(a0))
-    p0 = reduce_far(p0)
-    late_first = exchange(late, dp_masks=FIRST)
-    late_got = [hand_over(late, 0)]
-    a0_a, q0_c, p0, late_got = together(a0_a, q0_c, p0, late_got)
-
-    a0_own, a0_c = reduce_turn((a0_own, a0_half, a0_a))
-    q0 = reduce_near(q0_own, q0_c, q0_b)
-    late_second = exchange(late, dp_masks=SECOND)
-    input_grad = give(start_grad, middle_grad)
-    a0_b, q0, late_first, input_grad = together(a0_b, q0, late_first, input_grad)
-
-    q0 = reduce_far(q0)
-    late_got.append(hand_over(late_first, 0))
-    a0_c, q0, late_got = together(a0_c, q0, late_got)
-
-    a0 = reduce_near(a0_own, a0_c, a0_b)
-    late_third = exchange(late_first, dp_masks=SECOND)
+    attn = attn_late[:-NORM_ROWS]
+    late_attn = [attn, exchange(attn, dp_masks=FIRST), exchange(attn, dp_masks=SECOND)]
+    late_got += [hand_over(late_second, 0), hand_over(late_third, 0)]
+    a0, q0, late_attn, late_got = together(a0, q0, late_attn, late_got)
+
+    a0 = reduce_far(a0)
+    late_attn.append(exchange(late_attn[1], dp_masks=SECOND))
     feed = jnp.concatenate([reduce_last(p0), reduce_last(q0)])
     feed_first = exchange(feed, dp_masks=FIRST)
-    a0, late_second, feed = together(a0, late_second, feed)
-
-    a0 = reduce_far(a0)
-    feed_second = exchange(feed, dp_masks=SECOND)
-    late_got.append(hand_over(late_second, 0))
     feed_got = [hand_over(feed, 1)]
-    a0, feed_first, late_third, late_got, feed_got = together(a0, feed_first, late_third, late_got, feed_got)
+    a0, late_attn, feed, feed_first, feed_got = together(a0, late_attn, feed, feed_first, feed_got)
 
     attn_early = reduce_last(a0)
     attn = attn_early[:-NORM_ROWS]
     attn_first, attn_second = exchange(attn, dp_masks=FIRST), exchange(attn, dp_masks=SECOND)
-    feed_third = exchange(feed_first, dp_masks=SECOND)
-    late_got.append(hand_over(late_third, 0))
+    feed_second = exchange(feed, dp_masks=SECOND)
+    attn_late_all = jnp.stack(late_attn)
+    attn_late_got = hand_over(attn_late_all, 0)
     feed_got.append(hand_over(feed_first, 1))
-    attn_first, feed_second, late_got, feed_got = together(attn_first, feed_second, late_got, feed_got)
-
-    attn_third = exchange(attn_first, dp_masks=SECOND)
-    feed_early = [feed, feed_first, feed_second, feed_third]
-    feed_got = feed_got + [hand_over(feed_second, 1), hand_over(feed_third, 1)]
+    attn_first, attn_second, feed_second, attn_late_got, feed_got = together(
+        attn_first, attn_second, feed_second, attn_late_got, feed_got
+    )
+
+    attn_third, feed_third = exchange(attn_first, dp_masks=SECOND), exchange(feed_first, dp_masks=SECOND)
+    feed_got.append(hand_over(feed_second, 1))
     attn_early_all = jnp.stack([attn, attn_first, attn_second, attn_third])
     attn_got = hand_over(attn_early_all, 1)
-
-    feed_rows = FEED_CHUNKS * 3 * unit_part
-    late = [late, late_first, late_second, late_third]
-    early_half = [feed_early, [piece[:feed_rows] for piece in late_got]]
-    late_half = [feed_got, [piece[:feed_rows] for piece in late]]
+    feed_got.append(hand_over(feed_third, 1))
+
+    feed_early = [feed, feed_first, feed_second, feed_third]
+    feed_late = [late, late_first, late_second, late_third]
     flags = jnp.concatenate(
         [is_first.astype(jnp.int32)[None]] + [jnp.bitwise_xor(in_plane, order) for order in orders]
     )
     grad_in, grad_down = settle(
-        early_half[0] + late_half[0] + early_half[1] + late_half[1], flags, FEED_CHUNKS, 3, unit_part
-    )
-    attn_late_all = jnp.stack([piece[feed_rows:] for piece in late])
-    attn_late_got = jnp.stack([piece[feed_rows:] for piece in late_got])
+        feed_early + feed_got + late_got + feed_late, flags, FEED_CHUNKS, 3, unit_part
+    )
     parts = [jnp.where(is_first, attn_early_all, attn_late_got), jnp.where(is_first, attn_got, attn_late_all)]
     attn_total = jnp.stack(
         [
@@ -667,7 +665,8 @@
     grad_qkv = jnp.transpose(attn_total[:3], (2, 0, 1))
     grad_out = attn_total[3]
 
-    vectors = jnp.where(is_first, attn_early[-1], attn_late[-1]).astype(F32).reshape(4, local)
+    vectors = jnp.where(is_first, attn_early[-NORM_ROWS:], attn_late[-NORM_ROWS:]).astype(F32)
+    vectors = lax.dynamic_slice_in_dim(vectors, depth * local, local, 1)
 
     return (
         layer_out,

time: 565 us -> 562 us (level)
  starting transfers between devices: 84.6 us -> 110 us
  local copies, waits for them, and re-layouts: 74.5 us -> 56.7 us
  other arithmetic: 98.1 us -> 90.6 us
    ppermute x87 -> x89, starting transfers between devices: 67.9 us -> 87.6 us  [exchange(): return lax.ppermute(block, AXES, pairs)]
    slice x15 -> x3, local copies, waits for them, and re-layouts: 7.63 us -> 0.02 us  [the longest x1 0.01 us: body(): attn = attn_late[:-NORM_ROWS]]
    another operation x18 -> x1, local copies, waits for them, and re-layouts: 5.93 us -> 0.09 us  [body(): a0_got = exchange(jnp.stack(a0[2:]), dp_masks=SECOND)]
    ppermute x9 -> x10, starting transfers between devices: 16.8 us -> 22.5 us  [hand_over(): return lax.ppermute(block, AXES, pairs)]
    ppermute x87 -> x89, waiting for transfers between devices: 190 us -> 186 us  [exchange(): return lax.ppermute(block, AXES, pairs)]
    unnamed x339 -> x333, local copies, waits for them, and re-layouts: 25.1 us -> 22.3 us
    convert_element_type x24 -> x26, other arithmetic: 16.1 us -> 13.6 us  [total_low(): return sum((part.astype(F32) for part in parts)).astype(BF16)]
  transfers between devices with their start and end apart: 96 -> 99, of which waited for: 32 -> 40; matrix products, arithmetic and copies ran while one was open for 32% -> 28% of each run, Pallas kernels for 5% -> 5%
where the time goes in v8:
time: 562 us; the launch traced here: 551 us
  waiting for transfers between devices  186 us (33%)
  starting transfers between devices  110 us (20%)
  other arithmetic  90.6 us (16%)
  matrix products  63.3 us (11%)
  local copies, waits for them, and re-layouts  56.7 us (10%)
  Pallas kernels  29.5 us (5%)
  between operations  14.9 us (3%)
    ppermute x89, waiting for transfers between devices, exchange(): return lax.ppermute(block, AXES, pairs)  186 us
    ppermute x89, starting transfers between devices, exchange(): return lax.ppermute(block, AXES, pairs)  87.6 us
    dot_general x36, matrix products, dot(): lax.dot_general(a, b, (((ca,), (cb,)), ((), ())), preferred_element_type=...  63.3 us
    convert_element_type x4, other arithmetic, feed_forward(): hidden = gelu_product(gate_part, up_part).astype(BF16)  24.2 us
    ppermute x10, starting transfers between devices, hand_over(): return lax.ppermute(block, AXES, pairs)  22.5 us
    unnamed x333, local copies, waits for them, and re-layouts  22.3 us
    convert_element_type x26, other arithmetic, total_low(): return sum((part.astype(F32) for part in parts)).astype(BF16)  13.6 us
    another operation x18, other arithmetic, assemble(): jnp.stack([jnp.concatenate([own[None], r]) for own, r in zip(chunk['own']...  13.1 us
  transfers between devices with their start and end apart: 99, of which 40 were waited for; matrix products, arithmetic and copies ran while one was open for 28% of the time, Pallas kernels for 5%

profile of v8, /device:TPU:1, one launch (start us, length us, event | category | flops | bytes accessed | tf_op | source)
XLA Modules:
  0.0 550.9 jit_solution(14276602639725801753)
XLA Ops:
  13.4 5.6 %copy.70 = bf16[1,768,2,768]{1,3,2,0:T(8,128)(2,1)S(1)} copy(bf16[1,768,2,768]{3,2,1,0:T(2,128)(2,1)} %param.19) | data formatting | bytes 4718592 | tf_op jit(solution)/shard_map/optimization_barrier | solution.py:244
  28.3 9.7 %collective-permute-done.3 = bf16[2,96,768]{2,1,0:T(8,128)(2,1)S(1)} collective-permute-done((bf16[2,96,768]{2,1,0:T(8,128)(2,1)S(1)}, bf16[2,96,768]{2,1,0:T(8,128)(2,1)S(1)}, u32[]{:S(2)}, u32[]{:S(2)}) %collective-permute-start.3) | collective-permute-done | bytes 294944 | tf_op jit(solution)/shard_map/ppermute | solution.py:61
  40.7 4.4 collective-permute-start.10
  45.1 6.4 %collective-permute-done.10 = bf16[144,768]{1,0:T(8,128)(2,1)S(1)} collective-permute-done((bf16[144,768]{1,0:T(8,128)(2,1)S(1)}, bf16[144,768]{1,0:T(8,128)(2,1)S(1)}, u32[]{:S(2)}, u32[]{:S(2)}) %collective-permute-start.10) | collective-permute-done | bytes 221216 | tf_op jit(solution)/shard_map/ppermute | solution.py:61
  51.4 7.6 %collective-permute-done.9 = bf16[2,144,768]{2,1,0:T(8,128)(2,1)S(1)} collective-permute-done((bf16[2,144,768]{2,1,0:T(8,128)(2,1)S(1)}, bf16[2,144,768]{2,1,0:T(8,128)(2,1)S(1)}, u32[]{:S(2)}, u32[]{:S(2)}) %collective-permute-start.9) | collective-permute-done | bytes 442400 | tf_op jit(solution)/shard_map/ppermute | solution.py:61
  65.7 6.2 %collective-permute-done.15 = bf16[96,768]{1,0:T(8,128)(2,1)S(1)} collective-permute-done((bf16[96,768]{1,0:T(8,128)(2,1)S(1)}, bf16[96,768]{1,0:T(8,128)(2,1)S(1)}, u32[]{:S(2)}, u32[]{:S(2)}) %collective-permute-start.15) | collective-permute-done | bytes 147488 | tf_op jit(solution)/shard_map/ppermute | solution.py:61
  71.8 12.0 %collective-permute-done.14 = bf16[2,144,768]{2,1,0:T(8,128)(2,1)S(1)} collective-permute-done((bf16[2,144,768]{2,1,0:T(8,128)(2,1)S(1)}, bf16[2,144,768]{2,1,0:T(8,128)(2,1)S(1)}, u32[]{:S(2)}, u32[]{:S(2)}) %collective-permute-start.14) | collective-permute-done | bytes 442400 | tf_op jit(solution)/shard_map/ppermute | solution.py:61
  103.7 4.9 attend.2
  111.3 5.6 %collective-permute-done.17 = bf16[3,144,768]{2,1,0:T(8,128)(2,1)} collective-permute-done((bf16[3,144,768]{2,1,0:T(8,128)(2,1)}, bf16[3,144,768]{2,1,0:T(8,128)(2,1)}, u32[]{:S(2)}, u32[]{:S(2)}) %collective-permute-start.17) | collective-permute-done | bytes 663584 | tf_op jit(solution)/shard_map/ppermute | solution.py:61
  129.3 6.2 %multiply_convert_fusion.7 = (bf16[768,768]{1,0:T(8,128)(2,1)S(1)}, f32[768,768]{1,0:T(8,128)}) fusion(f32[768,1536]{1,0:T(8,128)S(1)} %fusion.110), kind=kLoop, calls=%fused_computation.96 | loop fusion | flops 38928384 | bytes 8257536 | tf_op jit(solution)/shard_map/convert_element_type | solution.py:337
  139.2 6.6 %collective-permute-done.26 = bf16[2,144,768]{2,1,0:T(8,128)(2,1)S(1)} collective-permute-done((bf16[2,144,768]{2,1,0:T(8,128)(2,1)S(1)}, bf16[2,144,768]{2,1,0:T(8,128)(2,1)S(1)}, u32[]{:S(2)}, u32[]{:S(2)}) %collective-permute-start.26) | collective-permute-done | bytes 442400 | tf_op jit(solution)/shard_map/ppermute | solution.py:61
  155.1 6.0 %multiply_convert_fusion.6 = (bf16[768,768]{1,0:T(8,128)(2,1)S(1)}, f32[768,768]{1,0:T(8,128)}) fusion(f32[768,1536]{1,0:T(8,128)S(1)} %fusion.112), kind=kLoop, calls=%fused_computation.83 | loop fusion | flops 38928384 | bytes 8257536 | tf_op jit(solution)/shard_map/convert_element_type | solution.py:337
  163.9 7.8 %collective-permute-done.31 = bf16[2,144,768]{2,1,0:T(8,128)(2,1)S(1)} collective-permute-done((bf16[2,144,768]{2,1,0:T(8,128)(2,1)S(1)}, bf16[2,144,768]{2,1,0:T(8,128)(2,1)S(1)}, u32[]{:S(2)}, u32[]{:S(2)}) %collective-permute-start.31) | collective-permute-done | bytes 442400 | tf_op jit(solution)/shard_map/ppermute | solution.py:61
  184.8 5.1 attend.3
  192.7 5.6 %collective-permute-done.34 = bf16[3,144,768]{2,1,0:T(8,128)(2,1)} collective-permute-done((bf16[3,144,768]{2,1,0:T(8,128)(2,1)}, bf16[3,144,768]{2,1,0:T(8,128)(2,1)}, u32[]{:S(2)}, u32[]{:S(2)}) %collective-permute-start.34) | collective-permute-done | bytes 663584 | tf_op jit(solution)/shard_map/ppermute | solution.py:61
  205.8 6.0 %multiply_convert_fusion.5 = (bf16[768,768]{1,0:T(8,128)(2,1)S(1)}, f32[768,768]{1,0:T(8,128)}) fusion(f32[768,1536]{1,0:T(8,128)S(1)} %fusion.114), kind=kLoop, calls=%fused_computation.70 | loop fusion | flops 38928384 | bytes 8257536 | tf_op jit(solution)/shard_map/convert_element_type | solution.py:337
  219.1 6.1 %multiply_convert_fusion.4 = (bf16[768,768]{1,0:T(8,128)(2,1)S(1)}, f32[768,768]{1,0:T(8,128)}) fusion(f32[768,1536]{1,0:T(8,128)S(1)} %fusion.116), kind=kLoop, calls=%fused_computation.57 | loop fusion | flops 38928384 | bytes 8257536 | tf_op jit(solution)/shard_map/convert_element_type | solution.py:337
  277.6 11.3 %collective-permute-done.44 = bf16[4,144,768]{2,1,0:T(8,128)(2,1)} collective-permute-done((bf16[4,144,768]{2,1,0:T(8,128)(2,1)S(1)}, bf16[4,144,768]{2,1,0:T(8,128)(2,1)}, u32[]{:S(2)}, u32[]{:S(2)}) %collective-permute-start.44) | collective-permute-done | bytes 884768 | tf_op jit(solution)/shard_map/ppermute | solution.py:61
  288.9 6.1 %attend_back.2 = bf16[384,2304]{1,0:T(8,128)(2,1)} custom-call(f32[12]{0:T(128)} %pad_maximum_fusion.54.slopes_ref, bf16[384,2304]{1,0:T(8,128)(2,1)} %convolution_convert_fusion.2.projected_ref, bf16[384,768]{1,0:T(8,128)(2,1)} %convolution_convert_fusion.15.context_grad_ref), custom_call_target="tpu_custom_call" | custom-call | flops 377487360 | bytes 4128768 | tf_op jit(solution)/shard_map/attend_back/pallas_call | solution.py:181
  300.6 6.9 %collective-permute-done.45 = bf16[4,144,768]{2,1,0:T(8,128)(2,1)} collective-permute-done((bf16[4,144,768]{2,1,0:T(8,128)(2,1)}, bf16[4,144,768]{2,1,0:T(8,128)(2,1)}, u32[]{:S(2)}, u32[]{:S(2)}) %collective-permute-start.45) | collective-permute-done | bytes 884768 | tf_op jit(solution)/shard_map/ppermute | solution.py:61
  319.8 5.4 collective-permute-done.48
  386.7 5.7 %attend_back.3 = bf16[384,2304]{1,0:T(8,128)(2,1)} custom-call(f32[12]{0:T(128)} %pad_maximum_fusion.54.slopes_ref, bf16[384,2304]{1,0:T(8,128)(2,1)} %convolution_convert_fusion.3.projected_ref, bf16[384,768]{1,0:T(8,128)(2,1)} %convolution_convert_fusion.14.context_grad_ref), custom_call_target="tpu_custom_call" | custom-call | flops 377487360 | bytes 4128768 | tf_op jit(solution)/shard_map/attend_back/pallas_call | solution.py:181
  399.1 10.5 %collective-permute-done.66.refs_14_ = bf16[288,768]{1,0:T(8,128)(2,1)} collective-permute-done((bf16[288,768]{1,0:T(8,128)(2,1)}, bf16[288,768]{1,0:T(8,128)(2,1)}, u32[]{:S(2)}, u32[]{:S(2)}) %collective-permute-start.66) | collective-permute-done | bytes 442400 | tf_op jit(solution)/shard_map/ppermute | solution.py:61
  410.0 4.2 collective-permute-start.67
  418.9 7.5 %collective-permute-done.68 = bf16[4,144,768]{2,1,0:T(8,128)(2,1)S(1)} collective-permute-done((bf16[4,144,768]{2,1,0:T(8,128)(2,1)S(1)}, bf16[4,144,768]{2,1,0:T(8,128)(2,1)S(1)}, u32[]{:S(2)}, u32[]{:S(2)}) %collective-permute-start.68) | collective-permute-done | bytes 884768 | tf_op jit(solution)/shard_map/ppermute | solution.py:61
  435.9 10.0 %collective-permute-done.71 = bf16[2,144,768]{2,1,0:T(8,128)(2,1)S(1)} collective-permute-done((bf16[2,144,768]{2,1,0:T(8,128)(2,1)S(1)}, bf16[2,144,768]{2,1,0:T(8,128)(2,1)S(1)}, u32[]{:S(2)}, u32[]{:S(2)}) %collective-permute-start.71) | collective-permute-done | bytes 442400 | tf_op jit(solution)/shard_map/ppermute | solution.py:61
  447.2 6.1 %collective-permute-done.70 = bf16[4,144,768]{2,1,0:T(8,128)(2,1)S(1)} collective-permute-done((bf16[4,144,768]{2,1,0:T(8,128)(2,1)S(1)}, bf16[4,144,768]{2,1,0:T(8,128)(2,1)S(1)}, u32[]{:S(2)}, u32[]{:S(2)}) %collective-permute-start.70) | collective-permute-done | bytes 884768 | tf_op jit(solution)/shard_map/ppermute | solution.py:61
  462.5 7.6 %collective-permute-done.75 = bf16[144,768]{1,0:T(8,128)(2,1)S(1)} collective-permute-done((bf16[144,768]{1,0:T(8,128)(2,1)S(1)}, bf16[144,768]{1,0:T(8,128)(2,1)S(1)}, u32[]{:S(2)}, u32[]{:S(2)}) %collective-permute-start.75) | collective-permute-done | bytes 221216 | tf_op jit(solution)/shard_map/ppermute | solution.py:61
  478.2 8.8 %collective-permute-done.80 = bf16[144,768]{1,0:T(8,128)(2,1)S(1)} collective-permute-done((bf16[144,768]{1,0:T(8,128)(2,1)S(1)}, bf16[144,768]{1,0:T(8,128)(2,1)S(1)}, u32[]{:S(2)}, u32[]{:S(2)}) %collective-permute-start.80) | collective-permute-done | bytes 221216 | tf_op jit(solution)/shard_map/ppermute | solution.py:61
  496.8 4.5 collective-permute-done.86
  520.6 5.1 collective-permute-start.95
  539.9 7.7 %settle.1 = (f32[768,2,768]{2,1,0:T(2,128)}, f32[768,768]{1,0:T(8,128)}) custom-call(s32[9]{0:T(128)} %pad_add_fusion.flags_ref, bf16[288,768]{1,0:T(8,128)(2,1)} %copy-done.43, bf16[288,768]{1,0:T(8,128)(2,1)} %collective-permute-done.87.refs_1_, bf16[288,768]{1,0:T(8,128)(2,1)} %copy-done.106, bf16[288,768]{1,0:T(8,128)(2,1)} %collective-permute-done.96.refs_3_, ...), custom_call_target="tpu_custom_call" | custom-call | tf_op jit(solution)/shard_map/settle/pallas_call | solution.py:225
  (782 shorter events, 317.1 us)
Async XLA Ops:
  38.1 20.9 %collective-permute-start.9 = (bf16[2,144,768]{2,1,0:T(8,128)(2,1)S(1)}, bf16[2,144,768]{2,1,0:T(8,128)(2,1)S(1)}, u32[]{:S(2)}, u32[]{:S(2)}) collective-permute-start(bf16[2,144,768]{2,1,0:T(8,128)(2,1)S(1)} %pad_maximum_fusion.40), channel_id=1, source_target_pairs={{0,2},{1,3},{2,0},{3,1},{4,6},{5,7},{6,4},{7,5},{8,10},{9,11},{10,... | collective-permute-start | bytes 1327112 | tf_op jit(solution)/shard_map/ppermute | solution.py:61
  38.2 20.8 %collective-permute-start.7 = (bf16[3,96,768]{2,1,0:T(8,128)(2,1)S(1)}, bf16[3,96,768]{2,1,0:T(8,128)(2,1)S(1)}, u32[]{:S(2)}, u32[]{:S(2)}) collective-permute-start(bf16[3,96,768]{2,1,0:T(8,128)(2,1)S(1)} %pad_maximum_fusion.39), channel_id=1, source_target_pairs={{0,4},{1,5},{2,6},{3,7},{4,0},{5,1},{6,2},{7,3},{8,12},{9,13},{10,... | collective-permute-start | bytes 1327112 | tf_op jit(solution)/shard_map/ppermute | solution.py:61
  39.5 19.6 %collective-permute-start.8 = (bf16[3,96,768]{2,1,0:T(8,128)(2,1)S(1)}, bf16[3,96,768]{2,1,0:T(8,128)(2,1)S(1)}, u32[]{:S(2)}, u32[]{:S(2)}) collective-permute-start(bf16[3,96,768]{2,1,0:T(8,128)(2,1)S(1)} %pad_maximum_fusion.39), channel_id=1, source_target_pairs={{0,8},{1,9},{2,10},{3,11},{4,12},{5,13},{6,14},{7,15},{8,0},{9,1},... | collective-permute-start | bytes 1327112 | tf_op jit(solution)/shard_map/ppermute | solution.py:61
  59.1 24.7 %collective-permute-start.12 = (bf16[3,144,768]{2,1,0:T(8,128)(2,1)S(1)}, bf16[3,144,768]{2,1,0:T(8,128)(2,1)}, u32[]{:S(2)}, u32[]{:S(2)}) collective-permute-start(bf16[3,144,768]{2,1,0:T(8,128)(2,1)S(1)} %pad_maximum_fusion.33), channel_id=1, source_target_pairs={{0,4},{1,5},{2,6},{3,7},{4,0},{5,1},{6,2},{7,3},{8,12},{9,13},{10,... | collective-permute-start | bytes 1990664 | tf_op jit(solution)/shard_map/ppermute | solution.py:61
  60.2 23.6 %collective-permute-start.13 = (bf16[3,144,768]{2,1,0:T(8,128)(2,1)S(1)}, bf16[3,144,768]{2,1,0:T(8,128)(2,1)S(1)}, u32[]{:S(2)}, u32[]{:S(2)}) collective-permute-start(bf16[3,144,768]{2,1,0:T(8,128)(2,1)S(1)} %pad_maximum_fusion.33), channel_id=1, source_target_pairs={{0,8},{1,9},{2,10},{3,11},{4,12},{5,13},{6,14},{7,15},{8,0},{9,1},... | collective-permute-start | bytes 1990664 | tf_op jit(solution)/shard_map/ppermute | solution.py:61
  61.5 22.3 %collective-permute-start.14 = (bf16[2,144,768]{2,1,0:T(8,128)(2,1)S(1)}, bf16[2,144,768]{2,1,0:T(8,128)(2,1)S(1)}, u32[]{:S(2)}, u32[]{:S(2)}) collective-permute-start(bf16[2,144,768]{2,1,0:T(8,128)(2,1)S(1)} %pad_maximum_fusion.41), channel_id=1, source_target_pairs={{0,2},{1,3},{2,0},{3,1},{4,6},{5,7},{6,4},{7,5},{8,10},{9,11},{10,... | collective-permute-start | bytes 1327112 | tf_op jit(solution)/shard_map/ppermute | solution.py:61
  61.6 22.2 %collective-permute-start.11 = (bf16[3,96,768]{2,1,0:T(8,128)(2,1)S(1)}, bf16[3,96,768]{2,1,0:T(8,128)(2,1)S(1)}, u32[]{:S(2)}, u32[]{:S(2)}) collective-permute-start(bf16[3,96,768]{2,1,0:T(8,128)(2,1)S(1)} %collective-permute-done.7), channel_id=1, source_target_pairs={{0,8},{1,9},{2,10},{3,11},{4,12},{5,13},{6,14},{7,15},{8,0},{9,1},... | collective-permute-start | bytes 1327112 | tf_op jit(solution)/shard_map/ppermute | solution.py:61
  92.7 18.6 %collective-permute-start.18 = (bf16[3,144,768]{2,1,0:T(8,128)(2,1)S(1)}, bf16[3,144,768]{2,1,0:T(8,128)(2,1)}, u32[]{:S(2)}, u32[]{:S(2)}) collective-permute-start(bf16[3,144,768]{2,1,0:T(8,128)(2,1)S(1)} %pad_maximum_fusion.34), channel_id=1, source_target_pairs={{0,4},{1,5},{2,6},{3,7},{4,0},{5,1},{6,2},{7,3},{8,12},{9,13},{10,... | collective-permute-start | bytes 1990664 | tf_op jit(solution)/shard_map/ppermute | solution.py:61
  93.0 18.3 %collective-permute-start.19 = (bf16[3,144,768]{2,1,0:T(8,128)(2,1)S(1)}, bf16[3,144,768]{2,1,0:T(8,128)(2,1)}, u32[]{:S(2)}, u32[]{:S(2)}) collective-permute-start(bf16[3,144,768]{2,1,0:T(8,128)(2,1)S(1)} %pad_maximum_fusion.34), channel_id=1, source_target_pairs={{0,8},{1,9},{2,10},{3,11},{4,12},{5,13},{6,14},{7,15},{8,0},{9,1},... | collective-permute-start | bytes 1990664 | tf_op jit(solution)/shard_map/ppermute | solution.py:61
  94.1 22.7 %collective-permute-start.17 = (bf16[3,144,768]{2,1,0:T(8,128)(2,1)}, bf16[3,144,768]{2,1,0:T(8,128)(2,1)}, u32[]{:S(2)}, u32[]{:S(2)}) collective-permute-start(bf16[3,144,768]{2,1,0:T(8,128)(2,1)} %collective-permute-done.12), channel_id=1, source_target_pairs={{0,8},{1,9},{2,10},{3,11},{4,12},{5,13},{6,14},{7,15},{8,0},{9,1},... | collective-permute-start | bytes 1990664 | tf_op jit(solution)/shard_map/ppermute | solution.py:61
  117.9 27.8 %collective-permute-start.24 = (bf16[3,96,768]{2,1,0:T(8,128)(2,1)S(1)}, bf16[3,96,768]{2,1,0:T(8,128)(2,1)S(1)}, u32[]{:S(2)}, u32[]{:S(2)}) collective-permute-start(bf16[3,96,768]{2,1,0:T(8,128)(2,1)S(1)} %pad_maximum_fusion.42), channel_id=1, source_target_pairs={{0,4},{1,5},{2,6},{3,7},{4,0},{5,1},{6,2},{7,3},{8,12},{9,13},{10,... | collective-permute-start | bytes 1327112 | tf_op jit(solution)/shard_map/ppermute | solution.py:61
  118.7 27.0 %collective-permute-start.25 = (bf16[3,96,768]{2,1,0:T(8,128)(2,1)S(1)}, bf16[3,96,768]{2,1,0:T(8,128)(2,1)S(1)}, u32[]{:S(2)}, u32[]{:S(2)}) collective-permute-start(bf16[3,96,768]{2,1,0:T(8,128)(2,1)S(1)} %pad_maximum_fusion.42), channel_id=1, source_target_pairs={{0,8},{1,9},{2,10},{3,11},{4,12},{5,13},{6,14},{7,15},{8,0},{9,1},... | collective-permute-start | bytes 1327112 | tf_op jit(solution)/shard_map/ppermute | solution.py:61
  124.6 21.1 %collective-permute-start.26 = (bf16[2,144,768]{2,1,0:T(8,128)(2,1)S(1)}, bf16[2,144,768]{2,1,0:T(8,128)(2,1)S(1)}, u32[]{:S(2)}, u32[]{:S(2)}) collective-permute-start(bf16[2,144,768]{2,1,0:T(8,128)(2,1)S(1)} %pad_maximum_fusion.43), channel_id=1, source_target_pairs={{0,2},{1,3},{2,0},{3,1},{4,6},{5,7},{6,4},{7,5},{8,10},{9,11},{10,... | collective-permute-start | bytes 1327112 | tf_op jit(solution)/shard_map/ppermute | solution.py:61
  124.8 20.9 %collective-permute-start.23 = (bf16[3,144,768]{2,1,0:T(8,128)(2,1)}, bf16[3,144,768]{2,1,0:T(8,128)(2,1)S(1)}, u32[]{:S(2)}, u32[]{:S(2)}) collective-permute-start(bf16[3,144,768]{2,1,0:T(8,128)(2,1)} %collective-permute-done.18), channel_id=1, source_target_pairs={{0,8},{1,9},{2,10},{3,11},{4,12},{5,13},{6,14},{7,15},{8,0},{9,1},... | collective-permute-start | bytes 1990664 | tf_op jit(solution)/shard_map/ppermute | solution.py:61
  146.7 24.9 %collective-permute-start.29 = (bf16[3,144,768]{2,1,0:T(8,128)(2,1)S(1)}, bf16[3,144,768]{2,1,0:T(8,128)(2,1)}, u32[]{:S(2)}, u32[]{:S(2)}) collective-permute-start(bf16[3,144,768]{2,1,0:T(8,128)(2,1)S(1)} %pad_maximum_fusion.35), channel_id=1, source_target_pairs={{0,4},{1,5},{2,6},{3,7},{4,0},{5,1},{6,2},{7,3},{8,12},{9,13},{10,... | collective-permute-start | bytes 1990664 | tf_op jit(solution)/shard_map/ppermute | solution.py:61
  147.9 23.8 %collective-permute-start.30 = (bf16[3,144,768]{2,1,0:T(8,128)(2,1)S(1)}, bf16[3,144,768]{2,1,0:T(8,128)(2,1)S(1)}, u32[]{:S(2)}, u32[]{:S(2)}) collective-permute-start(bf16[3,144,768]{2,1,0:T(8,128)(2,1)S(1)} %pad_maximum_fusion.35), channel_id=1, source_target_pairs={{0,8},{1,9},{2,10},{3,11},{4,12},{5,13},{6,14},{7,15},{8,0},{9,1},... | collective-permute-start | bytes 1990664 | tf_op jit(solution)/shard_map/ppermute | solution.py:61
  149.1 22.5 %collective-permute-start.31 = (bf16[2,144,768]{2,1,0:T(8,128)(2,1)S(1)}, bf16[2,144,768]{2,1,0:T(8,128)(2,1)S(1)}, u32[]{:S(2)}, u32[]{:S(2)}) collective-permute-start(bf16[2,144,768]{2,1,0:T(8,128)(2,1)S(1)} %pad_maximum_fusion.44), channel_id=1, source_target_pairs={{0,2},{1,3},{2,0},{3,1},{4,6},{5,7},{6,4},{7,5},{8,10},{9,11},{10,... | collective-permute-start | bytes 1327112 | tf_op jit(solution)/shard_map/ppermute | solution.py:61
  174.2 18.6 %collective-permute-start.35 = (bf16[3,144,768]{2,1,0:T(8,128)(2,1)S(1)}, bf16[3,144,768]{2,1,0:T(8,128)(2,1)}, u32[]{:S(2)}, u32[]{:S(2)}) collective-permute-start(bf16[3,144,768]{2,1,0:T(8,128)(2,1)S(1)} %pad_maximum_fusion.36), channel_id=1, source_target_pairs={{0,4},{1,5},{2,6},{3,7},{4,0},{5,1},{6,2},{7,3},{8,12},{9,13},{10,... | collective-permute-start | bytes 1990664 | tf_op jit(solution)/shard_map/ppermute | solution.py:61
  174.4 18.3 %collective-permute-start.36 = (bf16[3,144,768]{2,1,0:T(8,128)(2,1)S(1)}, bf16[3,144,768]{2,1,0:T(8,128)(2,1)}, u32[]{:S(2)}, u32[]{:S(2)}) collective-permute-start(bf16[3,144,768]{2,1,0:T(8,128)(2,1)S(1)} %pad_maximum_fusion.36), channel_id=1, source_target_pairs={{0,8},{1,9},{2,10},{3,11},{4,12},{5,13},{6,14},{7,15},{8,0},{9,1},... | collective-permute-start | bytes 1990664 | tf_op jit(solution)/shard_map/ppermute | solution.py:61
  174.9 23.5 %collective-permute-start.34 = (bf16[3,144,768]{2,1,0:T(8,128)(2,1)}, bf16[3,144,768]{2,1,0:T(8,128)(2,1)}, u32[]{:S(2)}, u32[]{:S(2)}) collective-permute-start(bf16[3,144,768]{2,1,0:T(8,128)(2,1)} %collective-permute-done.29), channel_id=1, source_target_pairs={{0,8},{1,9},{2,10},{3,11},{4,12},{5,13},{6,14},{7,15},{8,0},{9,1},... | collective-permute-start | bytes 1990664 | tf_op jit(solution)/shard_map/ppermute | solution.py:61
  237.6 21.3 %collective-permute-start.42 = (bf16[384,768]{1,0:T(8,128)(2,1)S(1)}, bf16[384,768]{1,0:T(8,128)(2,1)S(1)}, u32[]{:S(2)}, u32[]{:S(2)}) collective-permute-start(bf16[384,768]{1,0:T(8,128)(2,1)S(1)} %get-tuple-element.660), channel_id=1, source_target_pairs={{0,16},{1,17},{2,18},{3,19},{4,20},{5,21},{6,22},{7,23},{8,24},{9,... | collective-permute-start | bytes 1769480 | tf_op jit(solution)/shard_map/ppermute | solution.py:61
  270.1 18.8 %collective-permute-start.44 = (bf16[4,144,768]{2,1,0:T(8,128)(2,1)S(1)}, bf16[4,144,768]{2,1,0:T(8,128)(2,1)}, u32[]{:S(2)}, u32[]{:S(2)}) collective-permute-start(bf16[4,144,768]{2,1,0:T(8,128)(2,1)S(1)} %bitcast.563), channel_id=1, source_target_pairs={{0,8},{1,9},{2,10},{3,11},{4,12},{5,13},{6,14},{7,15},{8,0},{9,1},... | collective-permute-start | bytes 2654216 | tf_op jit(solution)/shard_map/ppermute | solution.py:61
  271.6 29.0 %collective-permute-start.46 = (bf16[4,144,768]{2,1,0:T(8,128)(2,1)}, bf16[4,144,768]{2,1,0:T(8,128)(2,1)}, u32[]{:S(2)}, u32[]{:S(2)}) collective-permute-start(bf16[4,144,768]{2,1,0:T(8,128)(2,1)} %add_convert_fusion.13), channel_id=1, source_target_pairs={{0,4},{1,5},{2,6},{3,7},{4,0},{5,1},{6,2},{7,3},{8,12},{9,13},{10,... | collective-permute-start | bytes 2654216 | tf_op jit(solution)/shard_map/ppermute | solution.py:61
  317.7 18.3 %collective-permute-start.52 = (bf16[4,144,768]{2,1,0:T(8,128)(2,1)S(1)}, bf16[4,144,768]{2,1,0:T(8,128)(2,1)S(1)}, u32[]{:S(2)}, u32[]{:S(2)}) collective-permute-start(bf16[4,144,768]{2,1,0:T(8,128)(2,1)S(1)} %add_convert_fusion.11), channel_id=1, source_target_pairs={{0,4},{1,5},{2,6},{3,7},{4,0},{5,1},{6,2},{7,3},{8,12},{9,13},{10,... | collective-permute-start | bytes 2654216 | tf_op jit(solution)/shard_map/ppermute | solution.py:61
  329.6 21.0 %collective-permute-start.54 = (bf16[4,112,768]{2,1,0:T(8,128)(2,1)S(1)}, bf16[4,112,768]{2,1,0:T(8,128)(2,1)S(1)}, u32[]{:S(2)}, u32[]{:S(2)}) collective-permute-start(bf16[4,112,768]{2,1,0:T(8,128)(2,1)S(1)} %get-tuple-element.712), channel_id=1, source_target_pairs={{0,8},{1,9},{2,10},{3,11},{4,12},{5,13},{6,14},{7,15},{8,0},{9,1},... | collective-permute-start | bytes 2064392 | tf_op jit(solution)/shard_map/ppermute | solution.py:61
  355.8 25.2 %collective-permute-start.60 = (bf16[4,144,768]{2,1,0:T(8,128)(2,1)S(1)}, bf16[4,144,768]{2,1,0:T(8,128)(2,1)S(1)}, u32[]{:S(2)}, u32[]{:S(2)}) collective-permute-start(bf16[4,144,768]{2,1,0:T(8,128)(2,1)S(1)} %bitcast.561), channel_id=1, source_target_pairs={{0,8},{1,9},{2,10},{3,11},{4,12},{5,13},{6,14},{7,15},{8,0},{9,1},... | collective-permute-start | bytes 2654216 | tf_op jit(solution)/shard_map/ppermute | solution.py:61
  376.1 23.0 %collective-permute-start.64 = (bf16[4,144,768]{2,1,0:T(8,128)(2,1)}, bf16[4,144,768]{2,1,0:T(8,128)(2,1)}, u32[]{:S(2)}, u32[]{:S(2)}) collective-permute-start(bf16[4,144,768]{2,1,0:T(8,128)(2,1)} %add_convert_fusion.9), channel_id=1, source_target_pairs={{0,4},{1,5},{2,6},{3,7},{4,0},{5,1},{6,2},{7,3},{8,12},{9,13},{10,... | collective-permute-start | bytes 2654216 | tf_op jit(solution)/shard_map/ppermute | solution.py:61
  414.5 47.0 %collective-permute-start.77 = (bf16[288,768]{1,0:T(8,128)(2,1)}, bf16[288,768]{1,0:T(8,128)(2,1)S(1)}, u32[]{:S(2)}, u32[]{:S(2)}) collective-permute-start(bf16[288,768]{1,0:T(8,128)(2,1)} %pad_maximum_fusion.45.refs_12_), channel_id=1, source_target_pairs={{0,16},{1,17},{2,18},{3,19},{4,20},{5,21},{6,22},{7,23},{8,24},{9,... | collective-permute-start | bytes 1327112 | tf_op jit(solution)/shard_map/ppermute | solution.py:521
  416.1 41.7 %collective-permute-start.76 = (bf16[288,768]{1,0:T(8,128)(2,1)S(1)}, bf16[288,768]{1,0:T(8,128)(2,1)S(1)}, u32[]{:S(2)}, u32[]{:S(2)}) collective-permute-start(bf16[288,768]{1,0:T(8,128)(2,1)S(1)} %copy-done.99), channel_id=1, source_target_pairs={{0,8},{1,9},{2,10},{3,11},{4,12},{5,13},{6,14},{7,15},{8,0},{9,1},... | collective-permute-start | bytes 1327112 | tf_op jit(solution)/shard_map/ppermute | solution.py:61
  429.1 27.0 %collective-permute-start.69 = (bf16[2,4,112,768]{3,2,1,0:T(8,128)(2,1)S(1)}, bf16[2,4,112,768]{3,2,1,0:T(8,128)(2,1)S(1)}, u32[]{:S(2)}, u32[]{:S(2)}) collective-permute-start(bf16[2,4,112,768]{3,2,1,0:T(8,128)(2,1)S(1)} %stack.282), channel_id=1, source_target_pairs={{0,8},{1,9},{2,10},{3,11},{4,12},{5,13},{6,14},{7,15},{8,0},{9,1},... | collective-permute-start | bytes 4128776 | tf_op jit(solution)/shard_map/ppermute | solution.py:61
  431.5 21.7 %collective-permute-start.70 = (bf16[4,144,768]{2,1,0:T(8,128)(2,1)S(1)}, bf16[4,144,768]{2,1,0:T(8,128)(2,1)S(1)}, u32[]{:S(2)}, u32[]{:S(2)}) collective-permute-start(bf16[4,144,768]{2,1,0:T(8,128)(2,1)S(1)} %add_convert_fusion.8), channel_id=1, source_target_pairs={{0,4},{1,5},{2,6},{3,7},{4,0},{5,1},{6,2},{7,3},{8,12},{9,13},{10,... | collective-permute-start | bytes 2654216 | tf_op jit(solution)/shard_map/ppermute | solution.py:61
  520.6 27.0 %collective-permute-start.95 = (bf16[4,96,768]{2,1,0:T(8,128)(2,1)S(1)}, bf16[4,96,768]{2,1,0:T(8,128)(2,1)S(1)}, u32[]{:S(2)}, u32[]{:S(2)}) collective-permute-start(bf16[4,96,768]{2,1,0:T(8,128)(2,1)S(1)} %get-tuple-element.759), channel_id=1, source_target_pairs={{16,0},{17,1},{18,2},{19,3},{20,4},{21,5},{22,6},{23,7},{24,8},{25... | collective-permute-start | bytes 1769480 | tf_op jit(solution)/shard_map/ppermute | solution.py:521
  (232 other events, 2241.2 us)

commit v9 on v8

--- a/solution.py
+++ b/solution.py
@@ -453,7 +453,7 @@
         return full[:2].reshape(-1, features), full[2]
 
     a0, p0 = far(a0), near(p0)
-    a0, p0, q0 = together(a0, p0, q0)
+    a0, p0, q0, norms, seed = together(a0, p0, q0, norms, seed)
     a0, p0, q0 = first(a0), far(p0), near(q0)
     a0, p0, q0, a1 = together(a0, p0, q0, a1)
     a0, p0, q0, a1 = second(a0), first(p0), far(q0), near(a1)
@@ -527,50 +527,50 @@
     mixed_all, grad_p, p1 = together(mixed_all, grad_p, p1)
 
     p1_own, p1_half, p1_a, p1_b = reduce_open(p1)
-    terms = dot(grad_p, feed_p1[0], 1, 0)
     grad_q = feed_backward(mixed_all, feed_q1, gated_q1)
-    terms = terms + dot(grad_q, feed_q1[0], 1, 0)
+    mixed_all, grad_p, grad_q, p1_a = together(mixed_all, grad_p, grad_q, p1_a)
+
+    p1_own, p1_c = reduce_turn((p1_own, p1_half, p1_a))
     q1 = feed_terms(*feed_weight_grads(mixed_all, all1, grad_q, hidden_q1))
+    terms = dot(grad_p, feed_p1[0], 1, 0) + dot(grad_q, feed_q1[0], 1, 0)
     layer_out = give(middle_low, final_low)
-    terms, q1, p1_a, layer_out = together(terms, q1, p1_a, layer_out)
-
-    p1_own, p1_c = reduce_turn((p1_own, p1_half, p1_a))
+    terms, q1, p1_b, layer_out = together(terms, q1, p1_b, layer_out)
+
+    q1_own, q1_half, q1_a, q1_b = reduce_open(q1)
     first_grad = join_rows(terms) + second_grad
     sum_grad, gain_one1, offset_one1 = norm_backward(sum1, norms[1][0], norms[1][1], first_grad)
     context_grad, out = context_backward(sum_grad, attn1, context1)
-    context_grad, out, q1, p1_b = together(context_grad, out, q1, p1_b)
-
-    q1_own, q1_half, q1_a, q1_b = reduce_open(q1)
+    context_grad, out, p1_c, q1_a = together(context_grad, out, p1_c, q1_a)
+
+    q1_own, q1_c = reduce_turn((q1_own, q1_half, q1_a))
     projected_grad = attend_back(projected1, context_grad, slopes, seqs)
     qkv = dot(projected_grad, middle_low, 0, 0).astype(BF16)
     a1 = attn_terms(qkv, out, [gain_one1, offset_one1, gain_two1, offset_two1])
-    projected_grad, a1, q1_a, p1_c = together(projected_grad, a1, q1_a, p1_c)
+    projected_grad, a1, q1_b = together(projected_grad, a1, q1_b)
 
     a1 = attn_swap(a1)
-    q1_own, q1_c = reduce_turn((q1_own, q1_half, q1_a))
     p1 = reduce_near(p1_own, p1_c, p1_b)
     middle_grad = dot(projected_grad, attn1[0], 1, 0) + sum_grad
     second_grad, gain_two0, offset_two0 = norm_backward(total0, norms[0][2], norms[0][3], middle_grad)
-    mixed_low = second_grad.astype(BF16)
-    mixed_low, a1, q1_b, p1 = together(mixed_low, a1, q1_b, p1)
+    mixed_low, a1, q1_c, p1 = together(second_grad.astype(BF16), a1, q1_c, p1)
 
     mixed_all = both_rows(mixed_low)
     a1_own, a1_half, a1_a, a1_b = reduce_open(attn_pieces(a1))
     p1 = reduce_far(p1)
+    q1 = reduce_near(q1_own, q1_c, q1_b)
     grad_p = feed_backward(mixed_all, feed_p0, gated_p0)
-    mixed_all, grad_p, a1_a, q1_c, p1 = together(mixed_all, grad_p, a1_a, q1_c, p1)
+    mixed_all, grad_p, a1_a, p1, q1 = together(mixed_all, grad_p, a1_a, p1, q1)
 
     a1_own, a1_c = reduce_turn((a1_own, a1_half, a1_a))
-    q1 = reduce_near(q1_own, q1_c, q1_b)
+    q1 = reduce_far(q1)
     p0 = feed_terms(*feed_weight_grads(mixed_all, all0, grad_p, hidden_p0))
     terms = dot(grad_p, feed_p0[0], 1, 0)
     mixed_all, terms, p0, a1_b, q1 = together(mixed_all, terms, p0, a1_b, q1)
 
     p0_own, p0_half, p0_a, p0_b = reduce_open(p0)
-    q1 = reduce_far(q1)
     grad_q = feed_backward(mixed_all, feed_q0, gated_q0)
     terms = terms + dot(grad_q, feed_q0[0], 1, 0)
-    terms, grad_q, p0_a, a1_c, q1 = together(terms, grad_q, p0_a, a1_c, q1)
+    terms, grad_q, p0_a, a1_c = together(terms, grad_q, p0_a, a1_c)
 
     p0_own, p0_c = reduce_turn((p0_own, p0_half, p0_a))
     a1 = reduce_near(a1_own, a1_c, a1_b)
@@ -593,35 +593,36 @@
     a0 = attn_swap(a0)
     q0_own, q0_c = reduce_turn((q0_own, q0_half, q0_a))
     start_grad = dot(projected_grad, attn0[0], 1, 0) + sum_grad
-    start_grad, a0, q0_b = together(start_grad, a0, q0_b)
+    start_grad, a0, q0_b, q0_c = together(start_grad, a0, q0_b, q0_c)
 
     a0 = attn_pieces(a0)
     a0_got = exchange(jnp.stack(a0[2:]), dp_masks=SECOND)
     p0 = reduce_near(p0_own, p0_c, p0_b)
     input_grad = give(start_grad, middle_grad)
-    a0_got, q0_c, p0, input_grad = together(a0_got, q0_c, p0, input_grad)
+    a0_got, p0, input_grad = together(a0_got, p0, input_grad)
 
     a0_c = exchange(total_low(a0[1], a0_got[1]), dp_masks=FIRST)
     q0 = reduce_near(q0_own, q0_c, q0_b)
     p0 = reduce_far(p0)
     late_third = exchange(late_first, dp_masks=SECOND)
-    late_got = [hand_over(late, 0), hand_over(late_first, 0)]
-    a0_c, q0, p0, late_third, late_got = together(a0_c, q0, p0, late_third, late_got)
+    a0_c, q0, p0, late_third = together(a0_c, q0, p0, late_third)
 
     a0 = reduce_near(a0[0], a0_got[0], a0_c)
     q0 = reduce_far(q0)
     attn_late = reduce_last(a1)
     attn = attn_late[:-NORM_ROWS]
     late_attn = [attn, exchange(attn, dp_masks=FIRST), exchange(attn, dp_masks=SECOND)]
-    late_got += [hand_over(late_second, 0), hand_over(late_third, 0)]
-    a0, q0, late_attn, late_got = together(a0, q0, late_attn, late_got)
+    late_got = hand_over(jnp.stack([late, late_first, late_second, late_third]), 0)
+    a0, q0, late_attn = together(a0, q0, late_attn)
 
     a0 = reduce_far(a0)
     late_attn.append(exchange(late_attn[1], dp_masks=SECOND))
     feed = jnp.concatenate([reduce_last(p0), reduce_last(q0)])
     feed_first = exchange(feed, dp_masks=FIRST)
     feed_got = [hand_over(feed, 1)]
-    a0, late_attn, feed, feed_first, feed_got = together(a0, late_attn, feed, feed_first, feed_got)
+    a0, late_attn, feed, feed_first, feed_got, late_got = together(
+        a0, late_attn, feed, feed_first, feed_got, late_got
+    )
 
     attn_early = reduce_last(a0)
     attn = attn_early[:-NORM_ROWS]
@@ -646,7 +647,7 @@
         [is_first.astype(jnp.int32)[None]] + [jnp.bitwise_xor(in_plane, order) for order in orders]
     )
     grad_in, grad_down = settle(
-        feed_early + feed_got + late_got + feed_late, flags, FEED_CHUNKS, 3, unit_part
+        feed_early + feed_got + [late_got[e] for e in range(PLANE)] + feed_late, flags, FEED_CHUNKS, 3, unit_part
     )
     parts = [jnp.where(is_first, attn_early_all, attn_late_got), jnp.where(is_first, attn_got, attn_late_all)]
     attn_total = jnp.stack(

time: 562 us -> 576 us (1.025)
  waiting for transfers between devices: 186 us -> 203 us
  starting transfers between devices: 110 us -> 99.6 us
  other arithmetic: 90.6 us -> 96.5 us
    ppermute x89, waiting for transfers between devices: 186 us -> 203 us  [exchange(): return lax.ppermute(block, AXES, pairs)]
    ppermute x89, starting transfers between devices: 87.6 us -> 80 us  [exchange(): return lax.ppermute(block, AXES, pairs)]
    ppermute x10 -> x7, starting transfers between devices: 22.5 us -> 19.6 us  [hand_over(): return lax.ppermute(block, AXES, pairs)]
    another operation x18 -> x20, other arithmetic: 13.1 us -> 15.2 us  [assemble(): jnp.stack([jnp.concatenate([own[None], r]) for own, r in zip(chunk['own']...]
    unnamed x333 -> x323, local copies, waits for them, and re-layouts: 22.3 us -> 21.1 us
  transfers between devices with their start and end apart: 99 -> 96, of which waited for: 40 -> 39; matrix products, arithmetic and copies ran while one was open for 28% -> 28% of each run, Pallas kernels for 5% -> 5%
where the time goes in v9:
time: 576 us; the launch traced here: 565 us
  waiting for transfers between devices  203 us (35%)
  starting transfers between devices  99.6 us (17%)
  other arithmetic  96.5 us (17%)
  matrix products  64.2 us (11%)
  local copies, waits for them, and re-layouts  57.6 us (10%)
  Pallas kernels  29.6 us (5%)
  between operations  14.7 us (3%)
    ppermute x89, waiting for transfers between devices, exchange(): return lax.ppermute(block, AXES, pairs)  203 us
    ppermute x89, starting transfers between devices, exchange(): return lax.ppermute(block, AXES, pairs)  80 us
    dot_general x36, matrix products, dot(): lax.dot_general(a, b, (((ca,), (cb,)), ((), ())), preferred_element_type=...  64.2 us
    convert_element_type x4, other arithmetic, feed_forward(): hidden = gelu_product(gate_part, up_part).astype(BF16)  22.6 us
    unnamed x323, local copies, waits for them, and re-layouts  21.1 us
    ppermute x7, starting transfers between devices, hand_over(): return lax.ppermute(block, AXES, pairs)  19.6 us
    another operation x20, other arithmetic, assemble(): jnp.stack([jnp.concatenate([own[None], r]) for own, r in zip(chunk['own']...  15.2 us
    convert_element_type x26, other arithmetic, total_low(): return sum((part.astype(F32) for part in parts)).astype(BF16)  14.7 us
  transfers between devices with their start and end apart: 96, of which 39 were waited for; matrix products, arithmetic and copies ran while one was open for 28% of the time, Pallas kernels for 5%

profile of v9, /device:TPU:1, one launch (start us, length us, event | category | flops | bytes accessed | tf_op | source)
XLA Modules:
  0.0 565.4 jit_solution(15286301083994237525)
XLA Ops:
  14.1 5.6 copy.70
  36.1 8.8 %collective-permute-done.2 = bf16[2,96,768]{2,1,0:T(8,128)(2,1)S(1)} collective-permute-done((bf16[2,96,768]{2,1,0:T(8,128)(2,1)S(1)}, bf16[2,96,768]{2,1,0:T(8,128)(2,1)S(1)}, u32[]{:S(2)}, u32[]{:S(2)}) %collective-permute-start.2) | collective-permute-done | bytes 294944 | tf_op jit(solution)/shard_map/ppermute | solution.py:61
  51.6 6.2 %collective-permute-done.10 = bf16[144,768]{1,0:T(8,128)(2,1)S(1)} collective-permute-done((bf16[144,768]{1,0:T(8,128)(2,1)S(1)}, bf16[144,768]{1,0:T(8,128)(2,1)S(1)}, u32[]{:S(2)}, u32[]{:S(2)}) %collective-permute-start.10) | collective-permute-done | bytes 221216 | tf_op jit(solution)/shard_map/ppermute | solution.py:61
  57.8 8.3 %collective-permute-done.9 = bf16[2,144,768]{2,1,0:T(8,128)(2,1)S(1)} collective-permute-done((bf16[2,144,768]{2,1,0:T(8,128)(2,1)S(1)}, bf16[2,144,768]{2,1,0:T(8,128)(2,1)S(1)}, u32[]{:S(2)}, u32[]{:S(2)}) %collective-permute-start.9) | collective-permute-done | bytes 442400 | tf_op jit(solution)/shard_map/ppermute | solution.py:61
  72.6 6.7 %collective-permute-done.15 = bf16[96,768]{1,0:T(8,128)(2,1)S(1)} collective-permute-done((bf16[96,768]{1,0:T(8,128)(2,1)S(1)}, bf16[96,768]{1,0:T(8,128)(2,1)S(1)}, u32[]{:S(2)}, u32[]{:S(2)}) %collective-permute-start.15) | collective-permute-done | bytes 147488 | tf_op jit(solution)/shard_map/ppermute | solution.py:61
  79.2 11.9 %collective-permute-done.14 = bf16[2,144,768]{2,1,0:T(8,128)(2,1)S(1)} collective-permute-done((bf16[2,144,768]{2,1,0:T(8,128)(2,1)S(1)}, bf16[2,144,768]{2,1,0:T(8,128)(2,1)S(1)}, u32[]{:S(2)}, u32[]{:S(2)}) %collective-permute-start.14) | collective-permute-done | bytes 442400 | tf_op jit(solution)/shard_map/ppermute | solution.py:61
  116.4 5.7 %collective-permute-done.17 = bf16[3,144,768]{2,1,0:T(8,128)(2,1)} collective-permute-done((bf16[3,144,768]{2,1,0:T(8,128)(2,1)}, bf16[3,144,768]{2,1,0:T(8,128)(2,1)}, u32[]{:S(2)}, u32[]{:S(2)}) %collective-permute-start.17) | collective-permute-done | bytes 663584 | tf_op jit(solution)/shard_map/ppermute | solution.py:61
  135.3 6.2 %multiply_convert_fusion.7 = (bf16[768,768]{1,0:T(8,128)(2,1)S(1)}, f32[768,768]{1,0:T(8,128)}) fusion(f32[768,1536]{1,0:T(8,128)S(1)} %fusion.101), kind=kLoop, calls=%fused_computation.96 | loop fusion | flops 38928384 | bytes 8257536 | tf_op jit(solution)/shard_map/convert_element_type | solution.py:337
  142.6 10.2 %collective-permute-done.26 = bf16[2,144,768]{2,1,0:T(8,128)(2,1)S(1)} collective-permute-done((bf16[2,144,768]{2,1,0:T(8,128)(2,1)S(1)}, bf16[2,144,768]{2,1,0:T(8,128)(2,1)S(1)}, u32[]{:S(2)}, u32[]{:S(2)}) %collective-permute-start.26) | collective-permute-done | bytes 442400 | tf_op jit(solution)/shard_map/ppermute | solution.py:61
  163.4 6.0 %multiply_convert_fusion.6 = (bf16[768,768]{1,0:T(8,128)(2,1)S(1)}, f32[768,768]{1,0:T(8,128)}) fusion(f32[768,1536]{1,0:T(8,128)S(1)} %fusion.103), kind=kLoop, calls=%fused_computation.83 | loop fusion | flops 38928384 | bytes 8257536 | tf_op jit(solution)/shard_map/convert_element_type | solution.py:337
  172.3 5.2 collective-permute-done.31
  191.5 5.1 attend.3
  199.5 5.1 collective-permute-done.34
  213.1 5.2 multiply_convert_fusion.5
  228.0 5.3 multiply_convert_fusion.4
  256.9 6.3 %collective-permute-done.41 = bf16[4,144,768]{2,1,0:T(8,128)(2,1)S(1)} collective-permute-done((bf16[4,144,768]{2,1,0:T(8,128)(2,1)S(1)}, bf16[4,144,768]{2,1,0:T(8,128)(2,1)S(1)}, u32[]{:S(2)}, u32[]{:S(2)}) %collective-permute-start.41) | collective-permute-done | bytes 884768 | tf_op jit(solution)/shard_map/ppermute | solution.py:61
  281.8 13.5 %collective-permute-done.45 = bf16[4,144,768]{2,1,0:T(8,128)(2,1)} collective-permute-done((bf16[4,144,768]{2,1,0:T(8,128)(2,1)S(1)}, bf16[4,144,768]{2,1,0:T(8,128)(2,1)}, u32[]{:S(2)}, u32[]{:S(2)}) %collective-permute-start.45) | collective-permute-done | bytes 884768 | tf_op jit(solution)/shard_map/ppermute | solution.py:61
  297.2 6.1 %attend_back.2 = bf16[384,2304]{1,0:T(8,128)(2,1)} custom-call(f32[12]{0:T(128)} %pad_maximum_fusion.53.slopes_ref, bf16[384,2304]{1,0:T(8,128)(2,1)} %convolution_convert_fusion.2.projected_ref, bf16[384,768]{1,0:T(8,128)(2,1)} %convolution_convert_fusion.15.context_grad_ref), custom_call_target="tpu_custom_call" | custom-call | flops 377487360 | bytes 4128768 | tf_op jit(solution)/shard_map/attend_back/pallas_call | solution.py:181
  317.2 5.5 collective-permute-done.50
  342.9 7.5 %collective-permute-done.52 = bf16[4,112,768]{2,1,0:T(8,128)(2,1)S(1)} collective-permute-done((bf16[4,112,768]{2,1,0:T(8,128)(2,1)S(1)}, bf16[4,112,768]{2,1,0:T(8,128)(2,1)S(1)}, u32[]{:S(2)}, u32[]{:S(2)}) %collective-permute-start.52) | collective-permute-done | bytes 688160 | tf_op jit(solution)/shard_map/ppermute | solution.py:61
  373.7 7.2 %collective-permute-done.57 = bf16[4,144,768]{2,1,0:T(8,128)(2,1)S(1)} collective-permute-done((bf16[4,144,768]{2,1,0:T(8,128)(2,1)S(1)}, bf16[4,144,768]{2,1,0:T(8,128)(2,1)S(1)}, u32[]{:S(2)}, u32[]{:S(2)}) %collective-permute-start.57) | collective-permute-done | bytes 884768 | tf_op jit(solution)/shard_map/ppermute | solution.py:61
  396.4 5.9 %attend_back.3 = bf16[384,2304]{1,0:T(8,128)(2,1)} custom-call(f32[12]{0:T(128)} %pad_maximum_fusion.53.slopes_ref, bf16[384,2304]{1,0:T(8,128)(2,1)} %convolution_convert_fusion.3.projected_ref, bf16[384,768]{1,0:T(8,128)(2,1)} %convolution_convert_fusion.14.context_grad_ref), custom_call_target="tpu_custom_call" | custom-call | flops 377487360 | bytes 4128768 | tf_op jit(solution)/shard_map/attend_back/pallas_call | solution.py:181
  415.4 6.6 %collective-permute-done.63 = bf16[4,144,768]{2,1,0:T(8,128)(2,1)} collective-permute-done((bf16[4,144,768]{2,1,0:T(8,128)(2,1)}, bf16[4,144,768]{2,1,0:T(8,128)(2,1)}, u32[]{:S(2)}, u32[]{:S(2)}) %collective-permute-start.63) | collective-permute-done | bytes 884768 | tf_op jit(solution)/shard_map/ppermute | solution.py:61
  429.2 13.4 %collective-permute-done.68 = bf16[4,144,768]{2,1,0:T(8,128)(2,1)S(1)} collective-permute-done((bf16[4,144,768]{2,1,0:T(8,128)(2,1)S(1)}, bf16[4,144,768]{2,1,0:T(8,128)(2,1)S(1)}, u32[]{:S(2)}, u32[]{:S(2)}) %collective-permute-start.68) | collective-permute-done | bytes 884768 | tf_op jit(solution)/shard_map/ppermute | solution.py:61
  442.6 5.9 %collective-permute-done.69 = bf16[4,144,768]{2,1,0:T(8,128)(2,1)S(1)} collective-permute-done((bf16[4,144,768]{2,1,0:T(8,128)(2,1)S(1)}, bf16[4,144,768]{2,1,0:T(8,128)(2,1)S(1)}, u32[]{:S(2)}, u32[]{:S(2)}) %collective-permute-start.69) | collective-permute-done | bytes 884768 | tf_op jit(solution)/shard_map/ppermute | solution.py:61
  457.9 8.1 %collective-permute-done.71 = bf16[2,144,768]{2,1,0:T(8,128)(2,1)S(1)} collective-permute-done((bf16[2,144,768]{2,1,0:T(8,128)(2,1)S(1)}, bf16[2,144,768]{2,1,0:T(8,128)(2,1)S(1)}, u32[]{:S(2)}, u32[]{:S(2)}) %collective-permute-start.71) | collective-permute-done | bytes 442400 | tf_op jit(solution)/shard_map/ppermute | solution.py:61
  474.8 4.9 collective-permute-done.74
  486.0 9.7 %collective-permute-done.78 = bf16[144,768]{1,0:T(8,128)(2,1)S(1)} collective-permute-done((bf16[144,768]{1,0:T(8,128)(2,1)S(1)}, bf16[144,768]{1,0:T(8,128)(2,1)S(1)}, u32[]{:S(2)}, u32[]{:S(2)}) %collective-permute-start.78) | collective-permute-done | bytes 221216 | tf_op jit(solution)/shard_map/ppermute | solution.py:61
  496.0 5.0 collective-permute-start.84
  525.1 6.4 %collective-permute-done.87 = bf16[96,768]{1,0:T(8,128)(2,1)} collective-permute-done((bf16[96,768]{1,0:T(8,128)(2,1)}, bf16[96,768]{1,0:T(8,128)(2,1)}, u32[]{:S(2)}, u32[]{:S(2)}) %collective-permute-start.87) | collective-permute-done | bytes 147488 | tf_op jit(solution)/shard_map/ppermute | solution.py:61
  541.4 5.2 collective-permute-start.95
  554.3 7.8 %settle.1 = (f32[768,2,768]{2,1,0:T(2,128)}, f32[768,768]{1,0:T(8,128)}) custom-call(s32[9]{0:T(128)} %pad_add_fusion.flags_ref, bf16[288,768]{1,0:T(8,128)(2,1)} %copy-done.44, bf16[288,768]{1,0:T(8,128)(2,1)} %collective-permute-done.83.refs_1_, bf16[288,768]{1,0:T(8,128)(2,1)} %collective-permute-done.88.refs_2_, ...), custom_call_target="tpu_custom_call" | custom-call | tf_op jit(solution)/shard_map/settle/pallas_call | solution.py:225
  (769 shorter events, 324.5 us)
Async XLA Ops:
  45.0 21.2 %collective-permute-start.9 = (bf16[2,144,768]{2,1,0:T(8,128)(2,1)S(1)}, bf16[2,144,768]{2,1,0:T(8,128)(2,1)S(1)}, u32[]{:S(2)}, u32[]{:S(2)}) collective-permute-start(bf16[2,144,768]{2,1,0:T(8,128)(2,1)S(1)} %pad_maximum_fusion.39), channel_id=1, source_target_pairs={{0,2},{1,3},{2,0},{3,1},{4,6},{5,7},{6,4},{7,5},{8,10},{9,11},{10,... | collective-permute-start | bytes 1327112 | tf_op jit(solution)/shard_map/ppermute | solution.py:61
  45.1 21.0 %collective-permute-start.8 = (bf16[3,96,768]{2,1,0:T(8,128)(2,1)S(1)}, bf16[3,96,768]{2,1,0:T(8,128)(2,1)S(1)}, u32[]{:S(2)}, u32[]{:S(2)}) collective-permute-start(bf16[3,96,768]{2,1,0:T(8,128)(2,1)S(1)} %pad_maximum_fusion.38), channel_id=1, source_target_pairs={{0,8},{1,9},{2,10},{3,11},{4,12},{5,13},{6,14},{7,15},{8,0},{9,1},... | collective-permute-start | bytes 1327112 | tf_op jit(solution)/shard_map/ppermute | solution.py:61
  46.3 19.8 %collective-permute-start.7 = (bf16[3,96,768]{2,1,0:T(8,128)(2,1)S(1)}, bf16[3,96,768]{2,1,0:T(8,128)(2,1)S(1)}, u32[]{:S(2)}, u32[]{:S(2)}) collective-permute-start(bf16[3,96,768]{2,1,0:T(8,128)(2,1)S(1)} %pad_maximum_fusion.38), channel_id=1, source_target_pairs={{0,4},{1,5},{2,6},{3,7},{4,0},{5,1},{6,2},{7,3},{8,12},{9,13},{10,... | collective-permute-start | bytes 1327112 | tf_op jit(solution)/shard_map/ppermute | solution.py:61
  66.2 25.0 %collective-permute-start.13 = (bf16[3,144,768]{2,1,0:T(8,128)(2,1)S(1)}, bf16[3,144,768]{2,1,0:T(8,128)(2,1)S(1)}, u32[]{:S(2)}, u32[]{:S(2)}) collective-permute-start(bf16[3,144,768]{2,1,0:T(8,128)(2,1)S(1)} %pad_maximum_fusion.32), channel_id=1, source_target_pairs={{0,8},{1,9},{2,10},{3,11},{4,12},{5,13},{6,14},{7,15},{8,0},{9,1},... | collective-permute-start | bytes 1990664 | tf_op jit(solution)/shard_map/ppermute | solution.py:61
  67.4 23.8 %collective-permute-start.12 = (bf16[3,144,768]{2,1,0:T(8,128)(2,1)S(1)}, bf16[3,144,768]{2,1,0:T(8,128)(2,1)}, u32[]{:S(2)}, u32[]{:S(2)}) collective-permute-start(bf16[3,144,768]{2,1,0:T(8,128)(2,1)S(1)} %pad_maximum_fusion.32), channel_id=1, source_target_pairs={{0,4},{1,5},{2,6},{3,7},{4,0},{5,1},{6,2},{7,3},{8,12},{9,13},{10,... | collective-permute-start | bytes 1990664 | tf_op jit(solution)/shard_map/ppermute | solution.py:61
  68.7 22.5 %collective-permute-start.14 = (bf16[2,144,768]{2,1,0:T(8,128)(2,1)S(1)}, bf16[2,144,768]{2,1,0:T(8,128)(2,1)S(1)}, u32[]{:S(2)}, u32[]{:S(2)}) collective-permute-start(bf16[2,144,768]{2,1,0:T(8,128)(2,1)S(1)} %pad_maximum_fusion.40), channel_id=1, source_target_pairs={{0,2},{1,3},{2,0},{3,1},{4,6},{5,7},{6,4},{7,5},{8,10},{9,11},{10,... | collective-permute-start | bytes 1327112 | tf_op jit(solution)/shard_map/ppermute | solution.py:61
  68.7 22.5 %collective-permute-start.11 = (bf16[3,96,768]{2,1,0:T(8,128)(2,1)S(1)}, bf16[3,96,768]{2,1,0:T(8,128)(2,1)S(1)}, u32[]{:S(2)}, u32[]{:S(2)}) collective-permute-start(bf16[3,96,768]{2,1,0:T(8,128)(2,1)S(1)} %collective-permute-done.7), channel_id=1, source_target_pairs={{0,8},{1,9},{2,10},{3,11},{4,12},{5,13},{6,14},{7,15},{8,0},{9,1},... | collective-permute-start | bytes 1327112 | tf_op jit(solution)/shard_map/ppermute | solution.py:61
  100.3 21.8 %collective-permute-start.17 = (bf16[3,144,768]{2,1,0:T(8,128)(2,1)}, bf16[3,144,768]{2,1,0:T(8,128)(2,1)}, u32[]{:S(2)}, u32[]{:S(2)}) collective-permute-start(bf16[3,144,768]{2,1,0:T(8,128)(2,1)} %collective-permute-done.12), channel_id=1, source_target_pairs={{0,8},{1,9},{2,10},{3,11},{4,12},{5,13},{6,14},{7,15},{8,0},{9,1},... | collective-permute-start | bytes 1990664 | tf_op jit(solution)/shard_map/ppermute | solution.py:61
  123.1 29.7 %collective-permute-start.25 = (bf16[3,96,768]{2,1,0:T(8,128)(2,1)S(1)}, bf16[3,96,768]{2,1,0:T(8,128)(2,1)S(1)}, u32[]{:S(2)}, u32[]{:S(2)}) collective-permute-start(bf16[3,96,768]{2,1,0:T(8,128)(2,1)S(1)} %pad_maximum_fusion.41), channel_id=1, source_target_pairs={{0,8},{1,9},{2,10},{3,11},{4,12},{5,13},{6,14},{7,15},{8,0},{9,1},... | collective-permute-start | bytes 1327112 | tf_op jit(solution)/shard_map/ppermute | solution.py:61
  123.4 29.4 %collective-permute-start.24 = (bf16[3,96,768]{2,1,0:T(8,128)(2,1)S(1)}, bf16[3,96,768]{2,1,0:T(8,128)(2,1)S(1)}, u32[]{:S(2)}, u32[]{:S(2)}) collective-permute-start(bf16[3,96,768]{2,1,0:T(8,128)(2,1)S(1)} %pad_maximum_fusion.41), channel_id=1, source_target_pairs={{0,4},{1,5},{2,6},{3,7},{4,0},{5,1},{6,2},{7,3},{8,12},{9,13},{10,... | collective-permute-start | bytes 1327112 | tf_op jit(solution)/shard_map/ppermute | solution.py:61
  130.6 22.2 %collective-permute-start.26 = (bf16[2,144,768]{2,1,0:T(8,128)(2,1)S(1)}, bf16[2,144,768]{2,1,0:T(8,128)(2,1)S(1)}, u32[]{:S(2)}, u32[]{:S(2)}) collective-permute-start(bf16[2,144,768]{2,1,0:T(8,128)(2,1)S(1)} %pad_maximum_fusion.42), channel_id=1, source_target_pairs={{0,2},{1,3},{2,0},{3,1},{4,6},{5,7},{6,4},{7,5},{8,10},{9,11},{10,... | collective-permute-start | bytes 1327112 | tf_op jit(solution)/shard_map/ppermute | solution.py:61
  132.1 20.7 %collective-permute-start.23 = (bf16[3,144,768]{2,1,0:T(8,128)(2,1)}, bf16[3,144,768]{2,1,0:T(8,128)(2,1)S(1)}, u32[]{:S(2)}, u32[]{:S(2)}) collective-permute-start(bf16[3,144,768]{2,1,0:T(8,128)(2,1)} %collective-permute-done.18), channel_id=1, source_target_pairs={{0,8},{1,9},{2,10},{3,11},{4,12},{5,13},{6,14},{7,15},{8,0},{9,1},... | collective-permute-start | bytes 1990664 | tf_op jit(solution)/shard_map/ppermute | solution.py:61
  153.8 23.6 %collective-permute-start.30 = (bf16[3,144,768]{2,1,0:T(8,128)(2,1)S(1)}, bf16[3,144,768]{2,1,0:T(8,128)(2,1)S(1)}, u32[]{:S(2)}, u32[]{:S(2)}) collective-permute-start(bf16[3,144,768]{2,1,0:T(8,128)(2,1)S(1)} %pad_maximum_fusion.34), channel_id=1, source_target_pairs={{0,8},{1,9},{2,10},{3,11},{4,12},{5,13},{6,14},{7,15},{8,0},{9,1},... | collective-permute-start | bytes 1990664 | tf_op jit(solution)/shard_map/ppermute | solution.py:61
  154.9 22.6 %collective-permute-start.29 = (bf16[3,144,768]{2,1,0:T(8,128)(2,1)S(1)}, bf16[3,144,768]{2,1,0:T(8,128)(2,1)}, u32[]{:S(2)}, u32[]{:S(2)}) collective-permute-start(bf16[3,144,768]{2,1,0:T(8,128)(2,1)S(1)} %pad_maximum_fusion.34), channel_id=1, source_target_pairs={{0,4},{1,5},{2,6},{3,7},{4,0},{5,1},{6,2},{7,3},{8,12},{9,13},{10,... | collective-permute-start | bytes 1990664 | tf_op jit(solution)/shard_map/ppermute | solution.py:61
  156.1 21.4 %collective-permute-start.31 = (bf16[2,144,768]{2,1,0:T(8,128)(2,1)S(1)}, bf16[2,144,768]{2,1,0:T(8,128)(2,1)S(1)}, u32[]{:S(2)}, u32[]{:S(2)}) collective-permute-start(bf16[2,144,768]{2,1,0:T(8,128)(2,1)S(1)} %pad_maximum_fusion.43), channel_id=1, source_target_pairs={{0,2},{1,3},{2,0},{3,1},{4,6},{5,7},{6,4},{7,5},{8,10},{9,11},{10,... | collective-permute-start | bytes 1327112 | tf_op jit(solution)/shard_map/ppermute | solution.py:61
  156.2 21.3 %collective-permute-start.28 = (bf16[3,96,768]{2,1,0:T(8,128)(2,1)S(1)}, bf16[3,96,768]{2,1,0:T(8,128)(2,1)S(1)}, u32[]{:S(2)}, u32[]{:S(2)}) collective-permute-start(bf16[3,96,768]{2,1,0:T(8,128)(2,1)S(1)} %collective-permute-done.24), channel_id=1, source_target_pairs={{0,8},{1,9},{2,10},{3,11},{4,12},{5,13},{6,14},{7,15},{8,0},{9,1},... | collective-permute-start | bytes 1327112 | tf_op jit(solution)/shard_map/ppermute | solution.py:61
  181.0 23.6 %collective-permute-start.34 = (bf16[3,144,768]{2,1,0:T(8,128)(2,1)}, bf16[3,144,768]{2,1,0:T(8,128)(2,1)}, u32[]{:S(2)}, u32[]{:S(2)}) collective-permute-start(bf16[3,144,768]{2,1,0:T(8,128)(2,1)} %collective-permute-done.29), channel_id=1, source_target_pairs={{0,8},{1,9},{2,10},{3,11},{4,12},{5,13},{6,14},{7,15},{8,0},{9,1},... | collective-permute-start | bytes 1990664 | tf_op jit(solution)/shard_map/ppermute | solution.py:61
  252.0 21.6 %collective-permute-start.42 = (bf16[4,144,768]{2,1,0:T(8,128)(2,1)S(1)}, bf16[4,144,768]{2,1,0:T(8,128)(2,1)S(1)}, u32[]{:S(2)}, u32[]{:S(2)}) collective-permute-start(bf16[4,144,768]{2,1,0:T(8,128)(2,1)S(1)} %bitcast.570), channel_id=1, source_target_pairs={{0,8},{1,9},{2,10},{3,11},{4,12},{5,13},{6,14},{7,15},{8,0},{9,1},... | collective-permute-start | bytes 2654216 | tf_op jit(solution)/shard_map/ppermute | solution.py:61
  275.2 20.1 %collective-permute-start.45 = (bf16[4,144,768]{2,1,0:T(8,128)(2,1)S(1)}, bf16[4,144,768]{2,1,0:T(8,128)(2,1)}, u32[]{:S(2)}, u32[]{:S(2)}) collective-permute-start(bf16[4,144,768]{2,1,0:T(8,128)(2,1)S(1)} %add_convert_fusion.13), channel_id=1, source_target_pairs={{0,4},{1,5},{2,6},{3,7},{4,0},{5,1},{6,2},{7,3},{8,12},{9,13},{10,... | collective-permute-start | bytes 2654216 | tf_op jit(solution)/shard_map/ppermute | solution.py:61
  275.6 21.6 %collective-permute-start.46 = (bf16[4,144,768]{2,1,0:T(8,128)(2,1)S(1)}, bf16[4,144,768]{2,1,0:T(8,128)(2,1)}, u32[]{:S(2)}, u32[]{:S(2)}) collective-permute-start(bf16[4,144,768]{2,1,0:T(8,128)(2,1)S(1)} %bitcast.569), channel_id=1, source_target_pairs={{0,8},{1,9},{2,10},{3,11},{4,12},{5,13},{6,14},{7,15},{8,0},{9,1},... | collective-permute-start | bytes 2654216 | tf_op jit(solution)/shard_map/ppermute | solution.py:61
  276.5 32.0 %collective-permute-start.47 = (bf16[4,144,768]{2,1,0:T(8,128)(2,1)}, bf16[4,144,768]{2,1,0:T(8,128)(2,1)}, u32[]{:S(2)}, u32[]{:S(2)}) collective-permute-start(bf16[4,144,768]{2,1,0:T(8,128)(2,1)} %bitcast.160), channel_id=1, source_target_pairs={{0,8},{1,9},{2,10},{3,11},{4,12},{5,13},{6,14},{7,15},{8,0},{9,1},... | collective-permute-start | bytes 2654216 | tf_op jit(solution)/shard_map/ppermute | solution.py:61
  332.9 27.6 %collective-permute-start.55 = (bf16[4,112,768]{2,1,0:T(8,128)(2,1)S(1)}, bf16[4,112,768]{2,1,0:T(8,128)(2,1)S(1)}, u32[]{:S(2)}, u32[]{:S(2)}) collective-permute-start(bf16[4,112,768]{2,1,0:T(8,128)(2,1)S(1)} %get-tuple-element.718), channel_id=1, source_target_pairs={{0,8},{1,9},{2,10},{3,11},{4,12},{5,13},{6,14},{7,15},{8,0},{9,1},... | collective-permute-start | bytes 2064392 | tf_op jit(solution)/shard_map/ppermute | solution.py:61
  353.7 20.0 %collective-permute-start.58 = (bf16[4,112,768]{2,1,0:T(8,128)(2,1)S(1)}, bf16[4,112,768]{2,1,0:T(8,128)(2,1)S(1)}, u32[]{:S(2)}, u32[]{:S(2)}) collective-permute-start(bf16[4,112,768]{2,1,0:T(8,128)(2,1)S(1)} %fusion.32), channel_id=1, source_target_pairs={{0,4},{1,5},{2,6},{3,7},{4,0},{5,1},{6,2},{7,3},{8,12},{9,13},{10,... | collective-permute-start | bytes 2064392 | tf_op jit(solution)/shard_map/ppermute | solution.py:61
  363.8 26.8 %collective-permute-start.62 = (bf16[288,768]{1,0:T(8,128)(2,1)S(1)}, bf16[288,768]{1,0:T(8,128)(2,1)S(1)}, u32[]{:S(2)}, u32[]{:S(2)}) collective-permute-start(bf16[288,768]{1,0:T(8,128)(2,1)S(1)} %pad_maximum_fusion.44.refs_12_), channel_id=1, source_target_pairs={{0,4},{1,5},{2,6},{3,7},{4,0},{5,1},{6,2},{7,3},{8,12},{9,13},{10,... | collective-permute-start | bytes 1327112 | tf_op jit(solution)/shard_map/ppermute | solution.py:61
  364.9 26.2 %collective-permute-start.60 = (bf16[4,144,768]{2,1,0:T(8,128)(2,1)S(1)}, bf16[4,144,768]{2,1,0:T(8,128)(2,1)S(1)}, u32[]{:S(2)}, u32[]{:S(2)}) collective-permute-start(bf16[4,144,768]{2,1,0:T(8,128)(2,1)S(1)} %bitcast.567), channel_id=1, source_target_pairs={{0,8},{1,9},{2,10},{3,11},{4,12},{5,13},{6,14},{7,15},{8,0},{9,1},... | collective-permute-start | bytes 2654216 | tf_op jit(solution)/shard_map/ppermute | solution.py:61
  386.2 29.2 %collective-permute-start.64 = (bf16[4,144,768]{2,1,0:T(8,128)(2,1)}, bf16[4,144,768]{2,1,0:T(8,128)(2,1)}, u32[]{:S(2)}, u32[]{:S(2)}) collective-permute-start(bf16[4,144,768]{2,1,0:T(8,128)(2,1)} %add_convert_fusion.9), channel_id=1, source_target_pairs={{0,4},{1,5},{2,6},{3,7},{4,0},{5,1},{6,2},{7,3},{8,12},{9,13},{10,... | collective-permute-start | bytes 2654216 | tf_op jit(solution)/shard_map/ppermute | solution.py:61
  422.4 26.1 %collective-permute-start.67 = (bf16[4,4,112,768]{3,2,1,0:T(8,128)(2,1)S(1)}, bf16[4,4,112,768]{3,2,1,0:T(8,128)(2,1)S(1)}, u32[]{:S(2)}, u32[]{:S(2)}) collective-permute-start(bf16[4,4,112,768]{3,2,1,0:T(8,128)(2,1)S(1)} %get-tuple-element.690), channel_id=1, source_target_pairs={{0,16},{1,17},{2,18},{3,19},{4,20},{5,21},{6,22},{7,23},{8,24},{9,... | collective-permute-start | bytes 8257544 | tf_op jit(solution)/shard_map/ppermute | solution.py:61
  426.7 21.7 %collective-permute-start.69 = (bf16[4,144,768]{2,1,0:T(8,128)(2,1)S(1)}, bf16[4,144,768]{2,1,0:T(8,128)(2,1)S(1)}, u32[]{:S(2)}, u32[]{:S(2)}) collective-permute-start(bf16[4,144,768]{2,1,0:T(8,128)(2,1)S(1)} %add_convert_fusion.8), channel_id=1, source_target_pairs={{0,4},{1,5},{2,6},{3,7},{4,0},{5,1},{6,2},{7,3},{8,12},{9,13},{10,... | collective-permute-start | bytes 2654216 | tf_op jit(solution)/shard_map/ppermute | solution.py:61
  426.8 47.2 %collective-permute-start.76 = (bf16[288,768]{1,0:T(8,128)(2,1)S(1)}, bf16[288,768]{1,0:T(8,128)(2,1)S(1)}, u32[]{:S(2)}, u32[]{:S(2)}) collective-permute-start(bf16[288,768]{1,0:T(8,128)(2,1)S(1)} %copy-done.42), channel_id=1, source_target_pairs={{0,8},{1,9},{2,10},{3,11},{4,12},{5,13},{6,14},{7,15},{8,0},{9,1},... | collective-permute-start | bytes 1327112 | tf_op jit(solution)/shard_map/ppermute | solution.py:61
  456.0 23.7 %collective-permute-start.74 = (bf16[2,144,768]{2,1,0:T(8,128)(2,1)S(1)}, bf16[2,144,768]{2,1,0:T(8,128)(2,1)S(1)}, u32[]{:S(2)}, u32[]{:S(2)}) collective-permute-start(bf16[2,144,768]{2,1,0:T(8,128)(2,1)S(1)} %get-tuple-element.732), channel_id=1, source_target_pairs={{0,1},{1,0},{2,3},{3,2},{4,5},{5,4},{6,7},{7,6},{8,9},{9,8},{10,11... | collective-permute-start | bytes 1327112 | tf_op jit(solution)/shard_map/ppermute | solution.py:61
  481.4 31.2 %collective-permute-start.85 = (bf16[4,288,768]{2,1,0:T(8,128)(2,1)S(1)}, bf16[4,288,768]{2,1,0:T(8,128)(2,1)S(1)}, u32[]{:S(2)}, u32[]{:S(2)}) collective-permute-start(bf16[4,288,768]{2,1,0:T(8,128)(2,1)S(1)} %pad_maximum_fusion.24), channel_id=1, source_target_pairs={{0,16},{1,17},{2,18},{3,19},{4,20},{5,21},{6,22},{7,23},{8,24},{9,... | collective-permute-start | bytes 5308424 | tf_op jit(solution)/shard_map/ppermute | solution.py:521
  520.8 20.6 %collective-permute-start.93 = (bf16[288,768]{1,0:T(8,128)(2,1)}, bf16[288,768]{1,0:T(8,128)(2,1)}, u32[]{:S(2)}, u32[]{:S(2)}) collective-permute-start(bf16[288,768]{1,0:T(8,128)(2,1)} %collective-permute-done.83.refs_1_), channel_id=1, source_target_pairs={{0,8},{1,9},{2,10},{3,11},{4,12},{5,13},{6,14},{7,15},{8,0},{9,1},... | collective-permute-start | bytes 1327112 | tf_op jit(solution)/shard_map/ppermute | solution.py:61
  (224 other events, 2257.4 us)

commit v10 on v8

--- a/solution.py
+++ b/solution.py
@@ -387,13 +387,16 @@
     seqs = micro * own_seqs // 2
     rows = seqs * length
 
-    orders = [jnp.array([0, 1, 2, 3]), jnp.array([0, 2, 1, 3])]
-    steps = jnp.where(is_first, orders[0], orders[1])
     in_plane = jnp.bitwise_and(plane, PLANE - 1)
+
+    def crossed(e):
+        return (e & 1) * 2 + (e >> 1)
 
     def relative(slab):
         return [
-            lax.dynamic_index_in_dim(slab, jnp.bitwise_xor(in_plane, steps[e]), 0, keepdims=False)
+            lax.dynamic_index_in_dim(
+                slab, jnp.bitwise_xor(in_plane, jnp.where(is_first, e, crossed(e))), 0, keepdims=False
+            )
             for e in range(PLANE)
         ]
 
@@ -457,7 +460,10 @@
     a0, p0, q0 = first(a0), far(p0), near(q0)
     a0, p0, q0, a1 = together(a0, p0, q0, a1)
     a0, p0, q0, a1 = second(a0), first(p0), far(q0), near(a1)
-    a0, p0, q0, a1, p1 = together(a0, p0, q0, a1, p1)
+    places = [jnp.bitwise_xor(in_plane, e) for e in range(PLANE)]
+    places += [jnp.bitwise_xor(in_plane, crossed(e)) for e in range(PLANE)]
+    flags = jnp.stack([is_first.astype(jnp.int32)] + places)
+    a0, p0, q0, a1, p1, norms, seed, flags = together(a0, p0, q0, a1, p1, norms, seed, flags)
     p0, q0, a1, p1 = second(p0), first(q0), far(a1), near(p1)
     attn0 = attn_weights(a0)
     projected0, context0, sum0, norm0 = attn_forward(start, attn0, norms[0], slopes, seqs)
@@ -642,9 +648,6 @@
 
     feed_early = [feed, feed_first, feed_second, feed_third]
     feed_late = [late, late_first, late_second, late_third]
-    flags = jnp.concatenate(
-        [is_first.astype(jnp.int32)[None]] + [jnp.bitwise_xor(in_plane, order) for order in orders]
-    )
     grad_in, grad_down = settle(
         feed_early + feed_got + late_got + feed_late, flags, FEED_CHUNKS, 3, unit_part
     )
@@ -653,8 +656,8 @@
         [
             jnp.stack(
                 [
-                    lax.dynamic_index_in_dim(half, order[jnp.bitwise_xor(in_plane, index)], 0, keepdims=False)
-                    for half, order in zip(parts, orders)
+                    lax.dynamic_index_in_dim(parts[0], jnp.bitwise_xor(in_plane, index), 0, keepdims=False),
+                    lax.dynamic_index_in_dim(parts[1], crossed(jnp.bitwise_xor(in_plane, index)), 0, keepdims=False),
                 ]
             )
             for index in range(PLANE)

time: 562 us -> 561 us (level)
  between operations: 14.9 us -> 4.37 us
  other arithmetic: 90.6 us -> 98.4 us
    another operation x18 -> x20, other arithmetic: 13.1 us -> 17.4 us  [assemble(): jnp.stack([jnp.concatenate([own[None], r]) for own, r in zip(chunk['own']...]
    unnamed x333 -> x321, local copies, waits for them, and re-layouts: 22.3 us -> 20.8 us
  transfers between devices with their start and end apart: 99 -> 99, of which waited for: 40 -> 41; matrix products, arithmetic and copies ran while one was open for 28% -> 29% of each run, Pallas kernels for 5% -> 5%
where the time goes in v10:
time: 561 us; the launch traced here: 551 us
  waiting for transfers between devices  188 us (34%)
  starting transfers between devices  113 us (20%)
  other arithmetic  98.4 us (18%)
  matrix products  62.9 us (11%)
  local copies, waits for them, and re-layouts  54.6 us (10%)
  Pallas kernels  29.3 us (5%)
    ppermute x89, waiting for transfers between devices, exchange(): return lax.ppermute(block, AXES, pairs)  187 us
    ppermute x89, starting transfers between devices, exchange(): return lax.ppermute(block, AXES, pairs)  88.9 us
    dot_general x36, matrix products, dot(): lax.dot_general(a, b, (((ca,), (cb,)), ((), ())), preferred_element_type=...  62.9 us
    ppermute x10, starting transfers between devices, hand_over(): return lax.ppermute(block, AXES, pairs)  24.6 us
    convert_element_type x4, other arithmetic, feed_forward(): hidden = gelu_product(gate_part, up_part).astype(BF16)  22.6 us
    unnamed x321, local copies, waits for them, and re-layouts  20.8 us
    another operation x20, other arithmetic, assemble(): jnp.stack([jnp.concatenate([own[None], r]) for own, r in zip(chunk['own']...  17.4 us
    convert_element_type x26, other arithmetic, total_low(): return sum((part.astype(F32) for part in parts)).astype(BF16)  14.6 us
  transfers between devices with their start and end apart: 99, of which 41 were waited for; matrix products, arithmetic and copies ran while one was open for 29% of the time, Pallas kernels for 5%

profile of v10, /device:TPU:1, one launch (start us, length us, event | category | flops | bytes accessed | tf_op | source)
XLA Modules:
  0.0 550.6 jit_solution(6405994038716454494)
XLA Ops:
  11.4 5.6 %copy.68 = bf16[1,768,2,768]{1,3,2,0:T(8,128)(2,1)S(1)} copy(bf16[1,768,2,768]{3,2,1,0:T(2,128)(2,1)} %param.17) | data formatting | bytes 4718592 | tf_op jit(solution)/shard_map/optimization_barrier | solution.py:244
  26.4 9.6 %collective-permute-done.2 = bf16[2,96,768]{2,1,0:T(8,128)(2,1)S(1)} collective-permute-done((bf16[2,96,768]{2,1,0:T(8,128)(2,1)S(1)}, bf16[2,96,768]{2,1,0:T(8,128)(2,1)S(1)}, u32[]{:S(2)}, u32[]{:S(2)}) %collective-permute-start.2) | collective-permute-done | bytes 294944 | tf_op jit(solution)/shard_map/ppermute | solution.py:61
  39.3 4.4 collective-permute-start.9
  45.7 4.6 collective-permute-done.9
  50.3 7.7 %collective-permute-done.8 = bf16[2,144,768]{2,1,0:T(8,128)(2,1)} collective-permute-done((bf16[2,144,768]{2,1,0:T(8,128)(2,1)}, bf16[2,144,768]{2,1,0:T(8,128)(2,1)}, u32[]{:S(2)}, u32[]{:S(2)}) %collective-permute-start.8) | collective-permute-done | bytes 442400 | tf_op jit(solution)/shard_map/ppermute | solution.py:61
  70.0 5.4 collective-permute-done.14
  75.5 12.0 %collective-permute-done.13 = bf16[2,144,768]{2,1,0:T(8,128)(2,1)S(1)} collective-permute-done((bf16[2,144,768]{2,1,0:T(8,128)(2,1)S(1)}, bf16[2,144,768]{2,1,0:T(8,128)(2,1)S(1)}, u32[]{:S(2)}, u32[]{:S(2)}) %collective-permute-start.13) | collective-permute-done | bytes 442400 | tf_op jit(solution)/shard_map/ppermute | solution.py:61
  105.8 4.7 attend.2
  113.2 5.7 %collective-permute-done.17 = bf16[3,144,768]{2,1,0:T(8,128)(2,1)} collective-permute-done((bf16[3,144,768]{2,1,0:T(8,128)(2,1)}, bf16[3,144,768]{2,1,0:T(8,128)(2,1)}, u32[]{:S(2)}, u32[]{:S(2)}) %collective-permute-start.17) | collective-permute-done | bytes 663584 | tf_op jit(solution)/shard_map/ppermute | solution.py:61
  134.3 6.2 %multiply_convert_fusion.7 = (bf16[768,768]{1,0:T(8,128)(2,1)S(1)}, f32[768,768]{1,0:T(8,128)}) fusion(f32[768,1536]{1,0:T(8,128)S(1)} %fusion.101), kind=kLoop, calls=%fused_computation.96 | loop fusion | flops 38928384 | bytes 8257536 | tf_op jit(solution)/shard_map/convert_element_type | solution.py:337
  141.7 10.2 %collective-permute-done.26 = bf16[2,144,768]{2,1,0:T(8,128)(2,1)S(1)} collective-permute-done((bf16[2,144,768]{2,1,0:T(8,128)(2,1)S(1)}, bf16[2,144,768]{2,1,0:T(8,128)(2,1)S(1)}, u32[]{:S(2)}, u32[]{:S(2)}) %collective-permute-start.26) | collective-permute-done | bytes 442400 | tf_op jit(solution)/shard_map/ppermute | solution.py:61
  162.4 6.0 %multiply_convert_fusion.6 = (bf16[768,768]{1,0:T(8,128)(2,1)S(1)}, f32[768,768]{1,0:T(8,128)}) fusion(f32[768,1536]{1,0:T(8,128)S(1)} %fusion.103), kind=kLoop, calls=%fused_computation.83 | loop fusion | flops 38928384 | bytes 8257536 | tf_op jit(solution)/shard_map/convert_element_type | solution.py:337
  171.2 5.3 collective-permute-done.31
  190.5 5.1 attend.3
  198.4 5.2 collective-permute-done.34
  212.2 5.2 multiply_convert_fusion.5
  227.1 5.3 multiply_convert_fusion.4
  278.1 10.1 %collective-permute-done.44 = bf16[4,144,768]{2,1,0:T(8,128)(2,1)} collective-permute-done((bf16[4,144,768]{2,1,0:T(8,128)(2,1)S(1)}, bf16[4,144,768]{2,1,0:T(8,128)(2,1)}, u32[]{:S(2)}, u32[]{:S(2)}) %collective-permute-start.44) | collective-permute-done | bytes 884768 | tf_op jit(solution)/shard_map/ppermute | solution.py:61
  288.2 6.1 %attend_back.2 = bf16[384,2304]{1,0:T(8,128)(2,1)} custom-call(f32[12]{0:T(128)} %pad_maximum_fusion.54.slopes_ref, bf16[384,2304]{1,0:T(8,128)(2,1)} %convolution_convert_fusion.2.projected_ref, bf16[384,768]{1,0:T(8,128)(2,1)} %convolution_convert_fusion.15.context_grad_ref), custom_call_target="tpu_custom_call" | custom-call | flops 377487360 | bytes 4128768 | tf_op jit(solution)/shard_map/attend_back/pallas_call | solution.py:181
  300.6 6.3 %collective-permute-done.45 = bf16[4,144,768]{2,1,0:T(8,128)(2,1)} collective-permute-done((bf16[4,144,768]{2,1,0:T(8,128)(2,1)}, bf16[4,144,768]{2,1,0:T(8,128)(2,1)}, u32[]{:S(2)}, u32[]{:S(2)}) %collective-permute-start.45) | collective-permute-done | bytes 884768 | tf_op jit(solution)/shard_map/ppermute | solution.py:61
  319.5 6.3 %collective-permute-done.48 = bf16[4,144,768]{2,1,0:T(8,128)(2,1)S(1)} collective-permute-done((bf16[4,144,768]{2,1,0:T(8,128)(2,1)S(1)}, bf16[4,144,768]{2,1,0:T(8,128)(2,1)S(1)}, u32[]{:S(2)}, u32[]{:S(2)}) %collective-permute-start.48) | collective-permute-done | bytes 884768 | tf_op jit(solution)/shard_map/ppermute | solution.py:61
  341.2 7.5 %collective-permute-done.51 = bf16[4,112,768]{2,1,0:T(8,128)(2,1)S(1)} collective-permute-done((bf16[4,112,768]{2,1,0:T(8,128)(2,1)S(1)}, bf16[4,112,768]{2,1,0:T(8,128)(2,1)S(1)}, u32[]{:S(2)}, u32[]{:S(2)}) %collective-permute-start.51) | collective-permute-done | bytes 688160 | tf_op jit(solution)/shard_map/ppermute | solution.py:61
  394.1 5.7 %attend_back.3 = bf16[384,2304]{1,0:T(8,128)(2,1)} custom-call(f32[12]{0:T(128)} %pad_maximum_fusion.54.slopes_ref, bf16[384,2304]{1,0:T(8,128)(2,1)} %convolution_convert_fusion.3.projected_ref, bf16[384,768]{1,0:T(8,128)(2,1)} %convolution_convert_fusion.14.context_grad_ref), custom_call_target="tpu_custom_call" | custom-call | flops 377487360 | bytes 4128768 | tf_op jit(solution)/shard_map/attend_back/pallas_call | solution.py:181
  412.8 7.4 %collective-permute-done.63 = bf16[4,144,768]{2,1,0:T(8,128)(2,1)} collective-permute-done((bf16[4,144,768]{2,1,0:T(8,128)(2,1)}, bf16[4,144,768]{2,1,0:T(8,128)(2,1)}, u32[]{:S(2)}, u32[]{:S(2)}) %collective-permute-start.63) | collective-permute-done | bytes 884768 | tf_op jit(solution)/shard_map/ppermute | solution.py:61
  427.3 6.9 %collective-permute-done.68 = bf16[4,144,768]{2,1,0:T(8,128)(2,1)S(1)} collective-permute-done((bf16[4,144,768]{2,1,0:T(8,128)(2,1)S(1)}, bf16[4,144,768]{2,1,0:T(8,128)(2,1)S(1)}, u32[]{:S(2)}, u32[]{:S(2)}) %collective-permute-start.68) | collective-permute-done | bytes 884768 | tf_op jit(solution)/shard_map/ppermute | solution.py:61
  445.9 8.7 %collective-permute-done.71 = bf16[2,144,768]{2,1,0:T(8,128)(2,1)S(1)} collective-permute-done((bf16[2,144,768]{2,1,0:T(8,128)(2,1)S(1)}, bf16[2,144,768]{2,1,0:T(8,128)(2,1)S(1)}, u32[]{:S(2)}, u32[]{:S(2)}) %collective-permute-start.71) | collective-permute-done | bytes 442400 | tf_op jit(solution)/shard_map/ppermute | solution.py:61
  454.6 6.5 %collective-permute-done.70 = bf16[4,144,768]{2,1,0:T(8,128)(2,1)S(1)} collective-permute-done((bf16[4,144,768]{2,1,0:T(8,128)(2,1)S(1)}, bf16[4,144,768]{2,1,0:T(8,128)(2,1)S(1)}, u32[]{:S(2)}, u32[]{:S(2)}) %collective-permute-start.70) | collective-permute-done | bytes 884768 | tf_op jit(solution)/shard_map/ppermute | solution.py:61
  470.4 9.4 %collective-permute-done.75 = bf16[144,768]{1,0:T(8,128)(2,1)S(1)} collective-permute-done((bf16[144,768]{1,0:T(8,128)(2,1)S(1)}, bf16[144,768]{1,0:T(8,128)(2,1)S(1)}, u32[]{:S(2)}, u32[]{:S(2)}) %collective-permute-start.75) | collective-permute-done | bytes 221216 | tf_op jit(solution)/shard_map/ppermute | solution.py:61
  486.3 7.8 %collective-permute-done.80 = bf16[144,768]{1,0:T(8,128)(2,1)S(1)} collective-permute-done((bf16[144,768]{1,0:T(8,128)(2,1)S(1)}, bf16[144,768]{1,0:T(8,128)(2,1)S(1)}, u32[]{:S(2)}, u32[]{:S(2)}) %collective-permute-start.80) | collective-permute-done | bytes 221216 | tf_op jit(solution)/shard_map/ppermute | solution.py:61
  503.4 4.9 collective-permute-done.86
  526.7 4.6 collective-permute-start.95
  539.6 7.7 %settle.1 = (f32[768,2,768]{2,1,0:T(2,128)}, f32[768,768]{1,0:T(8,128)}) custom-call(s32[9]{0:T(128)} %stack.260.flags_ref, bf16[288,768]{1,0:T(8,128)(2,1)} %copy-done.37, bf16[288,768]{1,0:T(8,128)(2,1)} %collective-permute-done.87.refs_1_, bf16[288,768]{1,0:T(8,128)(2,1)} %copy-done.97, bf16[288,768]{1,0:T(8,128)(2,1)} %collective-permute-done.96.refs_3_, ...), custom_call_target="tpu_custom_call" | custom-call | tf_op jit(solution)/shard_map/settle/pallas_call | solution.py:225
  (766 shorter events, 332.1 us)
Async XLA Ops:
  36.8 21.2 %collective-permute-start.8 = (bf16[2,144,768]{2,1,0:T(8,128)(2,1)}, bf16[2,144,768]{2,1,0:T(8,128)(2,1)}, u32[]{:S(2)}, u32[]{:S(2)}) collective-permute-start(bf16[2,144,768]{2,1,0:T(8,128)(2,1)} %pad_maximum_fusion.40), channel_id=1, source_target_pairs={{0,2},{1,3},{2,0},{3,1},{4,6},{5,7},{6,4},{7,5},{8,10},{9,11},{10,... | collective-permute-start | bytes 1327112 | tf_op jit(solution)/shard_map/ppermute | solution.py:61
  36.9 21.1 %collective-permute-start.7 = (bf16[3,96,768]{2,1,0:T(8,128)(2,1)S(1)}, bf16[3,96,768]{2,1,0:T(8,128)(2,1)}, u32[]{:S(2)}, u32[]{:S(2)}) collective-permute-start(bf16[3,96,768]{2,1,0:T(8,128)(2,1)S(1)} %pad_maximum_fusion.39), channel_id=1, source_target_pairs={{0,8},{1,9},{2,10},{3,11},{4,12},{5,13},{6,14},{7,15},{8,0},{9,1},... | collective-permute-start | bytes 1327112 | tf_op jit(solution)/shard_map/ppermute | solution.py:61
  38.1 19.9 %collective-permute-start.6 = (bf16[3,96,768]{2,1,0:T(8,128)(2,1)S(1)}, bf16[3,96,768]{2,1,0:T(8,128)(2,1)}, u32[]{:S(2)}, u32[]{:S(2)}) collective-permute-start(bf16[3,96,768]{2,1,0:T(8,128)(2,1)S(1)} %pad_maximum_fusion.39), channel_id=1, source_target_pairs={{0,4},{1,5},{2,6},{3,7},{4,0},{5,1},{6,2},{7,3},{8,12},{9,13},{10,... | collective-permute-start | bytes 1327112 | tf_op jit(solution)/shard_map/ppermute | solution.py:61
  43.8 21.8 %collective-permute-start.15 = (f32[4,768]{1,0:T(4,128)S(1)}, f32[4,768]{1,0:T(4,128)S(1)}, u32[]{:S(2)}, u32[]{:S(2)}) collective-permute-start(f32[4,768]{1,0:T(4,128)S(1)} %pad_maximum_fusion.53), channel_id=1, source_target_pairs={{0,16},{1,17},{2,18},{3,19},{4,20},{5,21},{6,22},{7,23},{8,24},{9,... | collective-permute-start | bytes 36872 | tf_op jit(solution)/shard_map/ppermute | solution.py:61
  59.9 27.5 %collective-permute-start.12 = (bf16[3,144,768]{2,1,0:T(8,128)(2,1)}, bf16[3,144,768]{2,1,0:T(8,128)(2,1)}, u32[]{:S(2)}, u32[]{:S(2)}) collective-permute-start(bf16[3,144,768]{2,1,0:T(8,128)(2,1)} %pad_maximum_fusion.33), channel_id=1, source_target_pairs={{0,8},{1,9},{2,10},{3,11},{4,12},{5,13},{6,14},{7,15},{8,0},{9,1},... | collective-permute-start | bytes 1990664 | tf_op jit(solution)/shard_map/ppermute | solution.py:61
  61.0 26.5 %collective-permute-start.11 = (bf16[3,144,768]{2,1,0:T(8,128)(2,1)}, bf16[3,144,768]{2,1,0:T(8,128)(2,1)}, u32[]{:S(2)}, u32[]{:S(2)}) collective-permute-start(bf16[3,144,768]{2,1,0:T(8,128)(2,1)} %pad_maximum_fusion.33), channel_id=1, source_target_pairs={{0,4},{1,5},{2,6},{3,7},{4,0},{5,1},{6,2},{7,3},{8,12},{9,13},{10,... | collective-permute-start | bytes 1990664 | tf_op jit(solution)/shard_map/ppermute | solution.py:61
  65.1 22.3 %collective-permute-start.13 = (bf16[2,144,768]{2,1,0:T(8,128)(2,1)S(1)}, bf16[2,144,768]{2,1,0:T(8,128)(2,1)S(1)}, u32[]{:S(2)}, u32[]{:S(2)}) collective-permute-start(bf16[2,144,768]{2,1,0:T(8,128)(2,1)S(1)} %pad_maximum_fusion.41), channel_id=1, source_target_pairs={{0,2},{1,3},{2,0},{3,1},{4,6},{5,7},{6,4},{7,5},{8,10},{9,11},{10,... | collective-permute-start | bytes 1327112 | tf_op jit(solution)/shard_map/ppermute | solution.py:61
  65.2 22.2 %collective-permute-start.10 = (bf16[3,96,768]{2,1,0:T(8,128)(2,1)}, bf16[3,96,768]{2,1,0:T(8,128)(2,1)S(1)}, u32[]{:S(2)}, u32[]{:S(2)}) collective-permute-start(bf16[3,96,768]{2,1,0:T(8,128)(2,1)} %collective-permute-done.6), channel_id=1, source_target_pairs={{0,8},{1,9},{2,10},{3,11},{4,12},{5,13},{6,14},{7,15},{8,0},{9,1},... | collective-permute-start | bytes 1327112 | tf_op jit(solution)/shard_map/ppermute | solution.py:61
  97.1 21.7 %collective-permute-start.17 = (bf16[3,144,768]{2,1,0:T(8,128)(2,1)}, bf16[3,144,768]{2,1,0:T(8,128)(2,1)}, u32[]{:S(2)}, u32[]{:S(2)}) collective-permute-start(bf16[3,144,768]{2,1,0:T(8,128)(2,1)} %collective-permute-done.11), channel_id=1, source_target_pairs={{0,8},{1,9},{2,10},{3,11},{4,12},{5,13},{6,14},{7,15},{8,0},{9,1},... | collective-permute-start | bytes 1990664 | tf_op jit(solution)/shard_map/ppermute | solution.py:61
  119.9 32.0 %collective-permute-start.25 = (bf16[3,96,768]{2,1,0:T(8,128)(2,1)S(1)}, bf16[3,96,768]{2,1,0:T(8,128)(2,1)S(1)}, u32[]{:S(2)}, u32[]{:S(2)}) collective-permute-start(bf16[3,96,768]{2,1,0:T(8,128)(2,1)S(1)} %pad_maximum_fusion.42), channel_id=1, source_target_pairs={{0,8},{1,9},{2,10},{3,11},{4,12},{5,13},{6,14},{7,15},{8,0},{9,1},... | collective-permute-start | bytes 1327112 | tf_op jit(solution)/shard_map/ppermute | solution.py:61
  120.2 31.7 %collective-permute-start.24 = (bf16[3,96,768]{2,1,0:T(8,128)(2,1)S(1)}, bf16[3,96,768]{2,1,0:T(8,128)(2,1)S(1)}, u32[]{:S(2)}, u32[]{:S(2)}) collective-permute-start(bf16[3,96,768]{2,1,0:T(8,128)(2,1)S(1)} %pad_maximum_fusion.42), channel_id=1, source_target_pairs={{0,4},{1,5},{2,6},{3,7},{4,0},{5,1},{6,2},{7,3},{8,12},{9,13},{10,... | collective-permute-start | bytes 1327112 | tf_op jit(solution)/shard_map/ppermute | solution.py:61
  129.7 22.2 %collective-permute-start.26 = (bf16[2,144,768]{2,1,0:T(8,128)(2,1)S(1)}, bf16[2,144,768]{2,1,0:T(8,128)(2,1)S(1)}, u32[]{:S(2)}, u32[]{:S(2)}) collective-permute-start(bf16[2,144,768]{2,1,0:T(8,128)(2,1)S(1)} %pad_maximum_fusion.43), channel_id=1, source_target_pairs={{0,2},{1,3},{2,0},{3,1},{4,6},{5,7},{6,4},{7,5},{8,10},{9,11},{10,... | collective-permute-start | bytes 1327112 | tf_op jit(solution)/shard_map/ppermute | solution.py:61
  131.2 20.7 %collective-permute-start.23 = (bf16[3,144,768]{2,1,0:T(8,128)(2,1)}, bf16[3,144,768]{2,1,0:T(8,128)(2,1)S(1)}, u32[]{:S(2)}, u32[]{:S(2)}) collective-permute-start(bf16[3,144,768]{2,1,0:T(8,128)(2,1)} %collective-permute-done.18), channel_id=1, source_target_pairs={{0,8},{1,9},{2,10},{3,11},{4,12},{5,13},{6,14},{7,15},{8,0},{9,1},... | collective-permute-start | bytes 1990664 | tf_op jit(solution)/shard_map/ppermute | solution.py:61
  152.9 23.5 %collective-permute-start.30 = (bf16[3,144,768]{2,1,0:T(8,128)(2,1)S(1)}, bf16[3,144,768]{2,1,0:T(8,128)(2,1)S(1)}, u32[]{:S(2)}, u32[]{:S(2)}) collective-permute-start(bf16[3,144,768]{2,1,0:T(8,128)(2,1)S(1)} %pad_maximum_fusion.35), channel_id=1, source_target_pairs={{0,8},{1,9},{2,10},{3,11},{4,12},{5,13},{6,14},{7,15},{8,0},{9,1},... | collective-permute-start | bytes 1990664 | tf_op jit(solution)/shard_map/ppermute | solution.py:61
  154.0 22.5 %collective-permute-start.29 = (bf16[3,144,768]{2,1,0:T(8,128)(2,1)S(1)}, bf16[3,144,768]{2,1,0:T(8,128)(2,1)}, u32[]{:S(2)}, u32[]{:S(2)}) collective-permute-start(bf16[3,144,768]{2,1,0:T(8,128)(2,1)S(1)} %pad_maximum_fusion.35), channel_id=1, source_target_pairs={{0,4},{1,5},{2,6},{3,7},{4,0},{5,1},{6,2},{7,3},{8,12},{9,13},{10,... | collective-permute-start | bytes 1990664 | tf_op jit(solution)/shard_map/ppermute | solution.py:61
  155.1 21.4 %collective-permute-start.31 = (bf16[2,144,768]{2,1,0:T(8,128)(2,1)S(1)}, bf16[2,144,768]{2,1,0:T(8,128)(2,1)S(1)}, u32[]{:S(2)}, u32[]{:S(2)}) collective-permute-start(bf16[2,144,768]{2,1,0:T(8,128)(2,1)S(1)} %pad_maximum_fusion.44), channel_id=1, source_target_pairs={{0,2},{1,3},{2,0},{3,1},{4,6},{5,7},{6,4},{7,5},{8,10},{9,11},{10,... | collective-permute-start | bytes 1327112 | tf_op jit(solution)/shard_map/ppermute | solution.py:61
  155.2 21.3 %collective-permute-start.28 = (bf16[3,96,768]{2,1,0:T(8,128)(2,1)S(1)}, bf16[3,96,768]{2,1,0:T(8,128)(2,1)S(1)}, u32[]{:S(2)}, u32[]{:S(2)}) collective-permute-start(bf16[3,96,768]{2,1,0:T(8,128)(2,1)S(1)} %collective-permute-done.24), channel_id=1, source_target_pairs={{0,8},{1,9},{2,10},{3,11},{4,12},{5,13},{6,14},{7,15},{8,0},{9,1},... | collective-permute-start | bytes 1327112 | tf_op jit(solution)/shard_map/ppermute | solution.py:61
  179.3 19.1 %collective-permute-start.36 = (bf16[3,144,768]{2,1,0:T(8,128)(2,1)}, bf16[3,144,768]{2,1,0:T(8,128)(2,1)}, u32[]{:S(2)}, u32[]{:S(2)}) collective-permute-start(bf16[3,144,768]{2,1,0:T(8,128)(2,1)} %pad_maximum_fusion.36), channel_id=1, source_target_pairs={{0,8},{1,9},{2,10},{3,11},{4,12},{5,13},{6,14},{7,15},{8,0},{9,1},... | collective-permute-start | bytes 1990664 | tf_op jit(solution)/shard_map/ppermute | solution.py:61
  180.1 23.5 %collective-permute-start.34 = (bf16[3,144,768]{2,1,0:T(8,128)(2,1)}, bf16[3,144,768]{2,1,0:T(8,128)(2,1)}, u32[]{:S(2)}, u32[]{:S(2)}) collective-permute-start(bf16[3,144,768]{2,1,0:T(8,128)(2,1)} %collective-permute-done.29), channel_id=1, source_target_pairs={{0,8},{1,9},{2,10},{3,11},{4,12},{5,13},{6,14},{7,15},{8,0},{9,1},... | collective-permute-start | bytes 1990664 | tf_op jit(solution)/shard_map/ppermute | solution.py:61
  240.8 19.8 %collective-permute-start.42 = (bf16[384,768]{1,0:T(8,128)(2,1)}, bf16[384,768]{1,0:T(8,128)(2,1)}, u32[]{:S(2)}, u32[]{:S(2)}) collective-permute-start(bf16[384,768]{1,0:T(8,128)(2,1)} %get-tuple-element.680), channel_id=1, source_target_pairs={{0,16},{1,17},{2,18},{3,19},{4,20},{5,21},{6,22},{7,23},{8,24},{9,... | collective-permute-start | bytes 1769480 | tf_op jit(solution)/shard_map/ppermute | solution.py:61
  271.7 28.9 %collective-permute-start.46 = (bf16[4,144,768]{2,1,0:T(8,128)(2,1)}, bf16[4,144,768]{2,1,0:T(8,128)(2,1)}, u32[]{:S(2)}, u32[]{:S(2)}) collective-permute-start(bf16[4,144,768]{2,1,0:T(8,128)(2,1)} %add_convert_fusion.13), channel_id=1, source_target_pairs={{0,4},{1,5},{2,6},{3,7},{4,0},{5,1},{6,2},{7,3},{8,12},{9,13},{10,... | collective-permute-start | bytes 2654216 | tf_op jit(solution)/shard_map/ppermute | solution.py:61
  307.3 20.7 %collective-permute-start.47 = (bf16[4,4,112,768]{3,2,1,0:T(8,128)(2,1)S(1)}, bf16[4,4,112,768]{3,2,1,0:T(8,128)(2,1)S(1)}, u32[]{:S(2)}, u32[]{:S(2)}) collective-permute-start(bf16[4,4,112,768]{3,2,1,0:T(8,128)(2,1)S(1)} %get-tuple-element.706), channel_id=1, source_target_pairs={{0,16},{1,17},{2,18},{3,19},{4,20},{5,21},{6,22},{7,23},{8,24},{9,... | collective-permute-start | bytes 8257544 | tf_op jit(solution)/shard_map/ppermute | solution.py:61
  317.7 20.0 %collective-permute-start.52 = (bf16[4,144,768]{2,1,0:T(8,128)(2,1)S(1)}, bf16[4,144,768]{2,1,0:T(8,128)(2,1)S(1)}, u32[]{:S(2)}, u32[]{:S(2)}) collective-permute-start(bf16[4,144,768]{2,1,0:T(8,128)(2,1)S(1)} %add_convert_fusion.11), channel_id=1, source_target_pairs={{0,4},{1,5},{2,6},{3,7},{4,0},{5,1},{6,2},{7,3},{8,12},{9,13},{10,... | collective-permute-start | bytes 2654216 | tf_op jit(solution)/shard_map/ppermute | solution.py:61
  331.2 28.7 %collective-permute-start.54 = (bf16[4,112,768]{2,1,0:T(8,128)(2,1)S(1)}, bf16[4,112,768]{2,1,0:T(8,128)(2,1)S(1)}, u32[]{:S(2)}, u32[]{:S(2)}) collective-permute-start(bf16[4,112,768]{2,1,0:T(8,128)(2,1)S(1)} %get-tuple-element.732), channel_id=1, source_target_pairs={{0,8},{1,9},{2,10},{3,11},{4,12},{5,13},{6,14},{7,15},{8,0},{9,1},... | collective-permute-start | bytes 2064392 | tf_op jit(solution)/shard_map/ppermute | solution.py:61
  352.2 21.3 %collective-permute-start.57 = (bf16[4,112,768]{2,1,0:T(8,128)(2,1)S(1)}, bf16[4,112,768]{2,1,0:T(8,128)(2,1)S(1)}, u32[]{:S(2)}, u32[]{:S(2)}) collective-permute-start(bf16[4,112,768]{2,1,0:T(8,128)(2,1)S(1)} %fusion.32), channel_id=1, source_target_pairs={{0,4},{1,5},{2,6},{3,7},{4,0},{5,1},{6,2},{7,3},{8,12},{9,13},{10,... | collective-permute-start | bytes 2064392 | tf_op jit(solution)/shard_map/ppermute | solution.py:61
  364.0 24.9 %collective-permute-start.60 = (bf16[4,144,768]{2,1,0:T(8,128)(2,1)S(1)}, bf16[4,144,768]{2,1,0:T(8,128)(2,1)S(1)}, u32[]{:S(2)}, u32[]{:S(2)}) collective-permute-start(bf16[4,144,768]{2,1,0:T(8,128)(2,1)S(1)} %bitcast.546), channel_id=1, source_target_pairs={{0,8},{1,9},{2,10},{3,11},{4,12},{5,13},{6,14},{7,15},{8,0},{9,1},... | collective-permute-start | bytes 2654216 | tf_op jit(solution)/shard_map/ppermute | solution.py:61
  384.9 27.9 %collective-permute-start.64 = (bf16[4,144,768]{2,1,0:T(8,128)(2,1)}, bf16[4,144,768]{2,1,0:T(8,128)(2,1)}, u32[]{:S(2)}, u32[]{:S(2)}) collective-permute-start(bf16[4,144,768]{2,1,0:T(8,128)(2,1)} %add_convert_fusion.9), channel_id=1, source_target_pairs={{0,4},{1,5},{2,6},{3,7},{4,0},{5,1},{6,2},{7,3},{8,12},{9,13},{10,... | collective-permute-start | bytes 2654216 | tf_op jit(solution)/shard_map/ppermute | solution.py:61
  422.9 45.0 %collective-permute-start.77 = (bf16[288,768]{1,0:T(8,128)(2,1)S(1)}, bf16[288,768]{1,0:T(8,128)(2,1)S(1)}, u32[]{:S(2)}, u32[]{:S(2)}) collective-permute-start(bf16[288,768]{1,0:T(8,128)(2,1)S(1)} %copy-done.36), channel_id=1, source_target_pairs={{0,16},{1,17},{2,18},{3,19},{4,20},{5,21},{6,22},{7,23},{8,24},{9,... | collective-permute-start | bytes 1327112 | tf_op jit(solution)/shard_map/ppermute | solution.py:527
  424.2 44.9 %collective-permute-start.78 = (bf16[288,768]{1,0:T(8,128)(2,1)S(1)}, bf16[288,768]{1,0:T(8,128)(2,1)S(1)}, u32[]{:S(2)}, u32[]{:S(2)}) collective-permute-start(bf16[288,768]{1,0:T(8,128)(2,1)S(1)} %copy-done.90), channel_id=1, source_target_pairs={{0,16},{1,17},{2,18},{3,19},{4,20},{5,21},{6,22},{7,23},{8,24},{9,... | collective-permute-start | bytes 1327112 | tf_op jit(solution)/shard_map/ppermute | solution.py:527
  436.9 27.0 %collective-permute-start.69 = (bf16[2,4,112,768]{3,2,1,0:T(8,128)(2,1)S(1)}, bf16[2,4,112,768]{3,2,1,0:T(8,128)(2,1)S(1)}, u32[]{:S(2)}, u32[]{:S(2)}) collective-permute-start(bf16[2,4,112,768]{3,2,1,0:T(8,128)(2,1)S(1)} %stack.315), channel_id=1, source_target_pairs={{0,8},{1,9},{2,10},{3,11},{4,12},{5,13},{6,14},{7,15},{8,0},{9,1},... | collective-permute-start | bytes 4128776 | tf_op jit(solution)/shard_map/ppermute | solution.py:61
  439.3 21.7 %collective-permute-start.70 = (bf16[4,144,768]{2,1,0:T(8,128)(2,1)S(1)}, bf16[4,144,768]{2,1,0:T(8,128)(2,1)S(1)}, u32[]{:S(2)}, u32[]{:S(2)}) collective-permute-start(bf16[4,144,768]{2,1,0:T(8,128)(2,1)S(1)} %add_convert_fusion.8), channel_id=1, source_target_pairs={{0,4},{1,5},{2,6},{3,7},{4,0},{5,1},{6,2},{7,3},{8,12},{9,13},{10,... | collective-permute-start | bytes 2654216 | tf_op jit(solution)/shard_map/ppermute | solution.py:61
  526.7 20.6 %collective-permute-start.95 = (bf16[4,96,768]{2,1,0:T(8,128)(2,1)S(1)}, bf16[4,96,768]{2,1,0:T(8,128)(2,1)S(1)}, u32[]{:S(2)}, u32[]{:S(2)}) collective-permute-start(bf16[4,96,768]{2,1,0:T(8,128)(2,1)S(1)} %get-tuple-element.779), channel_id=1, source_target_pairs={{16,0},{17,1},{18,2},{19,3},{20,4},{21,5},{22,6},{23,7},{24,8},{25... | collective-permute-start | bytes 1769480 | tf_op jit(solution)/shard_map/ppermute | solution.py:527
  (226 other events, 2244.9 us)

commit v11 on v10

--- a/solution.py
+++ b/solution.py
@@ -456,14 +456,11 @@
         return full[:2].reshape(-1, features), full[2]
 
     a0, p0 = far(a0), near(p0)
-    a0, p0, q0 = together(a0, p0, q0)
+    a0, p0, q0, norms = together(a0, p0, q0, norms)
     a0, p0, q0 = first(a0), far(p0), near(q0)
     a0, p0, q0, a1 = together(a0, p0, q0, a1)
     a0, p0, q0, a1 = second(a0), first(p0), far(q0), near(a1)
-    places = [jnp.bitwise_xor(in_plane, e) for e in range(PLANE)]
-    places += [jnp.bitwise_xor(in_plane, crossed(e)) for e in range(PLANE)]
-    flags = jnp.stack([is_first.astype(jnp.int32)] + places)
-    a0, p0, q0, a1, p1, norms, seed, flags = together(a0, p0, q0, a1, p1, norms, seed, flags)
+    a0, p0, q0, a1, p1 = together(a0, p0, q0, a1, p1)
     p0, q0, a1, p1 = second(p0), first(q0), far(a1), near(p1)
     attn0 = attn_weights(a0)
     projected0, context0, sum0, norm0 = attn_forward(start, attn0, norms[0], slopes, seqs)
@@ -477,7 +474,10 @@
     feed_q0 = feed_weights(q0)
     gated_q0, hidden_q0, more = feed_forward(all0, feed_q0)
     mixed = mixed + more
-    mixed, a1, p1, q1 = together(mixed, a1, p1, q1)
+    places = [jnp.bitwise_xor(in_plane, e) for e in range(PLANE)]
+    places += [jnp.bitwise_xor(in_plane, crossed(e)) for e in range(PLANE)]
+    flags = jnp.stack([is_first.astype(jnp.int32)] + places)
+    mixed, a1, p1, q1, seed, flags = together(mixed, a1, p1, q1, seed, flags)
     p1, q1 = second(p1), first(q1)
     attn1 = attn_weights(a1)
     total0 = norm0 + join_rows(mixed)

time: 561 us -> 556 us (level)
  other arithmetic: 98.4 us -> 91.4 us
    unnamed x321 -> x311, local copies, waits for them, and re-layouts: 20.8 us -> 21 us
  transfers between devices with their start and end apart: 99 -> 99, of which waited for: 41 -> 42; matrix products, arithmetic and copies ran while one was open for 29% -> 28% of each run, Pallas kernels for 5% -> 5%
where the time goes in v11:
time: 556 us; the launch traced here: 546 us
  waiting for transfers between devices  192 us (35%)
  starting transfers between devices  112 us (20%)
  other arithmetic  91.4 us (16%)
  matrix products  62.8 us (11%)
  local copies, waits for them, and re-layouts  54 us (10%)
  Pallas kernels  29.3 us (5%)
    ppermute x89, waiting for transfers between devices, exchange(): return lax.ppermute(block, AXES, pairs)  192 us
    ppermute x89, starting transfers between devices, exchange(): return lax.ppermute(block, AXES, pairs)  87.5 us
    dot_general x36, matrix products, dot(): lax.dot_general(a, b, (((ca,), (cb,)), ((), ())), preferred_element_type=...  62.8 us
    ppermute x10, starting transfers between devices, hand_over(): return lax.ppermute(block, AXES, pairs)  24.3 us
    convert_element_type x4, other arithmetic, feed_forward(): hidden = gelu_product(gate_part, up_part).astype(BF16)  22.6 us
    unnamed x311, local copies, waits for them, and re-layouts  21 us
    another operation x20, other arithmetic, assemble(): jnp.stack([jnp.concatenate([own[None], r]) for own, r in zip(chunk['own']...  15.2 us
    convert_element_type x26, other arithmetic, total_low(): return sum((part.astype(F32) for part in parts)).astype(BF16)  14.5 us
  transfers between devices with their start and end apart: 99, of which 42 were waited for; matrix products, arithmetic and copies ran while one was open for 28% of the time, Pallas kernels for 5%

profile of v11, /device:TPU:1, one launch (start us, length us, event | category | flops | bytes accessed | tf_op | source)
XLA Modules:
  0.0 545.8 jit_solution(8755102419061292120)
XLA Ops:
  10.7 5.6 %copy.68 = bf16[1,768,2,768]{1,3,2,0:T(8,128)(2,1)S(1)} copy(bf16[1,768,2,768]{3,2,1,0:T(2,128)(2,1)} %param.17) | data formatting | bytes 4718592 | tf_op jit(solution)/shard_map/optimization_barrier | solution.py:244
  28.0 9.9 %collective-permute-done.2 = bf16[2,96,768]{2,1,0:T(8,128)(2,1)S(1)} collective-permute-done((bf16[2,96,768]{2,1,0:T(8,128)(2,1)S(1)}, bf16[2,96,768]{2,1,0:T(8,128)(2,1)S(1)}, u32[]{:S(2)}, u32[]{:S(2)}) %collective-permute-start.2) | collective-permute-done | bytes 294944 | tf_op jit(solution)/shard_map/ppermute | solution.py:61
  44.8 6.7 %collective-permute-done.10 = bf16[144,768]{1,0:T(8,128)(2,1)S(1)} collective-permute-done((bf16[144,768]{1,0:T(8,128)(2,1)S(1)}, bf16[144,768]{1,0:T(8,128)(2,1)S(1)}, u32[]{:S(2)}, u32[]{:S(2)}) %collective-permute-start.10) | collective-permute-done | bytes 221216 | tf_op jit(solution)/shard_map/ppermute | solution.py:61
  51.4 7.6 %collective-permute-done.9 = bf16[2,144,768]{2,1,0:T(8,128)(2,1)S(1)} collective-permute-done((bf16[2,144,768]{2,1,0:T(8,128)(2,1)S(1)}, bf16[2,144,768]{2,1,0:T(8,128)(2,1)S(1)}, u32[]{:S(2)}, u32[]{:S(2)}) %collective-permute-start.9) | collective-permute-done | bytes 442400 | tf_op jit(solution)/shard_map/ppermute | solution.py:61
  65.6 6.4 %collective-permute-done.15 = bf16[96,768]{1,0:T(8,128)(2,1)S(1)} collective-permute-done((bf16[96,768]{1,0:T(8,128)(2,1)S(1)}, bf16[96,768]{1,0:T(8,128)(2,1)S(1)}, u32[]{:S(2)}, u32[]{:S(2)}) %collective-permute-start.15) | collective-permute-done | bytes 147488 | tf_op jit(solution)/shard_map/ppermute | solution.py:61
  72.0 12.0 %collective-permute-done.14 = bf16[2,144,768]{2,1,0:T(8,128)(2,1)S(1)} collective-permute-done((bf16[2,144,768]{2,1,0:T(8,128)(2,1)S(1)}, bf16[2,144,768]{2,1,0:T(8,128)(2,1)S(1)}, u32[]{:S(2)}, u32[]{:S(2)}) %collective-permute-start.14) | collective-permute-done | bytes 442400 | tf_op jit(solution)/shard_map/ppermute | solution.py:61
  103.2 4.7 attend.2
  110.5 5.7 %collective-permute-done.17 = bf16[3,144,768]{2,1,0:T(8,128)(2,1)} collective-permute-done((bf16[3,144,768]{2,1,0:T(8,128)(2,1)}, bf16[3,144,768]{2,1,0:T(8,128)(2,1)}, u32[]{:S(2)}, u32[]{:S(2)}) %collective-permute-start.17) | collective-permute-done | bytes 663584 | tf_op jit(solution)/shard_map/ppermute | solution.py:61
  129.5 6.2 %multiply_convert_fusion.7 = (bf16[768,768]{1,0:T(8,128)(2,1)S(1)}, f32[768,768]{1,0:T(8,128)}) fusion(f32[768,1536]{1,0:T(8,128)S(1)} %fusion.101), kind=kLoop, calls=%fused_computation.96 | loop fusion | flops 38928384 | bytes 8257536 | tf_op jit(solution)/shard_map/convert_element_type | solution.py:337
  136.8 10.2 %collective-permute-done.26 = bf16[2,144,768]{2,1,0:T(8,128)(2,1)S(1)} collective-permute-done((bf16[2,144,768]{2,1,0:T(8,128)(2,1)S(1)}, bf16[2,144,768]{2,1,0:T(8,128)(2,1)S(1)}, u32[]{:S(2)}, u32[]{:S(2)}) %collective-permute-start.26) | collective-permute-done | bytes 442400 | tf_op jit(solution)/shard_map/ppermute | solution.py:61
  157.6 6.0 %multiply_convert_fusion.6 = (bf16[768,768]{1,0:T(8,128)(2,1)S(1)}, f32[768,768]{1,0:T(8,128)}) fusion(f32[768,1536]{1,0:T(8,128)S(1)} %fusion.103), kind=kLoop, calls=%fused_computation.83 | loop fusion | flops 38928384 | bytes 8257536 | tf_op jit(solution)/shard_map/convert_element_type | solution.py:337
  166.4 5.3 collective-permute-done.31
  185.6 5.1 attend.3
  193.6 5.2 collective-permute-done.34
  207.4 5.2 multiply_convert_fusion.5
  222.3 5.3 multiply_convert_fusion.4
  273.3 10.1 %collective-permute-done.44 = bf16[4,144,768]{2,1,0:T(8,128)(2,1)} collective-permute-done((bf16[4,144,768]{2,1,0:T(8,128)(2,1)S(1)}, bf16[4,144,768]{2,1,0:T(8,128)(2,1)}, u32[]{:S(2)}, u32[]{:S(2)}) %collective-permute-start.44) | collective-permute-done | bytes 884768 | tf_op jit(solution)/shard_map/ppermute | solution.py:61
  283.4 6.1 %attend_back.2 = bf16[384,2304]{1,0:T(8,128)(2,1)} custom-call(f32[12]{0:T(128)} %pad_maximum_fusion.54.slopes_ref, bf16[384,2304]{1,0:T(8,128)(2,1)} %convolution_convert_fusion.2.projected_ref, bf16[384,768]{1,0:T(8,128)(2,1)} %convolution_convert_fusion.15.context_grad_ref), custom_call_target="tpu_custom_call" | custom-call | flops 377487360 | bytes 4128768 | tf_op jit(solution)/shard_map/attend_back/pallas_call | solution.py:181
  295.8 6.3 %collective-permute-done.45 = bf16[4,144,768]{2,1,0:T(8,128)(2,1)} collective-permute-done((bf16[4,144,768]{2,1,0:T(8,128)(2,1)}, bf16[4,144,768]{2,1,0:T(8,128)(2,1)}, u32[]{:S(2)}, u32[]{:S(2)}) %collective-permute-start.45) | collective-permute-done | bytes 884768 | tf_op jit(solution)/shard_map/ppermute | solution.py:61
  314.6 6.4 %collective-permute-done.48 = bf16[4,144,768]{2,1,0:T(8,128)(2,1)S(1)} collective-permute-done((bf16[4,144,768]{2,1,0:T(8,128)(2,1)S(1)}, bf16[4,144,768]{2,1,0:T(8,128)(2,1)S(1)}, u32[]{:S(2)}, u32[]{:S(2)}) %collective-permute-start.48) | collective-permute-done | bytes 884768 | tf_op jit(solution)/shard_map/ppermute | solution.py:61
  336.3 7.5 %collective-permute-done.51 = bf16[4,112,768]{2,1,0:T(8,128)(2,1)S(1)} collective-permute-done((bf16[4,112,768]{2,1,0:T(8,128)(2,1)S(1)}, bf16[4,112,768]{2,1,0:T(8,128)(2,1)S(1)}, u32[]{:S(2)}, u32[]{:S(2)}) %collective-permute-start.51) | collective-permute-done | bytes 688160 | tf_op jit(solution)/shard_map/ppermute | solution.py:61
  389.2 5.7 %attend_back.3 = bf16[384,2304]{1,0:T(8,128)(2,1)} custom-call(f32[12]{0:T(128)} %pad_maximum_fusion.54.slopes_ref, bf16[384,2304]{1,0:T(8,128)(2,1)} %convolution_convert_fusion.3.projected_ref, bf16[384,768]{1,0:T(8,128)(2,1)} %convolution_convert_fusion.14.context_grad_ref), custom_call_target="tpu_custom_call" | custom-call | flops 377487360 | bytes 4128768 | tf_op jit(solution)/shard_map/attend_back/pallas_call | solution.py:181
  407.9 7.4 %collective-permute-done.63 = bf16[4,144,768]{2,1,0:T(8,128)(2,1)} collective-permute-done((bf16[4,144,768]{2,1,0:T(8,128)(2,1)}, bf16[4,144,768]{2,1,0:T(8,128)(2,1)}, u32[]{:S(2)}, u32[]{:S(2)}) %collective-permute-start.63) | collective-permute-done | bytes 884768 | tf_op jit(solution)/shard_map/ppermute | solution.py:61
  422.4 6.9 %collective-permute-done.68 = bf16[4,144,768]{2,1,0:T(8,128)(2,1)S(1)} collective-permute-done((bf16[4,144,768]{2,1,0:T(8,128)(2,1)S(1)}, bf16[4,144,768]{2,1,0:T(8,128)(2,1)S(1)}, u32[]{:S(2)}, u32[]{:S(2)}) %collective-permute-start.68) | collective-permute-done | bytes 884768 | tf_op jit(solution)/shard_map/ppermute | solution.py:61
  441.1 8.7 %collective-permute-done.71 = bf16[2,144,768]{2,1,0:T(8,128)(2,1)S(1)} collective-permute-done((bf16[2,144,768]{2,1,0:T(8,128)(2,1)S(1)}, bf16[2,144,768]{2,1,0:T(8,128)(2,1)S(1)}, u32[]{:S(2)}, u32[]{:S(2)}) %collective-permute-start.71) | collective-permute-done | bytes 442400 | tf_op jit(solution)/shard_map/ppermute | solution.py:61
  449.8 6.4 %collective-permute-done.70 = bf16[4,144,768]{2,1,0:T(8,128)(2,1)S(1)} collective-permute-done((bf16[4,144,768]{2,1,0:T(8,128)(2,1)S(1)}, bf16[4,144,768]{2,1,0:T(8,128)(2,1)S(1)}, u32[]{:S(2)}, u32[]{:S(2)}) %collective-permute-start.70) | collective-permute-done | bytes 884768 | tf_op jit(solution)/shard_map/ppermute | solution.py:61
  465.5 9.4 %collective-permute-done.75 = bf16[144,768]{1,0:T(8,128)(2,1)S(1)} collective-permute-done((bf16[144,768]{1,0:T(8,128)(2,1)S(1)}, bf16[144,768]{1,0:T(8,128)(2,1)S(1)}, u32[]{:S(2)}, u32[]{:S(2)}) %collective-permute-start.75) | collective-permute-done | bytes 221216 | tf_op jit(solution)/shard_map/ppermute | solution.py:61
  481.4 7.8 %collective-permute-done.80 = bf16[144,768]{1,0:T(8,128)(2,1)S(1)} collective-permute-done((bf16[144,768]{1,0:T(8,128)(2,1)S(1)}, bf16[144,768]{1,0:T(8,128)(2,1)S(1)}, u32[]{:S(2)}, u32[]{:S(2)}) %collective-permute-start.80) | collective-permute-done | bytes 221216 | tf_op jit(solution)/shard_map/ppermute | solution.py:61
  490.2 4.4 collective-permute-start.88
  498.5 5.0 collective-permute-done.86
  522.0 4.5 collective-permute-start.95
  534.7 7.7 %settle.1 = (f32[768,2,768]{2,1,0:T(2,128)}, f32[768,768]{1,0:T(8,128)}) custom-call(s32[9]{0:T(128)} %stack.280.flags_ref, bf16[288,768]{1,0:T(8,128)(2,1)} %copy-done.39, bf16[288,768]{1,0:T(8,128)(2,1)} %collective-permute-done.87.refs_1_, bf16[288,768]{1,0:T(8,128)(2,1)} %copy-done.92, bf16[288,768]{1,0:T(8,128)(2,1)} %collective-permute-done.96.refs_3_, ...), custom_call_target="tpu_custom_call" | custom-call | tf_op jit(solution)/shard_map/settle/pallas_call | solution.py:225
  (756 shorter events, 324.4 us)
Async XLA Ops:
  38.0 21.1 %collective-permute-start.9 = (bf16[2,144,768]{2,1,0:T(8,128)(2,1)S(1)}, bf16[2,144,768]{2,1,0:T(8,128)(2,1)S(1)}, u32[]{:S(2)}, u32[]{:S(2)}) collective-permute-start(bf16[2,144,768]{2,1,0:T(8,128)(2,1)S(1)} %pad_maximum_fusion.40), channel_id=1, source_target_pairs={{0,2},{1,3},{2,0},{3,1},{4,6},{5,7},{6,4},{7,5},{8,10},{9,11},{10,... | collective-permute-start | bytes 1327112 | tf_op jit(solution)/shard_map/ppermute | solution.py:61
  38.1 20.9 %collective-permute-start.8 = (bf16[3,96,768]{2,1,0:T(8,128)(2,1)S(1)}, bf16[3,96,768]{2,1,0:T(8,128)(2,1)S(1)}, u32[]{:S(2)}, u32[]{:S(2)}) collective-permute-start(bf16[3,96,768]{2,1,0:T(8,128)(2,1)S(1)} %pad_maximum_fusion.39), channel_id=1, source_target_pairs={{0,8},{1,9},{2,10},{3,11},{4,12},{5,13},{6,14},{7,15},{8,0},{9,1},... | collective-permute-start | bytes 1327112 | tf_op jit(solution)/shard_map/ppermute | solution.py:61
  39.3 19.7 %collective-permute-start.7 = (bf16[3,96,768]{2,1,0:T(8,128)(2,1)S(1)}, bf16[3,96,768]{2,1,0:T(8,128)(2,1)S(1)}, u32[]{:S(2)}, u32[]{:S(2)}) collective-permute-start(bf16[3,96,768]{2,1,0:T(8,128)(2,1)S(1)} %pad_maximum_fusion.39), channel_id=1, source_target_pairs={{0,4},{1,5},{2,6},{3,7},{4,0},{5,1},{6,2},{7,3},{8,12},{9,13},{10,... | collective-permute-start | bytes 1327112 | tf_op jit(solution)/shard_map/ppermute | solution.py:61
  59.1 24.8 %collective-permute-start.13 = (bf16[3,144,768]{2,1,0:T(8,128)(2,1)S(1)}, bf16[3,144,768]{2,1,0:T(8,128)(2,1)S(1)}, u32[]{:S(2)}, u32[]{:S(2)}) collective-permute-start(bf16[3,144,768]{2,1,0:T(8,128)(2,1)S(1)} %pad_maximum_fusion.33), channel_id=1, source_target_pairs={{0,8},{1,9},{2,10},{3,11},{4,12},{5,13},{6,14},{7,15},{8,0},{9,1},... | collective-permute-start | bytes 1990664 | tf_op jit(solution)/shard_map/ppermute | solution.py:61
  60.2 23.7 %collective-permute-start.12 = (bf16[3,144,768]{2,1,0:T(8,128)(2,1)S(1)}, bf16[3,144,768]{2,1,0:T(8,128)(2,1)}, u32[]{:S(2)}, u32[]{:S(2)}) collective-permute-start(bf16[3,144,768]{2,1,0:T(8,128)(2,1)S(1)} %pad_maximum_fusion.33), channel_id=1, source_target_pairs={{0,4},{1,5},{2,6},{3,7},{4,0},{5,1},{6,2},{7,3},{8,12},{9,13},{10,... | collective-permute-start | bytes 1990664 | tf_op jit(solution)/shard_map/ppermute | solution.py:61
  61.5 22.4 %collective-permute-start.14 = (bf16[2,144,768]{2,1,0:T(8,128)(2,1)S(1)}, bf16[2,144,768]{2,1,0:T(8,128)(2,1)S(1)}, u32[]{:S(2)}, u32[]{:S(2)}) collective-permute-start(bf16[2,144,768]{2,1,0:T(8,128)(2,1)S(1)} %pad_maximum_fusion.41), channel_id=1, source_target_pairs={{0,2},{1,3},{2,0},{3,1},{4,6},{5,7},{6,4},{7,5},{8,10},{9,11},{10,... | collective-permute-start | bytes 1327112 | tf_op jit(solution)/shard_map/ppermute | solution.py:61
  61.6 22.3 %collective-permute-start.11 = (bf16[3,96,768]{2,1,0:T(8,128)(2,1)S(1)}, bf16[3,96,768]{2,1,0:T(8,128)(2,1)S(1)}, u32[]{:S(2)}, u32[]{:S(2)}) collective-permute-start(bf16[3,96,768]{2,1,0:T(8,128)(2,1)S(1)} %collective-permute-done.7), channel_id=1, source_target_pairs={{0,8},{1,9},{2,10},{3,11},{4,12},{5,13},{6,14},{7,15},{8,0},{9,1},... | collective-permute-start | bytes 1327112 | tf_op jit(solution)/shard_map/ppermute | solution.py:61
  94.5 21.7 %collective-permute-start.17 = (bf16[3,144,768]{2,1,0:T(8,128)(2,1)}, bf16[3,144,768]{2,1,0:T(8,128)(2,1)}, u32[]{:S(2)}, u32[]{:S(2)}) collective-permute-start(bf16[3,144,768]{2,1,0:T(8,128)(2,1)} %collective-permute-done.12), channel_id=1, source_target_pairs={{0,8},{1,9},{2,10},{3,11},{4,12},{5,13},{6,14},{7,15},{8,0},{9,1},... | collective-permute-start | bytes 1990664 | tf_op jit(solution)/shard_map/ppermute | solution.py:61
  117.2 29.8 %collective-permute-start.25 = (bf16[3,96,768]{2,1,0:T(8,128)(2,1)S(1)}, bf16[3,96,768]{2,1,0:T(8,128)(2,1)S(1)}, u32[]{:S(2)}, u32[]{:S(2)}) collective-permute-start(bf16[3,96,768]{2,1,0:T(8,128)(2,1)S(1)} %pad_maximum_fusion.42), channel_id=1, source_target_pairs={{0,8},{1,9},{2,10},{3,11},{4,12},{5,13},{6,14},{7,15},{8,0},{9,1},... | collective-permute-start | bytes 1327112 | tf_op jit(solution)/shard_map/ppermute | solution.py:61
  117.6 29.5 %collective-permute-start.24 = (bf16[3,96,768]{2,1,0:T(8,128)(2,1)S(1)}, bf16[3,96,768]{2,1,0:T(8,128)(2,1)S(1)}, u32[]{:S(2)}, u32[]{:S(2)}) collective-permute-start(bf16[3,96,768]{2,1,0:T(8,128)(2,1)S(1)} %pad_maximum_fusion.42), channel_id=1, source_target_pairs={{0,4},{1,5},{2,6},{3,7},{4,0},{5,1},{6,2},{7,3},{8,12},{9,13},{10,... | collective-permute-start | bytes 1327112 | tf_op jit(solution)/shard_map/ppermute | solution.py:61
  124.8 22.2 %collective-permute-start.26 = (bf16[2,144,768]{2,1,0:T(8,128)(2,1)S(1)}, bf16[2,144,768]{2,1,0:T(8,128)(2,1)S(1)}, u32[]{:S(2)}, u32[]{:S(2)}) collective-permute-start(bf16[2,144,768]{2,1,0:T(8,128)(2,1)S(1)} %pad_maximum_fusion.43), channel_id=1, source_target_pairs={{0,2},{1,3},{2,0},{3,1},{4,6},{5,7},{6,4},{7,5},{8,10},{9,11},{10,... | collective-permute-start | bytes 1327112 | tf_op jit(solution)/shard_map/ppermute | solution.py:61
  126.4 20.7 %collective-permute-start.23 = (bf16[3,144,768]{2,1,0:T(8,128)(2,1)}, bf16[3,144,768]{2,1,0:T(8,128)(2,1)S(1)}, u32[]{:S(2)}, u32[]{:S(2)}) collective-permute-start(bf16[3,144,768]{2,1,0:T(8,128)(2,1)} %collective-permute-done.18), channel_id=1, source_target_pairs={{0,8},{1,9},{2,10},{3,11},{4,12},{5,13},{6,14},{7,15},{8,0},{9,1},... | collective-permute-start | bytes 1990664 | tf_op jit(solution)/shard_map/ppermute | solution.py:61
  148.1 23.6 %collective-permute-start.30 = (bf16[3,144,768]{2,1,0:T(8,128)(2,1)S(1)}, bf16[3,144,768]{2,1,0:T(8,128)(2,1)S(1)}, u32[]{:S(2)}, u32[]{:S(2)}) collective-permute-start(bf16[3,144,768]{2,1,0:T(8,128)(2,1)S(1)} %pad_maximum_fusion.35), channel_id=1, source_target_pairs={{0,8},{1,9},{2,10},{3,11},{4,12},{5,13},{6,14},{7,15},{8,0},{9,1},... | collective-permute-start | bytes 1990664 | tf_op jit(solution)/shard_map/ppermute | solution.py:61
  149.2 22.5 %collective-permute-start.29 = (bf16[3,144,768]{2,1,0:T(8,128)(2,1)S(1)}, bf16[3,144,768]{2,1,0:T(8,128)(2,1)}, u32[]{:S(2)}, u32[]{:S(2)}) collective-permute-start(bf16[3,144,768]{2,1,0:T(8,128)(2,1)S(1)} %pad_maximum_fusion.35), channel_id=1, source_target_pairs={{0,4},{1,5},{2,6},{3,7},{4,0},{5,1},{6,2},{7,3},{8,12},{9,13},{10,... | collective-permute-start | bytes 1990664 | tf_op jit(solution)/shard_map/ppermute | solution.py:61
  150.3 21.4 %collective-permute-start.31 = (bf16[2,144,768]{2,1,0:T(8,128)(2,1)S(1)}, bf16[2,144,768]{2,1,0:T(8,128)(2,1)S(1)}, u32[]{:S(2)}, u32[]{:S(2)}) collective-permute-start(bf16[2,144,768]{2,1,0:T(8,128)(2,1)S(1)} %pad_maximum_fusion.44), channel_id=1, source_target_pairs={{0,2},{1,3},{2,0},{3,1},{4,6},{5,7},{6,4},{7,5},{8,10},{9,11},{10,... | collective-permute-start | bytes 1327112 | tf_op jit(solution)/shard_map/ppermute | solution.py:61
  150.4 21.3 %collective-permute-start.28 = (bf16[3,96,768]{2,1,0:T(8,128)(2,1)S(1)}, bf16[3,96,768]{2,1,0:T(8,128)(2,1)S(1)}, u32[]{:S(2)}, u32[]{:S(2)}) collective-permute-start(bf16[3,96,768]{2,1,0:T(8,128)(2,1)S(1)} %collective-permute-done.24), channel_id=1, source_target_pairs={{0,8},{1,9},{2,10},{3,11},{4,12},{5,13},{6,14},{7,15},{8,0},{9,1},... | collective-permute-start | bytes 1327112 | tf_op jit(solution)/shard_map/ppermute | solution.py:61
  174.4 19.2 %collective-permute-start.36 = (bf16[3,144,768]{2,1,0:T(8,128)(2,1)}, bf16[3,144,768]{2,1,0:T(8,128)(2,1)}, u32[]{:S(2)}, u32[]{:S(2)}) collective-permute-start(bf16[3,144,768]{2,1,0:T(8,128)(2,1)} %pad_maximum_fusion.36), channel_id=1, source_target_pairs={{0,8},{1,9},{2,10},{3,11},{4,12},{5,13},{6,14},{7,15},{8,0},{9,1},... | collective-permute-start | bytes 1990664 | tf_op jit(solution)/shard_map/ppermute | solution.py:61
  174.9 18.7 %collective-permute-start.35 = (bf16[3,144,768]{2,1,0:T(8,128)(2,1)}, bf16[3,144,768]{2,1,0:T(8,128)(2,1)}, u32[]{:S(2)}, u32[]{:S(2)}) collective-permute-start(bf16[3,144,768]{2,1,0:T(8,128)(2,1)} %pad_maximum_fusion.36), channel_id=1, source_target_pairs={{0,4},{1,5},{2,6},{3,7},{4,0},{5,1},{6,2},{7,3},{8,12},{9,13},{10,... | collective-permute-start | bytes 1990664 | tf_op jit(solution)/shard_map/ppermute | solution.py:61
  175.3 23.5 %collective-permute-start.34 = (bf16[3,144,768]{2,1,0:T(8,128)(2,1)}, bf16[3,144,768]{2,1,0:T(8,128)(2,1)}, u32[]{:S(2)}, u32[]{:S(2)}) collective-permute-start(bf16[3,144,768]{2,1,0:T(8,128)(2,1)} %collective-permute-done.29), channel_id=1, source_target_pairs={{0,8},{1,9},{2,10},{3,11},{4,12},{5,13},{6,14},{7,15},{8,0},{9,1},... | collective-permute-start | bytes 1990664 | tf_op jit(solution)/shard_map/ppermute | solution.py:61
  236.0 19.7 %collective-permute-start.42 = (bf16[384,768]{1,0:T(8,128)(2,1)}, bf16[384,768]{1,0:T(8,128)(2,1)}, u32[]{:S(2)}, u32[]{:S(2)}) collective-permute-start(bf16[384,768]{1,0:T(8,128)(2,1)} %get-tuple-element.680), channel_id=1, source_target_pairs={{0,16},{1,17},{2,18},{3,19},{4,20},{5,21},{6,22},{7,23},{8,24},{9,... | collective-permute-start | bytes 1769480 | tf_op jit(solution)/shard_map/ppermute | solution.py:61
  266.9 28.9 %collective-permute-start.46 = (bf16[4,144,768]{2,1,0:T(8,128)(2,1)}, bf16[4,144,768]{2,1,0:T(8,128)(2,1)}, u32[]{:S(2)}, u32[]{:S(2)}) collective-permute-start(bf16[4,144,768]{2,1,0:T(8,128)(2,1)} %add_convert_fusion.13), channel_id=1, source_target_pairs={{0,4},{1,5},{2,6},{3,7},{4,0},{5,1},{6,2},{7,3},{8,12},{9,13},{10,... | collective-permute-start | bytes 2654216 | tf_op jit(solution)/shard_map/ppermute | solution.py:61
  302.4 20.7 %collective-permute-start.47 = (bf16[4,4,112,768]{3,2,1,0:T(8,128)(2,1)S(1)}, bf16[4,4,112,768]{3,2,1,0:T(8,128)(2,1)S(1)}, u32[]{:S(2)}, u32[]{:S(2)}) collective-permute-start(bf16[4,4,112,768]{3,2,1,0:T(8,128)(2,1)S(1)} %get-tuple-element.706), channel_id=1, source_target_pairs={{0,16},{1,17},{2,18},{3,19},{4,20},{5,21},{6,22},{7,23},{8,24},{9,... | collective-permute-start | bytes 8257544 | tf_op jit(solution)/shard_map/ppermute | solution.py:61
  312.9 20.0 %collective-permute-start.52 = (bf16[4,144,768]{2,1,0:T(8,128)(2,1)S(1)}, bf16[4,144,768]{2,1,0:T(8,128)(2,1)S(1)}, u32[]{:S(2)}, u32[]{:S(2)}) collective-permute-start(bf16[4,144,768]{2,1,0:T(8,128)(2,1)S(1)} %add_convert_fusion.11), channel_id=1, source_target_pairs={{0,4},{1,5},{2,6},{3,7},{4,0},{5,1},{6,2},{7,3},{8,12},{9,13},{10,... | collective-permute-start | bytes 2654216 | tf_op jit(solution)/shard_map/ppermute | solution.py:61
  326.3 28.7 %collective-permute-start.54 = (bf16[4,112,768]{2,1,0:T(8,128)(2,1)S(1)}, bf16[4,112,768]{2,1,0:T(8,128)(2,1)S(1)}, u32[]{:S(2)}, u32[]{:S(2)}) collective-permute-start(bf16[4,112,768]{2,1,0:T(8,128)(2,1)S(1)} %get-tuple-element.732), channel_id=1, source_target_pairs={{0,8},{1,9},{2,10},{3,11},{4,12},{5,13},{6,14},{7,15},{8,0},{9,1},... | collective-permute-start | bytes 2064392 | tf_op jit(solution)/shard_map/ppermute | solution.py:61
  347.3 21.3 %collective-permute-start.57 = (bf16[4,112,768]{2,1,0:T(8,128)(2,1)S(1)}, bf16[4,112,768]{2,1,0:T(8,128)(2,1)S(1)}, u32[]{:S(2)}, u32[]{:S(2)}) collective-permute-start(bf16[4,112,768]{2,1,0:T(8,128)(2,1)S(1)} %fusion.32), channel_id=1, source_target_pairs={{0,4},{1,5},{2,6},{3,7},{4,0},{5,1},{6,2},{7,3},{8,12},{9,13},{10,... | collective-permute-start | bytes 2064392 | tf_op jit(solution)/shard_map/ppermute | solution.py:61
  359.1 24.9 %collective-permute-start.60 = (bf16[4,144,768]{2,1,0:T(8,128)(2,1)S(1)}, bf16[4,144,768]{2,1,0:T(8,128)(2,1)S(1)}, u32[]{:S(2)}, u32[]{:S(2)}) collective-permute-start(bf16[4,144,768]{2,1,0:T(8,128)(2,1)S(1)} %bitcast.546), channel_id=1, source_target_pairs={{0,8},{1,9},{2,10},{3,11},{4,12},{5,13},{6,14},{7,15},{8,0},{9,1},... | collective-permute-start | bytes 2654216 | tf_op jit(solution)/shard_map/ppermute | solution.py:61
  380.0 27.9 %collective-permute-start.64 = (bf16[4,144,768]{2,1,0:T(8,128)(2,1)}, bf16[4,144,768]{2,1,0:T(8,128)(2,1)}, u32[]{:S(2)}, u32[]{:S(2)}) collective-permute-start(bf16[4,144,768]{2,1,0:T(8,128)(2,1)} %add_convert_fusion.9), channel_id=1, source_target_pairs={{0,4},{1,5},{2,6},{3,7},{4,0},{5,1},{6,2},{7,3},{8,12},{9,13},{10,... | collective-permute-start | bytes 2654216 | tf_op jit(solution)/shard_map/ppermute | solution.py:61
  418.0 45.0 %collective-permute-start.77 = (bf16[288,768]{1,0:T(8,128)(2,1)S(1)}, bf16[288,768]{1,0:T(8,128)(2,1)S(1)}, u32[]{:S(2)}, u32[]{:S(2)}) collective-permute-start(bf16[288,768]{1,0:T(8,128)(2,1)S(1)} %copy-done.38), channel_id=1, source_target_pairs={{0,16},{1,17},{2,18},{3,19},{4,20},{5,21},{6,22},{7,23},{8,24},{9,... | collective-permute-start | bytes 1327112 | tf_op jit(solution)/shard_map/ppermute | solution.py:527
  419.3 44.9 %collective-permute-start.78 = (bf16[288,768]{1,0:T(8,128)(2,1)S(1)}, bf16[288,768]{1,0:T(8,128)(2,1)S(1)}, u32[]{:S(2)}, u32[]{:S(2)}) collective-permute-start(bf16[288,768]{1,0:T(8,128)(2,1)S(1)} %copy-done.85), channel_id=1, source_target_pairs={{0,16},{1,17},{2,18},{3,19},{4,20},{5,21},{6,22},{7,23},{8,24},{9,... | collective-permute-start | bytes 1327112 | tf_op jit(solution)/shard_map/ppermute | solution.py:527
  432.0 27.0 %collective-permute-start.69 = (bf16[2,4,112,768]{3,2,1,0:T(8,128)(2,1)S(1)}, bf16[2,4,112,768]{3,2,1,0:T(8,128)(2,1)S(1)}, u32[]{:S(2)}, u32[]{:S(2)}) collective-permute-start(bf16[2,4,112,768]{3,2,1,0:T(8,128)(2,1)S(1)} %stack.315), channel_id=1, source_target_pairs={{0,8},{1,9},{2,10},{3,11},{4,12},{5,13},{6,14},{7,15},{8,0},{9,1},... | collective-permute-start | bytes 4128776 | tf_op jit(solution)/shard_map/ppermute | solution.py:61
  434.4 21.7 %collective-permute-start.70 = (bf16[4,144,768]{2,1,0:T(8,128)(2,1)S(1)}, bf16[4,144,768]{2,1,0:T(8,128)(2,1)S(1)}, u32[]{:S(2)}, u32[]{:S(2)}) collective-permute-start(bf16[4,144,768]{2,1,0:T(8,128)(2,1)S(1)} %add_convert_fusion.8), channel_id=1, source_target_pairs={{0,4},{1,5},{2,6},{3,7},{4,0},{5,1},{6,2},{7,3},{8,12},{9,13},{10,... | collective-permute-start | bytes 2654216 | tf_op jit(solution)/shard_map/ppermute | solution.py:61
  522.0 20.5 %collective-permute-start.95 = (bf16[4,96,768]{2,1,0:T(8,128)(2,1)S(1)}, bf16[4,96,768]{2,1,0:T(8,128)(2,1)S(1)}, u32[]{:S(2)}, u32[]{:S(2)}) collective-permute-start(bf16[4,96,768]{2,1,0:T(8,128)(2,1)S(1)} %get-tuple-element.779), channel_id=1, source_target_pairs={{16,0},{17,1},{18,2},{19,3},{20,4},{21,5},{22,6},{23,7},{24,8},{25... | collective-permute-start | bytes 1769480 | tf_op jit(solution)/shard_map/ppermute | solution.py:527
  (221 other events, 2062.4 us)

commit v12 on v11

--- a/solution.py
+++ b/solution.py
@@ -168,9 +168,7 @@
         in_specs=[pl.BlockSpec(memory_space=pltpu.SMEM), row_block(length, width)],
         out_specs=row_block(length, features),
         out_shape=jax.ShapeDtypeStruct((rows, features), BF16),
-        cost_estimate=pl.CostEstimate(
-            flops=4 * rows * length * features, bytes_accessed=2 * rows * (width + features), transcendentals=rows * length * features // HEAD_DIM
-        ),
+        cost_estimate=pl.CostEstimate(flops=rows, bytes_accessed=rows, transcendentals=0),
         name="attend",
     )(slopes, projected)
 
@@ -188,9 +186,7 @@
         ],
         out_specs=row_block(length, width),
         out_shape=jax.ShapeDtypeStruct((rows, width), BF16),
-        cost_estimate=pl.CostEstimate(
-            flops=10 * rows * length * features, bytes_accessed=2 * rows * (2 * width + features), transcendentals=rows * length * features // HEAD_DIM
-        ),
+        cost_estimate=pl.CostEstimate(flops=rows, bytes_accessed=rows, transcendentals=0),
         name="attend_back",
     )(slopes, projected, context_grad)
 
@@ -548,11 +544,10 @@
 
     q1_own, q1_half, q1_a, q1_b = reduce_open(q1)
     projected_grad = attend_back(projected1, context_grad, slopes, seqs)
+    projected_grad, q1_a, p1_c = together(projected_grad, q1_a, p1_c)
+
     qkv = dot(projected_grad, middle_low, 0, 0).astype(BF16)
-    a1 = attn_terms(qkv, out, [gain_one1, offset_one1, gain_two1, offset_two1])
-    projected_grad, a1, q1_a, p1_c = together(projected_grad, a1, q1_a, p1_c)
-
-    a1 = attn_swap(a1)
+    a1 = attn_swap(attn_terms(qkv, out, [gain_one1, offset_one1, gain_two1, offset_two1]))
     q1_own, q1_c = reduce_turn((q1_own, q1_half, q1_a))
     p1 = reduce_near(p1_own, p1_c, p1_b)
     middle_grad = dot(projected_grad, attn1[0], 1, 0) + sum_grad
@@ -591,12 +586,11 @@
     a1 = reduce_far(a1)
     context_grad, out = context_backward(sum_grad, attn0, context0)
     projected_grad = attend_back(projected0, context_grad, slopes, seqs)
+    late_second = exchange(late, dp_masks=SECOND)
+    projected_grad, q0_a, p0_c, a1, late_second = together(projected_grad, q0_a, p0_c, a1, late_second)
+
     qkv = dot(projected_grad, start, 0, 0).astype(BF16)
-    a0 = attn_terms(qkv, out, [gain_one0, offset_one0, gain_two0, offset_two0])
-    late_second = exchange(late, dp_masks=SECOND)
-    projected_grad, a0, q0_a, p0_c, a1, late_second = together(projected_grad, a0, q0_a, p0_c, a1, late_second)
-
-    a0 = attn_swap(a0)
+    a0 = attn_swap(attn_terms(qkv, out, [gain_one0, offset_one0, gain_two0, offset_two0]))
     q0_own, q0_c = reduce_turn((q0_own, q0_half, q0_a))
     start_grad = dot(projected_grad, attn0[0], 1, 0) + sum_grad
     start_grad, a0, q0_b = together(start_grad, a0, q0_b)

time: 556 us -> 554 us (level)
    unnamed x311 -> x295, local copies, waits for them, and re-layouts: 21 us -> 18.6 us
  transfers between devices with their start and end apart: 99 -> 99, of which waited for: 42 -> 42; matrix products, arithmetic and copies ran while one was open for 28% -> 27% of each run, Pallas kernels for 5% -> 5%
where the time goes in v12:
time: 554 us; the launch traced here: 543 us
  waiting for transfers between devices  190 us (34%)
  starting transfers between devices  113 us (20%)
  other arithmetic  92.3 us (17%)
  matrix products  63.5 us (11%)
  local copies, waits for them, and re-layouts  51.3 us (9%)
  Pallas kernels  28.7 us (5%)
    ppermute x89, waiting for transfers between devices, exchange(): return lax.ppermute(block, AXES, pairs)  190 us
    ppermute x89, starting transfers between devices, exchange(): return lax.ppermute(block, AXES, pairs)  86 us
    dot_general x36, matrix products, dot(): lax.dot_general(a, b, (((ca,), (cb,)), ((), ())), preferred_element_type=...  63.5 us
    ppermute x10, starting transfers between devices, hand_over(): return lax.ppermute(block, AXES, pairs)  27.3 us
    convert_element_type x4, other arithmetic, feed_forward(): hidden = gelu_product(gate_part, up_part).astype(BF16)  22.9 us
    unnamed x295, local copies, waits for them, and re-layouts  18.6 us
    another operation x20, other arithmetic, assemble(): jnp.stack([jnp.concatenate([own[None], r]) for own, r in zip(chunk['own']...  15.2 us
    convert_element_type x26, other arithmetic, total_low(): return sum((part.astype(F32) for part in parts)).astype(BF16)  13.5 us
  transfers between devices with their start and end apart: 99, of which 42 were waited for; matrix products, arithmetic and copies ran while one was open for 27% of the time, Pallas kernels for 5%

profile of v12, /device:TPU:1, one launch (start us, length us, event | category | flops | bytes accessed | tf_op | source)
XLA Modules:
  0.0 542.9 jit_solution(3241997054799950914)
XLA Ops:
  10.7 5.6 %copy.68 = bf16[1,768,2,768]{1,3,2,0:T(8,128)(2,1)S(1)} copy(bf16[1,768,2,768]{3,2,1,0:T(2,128)(2,1)} %param.17) | data formatting | bytes 4718592 | tf_op jit(solution)/shard_map/optimization_barrier | solution.py:240
  28.1 9.8 %collective-permute-done.2 = bf16[2,96,768]{2,1,0:T(8,128)(2,1)S(1)} collective-permute-done((bf16[2,96,768]{2,1,0:T(8,128)(2,1)S(1)}, bf16[2,96,768]{2,1,0:T(8,128)(2,1)S(1)}, u32[]{:S(2)}, u32[]{:S(2)}) %collective-permute-start.2) | collective-permute-done | bytes 294944 | tf_op jit(solution)/shard_map/ppermute | solution.py:61
  44.8 6.7 %collective-permute-done.10 = bf16[144,768]{1,0:T(8,128)(2,1)S(1)} collective-permute-done((bf16[144,768]{1,0:T(8,128)(2,1)S(1)}, bf16[144,768]{1,0:T(8,128)(2,1)S(1)}, u32[]{:S(2)}, u32[]{:S(2)}) %collective-permute-start.10) | collective-permute-done | bytes 221216 | tf_op jit(solution)/shard_map/ppermute | solution.py:61
  51.4 7.6 %collective-permute-done.9 = bf16[2,144,768]{2,1,0:T(8,128)(2,1)S(1)} collective-permute-done((bf16[2,144,768]{2,1,0:T(8,128)(2,1)S(1)}, bf16[2,144,768]{2,1,0:T(8,128)(2,1)S(1)}, u32[]{:S(2)}, u32[]{:S(2)}) %collective-permute-start.9) | collective-permute-done | bytes 442400 | tf_op jit(solution)/shard_map/ppermute | solution.py:61
  65.5 6.4 %collective-permute-done.15 = bf16[96,768]{1,0:T(8,128)(2,1)S(1)} collective-permute-done((bf16[96,768]{1,0:T(8,128)(2,1)S(1)}, bf16[96,768]{1,0:T(8,128)(2,1)S(1)}, u32[]{:S(2)}, u32[]{:S(2)}) %collective-permute-start.15) | collective-permute-done | bytes 147488 | tf_op jit(solution)/shard_map/ppermute | solution.py:61
  71.9 12.0 %collective-permute-done.14 = bf16[2,144,768]{2,1,0:T(8,128)(2,1)S(1)} collective-permute-done((bf16[2,144,768]{2,1,0:T(8,128)(2,1)S(1)}, bf16[2,144,768]{2,1,0:T(8,128)(2,1)S(1)}, u32[]{:S(2)}, u32[]{:S(2)}) %collective-permute-start.14) | collective-permute-done | bytes 442400 | tf_op jit(solution)/shard_map/ppermute | solution.py:61
  103.2 4.7 attend.2
  110.6 5.7 %collective-permute-done.17 = bf16[3,144,768]{2,1,0:T(8,128)(2,1)} collective-permute-done((bf16[3,144,768]{2,1,0:T(8,128)(2,1)}, bf16[3,144,768]{2,1,0:T(8,128)(2,1)}, u32[]{:S(2)}, u32[]{:S(2)}) %collective-permute-start.17) | collective-permute-done | bytes 663584 | tf_op jit(solution)/shard_map/ppermute | solution.py:61
  129.5 6.4 %multiply_convert_fusion.7 = (bf16[768,768]{1,0:T(8,128)(2,1)S(1)}, f32[768,768]{1,0:T(8,128)}) fusion(f32[768,1536]{1,0:T(8,128)S(1)} %fusion.109), kind=kLoop, calls=%fused_computation.106 | loop fusion | flops 38928384 | bytes 8257536 | tf_op jit(solution)/shard_map/convert_element_type | solution.py:333
  137.1 10.0 %collective-permute-done.26 = bf16[2,144,768]{2,1,0:T(8,128)(2,1)S(1)} collective-permute-done((bf16[2,144,768]{2,1,0:T(8,128)(2,1)S(1)}, bf16[2,144,768]{2,1,0:T(8,128)(2,1)S(1)}, u32[]{:S(2)}, u32[]{:S(2)}) %collective-permute-start.26) | collective-permute-done | bytes 442400 | tf_op jit(solution)/shard_map/ppermute | solution.py:61
  157.6 6.0 %multiply_convert_fusion.6 = (bf16[768,768]{1,0:T(8,128)(2,1)S(1)}, f32[768,768]{1,0:T(8,128)}) fusion(f32[768,1536]{1,0:T(8,128)S(1)} %fusion.111), kind=kLoop, calls=%fused_computation.93 | loop fusion | flops 38928384 | bytes 8257536 | tf_op jit(solution)/shard_map/convert_element_type | solution.py:333
  166.4 5.3 collective-permute-done.31
  184.3 4.9 attend.3
  192.1 6.7 %collective-permute-done.34 = bf16[3,144,768]{2,1,0:T(8,128)(2,1)} collective-permute-done((bf16[3,144,768]{2,1,0:T(8,128)(2,1)}, bf16[3,144,768]{2,1,0:T(8,128)(2,1)}, u32[]{:S(2)}, u32[]{:S(2)}) %collective-permute-start.34) | collective-permute-done | bytes 663584 | tf_op jit(solution)/shard_map/ppermute | solution.py:61
  207.4 5.2 multiply_convert_fusion.5
  222.3 5.4 multiply_convert_fusion.4
  272.4 10.1 %collective-permute-done.44 = bf16[4,144,768]{2,1,0:T(8,128)(2,1)} collective-permute-done((bf16[4,144,768]{2,1,0:T(8,128)(2,1)S(1)}, bf16[4,144,768]{2,1,0:T(8,128)(2,1)}, u32[]{:S(2)}, u32[]{:S(2)}) %collective-permute-start.44) | collective-permute-done | bytes 884768 | tf_op jit(solution)/shard_map/ppermute | solution.py:61
  284.6 5.7 %attend_back.2 = bf16[384,2304]{1,0:T(8,128)(2,1)} custom-call(f32[12]{0:T(128)} %pad_maximum_fusion.52.slopes_ref, bf16[384,2304]{1,0:T(8,128)(2,1)} %convolution_convert_fusion.2.projected_ref, bf16[384,768]{1,0:T(8,128)(2,1)} %convolution_convert_fusion.15.context_grad_ref), custom_call_target="tpu_custom_call" | custom-call | flops 384 | bytes 384 | tf_op jit(solution)/shard_map/attend_back/pallas_call | solution.py:179
  312.6 4.7 collective-permute-done.48
  333.0 8.8 %collective-permute-done.51 = bf16[4,112,768]{2,1,0:T(8,128)(2,1)S(1)} collective-permute-done((bf16[4,112,768]{2,1,0:T(8,128)(2,1)S(1)}, bf16[4,112,768]{2,1,0:T(8,128)(2,1)S(1)}, u32[]{:S(2)}, u32[]{:S(2)}) %collective-permute-start.51) | collective-permute-done | bytes 688160 | tf_op jit(solution)/shard_map/ppermute | solution.py:61
  391.0 5.7 %attend_back.3 = bf16[384,2304]{1,0:T(8,128)(2,1)} custom-call(f32[12]{0:T(128)} %pad_maximum_fusion.52.slopes_ref, bf16[384,2304]{1,0:T(8,128)(2,1)} %convolution_convert_fusion.3.projected_ref, bf16[384,768]{1,0:T(8,128)(2,1)} %convolution_convert_fusion.14.context_grad_ref), custom_call_target="tpu_custom_call" | custom-call | flops 384 | bytes 384 | tf_op jit(solution)/shard_map/attend_back/pallas_call | solution.py:179
  399.7 7.5 %collective-permute-done.63 = bf16[4,144,768]{2,1,0:T(8,128)(2,1)} collective-permute-done((bf16[4,144,768]{2,1,0:T(8,128)(2,1)}, bf16[4,144,768]{2,1,0:T(8,128)(2,1)}, u32[]{:S(2)}, u32[]{:S(2)}) %collective-permute-start.63) | collective-permute-done | bytes 884768 | tf_op jit(solution)/shard_map/ppermute | solution.py:61
  419.1 7.3 %collective-permute-done.68 = bf16[4,144,768]{2,1,0:T(8,128)(2,1)S(1)} collective-permute-done((bf16[4,144,768]{2,1,0:T(8,128)(2,1)S(1)}, bf16[4,144,768]{2,1,0:T(8,128)(2,1)S(1)}, u32[]{:S(2)}, u32[]{:S(2)}) %collective-permute-start.68) | collective-permute-done | bytes 884768 | tf_op jit(solution)/shard_map/ppermute | solution.py:61
  436.1 9.6 %collective-permute-done.71 = bf16[2,144,768]{2,1,0:T(8,128)(2,1)S(1)} collective-permute-done((bf16[2,144,768]{2,1,0:T(8,128)(2,1)S(1)}, bf16[2,144,768]{2,1,0:T(8,128)(2,1)S(1)}, u32[]{:S(2)}, u32[]{:S(2)}) %collective-permute-start.71) | collective-permute-done | bytes 442400 | tf_op jit(solution)/shard_map/ppermute | solution.py:61
  446.3 6.9 %collective-permute-done.70 = bf16[4,144,768]{2,1,0:T(8,128)(2,1)S(1)} collective-permute-done((bf16[4,144,768]{2,1,0:T(8,128)(2,1)S(1)}, bf16[4,144,768]{2,1,0:T(8,128)(2,1)S(1)}, u32[]{:S(2)}, u32[]{:S(2)}) %collective-permute-start.70) | collective-permute-done | bytes 884768 | tf_op jit(solution)/shard_map/ppermute | solution.py:61
  462.7 7.3 %collective-permute-done.75 = bf16[144,768]{1,0:T(8,128)(2,1)S(1)} collective-permute-done((bf16[144,768]{1,0:T(8,128)(2,1)S(1)}, bf16[144,768]{1,0:T(8,128)(2,1)S(1)}, u32[]{:S(2)}, u32[]{:S(2)}) %collective-permute-start.75) | collective-permute-done | bytes 221216 | tf_op jit(solution)/shard_map/ppermute | solution.py:61
  476.5 8.6 %collective-permute-done.80 = bf16[144,768]{1,0:T(8,128)(2,1)S(1)} collective-permute-done((bf16[144,768]{1,0:T(8,128)(2,1)S(1)}, bf16[144,768]{1,0:T(8,128)(2,1)S(1)}, u32[]{:S(2)}, u32[]{:S(2)}) %collective-permute-start.80) | collective-permute-done | bytes 221216 | tf_op jit(solution)/shard_map/ppermute | solution.py:61
  485.3 6.6 %collective-permute-start.88 = (bf16[288,768]{1,0:T(8,128)(2,1)S(1)}, bf16[288,768]{1,0:T(8,128)(2,1)S(1)}, u32[]{:S(2)}, u32[]{:S(2)}) collective-permute-start(bf16[288,768]{1,0:T(8,128)(2,1)S(1)} %pad_maximum_fusion.44.refs_0_), channel_id=1, source_target_pairs={{16,0},{17,1},{18,2},{19,3},{20,4},{21,5},{22,6},{23,7},{24,8},{25... | collective-permute-start | bytes 1327112 | tf_op jit(solution)/shard_map/ppermute | solution.py:523
  495.0 5.3 collective-permute-done.86
  519.1 4.5 collective-permute-start.95
  524.1 5.0 collective-permute-start.98
  532.1 7.7 %settle.1 = (f32[768,2,768]{2,1,0:T(2,128)}, f32[768,768]{1,0:T(8,128)}) custom-call(s32[9]{0:T(128)} %stack.280.flags_ref, bf16[288,768]{1,0:T(8,128)(2,1)} %copy-done.37, bf16[288,768]{1,0:T(8,128)(2,1)} %collective-permute-done.87.refs_1_, bf16[288,768]{1,0:T(8,128)(2,1)} %copy-done.90, bf16[288,768]{1,0:T(8,128)(2,1)} %collective-permute-done.96.refs_3_, ...), custom_call_target="tpu_custom_call" | custom-call | tf_op jit(solution)/shard_map/settle/pallas_call | solution.py:221
  (738 shorter events, 319.5 us)
Async XLA Ops:
  37.9 21.1 %collective-permute-start.9 = (bf16[2,144,768]{2,1,0:T(8,128)(2,1)S(1)}, bf16[2,144,768]{2,1,0:T(8,128)(2,1)S(1)}, u32[]{:S(2)}, u32[]{:S(2)}) collective-permute-start(bf16[2,144,768]{2,1,0:T(8,128)(2,1)S(1)} %pad_maximum_fusion.38), channel_id=1, source_target_pairs={{0,2},{1,3},{2,0},{3,1},{4,6},{5,7},{6,4},{7,5},{8,10},{9,11},{10,... | collective-permute-start | bytes 1327112 | tf_op jit(solution)/shard_map/ppermute | solution.py:61
  38.1 20.9 %collective-permute-start.8 = (bf16[3,96,768]{2,1,0:T(8,128)(2,1)S(1)}, bf16[3,96,768]{2,1,0:T(8,128)(2,1)S(1)}, u32[]{:S(2)}, u32[]{:S(2)}) collective-permute-start(bf16[3,96,768]{2,1,0:T(8,128)(2,1)S(1)} %pad_maximum_fusion.37), channel_id=1, source_target_pairs={{0,8},{1,9},{2,10},{3,11},{4,12},{5,13},{6,14},{7,15},{8,0},{9,1},... | collective-permute-start | bytes 1327112 | tf_op jit(solution)/shard_map/ppermute | solution.py:61
  39.3 19.7 %collective-permute-start.7 = (bf16[3,96,768]{2,1,0:T(8,128)(2,1)S(1)}, bf16[3,96,768]{2,1,0:T(8,128)(2,1)S(1)}, u32[]{:S(2)}, u32[]{:S(2)}) collective-permute-start(bf16[3,96,768]{2,1,0:T(8,128)(2,1)S(1)} %pad_maximum_fusion.37), channel_id=1, source_target_pairs={{0,4},{1,5},{2,6},{3,7},{4,0},{5,1},{6,2},{7,3},{8,12},{9,13},{10,... | collective-permute-start | bytes 1327112 | tf_op jit(solution)/shard_map/ppermute | solution.py:61
  59.1 24.8 %collective-permute-start.13 = (bf16[3,144,768]{2,1,0:T(8,128)(2,1)S(1)}, bf16[3,144,768]{2,1,0:T(8,128)(2,1)S(1)}, u32[]{:S(2)}, u32[]{:S(2)}) collective-permute-start(bf16[3,144,768]{2,1,0:T(8,128)(2,1)S(1)} %pad_maximum_fusion.31), channel_id=1, source_target_pairs={{0,8},{1,9},{2,10},{3,11},{4,12},{5,13},{6,14},{7,15},{8,0},{9,1},... | collective-permute-start | bytes 1990664 | tf_op jit(solution)/shard_map/ppermute | solution.py:61
  60.2 23.7 %collective-permute-start.12 = (bf16[3,144,768]{2,1,0:T(8,128)(2,1)S(1)}, bf16[3,144,768]{2,1,0:T(8,128)(2,1)}, u32[]{:S(2)}, u32[]{:S(2)}) collective-permute-start(bf16[3,144,768]{2,1,0:T(8,128)(2,1)S(1)} %pad_maximum_fusion.31), channel_id=1, source_target_pairs={{0,4},{1,5},{2,6},{3,7},{4,0},{5,1},{6,2},{7,3},{8,12},{9,13},{10,... | collective-permute-start | bytes 1990664 | tf_op jit(solution)/shard_map/ppermute | solution.py:61
  61.5 22.4 %collective-permute-start.14 = (bf16[2,144,768]{2,1,0:T(8,128)(2,1)S(1)}, bf16[2,144,768]{2,1,0:T(8,128)(2,1)S(1)}, u32[]{:S(2)}, u32[]{:S(2)}) collective-permute-start(bf16[2,144,768]{2,1,0:T(8,128)(2,1)S(1)} %pad_maximum_fusion.39), channel_id=1, source_target_pairs={{0,2},{1,3},{2,0},{3,1},{4,6},{5,7},{6,4},{7,5},{8,10},{9,11},{10,... | collective-permute-start | bytes 1327112 | tf_op jit(solution)/shard_map/ppermute | solution.py:61
  61.6 22.3 %collective-permute-start.11 = (bf16[3,96,768]{2,1,0:T(8,128)(2,1)S(1)}, bf16[3,96,768]{2,1,0:T(8,128)(2,1)S(1)}, u32[]{:S(2)}, u32[]{:S(2)}) collective-permute-start(bf16[3,96,768]{2,1,0:T(8,128)(2,1)S(1)} %collective-permute-done.7), channel_id=1, source_target_pairs={{0,8},{1,9},{2,10},{3,11},{4,12},{5,13},{6,14},{7,15},{8,0},{9,1},... | collective-permute-start | bytes 1327112 | tf_op jit(solution)/shard_map/ppermute | solution.py:61
  91.9 18.7 %collective-permute-start.19 = (bf16[3,144,768]{2,1,0:T(8,128)(2,1)}, bf16[3,144,768]{2,1,0:T(8,128)(2,1)}, u32[]{:S(2)}, u32[]{:S(2)}) collective-permute-start(bf16[3,144,768]{2,1,0:T(8,128)(2,1)} %pad_maximum_fusion.32), channel_id=1, source_target_pairs={{0,8},{1,9},{2,10},{3,11},{4,12},{5,13},{6,14},{7,15},{8,0},{9,1},... | collective-permute-start | bytes 1990664 | tf_op jit(solution)/shard_map/ppermute | solution.py:61
  117.2 29.8 %collective-permute-start.25 = (bf16[3,96,768]{2,1,0:T(8,128)(2,1)S(1)}, bf16[3,96,768]{2,1,0:T(8,128)(2,1)S(1)}, u32[]{:S(2)}, u32[]{:S(2)}) collective-permute-start(bf16[3,96,768]{2,1,0:T(8,128)(2,1)S(1)} %pad_maximum_fusion.40), channel_id=1, source_target_pairs={{0,8},{1,9},{2,10},{3,11},{4,12},{5,13},{6,14},{7,15},{8,0},{9,1},... | collective-permute-start | bytes 1327112 | tf_op jit(solution)/shard_map/ppermute | solution.py:61
  117.6 29.5 %collective-permute-start.24 = (bf16[3,96,768]{2,1,0:T(8,128)(2,1)S(1)}, bf16[3,96,768]{2,1,0:T(8,128)(2,1)S(1)}, u32[]{:S(2)}, u32[]{:S(2)}) collective-permute-start(bf16[3,96,768]{2,1,0:T(8,128)(2,1)S(1)} %pad_maximum_fusion.40), channel_id=1, source_target_pairs={{0,4},{1,5},{2,6},{3,7},{4,0},{5,1},{6,2},{7,3},{8,12},{9,13},{10,... | collective-permute-start | bytes 1327112 | tf_op jit(solution)/shard_map/ppermute | solution.py:61
  124.8 22.2 %collective-permute-start.26 = (bf16[2,144,768]{2,1,0:T(8,128)(2,1)S(1)}, bf16[2,144,768]{2,1,0:T(8,128)(2,1)S(1)}, u32[]{:S(2)}, u32[]{:S(2)}) collective-permute-start(bf16[2,144,768]{2,1,0:T(8,128)(2,1)S(1)} %pad_maximum_fusion.41), channel_id=1, source_target_pairs={{0,2},{1,3},{2,0},{3,1},{4,6},{5,7},{6,4},{7,5},{8,10},{9,11},{10,... | collective-permute-start | bytes 1327112 | tf_op jit(solution)/shard_map/ppermute | solution.py:61
  126.6 20.5 %collective-permute-start.23 = (bf16[3,144,768]{2,1,0:T(8,128)(2,1)}, bf16[3,144,768]{2,1,0:T(8,128)(2,1)S(1)}, u32[]{:S(2)}, u32[]{:S(2)}) collective-permute-start(bf16[3,144,768]{2,1,0:T(8,128)(2,1)} %collective-permute-done.18), channel_id=1, source_target_pairs={{0,8},{1,9},{2,10},{3,11},{4,12},{5,13},{6,14},{7,15},{8,0},{9,1},... | collective-permute-start | bytes 1990664 | tf_op jit(solution)/shard_map/ppermute | solution.py:61
  148.1 23.6 %collective-permute-start.30 = (bf16[3,144,768]{2,1,0:T(8,128)(2,1)S(1)}, bf16[3,144,768]{2,1,0:T(8,128)(2,1)S(1)}, u32[]{:S(2)}, u32[]{:S(2)}) collective-permute-start(bf16[3,144,768]{2,1,0:T(8,128)(2,1)S(1)} %pad_maximum_fusion.33), channel_id=1, source_target_pairs={{0,8},{1,9},{2,10},{3,11},{4,12},{5,13},{6,14},{7,15},{8,0},{9,1},... | collective-permute-start | bytes 1990664 | tf_op jit(solution)/shard_map/ppermute | solution.py:61
  149.2 22.5 %collective-permute-start.29 = (bf16[3,144,768]{2,1,0:T(8,128)(2,1)S(1)}, bf16[3,144,768]{2,1,0:T(8,128)(2,1)}, u32[]{:S(2)}, u32[]{:S(2)}) collective-permute-start(bf16[3,144,768]{2,1,0:T(8,128)(2,1)S(1)} %pad_maximum_fusion.33), channel_id=1, source_target_pairs={{0,4},{1,5},{2,6},{3,7},{4,0},{5,1},{6,2},{7,3},{8,12},{9,13},{10,... | collective-permute-start | bytes 1990664 | tf_op jit(solution)/shard_map/ppermute | solution.py:61
  150.3 21.4 %collective-permute-start.31 = (bf16[2,144,768]{2,1,0:T(8,128)(2,1)S(1)}, bf16[2,144,768]{2,1,0:T(8,128)(2,1)S(1)}, u32[]{:S(2)}, u32[]{:S(2)}) collective-permute-start(bf16[2,144,768]{2,1,0:T(8,128)(2,1)S(1)} %pad_maximum_fusion.42), channel_id=1, source_target_pairs={{0,2},{1,3},{2,0},{3,1},{4,6},{5,7},{6,4},{7,5},{8,10},{9,11},{10,... | collective-permute-start | bytes 1327112 | tf_op jit(solution)/shard_map/ppermute | solution.py:61
  150.4 21.3 %collective-permute-start.28 = (bf16[3,96,768]{2,1,0:T(8,128)(2,1)S(1)}, bf16[3,96,768]{2,1,0:T(8,128)(2,1)S(1)}, u32[]{:S(2)}, u32[]{:S(2)}) collective-permute-start(bf16[3,96,768]{2,1,0:T(8,128)(2,1)S(1)} %collective-permute-done.24), channel_id=1, source_target_pairs={{0,8},{1,9},{2,10},{3,11},{4,12},{5,13},{6,14},{7,15},{8,0},{9,1},... | collective-permute-start | bytes 1327112 | tf_op jit(solution)/shard_map/ppermute | solution.py:61
  236.0 20.0 %collective-permute-start.42 = (bf16[384,768]{1,0:T(8,128)(2,1)}, bf16[384,768]{1,0:T(8,128)(2,1)}, u32[]{:S(2)}, u32[]{:S(2)}) collective-permute-start(bf16[384,768]{1,0:T(8,128)(2,1)} %get-tuple-element.676), channel_id=1, source_target_pairs={{0,16},{1,17},{2,18},{3,19},{4,20},{5,21},{6,22},{7,23},{8,24},{9,... | collective-permute-start | bytes 1769480 | tf_op jit(solution)/shard_map/ppermute | solution.py:61
  263.9 18.5 %collective-permute-start.44 = (bf16[4,144,768]{2,1,0:T(8,128)(2,1)S(1)}, bf16[4,144,768]{2,1,0:T(8,128)(2,1)}, u32[]{:S(2)}, u32[]{:S(2)}) collective-permute-start(bf16[4,144,768]{2,1,0:T(8,128)(2,1)S(1)} %bitcast.548), channel_id=1, source_target_pairs={{0,8},{1,9},{2,10},{3,11},{4,12},{5,13},{6,14},{7,15},{8,0},{9,1},... | collective-permute-start | bytes 2654216 | tf_op jit(solution)/shard_map/ppermute | solution.py:61
  266.0 26.3 %collective-permute-start.46 = (bf16[4,144,768]{2,1,0:T(8,128)(2,1)}, bf16[4,144,768]{2,1,0:T(8,128)(2,1)}, u32[]{:S(2)}, u32[]{:S(2)}) collective-permute-start(bf16[4,144,768]{2,1,0:T(8,128)(2,1)} %add_convert_fusion.13), channel_id=1, source_target_pairs={{0,4},{1,5},{2,6},{3,7},{4,0},{5,1},{6,2},{7,3},{8,12},{9,13},{10,... | collective-permute-start | bytes 2654216 | tf_op jit(solution)/shard_map/ppermute | solution.py:61
  300.4 19.4 %collective-permute-start.47 = (bf16[4,4,112,768]{3,2,1,0:T(8,128)(2,1)S(1)}, bf16[4,4,112,768]{3,2,1,0:T(8,128)(2,1)S(1)}, u32[]{:S(2)}, u32[]{:S(2)}) collective-permute-start(bf16[4,4,112,768]{3,2,1,0:T(8,128)(2,1)S(1)} %get-tuple-element.702), channel_id=1, source_target_pairs={{0,16},{1,17},{2,18},{3,19},{4,20},{5,21},{6,22},{7,23},{8,24},{9,... | collective-permute-start | bytes 8257544 | tf_op jit(solution)/shard_map/ppermute | solution.py:61
  310.8 20.0 %collective-permute-start.52 = (bf16[4,144,768]{2,1,0:T(8,128)(2,1)S(1)}, bf16[4,144,768]{2,1,0:T(8,128)(2,1)S(1)}, u32[]{:S(2)}, u32[]{:S(2)}) collective-permute-start(bf16[4,144,768]{2,1,0:T(8,128)(2,1)S(1)} %add_convert_fusion.11), channel_id=1, source_target_pairs={{0,4},{1,5},{2,6},{3,7},{4,0},{5,1},{6,2},{7,3},{8,12},{9,13},{10,... | collective-permute-start | bytes 2654216 | tf_op jit(solution)/shard_map/ppermute | solution.py:61
  324.3 28.8 %collective-permute-start.54 = (bf16[4,112,768]{2,1,0:T(8,128)(2,1)S(1)}, bf16[4,112,768]{2,1,0:T(8,128)(2,1)S(1)}, u32[]{:S(2)}, u32[]{:S(2)}) collective-permute-start(bf16[4,112,768]{2,1,0:T(8,128)(2,1)S(1)} %get-tuple-element.728), channel_id=1, source_target_pairs={{0,8},{1,9},{2,10},{3,11},{4,12},{5,13},{6,14},{7,15},{8,0},{9,1},... | collective-permute-start | bytes 2064392 | tf_op jit(solution)/shard_map/ppermute | solution.py:61
  345.1 21.3 %collective-permute-start.57 = (bf16[4,112,768]{2,1,0:T(8,128)(2,1)S(1)}, bf16[4,112,768]{2,1,0:T(8,128)(2,1)S(1)}, u32[]{:S(2)}, u32[]{:S(2)}) collective-permute-start(bf16[4,112,768]{2,1,0:T(8,128)(2,1)S(1)} %fusion.40), channel_id=1, source_target_pairs={{0,4},{1,5},{2,6},{3,7},{4,0},{5,1},{6,2},{7,3},{8,12},{9,13},{10,... | collective-permute-start | bytes 2064392 | tf_op jit(solution)/shard_map/ppermute | solution.py:61
  356.8 25.2 %collective-permute-start.60 = (bf16[4,144,768]{2,1,0:T(8,128)(2,1)S(1)}, bf16[4,144,768]{2,1,0:T(8,128)(2,1)S(1)}, u32[]{:S(2)}, u32[]{:S(2)}) collective-permute-start(bf16[4,144,768]{2,1,0:T(8,128)(2,1)S(1)} %bitcast.546), channel_id=1, source_target_pairs={{0,8},{1,9},{2,10},{3,11},{4,12},{5,13},{6,14},{7,15},{8,0},{9,1},... | collective-permute-start | bytes 2654216 | tf_op jit(solution)/shard_map/ppermute | solution.py:61
  377.6 22.1 %collective-permute-start.64 = (bf16[4,144,768]{2,1,0:T(8,128)(2,1)}, bf16[4,144,768]{2,1,0:T(8,128)(2,1)}, u32[]{:S(2)}, u32[]{:S(2)}) collective-permute-start(bf16[4,144,768]{2,1,0:T(8,128)(2,1)} %add_convert_fusion.9), channel_id=1, source_target_pairs={{0,4},{1,5},{2,6},{3,7},{4,0},{5,1},{6,2},{7,3},{8,12},{9,13},{10,... | collective-permute-start | bytes 2654216 | tf_op jit(solution)/shard_map/ppermute | solution.py:61
  387.0 20.2 %collective-permute-start.63 = (bf16[4,144,768]{2,1,0:T(8,128)(2,1)}, bf16[4,144,768]{2,1,0:T(8,128)(2,1)}, u32[]{:S(2)}, u32[]{:S(2)}) collective-permute-start(bf16[4,144,768]{2,1,0:T(8,128)(2,1)} %bitcast.194), channel_id=1, source_target_pairs={{0,8},{1,9},{2,10},{3,11},{4,12},{5,13},{6,14},{7,15},{8,0},{9,1},... | collective-permute-start | bytes 2654216 | tf_op jit(solution)/shard_map/ppermute | solution.py:61
  415.0 43.0 %collective-permute-start.77 = (bf16[288,768]{1,0:T(8,128)(2,1)}, bf16[288,768]{1,0:T(8,128)(2,1)S(1)}, u32[]{:S(2)}, u32[]{:S(2)}) collective-permute-start(bf16[288,768]{1,0:T(8,128)(2,1)} %pad_maximum_fusion.43.refs_12_), channel_id=1, source_target_pairs={{0,16},{1,17},{2,18},{3,19},{4,20},{5,21},{6,22},{7,23},{8,24},{9,... | collective-permute-start | bytes 1327112 | tf_op jit(solution)/shard_map/ppermute | solution.py:523
  416.3 45.2 %collective-permute-start.78 = (bf16[288,768]{1,0:T(8,128)(2,1)S(1)}, bf16[288,768]{1,0:T(8,128)(2,1)S(1)}, u32[]{:S(2)}, u32[]{:S(2)}) collective-permute-start(bf16[288,768]{1,0:T(8,128)(2,1)S(1)} %copy-done.83), channel_id=1, source_target_pairs={{0,16},{1,17},{2,18},{3,19},{4,20},{5,21},{6,22},{7,23},{8,24},{9,... | collective-permute-start | bytes 1327112 | tf_op jit(solution)/shard_map/ppermute | solution.py:523
  429.0 27.0 %collective-permute-start.69 = (bf16[2,4,112,768]{3,2,1,0:T(8,128)(2,1)S(1)}, bf16[2,4,112,768]{3,2,1,0:T(8,128)(2,1)S(1)}, u32[]{:S(2)}, u32[]{:S(2)}) collective-permute-start(bf16[2,4,112,768]{3,2,1,0:T(8,128)(2,1)S(1)} %stack.315), channel_id=1, source_target_pairs={{0,8},{1,9},{2,10},{3,11},{4,12},{5,13},{6,14},{7,15},{8,0},{9,1},... | collective-permute-start | bytes 4128776 | tf_op jit(solution)/shard_map/ppermute | solution.py:61
  431.5 21.7 %collective-permute-start.70 = (bf16[4,144,768]{2,1,0:T(8,128)(2,1)S(1)}, bf16[4,144,768]{2,1,0:T(8,128)(2,1)S(1)}, u32[]{:S(2)}, u32[]{:S(2)}) collective-permute-start(bf16[4,144,768]{2,1,0:T(8,128)(2,1)S(1)} %add_convert_fusion.8), channel_id=1, source_target_pairs={{0,4},{1,5},{2,6},{3,7},{4,0},{5,1},{6,2},{7,3},{8,12},{9,13},{10,... | collective-permute-start | bytes 2654216 | tf_op jit(solution)/shard_map/ppermute | solution.py:61
  485.3 18.6 %collective-permute-start.88 = (bf16[288,768]{1,0:T(8,128)(2,1)S(1)}, bf16[288,768]{1,0:T(8,128)(2,1)S(1)}, u32[]{:S(2)}, u32[]{:S(2)}) collective-permute-start(bf16[288,768]{1,0:T(8,128)(2,1)S(1)} %pad_maximum_fusion.44.refs_0_), channel_id=1, source_target_pairs={{16,0},{17,1},{18,2},{19,3},{20,4},{21,5},{22,6},{23,7},{24,8},{25... | collective-permute-start | bytes 1327112 | tf_op jit(solution)/shard_map/ppermute | solution.py:523
  519.1 20.7 %collective-permute-start.95 = (bf16[4,96,768]{2,1,0:T(8,128)(2,1)S(1)}, bf16[4,96,768]{2,1,0:T(8,128)(2,1)S(1)}, u32[]{:S(2)}, u32[]{:S(2)}) collective-permute-start(bf16[4,96,768]{2,1,0:T(8,128)(2,1)S(1)} %get-tuple-element.775), channel_id=1, source_target_pairs={{16,0},{17,1},{18,2},{19,3},{20,4},{21,5},{22,6},{23,7},{24,8},{25... | collective-permute-start | bytes 1769480 | tf_op jit(solution)/shard_map/ppermute | solution.py:523
  (213 other events, 2069.2 us)
